TPU v7x, 128 devices: a whole 4x4x4 slice. The times are simulated.
128 devices in a mesh: rep: 16 (over y_hi, x, core), shard: 8 (over z, y_lo).
Axes of the slice: x: 4, y: 4 (y_hi: 2, y_lo: 2; y = y_hi * 2 + y_lo), z: 4, core: 2. Of those that a mesh axis runs over, the one named last changes fastest.
Arguments:
- layer_in: float32 [32768, 1024], P(('rep', 'shard')), may hold values from -6 to 6
- cotangent: float32 [32768, 1024], P(('rep', 'shard')), may hold values from -6 to 6
- seq_lengths: int32 [128, 2], P(('rep', 'shard')), may hold values from 1 to 192, 256 in all within a row
- norm_gain: float32 [1024], P('shard'), may hold values from 0.5 to 1.5
- in_weight: bfloat16 [1024, 4384], P('shard'), may hold values from -0.1875 to 0.1875
- conv_weight: float32 [2304, 4], P('shard'), may hold values from -3 to 3
- conv_bias: float32 [2304], P('shard'), may hold values from -0.5 to 0.5
- step_bias: float32 [32], P('shard'), may hold values from -6.9 to -2.3
- decay_log: float32 [32], P('shard'), may hold values from 0 to 2.77
- skip_gain: float32 [32], P('shard'), may hold values from 0.5 to 1.5
- gate_gain: float32 [2048], P('shard'), may hold values from 0.5 to 1.5
- out_weight: bfloat16 [2048, 1024], P('shard'), may hold values from -0.125 to 0.125
Outputs:
- layer_out: float32 [32768, 1024], P(('rep', 'shard'))
- input_grad: float32 [32768, 1024], P(('rep', 'shard'))
- norm_gain_grad: float32 [1024], P('shard')
- in_weight_grad: float32 [1024, 4384], P('shard')
- conv_weight_grad: float32 [2304, 4], P('shard')
- conv_bias_grad: float32 [2304], P('shard')
- step_bias_grad: float32 [32], P('shard')
- decay_log_grad: float32 [32], P('shard')
- skip_gain_grad: float32 [32], P('shard')
- gate_gain_grad: float32 [2048], P('shard')
- out_weight_grad: float32 [2048, 1024], P('shard')
Inputs may be any that keep to these rules, and one draw needn't show every extreme that they name: `seq_lengths`: each device's row of 2 lengths sums to 256.
All inputs are finite; a program needn't handle non-finite values.
Results may differ from a plain program's by a relative error of at most 0.0064.
Values may be sent and summed in bfloat16 or wider, within the bound.
No kernel may reach another device: no remote copies, remote signals or barrier semaphores. Data moves between devices by JAX's collectives and lax.ppermute only.
A program may use at most 128 MiB of HBM per device.

v0:
```python
import math

import jax
import jax.numpy as jnp
from jax import lax
from jax.sharding import Mesh
from jax.sharding import PartitionSpec as P

SPAN = 256
SHARD = ("shard_0", "shard_1")
REP_SHARD = ("rep", "shard_0", "shard_1")


EPS = 1e-05
HIGH = lax.Precision.HIGHEST


def side_by_side(arrays, axis, dim, along):
    widths = [math.prod(a.shape[along:]) for a in arrays]
    both = jnp.concatenate(
        [a.reshape(*a.shape[:along], w) for a, w in zip(arrays, widths)], axis=along
    )
    result = lax.all_gather(both, axis, axis=dim, tiled=True)
    blocks = jnp.split(result, [sum(widths[:k]) for k in range(1, len(widths))], axis=along)
    return tuple(
        (b.reshape(*result.shape[:along], *a.shape[along:]) for a, b in zip(arrays, blocks))
    )


def sum_by_axis(total, axes):
    for axis in axes:
        total = lax.psum_scatter(total, axis, scatter_dimension=0, tiled=True)
    return total


def in_blocks(shard, dim, size):
    before, after = (shard.shape[:dim], shard.shape[dim + 1 :])
    return jnp.moveaxis(shard.reshape(*before, size, -1, *after), dim, 0)


def sum_at_owner(shard, axis, dim):
    size = lax.axis_size(axis)
    blocks = lax.all_to_all(in_blocks(shard, dim, size), axis, 0, 0, tiled=True)
    return jnp.sum(blocks, axis=0)


def sent_together(arrays, axis, dim, along):
    widths = [math.prod(a.shape[along:]) for a in arrays]
    both = jnp.concatenate(
        [a.reshape(*a.shape[:along], w) for a, w in zip(arrays, widths)], axis=along
    )
    result = sum_at_owner(both, axis, dim)
    blocks = jnp.split(result, [sum(widths[:k]) for k in range(1, len(widths))], axis=along)
    return tuple(
        (b.reshape(*result.shape[:along], *a.shape[along:]) for a, b in zip(arrays, blocks))
    )


def shifted(values, lag):
    zeros_top = jnp.zeros((lag,) + values.shape[1:], values.dtype)
    return jnp.concatenate([zeros_top, values[:-lag]], axis=0)


def segment_ids(lengths_row, count):
    offsets = jnp.cumsum(lengths_row, dtype=jnp.int32) - lengths_row
    places = jnp.arange(count, dtype=jnp.int32)
    return (
        jnp.sum((places[:, None] >= offsets[None, :]).astype(jnp.int32), axis=1, dtype=jnp.int32)
        - 1
    )


def row_product(left, right):
    return lax.dot_general(
        left, right, (((0,), (0,)), ((), ())), preferred_element_type=jnp.float32
    )


def back_product(left, right):
    return lax.dot_general(
        left, right, (((1,), (1,)), ((), ())), preferred_element_type=jnp.float32
    )


def norm_input(inputs, gain_one):
    scaling = lax.rsqrt(jnp.mean(inputs * inputs, axis=1, keepdims=True) + EPS)
    return inputs * scaling * gain_one[None, :]


def mixer(projected, segment, conv_weight, conv_bias, step_bias, decay_log, skip_gain, gate_gain):
    count = projected.shape[0]
    inner = gate_gain.shape[0]
    heads = step_bias.shape[0]
    head_dim = inner // heads
    channels = conv_weight.shape[0]
    state_dim = (channels - inner) // 2
    taps = conv_weight.shape[1]
    gate_part = projected[:, :inner]
    conv_in = projected[:, inner : inner + channels]
    step_raw = projected[:, inner + channels :]
    places = jnp.arange(count, dtype=jnp.int32)
    conv_out = conv_bias[None, :] + conv_weight[:, taps - 1][None, :] * conv_in
    for lag in range(1, taps):
        same = (shifted(segment, lag) == segment) & (places >= lag)
        conv_out = conv_out + jnp.where(
            same[:, None], conv_weight[:, taps - 1 - lag][None, :] * shifted(conv_in, lag), 0.0
        )
    activated = jax.nn.silu(conv_out)
    values = activated[:, :inner].reshape(count, heads, head_dim)
    b_matrix = activated[:, inner : inner + state_dim]
    c_matrix = activated[:, inner + state_dim :]
    step_size = jax.nn.softplus(step_raw + step_bias[None, :])
    decay = -jnp.exp(decay_log)[None, :] * step_size
    blocks = count // SPAN
    values_c = values.reshape(blocks, SPAN, heads, head_dim)
    b_spans = b_matrix.reshape(blocks, SPAN, state_dim)
    c_spans = c_matrix.reshape(blocks, SPAN, state_dim)
    step_c = step_size.reshape(blocks, SPAN, heads)
    cumul = jnp.cumsum(decay.reshape(blocks, SPAN, heads), axis=1)
    seg_c = segment.reshape(blocks, SPAN)
    rows_in = jnp.arange(SPAN, dtype=jnp.int32)
    lower = rows_in[:, None] >= rows_in[None, :]
    allowed = lower[None] & (seg_c[:, :, None] == seg_c[:, None, :])
    cumul_t = jnp.transpose(cumul, (0, 2, 1))
    differ = cumul_t[:, :, :, None] - cumul_t[:, :, None, :]
    weights_l = jnp.exp(jnp.where(allowed[:, None], differ, -10000.0))
    scores = jnp.einsum("cin,cjn->cij", c_spans, b_spans, precision=HIGH)
    mixing = weights_l * scores[:, None]
    scaled_in = values_c * step_c[..., None]
    y_intra = jnp.einsum("chij,cjhp->cihp", mixing, scaled_in, precision=HIGH)
    carried = jnp.zeros((heads, head_dim, state_dim), jnp.float32)
    before_seg = jnp.int32(-1)
    linked = (seg_c[0] == before_seg).astype(jnp.float32)
    reach = jnp.exp(cumul[0]) * linked[:, None]
    inter = jnp.einsum("in,hpn->ihp", c_spans[0], carried, precision=HIGH) * reach[:, :, None]
    pieces = [y_intra[0] + inter]
    y_all = jnp.concatenate(pieces, axis=0) + skip_gain[None, :, None] * values
    gated_pre = y_all.reshape(count, inner) * jax.nn.silu(gate_part)
    scaling = lax.rsqrt(jnp.mean(gated_pre * gated_pre, axis=1, keepdims=True) + EPS)
    return gated_pre * scaling * gate_gain[None, :]


def on_device(
    layer_in,
    cotangent,
    seq_lengths,
    norm_gain,
    in_weight,
    conv_weight,
    conv_bias,
    step_bias,
    decay_log,
    skip_gain,
    gate_gain,
    out_weight,
):
    count = layer_in.shape[0]
    segment = segment_ids(seq_lengths[0], count)
    norm_full, convw_full, convb_full, stepb_full, decay_full, skip_full, gategain_full = (
        lax.all_gather(norm_gain, SHARD, axis=0, tiled=True),
        *side_by_side((conv_weight, conv_bias), SHARD, 0, 1),
        lax.all_gather(step_bias, SHARD, axis=0, tiled=True),
        lax.all_gather(decay_log, SHARD, axis=0, tiled=True),
        lax.all_gather(skip_gain, SHARD, axis=0, tiled=True),
        lax.all_gather(gate_gain, SHARD, axis=0, tiled=True),
    )
    normed_f, norm_back = jax.vjp(norm_input, layer_in, norm_full)
    normed = normed_f.astype(jnp.bfloat16)
    in_whole = lax.all_gather(in_weight, SHARD, axis=0, tiled=True)
    out_whole = lax.all_gather(out_weight, SHARD, axis=0, tiled=True)
    projected = jnp.dot(normed, in_whole, preferred_element_type=jnp.float32)

    def bound_mixer(proj_arg, cw_arg, cb_arg, sb_arg, dl_arg, sk_arg, gg_arg):
        return mixer(proj_arg, segment, cw_arg, cb_arg, sb_arg, dl_arg, sk_arg, gg_arg)

    gated_f, mixer_back = jax.vjp(
        bound_mixer,
        projected,
        convw_full,
        convb_full,
        stepb_full,
        decay_full,
        skip_full,
        gategain_full,
    )
    gated = gated_f.astype(jnp.bfloat16)
    branch_out = jnp.dot(gated, out_whole, preferred_element_type=jnp.float32)
    layer_out = layer_in + branch_out
    cot_low = cotangent.astype(jnp.bfloat16)
    out_owned = lax.psum_scatter(
        row_product(gated, cot_low), SHARD, scatter_dimension=0, tiled=True
    )
    gated_grad = back_product(cot_low, out_whole)
    proj_grad, g_convw, g_convb, g_stepb, g_decay, g_skip, g_gategain = mixer_back(gated_grad)
    proj_low = proj_grad.astype(jnp.bfloat16)
    in_owned = sum_by_axis(row_product(normed, proj_low), SHARD)
    normed_grad = back_product(proj_low, in_whole)
    back_in, g_norm = norm_back(normed_grad)
    input_grad = cotangent + back_in
    small_owned = (
        sum_at_owner(g_norm, SHARD, 0),
        *sent_together((g_convw, g_convb), SHARD, 0, 1),
        sum_at_owner(g_stepb, SHARD, 0),
        sum_at_owner(g_decay, SHARD, 0),
        sum_at_owner(g_skip, SHARD, 0),
        sum_at_owner(g_gategain, SHARD, 0),
    )
    summed = lax.psum((in_owned, out_owned) + tuple(small_owned), "rep")
    in_final = summed[0]
    out_final = summed[1]
    small_final = summed[2:]
    return (
        layer_out,
        input_grad,
        small_final[0],
        in_final,
        small_final[1],
        small_final[2],
        small_final[3],
        small_final[4],
        small_final[5],
        small_final[6],
        out_final,
    )


def solution(mesh):
    split = Mesh(mesh.devices.reshape(mesh.shape["rep"], 4, 2), ("rep", "shard_0", "shard_1"))
    in_specs = (
        P(REP_SHARD, None),
        P(REP_SHARD, None),
        P(REP_SHARD, None),
        P(SHARD),
        P(SHARD, None),
        P(SHARD, None),
        P(SHARD),
        P(SHARD),
        P(SHARD),
        P(SHARD),
        P(SHARD),
        P(SHARD, None),
    )
    out_specs = (
        P(REP_SHARD, None),
        P(REP_SHARD, None),
        P(SHARD),
        P(SHARD, None),
        P(SHARD, None),
        P(SHARD),
        P(SHARD),
        P(SHARD),
        P(SHARD),
        P(SHARD),
        P(SHARD, None),
    )
    return jax.shard_map(
        on_device, mesh=split, in_specs=in_specs, out_specs=out_specs, check_vma=False
    )
```

profile of v0, /device:TPU:1, one launch (start us, length us, event | category | flops | bytes accessed | tf_op | source)
XLA Modules:
  0.0 902.4 jit_solution(6898816657262780517)
XLA Ops:
  9.4 1.2 dynamic-slice
  13.8 19.1 %all-reduce.23 = (f32[32]{0:T(128)S(1)}, f32[32]{0:T(128)S(1)}, f32[32]{0:T(128)S(1)}) all-reduce(f32[32]{0:T(128)S(1)} %dynamic-update-slice, f32[32]{0:T(128)S(1)} %dynamic-update-slice.1, f32[32]{0:T(128)S(1)} %dynamic-update-slice.2), channel_id=1, replica_groups=mesh['rep'=16,'shard_0'=4,'shard_1'=2] {'shard_0','shard_1'}, use_global_device_ids=true, to_apply=%add.18 | all-reduce | flops 96 | bytes 768
  34.5 24.4 %all-gather = f32[8,288,5]{1,2,0:T(8,128)S(1)} all-gather(f32[1,288,5]{1,2,0:T(8,128)S(1)} %maximum_bitcast_fusion), channel_id=1, replica_groups=mesh['rep'=16,'shard_0'=4,'shard_1'=2] {'shard_0','shard_1'}, dimensions={0}, use_global_device_ids=true | all-gather | bytes 51840 | tf_op jit(solution)/shard_map/all_gather | solution.py:23
  59.8 12.5 %all-gather.1 = f32[8,1,128]{2,1,0:T(1,128)S(1)} all-gather(f32[1,1,128]{2,1,0:T(1,128)} %bitcast.154), channel_id=1, replica_groups=mesh['rep'=16,'shard_0'=4,'shard_1'=2] {'shard_0','shard_1'}, dimensions={0}, use_global_device_ids=true | all-gather | bytes 4608 | tf_op jit(solution)/shard_map/all_gather | solution.py:160
  72.3 14.4 %all-gather.2 = f32[8,1,256]{2,1,0:T(1,128)S(1)} all-gather(f32[1,1,256]{2,1,0:T(1,128)} %bitcast.153), channel_id=1, replica_groups=mesh['rep'=16,'shard_0'=4,'shard_1'=2] {'shard_0','shard_1'}, dimensions={0}, use_global_device_ids=true | all-gather | bytes 9216 | tf_op jit(solution)/shard_map/all_gather | solution.py:165
  89.8 104.7 %all-gather.6.cloned.1.call-done = bf16[1024,4384]{0,1:T(8,128)(2,1)} async-done(((bf16[128,4384]{0,1:T(8,128)(2,1)}), bf16[1024,4384]{0,1:T(8,128)(2,1)}) %all-gather.6.cloned.1.call-update) | async-done | bytes 8978448 | tf_op jit(solution)/shard_map/all_gather | solution.py:169
  194.5 6.4 fusion.70
  200.9 2.0 copy-done
  203.7 3.4 slice.94
  207.4 1.7 slice.90
  210.6 7.2 fusion.19
  219.2 1.8 fusion.43
  221.1 9.2 %fusion.22 = f32[256,32,64]{0,2,1:T(8,128)S(1)} fusion(f32[256,32,64]{0,2,1:T(8,128)S(1)} %bitcast.130, f32[256,32,64]{0,2,1:T(8,128)S(1)} %fusion.43, f32[256,256]{1,0:T(8,128)S(1)} %fusion.52, f32[32,256]{1,0:T(8,128)S(1)} %bitcast_add_fusion.2, pred[256,256]{1,0:T(8,128)(4,1)S(1)} %copy-done.27, f32[32]{0:T(128)S(1)} %copy-done.47, ...), kind=kOutput, calls=%fused_computation.38 | convolution fusion | flops 1619525632 | bytes 6717568 | tf_op jit(solution)/shard_map/jvp(chij,cjhp->cihp)/dot_general | solution.py:130
  230.3 3.1 multiply_reduce_fusion.9
  233.4 54.4 %all-gather.8.cloned.1.call-done = bf16[2048,1024]{1,0:T(8,128)(2,1)} async-done(((bf16[256,1024]{1,0:T(8,128)(2,1)}), bf16[2048,1024]{1,0:T(8,128)(2,1)}) %all-gather.8.cloned.1.call-update) | async-done | bytes 4194320 | tf_op jit(solution)/shard_map/all_gather | solution.py:170
  287.8 5.1 multiply_reduce_fusion.5
  292.9 4.6 multiply_reduce_fusion.6
  298.0 1.4 fusion.34
  299.9 11.4 %fusion.6 = (f32[32,256]{1,0:T(8,128)S(1)}, f32[32,256]{1,0:T(8,128)S(1)}, f32[256,256]{1,0:T(8,128)S(1)}) fusion(f32[256,256]{1,0:T(8,128)S(1)} %fusion.52, f32[32,256]{1,0:T(8,128)S(1)} %copy-done.32, pred[256,256]{1,0:T(8,128)(4,1)S(1)} %copy-done.28, f32[32,64,256]{2,1,0:T(8,128)S(1)} %bitcast.128, f32[256,32,64]{0,2,1:T(8,128)S(1)} %bitcast.131, ...), kind=kOutput, calls=%fused_computation.7 | convolution fusion | flops 1629929472 | bytes 4915200 | tf_op jit(solution)/shard_map/transpose(jvp(chij,cjhp->cihp))/dot_general | solution.py:130
  311.3 8.7 fusion.23
  320.8 2.5 reduce-window.19
  323.7 2.7 bitcast_add_fusion.1
  327.4 2.6 multiply_reduce_fusion.4
  330.0 2.3 multiply_reduce_fusion.3
  335.6 1.8 multiply_reduce_fusion.1
  337.5 1.4 copy-done.10
  338.9 8.7 fusion.69
  348.3 5.8 fusion.45
  354.1 151.4 %reduce-scatter.4.cloned.1.call-done = f32[256,4384]{0,1:T(8,128)} async-done(((f32[1024,4384]{0,1:T(8,128)}), f32[256,4384]{0,1:T(8,128)}) %reduce-scatter.4.cloned.1.call-update) | async-done | bytes 4489232 | tf_op jit(solution)/shard_map/reduce_scatter | solution.py:32
  505.6 170.9 %reduce-scatter.8.cloned.1.call-done = f32[256,1024]{1,0:T(8,128)} async-done(((f32[2048,1024]{1,0:T(8,128)}), f32[256,1024]{1,0:T(8,128)}) %reduce-scatter.8.cloned.1.call-update) | async-done | bytes 1048592 | tf_op jit(solution)/shard_map/reduce_scatter | solution.py:190
  676.6 63.3 %reduce-scatter.6.cloned.1.call-done = f32[128,4384]{0,1:T(8,128)} async-done(((f32[256,4384]{0,1:T(8,128)}), f32[128,4384]{0,1:T(8,128)}) %reduce-scatter.6.cloned.1.call-update) | async-done | bytes 2244624 | tf_op jit(solution)/shard_map/reduce_scatter | solution.py:32
  740.8 4.4 all-to-all-start.4
  746.5 4.7 convolution_add_fusion
  751.2 7.3 multiply_reduce_fusion.10
  758.5 5.2 all-to-all-start.2
  763.7 5.4 all-to-all-done.2
  769.0 3.3 all-to-all-start.3
  772.4 5.3 all-to-all-done.3
  777.7 3.3 all-to-all-start
  781.3 5.1 all-to-all-done
  786.4 3.3 all-to-all-start.5
  790.5 4.6 all-to-all-done.5
  795.1 3.3 all-to-all-start.1
  798.4 1.2 fusion.37
  799.8 4.3 all-to-all-done.1
  805.6 63.8 %all-reduce.21 = (f32[128]{0:T(128)}, f32[288,4]{0,1:T(4,128)}, f32[288]{0:T(512)}, f32[4]{0:T(128)}, f32[4]{0:T(128)}, /*index=5*/f32[4]{0:T(128)}, f32[256]{0:T(256)}) all-reduce(f32[128]{0:T(128)S(1)} %reduce_sum.265, f32[288,4]{0,1:T(4,128)S(1)} %split.29, ...), channel_id=1, replica_groups=mesh['rep'=16,'shard_0'=4,'shard_1'=2] {'rep'}, use_global_device_ids=true, to_apply=%region_17.18 | all-reduce | flops 1836 | bytes 14688 | tf_op jit(solution)/shard_map/psum | solution.py:208
  869.4 21.8 %all-reduce.26.cloned.1.call-done = (f32[128,4384]{0,1:T(8,128)}, f32[256,1024]{1,0:T(8,128)}) async-done(((f32[128,4384]{0,1:T(8,128)}, f32[256,1024]{1,0:T(8,128)}), (f32[128,4384]{0,1:T(8,128)}, f32[256,1024]{1,0:T(8,128)})) %all-reduce.26.cloned.1.call-update) | async-done | bytes 3293200 | tf_op jit(solution)/shard_map/psum | solution.py:208
  891.2 3.2 copy.126
  (201 shorter events, 26.9 us)
Async XLA Ops:
  7.2 81.0 %copy-start.3 = (f32[256,1024]{1,0:T(8,128)S(1)}, f32[256,1024]{1,0:T(8,128)}, u32[]{:S(2)}) copy-start(f32[256,1024]{1,0:T(8,128)} %param.12) | copy-start | bytes 3145732
  7.2 187.3 %all-gather.6.cloned.1.call-start = ((), (), s32[]{:S(2)}) async-start(), calls=%async_computation.9 | async-start | bytes 10100736 | tf_op jit(solution)/shard_map/all_gather | solution.py:169
  7.9 279.9 %all-gather.8.cloned.1.call-start = ((), (), s32[]{:S(2)}) async-start(), calls=%async_computation.10 | async-start | bytes 4718592 | tf_op jit(solution)/shard_map/all_gather | solution.py:170
  8.7 496.9 %reduce-scatter.4.cloned.1.call-start = ((), (), s32[]{:S(2)}) async-start(), calls=%async_computation.11 | async-start | bytes 22446080 | tf_op jit(solution)/shard_map/reduce_scatter | solution.py:32
  33.0 55.4 %copy-start.48 = (f32[32]{0:T(128)}, f32[32]{0:T(128)S(1)}, u32[]{:S(2)}) copy-start(f32[32]{0:T(128)S(1)} %get-tuple-element.35) | copy-start | bytes 388
  33.0 167.9 %copy-start.42 = (f32[32]{0:T(128)}, f32[32]{0:T(128)S(1)}, u32[]{:S(2)}) copy-start(f32[32]{0:T(128)S(1)} %get-tuple-element.34) | copy-start | bytes 388
  88.4 112.5 %copy-start.37 = (f32[256]{0:T(256)}, f32[256]{0:T(256)S(1)}, u32[]{:S(2)}) copy-start(f32[256]{0:T(256)S(1)} %multiply_reduce_fusion.12) | copy-start | bytes 3076
  88.4 112.5 %copy-start.44 = (f32[32]{0:T(128)}, f32[32]{0:T(128)S(1)}, u32[]{:S(2)}) copy-start(f32[32]{0:T(128)S(1)} %exponential_negate_fusion) | copy-start | bytes 388
  203.7 3.6 copy-start.1
  207.4 3.2 copy-start.6
  218.0 12.3 %copy-start.20 = (f32[256,2048]{0,1:T(8,128)}, f32[256,2048]{0,1:T(8,128)S(1)}, u32[]{:S(2)}) copy-start(f32[256,2048]{0,1:T(8,128)S(1)} %slice.95) | copy-start | bytes 6291460
  218.0 3.1 copy-start.27
  218.0 3.1 copy-start.47
  218.5 11.7 %copy-start.31 = (f32[32,256]{1,0:T(8,128)}, f32[32,256]{1,0:T(8,128)S(1)}, u32[]{:S(2)}) copy-start(f32[32,256]{1,0:T(8,128)S(1)} %bitcast_add_fusion.2) | copy-start | bytes 98308
  221.0 9.2 %copy-start.17 = (f32[256,32,64]{0,2,1:T(8,128)}, f32[256,32,64]{0,2,1:T(8,128)S(1)}, u32[]{:S(2)}) copy-start(f32[256,32,64]{0,2,1:T(8,128)S(1)} %fusion.43) | copy-start | bytes 6291460
  230.3 3.1 copy-start.15
  233.4 59.5 %copy-start.33 = (f32[256]{0:T(256)}, f32[256]{0:T(256)S(1)}, u32[]{:S(2)}) copy-start(f32[256]{0:T(256)S(1)} %fusion.64) | copy-start | bytes 3076
  287.8 5.1 copy-start.5
  287.8 5.1 copy-start.16
  292.9 4.6 copy-start.18
  297.5 13.7 %copy-start.2 = (f32[256,2048]{0,1:T(8,128)}, f32[256,2048]{0,1:T(8,128)S(1)}, u32[]{:S(2)}) copy-start(f32[256,2048]{0,1:T(8,128)S(1)} %get-tuple-element.38) | copy-start | bytes 6291460
  297.5 2.3 copy-start.28
  311.3 9.5 %copy-start.36 = (f32[256]{0:T(256)S(1)}, f32[256]{0:T(256)}, u32[]{:S(2)}) copy-start(f32[256]{0:T(256)} %get-tuple-element.61) | copy-start | bytes 3076
  323.7 2.9 copy-start.9
  323.7 3.6 copy-start.12
  323.7 3.6 copy-start.41
  327.4 2.6 copy-start.7
  327.4 2.6 copy-start.8
  327.4 2.6 copy-start.39
  327.4 2.6 copy-start.40
  332.3 3.0 slice-start
  335.6 3.3 copy-start.13
  347.7 328.9 %reduce-scatter.8.cloned.1.call-start = ((), (), s32[]{:S(2)}) async-start(), calls=%async_computation.13 | async-start | bytes 9437184 | tf_op jit(solution)/shard_map/reduce_scatter | solution.py:190
  354.1 385.8 %reduce-scatter.6.cloned.1.call-start = ((), (), s32[]{:S(2)}) async-start(), calls=%async_computation.12 | async-start | bytes 6733824 | tf_op jit(solution)/shard_map/reduce_scatter | solution.py:32
  505.6 234.3 %copy-start.29 = (f32[2048]{0:T(1024)S(1)}, f32[2048]{0:T(1024)}, u32[]{:S(2)}) copy-start(f32[2048]{0:T(1024)} %get-tuple-element.37) | copy-start | bytes 24580
  505.6 239.6 %copy-start.49 = (f32[32]{0:T(128)S(1)}, f32[32]{0:T(128)}, u32[]{:S(2)}) copy-start(f32[32]{0:T(128)} %copy-done.48) | copy-start | bytes 388
  505.6 385.6 %all-reduce.26.cloned.1.call-start = ((), (), s32[]{:S(2)}) async-start(), calls=%async_computation.14 | async-start | bytes 6586368 | tf_op jit(solution)/shard_map/psum | solution.py:208
  740.8 17.7 %all-to-all-start.4 = ((f32[8,1,4]{2,1,0:T(1,128)}), f32[8,1,4]{2,1,0:T(1,128)S(1)}, u32[]{:S(2)}, u32[]{:S(2)}) async-start(f32[8,1,4]{2,1,0:T(1,128)} %bitcast.42), calls=%async_computation.6 | async-start | bytes 8192 | tf_op jit(solution)/shard_map/all_to_all | solution.py:43
  746.5 4.7 copy-start.11
  746.5 4.7 copy-start.14
  751.2 29.8 %copy-start.38 = (f32[256]{0:T(256)S(1)}, f32[256]{0:T(256)}, u32[]{:S(2)}) copy-start(f32[256]{0:T(256)} %copy-done.37) | copy-start | bytes 3076
  751.2 47.2 %copy-start.19 = (f32[256,1024]{1,0:T(8,128)S(1)}, f32[256,1024]{1,0:T(8,128)}, u32[]{:S(2)}) copy-start(f32[256,1024]{1,0:T(8,128)} %param.13) | copy-start | bytes 3145732
  758.5 10.5 %all-to-all-start.2 = ((f32[8,1,4]{2,1,0:T(1,128)}), f32[8,1,4]{2,1,0:T(1,128)S(1)}, u32[]{:S(2)}, u32[]{:S(2)}) async-start(f32[8,1,4]{2,1,0:T(1,128)} %bitcast.39), calls=%async_computation.4 | async-start | bytes 8192 | tf_op jit(solution)/shard_map/all_to_all | solution.py:43
  769.0 8.7 all-to-all-start.3
  777.7 8.7 all-to-all-start
  786.4 8.7 all-to-all-start.5
  795.1 9.1 %all-to-all-start.1 = ((f32[8,1,1440]{2,1,0:T(1,128)}), f32[8,1,1440]{2,1,0:T(1,128)S(1)}, u32[]{:S(2)}, u32[]{:S(2)}) async-start(f32[8,1,1440]{2,1,0:T(1,128)} %reshape.565), calls=%async_computation.3 | async-start | bytes 98304 | tf_op jit(solution)/shard_map/all_to_all | solution.py:43
  891.1 3.2 copy-start.22
  (16 other events, 23.1 us)
Sparse Core Ops, SparseCore 0:
  9.6 184.8 all-gather.5
  196.1 91.6 all-gather.7
  347.8 157.7 reduce-scatter.3
  507.8 168.7 reduce-scatter.7
  678.8 60.9 reduce-scatter.5
  742.5 148.5 all-reduce.25
where the time goes:
time: 908 us; the launch traced here: 902 us
  waiting for transfers between devices  593 us (65%)
  blocking collectives  134 us (15%)
  matrix products  71.4 us (8%)
  other arithmetic  38.1 us (4%)
  local copies, waits for them, and re-layouts  26.9 us (3%)
  starting transfers between devices  23 us (3%)
  between operations  15.9 us (2%)
    reduce_scatter x2, waiting for transfers between devices, sum_by_axis(): total = lax.psum_scatter(total, axis, scatter_dimension=0, tiled=True)  215 us
    reduce_scatter x1, waiting for transfers between devices, on_device(): lax.psum_scatter(row_product(gated, cot_low), SHARD, scatter_dimension=0,...  171 us
    all_gather x1, waiting for transfers between devices, on_device(): in_whole = lax.all_gather(in_weight, SHARD, axis=0, tiled=True)  105 us
    psum x1, blocking collectives, on_device(): summed = lax.psum((in_owned, out_owned) + tuple(small_owned), 'rep')  63.8 us
    all_gather x1, waiting for transfers between devices, on_device(): out_whole = lax.all_gather(out_weight, SHARD, axis=0, tiled=True)  54.4 us
    dot_general x3, matrix products, mixer(): y_intra = jnp.einsum('chij,cjhp->cihp', mixing, scaled_in, precision=HIGH)  29.3 us
    all_to_all x6, waiting for transfers between devices, sum_at_owner(): blocks = lax.all_to_all(in_blocks(shard, dim, size), axis, 0, 0, tiled=True)  24.7 us
    all_gather x1, blocking collectives, side_by_side(): result = lax.all_gather(both, axis, axis=dim, tiled=True)  24.4 us
  transfers between devices with their start and end apart: 12, of which 11 were waited for; matrix products, arithmetic and copies ran while one was open for 7% of the time, Pallas kernels for 0%

commit v1 on v0

--- a/solution.py
+++ b/solution.py
@@ -8,7 +8,9 @@
 
 SPAN = 256
 SHARD = ("shard_0", "shard_1")
-REP_SHARD = ("rep", "shard_0", "shard_1")
+REP = ("rep_hi", "core")
+REP_SHARD = ("rep_hi", "core", "shard_0", "shard_1")
+ALL = REP_SHARD
 
 
 EPS = 1e-05
@@ -140,6 +142,26 @@
     return gated_pre * scaling * gate_gain[None, :]
 
 
+def gather_rows(weight):
+    rows = weight.shape[0]
+    half = rows // 2
+    core = lax.axis_index("core")
+    mine = lax.dynamic_slice_in_dim(weight, core * half, half, axis=0)
+    part = lax.all_gather(mine, SHARD, axis=0, tiled=False)
+    both = lax.all_gather(part, "core", axis=1, tiled=False)
+    return both.reshape(-1, weight.shape[1])
+
+
+def reduce_rows(partial):
+    groups = lax.axis_size(SHARD)
+    cols = partial.shape[1]
+    blocks = partial.reshape(groups, 2, -1, cols)
+    halves = lax.psum_scatter(blocks, "core", scatter_dimension=1, tiled=False)
+    owned = lax.psum_scatter(halves, SHARD, scatter_dimension=0, tiled=False)
+    owned = lax.psum(owned, "rep_hi")
+    return lax.all_gather(owned, "core", axis=0, tiled=True)
+
+
 def on_device(
     layer_in,
     cotangent,
@@ -155,19 +177,23 @@
     out_weight,
 ):
     count = layer_in.shape[0]
+    groups = lax.axis_size(SHARD)
     segment = segment_ids(seq_lengths[0], count)
-    norm_full, convw_full, convb_full, stepb_full, decay_full, skip_full, gategain_full = (
-        lax.all_gather(norm_gain, SHARD, axis=0, tiled=True),
-        *side_by_side((conv_weight, conv_bias), SHARD, 0, 1),
-        lax.all_gather(step_bias, SHARD, axis=0, tiled=True),
-        lax.all_gather(decay_log, SHARD, axis=0, tiled=True),
-        lax.all_gather(skip_gain, SHARD, axis=0, tiled=True),
-        lax.all_gather(gate_gain, SHARD, axis=0, tiled=True),
-    )
+    smalls = (norm_gain, conv_weight, conv_bias, step_bias, decay_log, skip_gain, gate_gain)
+    flat = jnp.concatenate([a.reshape(-1) for a in smalls])
+    flat_all = lax.all_gather(flat, SHARD, axis=0, tiled=False)
+    pieces_full = []
+    offset = 0
+    for a in smalls:
+        size = a.size
+        block = flat_all[:, offset : offset + size]
+        pieces_full.append(block.reshape((groups * a.shape[0],) + a.shape[1:]))
+        offset += size
+    norm_full, convw_full, convb_full, stepb_full, decay_full, skip_full, gategain_full = pieces_full
     normed_f, norm_back = jax.vjp(norm_input, layer_in, norm_full)
     normed = normed_f.astype(jnp.bfloat16)
-    in_whole = lax.all_gather(in_weight, SHARD, axis=0, tiled=True)
-    out_whole = lax.all_gather(out_weight, SHARD, axis=0, tiled=True)
+    in_whole = gather_rows(in_weight)
+    out_whole = gather_rows(out_weight)
     projected = jnp.dot(normed, in_whole, preferred_element_type=jnp.float32)
 
     def bound_mixer(proj_arg, cw_arg, cb_arg, sb_arg, dl_arg, sk_arg, gg_arg):
@@ -187,45 +213,47 @@
     branch_out = jnp.dot(gated, out_whole, preferred_element_type=jnp.float32)
     layer_out = layer_in + branch_out
     cot_low = cotangent.astype(jnp.bfloat16)
-    out_owned = lax.psum_scatter(
-        row_product(gated, cot_low), SHARD, scatter_dimension=0, tiled=True
-    )
+    out_owned = reduce_rows(row_product(gated, cot_low))
     gated_grad = back_product(cot_low, out_whole)
     proj_grad, g_convw, g_convb, g_stepb, g_decay, g_skip, g_gategain = mixer_back(gated_grad)
     proj_low = proj_grad.astype(jnp.bfloat16)
-    in_owned = sum_by_axis(row_product(normed, proj_low), SHARD)
+    cols = proj_low.shape[1]
+    wide = -(-cols // 128) * 128
+    proj_wide = jnp.pad(proj_low, ((0, 0), (0, wide - cols)))
+    in_owned = reduce_rows(row_product(normed, proj_wide))[:, :cols]
     normed_grad = back_product(proj_low, in_whole)
     back_in, g_norm = norm_back(normed_grad)
     input_grad = cotangent + back_in
-    small_owned = (
-        sum_at_owner(g_norm, SHARD, 0),
-        *sent_together((g_convw, g_convb), SHARD, 0, 1),
-        sum_at_owner(g_stepb, SHARD, 0),
-        sum_at_owner(g_decay, SHARD, 0),
-        sum_at_owner(g_skip, SHARD, 0),
-        sum_at_owner(g_gategain, SHARD, 0),
-    )
-    summed = lax.psum((in_owned, out_owned) + tuple(small_owned), "rep")
-    in_final = summed[0]
-    out_final = summed[1]
-    small_final = summed[2:]
+    grads = (g_norm, g_convw, g_convb, g_stepb, g_decay, g_skip, g_gategain)
+    small_blocks = jnp.concatenate([g.reshape(groups, -1) for g in grads], axis=1)
+    small_sum = lax.psum(small_blocks, ALL)
+    mine = lax.dynamic_index_in_dim(small_sum, lax.axis_index(SHARD), axis=0, keepdims=False)
+    small_final = []
+    offset = 0
+    for g in grads:
+        size = g.size // groups
+        small_final.append(mine[offset : offset + size].reshape((g.shape[0] // groups,) + g.shape[1:]))
+        offset += size
     return (
         layer_out,
         input_grad,
         small_final[0],
-        in_final,
+        in_owned,
         small_final[1],
         small_final[2],
         small_final[3],
         small_final[4],
         small_final[5],
         small_final[6],
-        out_final,
+        out_owned,
     )
 
 
 def solution(mesh):
-    split = Mesh(mesh.devices.reshape(mesh.shape["rep"], 4, 2), ("rep", "shard_0", "shard_1"))
+    split = Mesh(
+        mesh.devices.reshape(mesh.shape["rep"] // 2, 2, 4, 2),
+        ("rep_hi", "core", "shard_0", "shard_1"),
+    )
     in_specs = (
         P(REP_SHARD, None),
         P(REP_SHARD, None),

time: 908 us -> 835 us (0.920)
  waiting for transfers between devices: 593 us -> 551 us
  blocking collectives: 134 us -> 95.2 us
  local copies, waits for them, and re-layouts: 26.9 us -> 64.2 us
  starting transfers between devices: 23 us -> 0.69 us
    reduce_scatter x3 -> x4, waiting for transfers between devices: 386 us -> 313 us  [the longest x2 281 us: reduce_rows(): owned = lax.psum_scatter(halves, SHARD, scatter_dimension=0, tiled=False)]
    psum x1, waiting for transfers between devices: 21.8 us -> 89.9 us  [reduce_rows(): owned = lax.psum(owned, 'rep_hi')]
    all_gather x3 -> x0, blocking collectives: 51.4 us -> none  [the longest x1 24.4 us: side_by_side(): result = lax.all_gather(both, axis, axis=dim, tiled=True)]
    all_to_all x6 -> x0, waiting for transfers between devices: 24.7 us -> none  [sum_at_owner(): blocks = lax.all_to_all(in_blocks(shard, dim, size), axis, 0, 0, tiled=True)]
    reshape x1 -> x10, local copies, waits for them, and re-layouts: 0.68 us -> 24.4 us  [the longest x2 20.6 us: reduce_rows(): blocks = partial.reshape(groups, 2, -1, cols)]
    all_to_all x6 -> x0, starting transfers between devices: 22.8 us -> none  [sum_at_owner(): blocks = lax.all_to_all(in_blocks(shard, dim, size), axis, 0, 0, tiled=True)]
    all_gather x2 -> x6, waiting for transfers between devices: 159 us -> 147 us  [the longest x2 122 us: gather_rows(): part = lax.all_gather(mine, SHARD, axis=0, tiled=False)]
    dot_general x2, matrix products: 14.5 us -> 4.09 us  [row_product(): lax.dot_general(left, right, (((0,), (0,)), ((), ())), preferred_element_...]
  transfers between devices with their start and end apart: 12 -> 11, of which waited for: 11 -> 7; matrix products, arithmetic and copies ran while one was open for 7% -> 18% of each run, Pallas kernels for 0% -> 0%
where the time goes in v1:
time: 835 us; the launch traced here: 827 us
  waiting for transfers between devices  551 us (66%)
  blocking collectives  95.2 us (11%)
  local copies, waits for them, and re-layouts  64.2 us (8%)
  matrix products  64 us (8%)
  other arithmetic  35.6 us (4%)
  between operations  16.2 us (2%)
    reduce_scatter x2, waiting for transfers between devices, reduce_rows(): owned = lax.psum_scatter(halves, SHARD, scatter_dimension=0, tiled=False)  281 us
    all_gather x2, waiting for transfers between devices, gather_rows(): part = lax.all_gather(mine, SHARD, axis=0, tiled=False)  122 us
    psum x1, waiting for transfers between devices, reduce_rows(): owned = lax.psum(owned, 'rep_hi')  89.9 us
    psum x1, blocking collectives, on_device(): small_sum = lax.psum(small_blocks, ALL)  68.5 us
    reduce_scatter x2, waiting for transfers between devices, reduce_rows(): halves = lax.psum_scatter(blocks, 'core', scatter_dimension=1, tiled=False)  31.1 us
    dot_general x3, matrix products, mixer(): y_intra = jnp.einsum('chij,cjhp->cihp', mixing, scaled_in, precision=HIGH)  29.5 us
    unnamed x1, blocking collectives  26.8 us
    all_gather x2, waiting for transfers between devices, gather_rows(): both = lax.all_gather(part, 'core', axis=1, tiled=False)  25.5 us
  transfers between devices with their start and end apart: 11, of which 7 were waited for; matrix products, arithmetic and copies ran while one was open for 18% of the time, Pallas kernels for 0%

profile of v1, /device:TPU:1, one launch (start us, length us, event | category | flops | bytes accessed | tf_op | source)
XLA Modules:
  0.0 826.9 jit_solution(1690237678751658720)
XLA Ops:
  8.8 1.6 copy.77
  11.3 100.5 %all-gather.16.cloned.1.call-done = bf16[512,4384]{1,0:T(8,128)(2,1)} async-done(((bf16[64,4384]{1,0:T(8,128)(2,1)}), bf16[512,4384]{1,0:T(8,128)(2,1)}) %all-gather.16.cloned.1.call-update) | async-done | bytes 4489232 | tf_op jit(solution)/shard_map/all_gather | solution.py:150
  114.2 26.8 %all-reduce.19 = f32[14688]{0:T(1024)S(1)} all-reduce(f32[14688]{0:T(1024)S(1)} %dynamic-update-slice), channel_id=2, replica_groups=mesh['rep_hi'=8,'core'=2,'shard_0'=4,'shard_1'=2] {'shard_0','shard_1'}, use_global_device_ids=true, to_apply=%add.19 | all-reduce | flops 14688 | bytes 117504
  141.7 1.2 reshape.539
  143.2 2.2 slice_reduce_fusion.3
  146.4 21.5 %all-gather.20.cloned.1.call-done = bf16[1024,1024]{1,0:T(8,128)(2,1)} async-done(((bf16[128,1024]{1,0:T(8,128)(2,1)}), bf16[1024,1024]{1,0:T(8,128)(2,1)}) %all-gather.20.cloned.1.call-update) | async-done | bytes 2097168 | tf_op jit(solution)/shard_map/all_gather | solution.py:150
  168.0 25.5 %all-gather.18.cloned.1.call-done = bf16[8,128,4384]{2,1,0:T(8,128)(2,1)} async-done(((bf16[8,64,4384]{2,1,0:T(8,128)(2,1)}), bf16[8,128,4384]{2,1,0:T(8,128)(2,1)}) %all-gather.18.cloned.1.call-update) | async-done | bytes 8978448 | tf_op jit(solution)/shard_map/all_gather | solution.py:151
  193.4 7.5 fusion.74
  201.0 2.1 copy-done.2
  204.6 3.7 slice.178
  209.3 1.5 slice.176
  210.9 1.6 slice.174
  212.6 7.5 fusion.19
  221.6 1.8 fusion.45
  223.4 1.4 copy-done.17
  224.8 9.2 %fusion.24 = f32[256,32,64]{0,2,1:T(8,128)S(1)} fusion(f32[256,32,64]{0,2,1:T(8,128)S(1)} %bitcast.148, f32[256,32,64]{0,2,1:T(8,128)S(1)} %fusion.45, f32[256,256]{1,0:T(8,128)S(1)} %fusion.53, f32[32,256]{1,0:T(8,128)S(1)} %bitcast_add_fusion.2, pred[256,256]{1,0:T(8,128)(4,1)S(1)} %copy-done.39, f32[32]{0:T(128)S(1)} %mul.424, ...), kind=kOutput, calls=%fused_computation.41 | convolution fusion | flops 1619525632 | bytes 6717568 | tf_op jit(solution)/shard_map/jvp(chij,cjhp->cihp)/dot_general | solution.py:132
  234.0 3.1 multiply_reduce_fusion.9
  237.1 1.3 fusion.47
  238.4 14.0 %copy.71 = f32[8,2,128,1024]{3,2,0,1:T(8,128)} copy(f32[8,2,128,1024]{3,2,1,0:T(8,128)S(1)} %bitcast.137) | data formatting | bytes 16777216 | tf_op jit(solution)/shard_map/reshape | solution.py:158
  253.2 4.8 multiply_reduce_fusion.5
  258.1 4.1 multiply_reduce_fusion.6
  262.2 11.4 %fusion.6 = (f32[32,256]{1,0:T(8,128)S(1)}, f32[32,256]{1,0:T(8,128)S(1)}, f32[256,256]{1,0:T(8,128)S(1)}) fusion(f32[256,256]{1,0:T(8,128)S(1)} %copy-done.25, f32[32,256]{1,0:T(8,128)S(1)} %copy-done.43, pred[256,256]{1,0:T(8,128)(4,1)S(1)} %copy-done.40, f32[32,64,256]{2,1,0:T(8,128)S(1)} %bitcast.138, f32[256,32,64]{0,2,1:T(8,128)S(1)} %bitcast.150, ...), kind=kOutput, calls=%fused_computation.7 | convolution fusion | flops 1629929472 | bytes 4915200 | tf_op jit(solution)/shard_map/transpose(jvp(chij,cjhp->cihp))/dot_general | solution.py:132
  275.0 3.2 reduce-window.19
  278.8 1.3 reduce-window.24
  280.1 1.2 slice_bitcast_fusion.2
  281.4 1.4 copy.68
  282.7 1.4 broadcast.255
  284.1 1.4 reshape.560
  285.5 3.0 fusion.36
  288.7 9.0 %fusion.25 = (f32[256,32]{0,1:T(8,128)S(1)}, f32[1,256,32,64]{1,3,2,0:T(8,128)S(1)}) fusion(f32[1,256,32,64]{1,3,2,0:T(8,128)} %bitcast.149, f32[256,32]{0,1:T(8,128)} %get-tuple-element.73, f32[32,64,256]{2,1,0:T(8,128)} %bitcast.140, f32[256,256]{1,0:T(8,128)} %copy-done.24, f32[32,256]{1,0:T(8,128)} %copy-done.42, pred[256,256]{1,0:T(8,128)(4,1)} %fusion.50), kind=kOutput, calls=%fused_computation.45 | convolution fusion | flops 1618468864 | bytes 6717440 | tf_op jit(solution)/shard_map/transpose(jvp(chij,cjhp->cihp))/dot_general | solution.py:132
  299.2 1.3 convolution_add_fusion.1
  300.9 1.3 copy-done.10
  302.9 2.4 multiply_reduce_fusion.4
  305.3 2.3 multiply_reduce_fusion.3
  310.6 1.8 fusion.75
  313.2 2.8 fusion.20
  316.0 6.6 copy.70
  323.4 31.1 %reduce-scatter.5.cloned.1.call-done = f32[8,1,64,4480]{3,2,0,1:T(8,128)} async-done(((f32[8,2,64,4480]{3,2,0,1:T(8,128)}), f32[8,1,64,4480]{3,2,0,1:T(8,128)}) %reduce-scatter.5.cloned.1.call-update) | async-done | bytes 9175056 | tf_op jit(solution)/shard_map/reduce_scatter | solution.py:159
  354.6 94.9 %reduce-scatter.11.cloned.1.call-done = f32[1,128,1024]{2,1,0:T(8,128)} async-done(((f32[8,128,1024]{2,1,0:T(8,128)}), f32[1,128,1024]{2,1,0:T(8,128)}) %reduce-scatter.11.cloned.1.call-update) | async-done | bytes 524304 | tf_op jit(solution)/shard_map/reduce_scatter | solution.py:160
  449.4 186.6 %reduce-scatter.7.cloned.1.call-done = f32[1,64,4480]{2,1,0:T(8,128)} async-done(((f32[8,64,4480]{2,1,0:T(8,128)}), f32[1,64,4480]{2,1,0:T(8,128)}) %reduce-scatter.7.cloned.1.call-update) | async-done | bytes 1146896 | tf_op jit(solution)/shard_map/reduce_scatter | solution.py:160
  636.1 89.9 %all-reduce.23.cloned.1.call-done = (f32[64,4480]{1,0:T(8,128)}, f32[128,1024]{1,0:T(8,128)}) async-done(((f32[64,4480]{1,0:T(8,128)}, f32[128,1024]{1,0:T(8,128)}), (f32[64,4480]{1,0:T(8,128)}, f32[128,1024]{1,0:T(8,128)})) %all-reduce.23.cloned.1.call-update) | async-done | bytes 1671184 | tf_op jit(solution)/shard_map/psum | solution.py:161
  727.3 1.4 copy.69
  728.7 2.0 reshape.564
  730.8 7.9 multiply_reduce_fusion.10
  738.8 68.5 %psum.21 = f32[8,1836]{1,0:T(8,128)S(1)} all-reduce(f32[8,1836]{1,0:T(8,128)S(1)} %concatenate.35), channel_id=1, replica_groups=mesh['rep_hi'=8,'core'=2,'shard_0'=4,'shard_1'=2] {'rep_hi','core','shar..., use_global_device_ids=true, to_apply=%region_26.27 | all-reduce | flops 14688 | bytes 117504 | tf_op jit(solution)/shard_map/psum | solution.py:229
  810.6 2.8 fusion.39
  813.4 2.4 convolution_add_fusion
  815.8 3.2 copy.72
  (254 shorter events, 25.5 us)
Async XLA Ops:
  7.2 104.6 %all-gather.16.cloned.1.call-start = ((), (), s32[]{:S(2)}) async-start(), calls=%async_computation.10 | async-start | bytes 5160960 | tf_op jit(solution)/shard_map/all_gather | solution.py:150
  10.5 157.4 %all-gather.20.cloned.1.call-start = ((), (), s32[]{:S(2)}) async-start(), calls=%async_computation.12 | async-start | bytes 2359296 | tf_op jit(solution)/shard_map/all_gather | solution.py:150
  11.3 100.7 %copy-start.53 = (f32[288,4]{0,1:T(4,128)S(1)}, f32[288,4]{0,1:T(4,128)}, u32[]{:S(2)}) copy-start(f32[288,4]{0,1:T(4,128)} %param.17) | copy-start | bytes 13828
  11.3 182.1 %all-gather.18.cloned.1.call-start = ((), (), s32[]{:S(2)}) async-start(), calls=%async_computation.11 | async-start | bytes 13762560 | tf_op jit(solution)/shard_map/all_gather | solution.py:151
  111.8 29.2 %copy-start.70 = (s32[1,2]{1,0:T(1,128)S(1)}, s32[1,2]{1,0:T(1,128)}, u32[]{:S(2)}) copy-start(s32[1,2]{1,0:T(1,128)} %param.14) | copy-start | bytes 28
  111.9 31.2 %copy-start.11 = (f32[256,1024]{1,0:T(8,128)S(1)}, f32[256,1024]{1,0:T(8,128)}, u32[]{:S(2)}) copy-start(f32[256,1024]{1,0:T(8,128)} %param.12) | copy-start | bytes 3145732
  111.9 141.3 %all-gather.22.cloned.1.call-start = ((), (), s32[]{:S(2)}) async-start(), calls=%async_computation.13 | async-start | bytes 6291456 | tf_op jit(solution)/shard_map/all_gather | solution.py:151
  141.6 59.3 %copy-start.60 = (f32[32]{0:T(128)}, f32[32]{0:T(128)S(1)}, u32[]{:S(2)}) copy-start(f32[32]{0:T(128)S(1)} %neg.39) | copy-start | bytes 388
  141.7 59.2 %copy-start.62 = (f32[32]{0:T(128)}, f32[32]{0:T(128)S(1)}, u32[]{:S(2)}) copy-start(f32[32]{0:T(128)S(1)} %add.163) | copy-start | bytes 388
  145.4 67.1 %copy-start.31 = (f32[2304]{0:T(1024)}, f32[2304]{0:T(1024)S(1)}, u32[]{:S(2)}) copy-start(f32[2304]{0:T(1024)S(1)} %get-tuple-element.53) | copy-start | bytes 27652
  145.4 67.1 %copy-start.33 = (f32[2304]{0:T(1024)}, f32[2304]{0:T(1024)S(1)}, u32[]{:S(2)}) copy-start(f32[2304]{0:T(1024)S(1)} %get-tuple-element.54) | copy-start | bytes 27652
  145.4 67.1 %copy-start.35 = (f32[2304]{0:T(1024)}, f32[2304]{0:T(1024)S(1)}, u32[]{:S(2)}) copy-start(f32[2304]{0:T(1024)S(1)} %get-tuple-element.56) | copy-start | bytes 27652
  145.5 67.1 %copy-start.37 = (f32[2304]{0:T(1024)}, f32[2304]{0:T(1024)S(1)}, u32[]{:S(2)}) copy-start(f32[2304]{0:T(1024)S(1)} %get-tuple-element.55) | copy-start | bytes 27652
  145.5 47.9 %copy-start.44 = (f32[256]{0:T(256)}, f32[256]{0:T(256)S(1)}, u32[]{:S(2)}) copy-start(f32[256]{0:T(256)S(1)} %fusion.66) | copy-start | bytes 3076
  145.6 67.0 %copy-start.54 = (pred[256]{0:T(512)(128)(4,1)}, pred[256]{0:T(512)(128)(4,1)S(1)}, u32[]{:S(2)}) copy-start(pred[256]{0:T(512)(128)(4,1)S(1)} %get-tuple-element.90) | copy-start | bytes 772
  145.6 67.0 %copy-start.56 = (pred[256]{0:T(512)(128)(4,1)}, pred[256]{0:T(512)(128)(4,1)S(1)}, u32[]{:S(2)}) copy-start(pred[256]{0:T(512)(128)(4,1)S(1)} %get-tuple-element.91) | copy-start | bytes 772
  145.6 67.0 %copy-start.58 = (pred[256]{0:T(512)(128)(4,1)}, pred[256]{0:T(512)(128)(4,1)S(1)}, u32[]{:S(2)}) copy-start(pred[256]{0:T(512)(128)(4,1)S(1)} %get-tuple-element.92) | copy-start | bytes 772
  145.6 74.8 %copy-start.48 = (f32[256]{0:T(256)}, f32[256]{0:T(256)S(1)}, u32[]{:S(2)}) copy-start(f32[256]{0:T(256)S(1)} %get-tuple-element.89) | copy-start | bytes 3076
  167.9 154.8 %reduce-scatter.9.cloned.1.call-start = ((), (), s32[]{:S(2)}) async-start(), calls=%async_computation.7 | async-start | bytes 12582912 | tf_op jit(solution)/shard_map/reduce_scatter | solution.py:159
  204.6 4.7 copy-start.3
  220.2 13.7 %copy-start.21 = (f32[256,2048]{0,1:T(8,128)}, f32[256,2048]{0,1:T(8,128)S(1)}, u32[]{:S(2)}) copy-start(f32[256,2048]{0,1:T(8,128)S(1)} %slice.179) | copy-start | bytes 6291460
  220.3 4.5 copy-start.26
  220.3 4.5 copy-start.39
  220.5 13.5 %copy-start.42 = (f32[32,256]{1,0:T(8,128)}, f32[32,256]{1,0:T(8,128)S(1)}, u32[]{:S(2)}) copy-start(f32[32,256]{1,0:T(8,128)S(1)} %bitcast_add_fusion.2) | copy-start | bytes 98308
  221.5 12.4 %copy-start.24 = (f32[256,256]{1,0:T(8,128)}, f32[256,256]{1,0:T(8,128)S(1)}, u32[]{:S(2)}) copy-start(f32[256,256]{1,0:T(8,128)S(1)} %fusion.53) | copy-start | bytes 786436
  237.1 20.9 %copy-start.46 = (f32[256]{0:T(256)}, f32[256]{0:T(256)S(1)}, u32[]{:S(2)}) copy-start(f32[256]{0:T(256)S(1)} %fusion.67) | copy-start | bytes 3076
  252.4 102.1 %reduce-scatter.5.cloned.1.call-start = ((), (), s32[]{:S(2)}) async-start(), calls=%async_computation.4 | async-start | bytes 27525120 | tf_op jit(solution)/shard_map/reduce_scatter | solution.py:159
  253.2 4.8 copy-start.7
  253.2 4.8 copy-start.16
  262.2 11.4 %copy-start.4 = (f32[256,2048]{0,1:T(8,128)}, f32[256,2048]{0,1:T(8,128)S(1)}, u32[]{:S(2)}) copy-start(f32[256,2048]{0,1:T(8,128)S(1)} %get-tuple-element.60) | copy-start | bytes 6291460
  262.2 11.4 %copy-start.18 = (f32[256,32,64]{0,2,1:T(8,128)S(1)}, f32[256,32,64]{0,2,1:T(8,128)}, u32[]{:S(2)}) copy-start(f32[256,32,64]{0,2,1:T(8,128)} %copy-done.17) | copy-start | bytes 6291460
  285.5 12.1 %slice-start = ((s8[4489216]{0:T(1024)(128)(4,1)}), s8[4194304]{0:T(1024)(128)(4,1)S(1)}, s32[]{:S(2)}) async-start(s8[4489216]{0:T(1024)(128)(4,1)} %bitcast.135), calls=%async_computation.15 | async-start | bytes 8388608
  288.6 9.1 %slice-start.1 = ((s8[4489216]{0:T(1024)(128)(4,1)}), s8[294912]{0:T(1024)(128)(4,1)S(1)}, s32[]{:S(2)}) async-start(s8[4489216]{0:T(1024)(128)(4,1)} %bitcast.135), calls=%async_computation.16 | async-start | bytes 589824
  288.6 9.1 %copy-start.28 = (f32[256,32]{0,1:T(8,128)S(1)}, f32[256,32]{0,1:T(8,128)}, u32[]{:S(2)}) copy-start(f32[256,32]{0,1:T(8,128)} %get-tuple-element.73) | copy-start | bytes 98308
  288.6 9.1 %copy-start.30 = (f32[1,32,256]{2,1,0:T(8,128)S(1)}, f32[1,32,256]{2,1,0:T(8,128)}, u32[]{:S(2)}) copy-start(f32[1,32,256]{2,1,0:T(8,128)} %reshape.560) | copy-start | bytes 98308
  288.6 9.1 %copy-start.61 = (f32[32]{0:T(128)S(1)}, f32[32]{0:T(128)}, u32[]{:S(2)}) copy-start(f32[32]{0:T(128)} %copy-done.60) | copy-start | bytes 388
  288.6 9.1 %copy-start.63 = (f32[32]{0:T(128)S(1)}, f32[32]{0:T(128)}, u32[]{:S(2)}) copy-start(f32[32]{0:T(128)} %copy-done.62) | copy-start | bytes 388
  288.6 11.8 %copy-start.5 = (f32[256,2048]{0,1:T(8,128)S(1)}, f32[256,2048]{0,1:T(8,128)}, u32[]{:S(2)}) copy-start(f32[256,2048]{0,1:T(8,128)} %copy-done.4) | copy-start | bytes 6291460
  288.6 11.8 %copy-start.41 = (f32[2048]{0:T(1024)S(1)}, f32[2048]{0:T(1024)}, u32[]{:S(2)}) copy-start(f32[2048]{0:T(1024)} %mul.455) | copy-start | bytes 24580
  322.6 126.8 %reduce-scatter.11.cloned.1.call-start = ((), (), s32[]{:S(2)}) async-start(), calls=%async_computation.8 | async-start | bytes 4718592 | tf_op jit(solution)/shard_map/reduce_scatter | solution.py:160
  323.4 312.6 %reduce-scatter.7.cloned.1.call-start = ((), (), s32[]{:S(2)}) async-start(), calls=%async_computation.5 | async-start | bytes 10321920 | tf_op jit(solution)/shard_map/reduce_scatter | solution.py:160
  354.5 372.4 %copy-start.52 = (f32[2048]{0:T(1024)S(1)}, f32[2048]{0:T(1024)}, u32[]{:S(2)}) copy-start(f32[2048]{0:T(1024)} %get-tuple-element.47) | copy-start | bytes 24580
  354.5 371.5 %all-reduce.23.cloned.1.call-start = ((), (), s32[]{:S(2)}) async-start(), calls=%async_computation.14 | async-start | bytes 3342336 | tf_op jit(solution)/shard_map/psum | solution.py:161
  636.0 179.8 %all-gather.14.cloned.1.call-start = ((), (), s32[]{:S(2)}) async-start(), calls=%async_computation.9 | async-start | bytes 1572864 | tf_op jit(solution)/shard_map/all_gather | solution.py:162
  726.0 89.8 %all-gather.12.cloned.1.call-start = ((), (), s32[]{:S(2)}) async-start(), calls=%async_computation.6 | async-start | bytes 3440640 | tf_op jit(solution)/shard_map/all_gather | solution.py:162
  730.8 79.9 %copy-start.51 = (f32[256]{0:T(256)S(1)}, f32[256]{0:T(256)}, u32[]{:S(2)}) copy-start(f32[256]{0:T(256)} %copy-done.50) | copy-start | bytes 3076
  738.8 74.6 %copy-start.47 = (f32[256]{0:T(256)S(1)}, f32[256]{0:T(256)}, u32[]{:S(2)}) copy-start(f32[256]{0:T(256)} %copy-done.46) | copy-start | bytes 3076
  808.8 4.6 copy-start.20
  (37 other events, 85.7 us)
Sparse Core Ops, SparseCore 0:
  10.6 101.1 all-gather.15
  114.0 53.8 all-gather.19
  169.6 23.8 all-gather.17
  194.9 17.6 all-gather.21
  252.5 20.8 reduce-scatter.8
  322.8 31.6 reduce-scatter.4
  357.0 92.3 reduce-scatter.10
  452.0 183.9 reduce-scatter.6
  638.8 87.1 all-reduce.22
  727.5 15.0 all-gather.13
  744.3 14.8 all-gather.11

commit v2 on v1

--- a/solution.py
+++ b/solution.py
@@ -152,14 +152,32 @@
     return both.reshape(-1, weight.shape[1])
 
 
-def reduce_rows(partial):
+def reduce_rows(partial, extra=None, at=None):
     groups = lax.axis_size(SHARD)
     cols = partial.shape[1]
     blocks = partial.reshape(groups, 2, -1, cols)
+    if extra is not None:
+        width = extra.shape[1]
+        pad_cols = cols - at
+        extra_rows = -(-width // pad_cols)
+        extra = jnp.pad(extra, ((0, 0), (0, extra_rows * pad_cols - width)))
+        extra = extra.reshape(groups, 1, extra_rows, pad_cols)
+        blocks = lax.dynamic_update_slice(blocks, extra, (0, 0, 0, cols - pad_cols))
     halves = lax.psum_scatter(blocks, "core", scatter_dimension=1, tiled=False)
-    owned = lax.psum_scatter(halves, SHARD, scatter_dimension=0, tiled=False)
-    owned = lax.psum(owned, "rep_hi")
-    return lax.all_gather(owned, "core", axis=0, tiled=True)
+    owned = lax.psum_scatter(halves.astype(jnp.bfloat16), SHARD, scatter_dimension=0, tiled=False)
+    owned = owned.astype(jnp.float32)
+    if extra is not None:
+        small = halves[:, :extra_rows, cols - pad_cols :]
+        small = lax.psum_scatter(small, SHARD, scatter_dimension=0, tiled=False)
+        owned, small = lax.psum((owned, small), "rep_hi")
+        owned = lax.dynamic_update_slice(owned, small, (0, cols - pad_cols))
+    else:
+        owned = lax.psum(owned, "rep_hi")
+    whole = lax.all_gather(owned, "core", axis=0, tiled=True)
+    if extra is None:
+        return whole
+    small = whole[:extra_rows, cols - pad_cols :].reshape(-1)[:width]
+    return whole, small
 
 
 def on_device(
@@ -181,7 +199,11 @@
     segment = segment_ids(seq_lengths[0], count)
     smalls = (norm_gain, conv_weight, conv_bias, step_bias, decay_log, skip_gain, gate_gain)
     flat = jnp.concatenate([a.reshape(-1) for a in smalls])
+    flat_len = flat.shape[0]
+    tile_rows = -(-flat_len // 1024) * 8
+    flat = jnp.pad(flat, (0, tile_rows * 128 - flat_len)).reshape(tile_rows, 128)
     flat_all = lax.all_gather(flat, SHARD, axis=0, tiled=False)
+    flat_all = flat_all.reshape(groups, -1)[:, :flat_len]
     pieces_full = []
     offset = 0
     for a in smalls:
@@ -217,17 +239,16 @@
     gated_grad = back_product(cot_low, out_whole)
     proj_grad, g_convw, g_convb, g_stepb, g_decay, g_skip, g_gategain = mixer_back(gated_grad)
     proj_low = proj_grad.astype(jnp.bfloat16)
-    cols = proj_low.shape[1]
-    wide = -(-cols // 128) * 128
-    proj_wide = jnp.pad(proj_low, ((0, 0), (0, wide - cols)))
-    in_owned = reduce_rows(row_product(normed, proj_wide))[:, :cols]
     normed_grad = back_product(proj_low, in_whole)
     back_in, g_norm = norm_back(normed_grad)
     input_grad = cotangent + back_in
     grads = (g_norm, g_convw, g_convb, g_stepb, g_decay, g_skip, g_gategain)
     small_blocks = jnp.concatenate([g.reshape(groups, -1) for g in grads], axis=1)
-    small_sum = lax.psum(small_blocks, ALL)
-    mine = lax.dynamic_index_in_dim(small_sum, lax.axis_index(SHARD), axis=0, keepdims=False)
+    cols = proj_low.shape[1]
+    wide = -(-cols // 128) * 128
+    proj_wide = jnp.pad(proj_low, ((0, 0), (0, wide - cols)))
+    in_wide, mine = reduce_rows(row_product(normed, proj_wide), small_blocks, cols)
+    in_owned = in_wide[:, :cols]
     small_final = []
     offset = 0
     for g in grads:

time: 835 us -> 738 us (0.88)
  waiting for transfers between devices: 551 us -> 468 us
  blocking collectives: 95.2 us -> 56.9 us
  other arithmetic: 35.6 us -> 60.2 us
    reduce_scatter x2, waiting for transfers between devices: 281 us -> 149 us  [reduce_rows(): lax.psum_scatter(halves.astype(jnp.bfloat16), SHARD, scatter_dimension=0,...]
    unnamed x11 -> x13, waiting for transfers between devices: 1.04 us -> 37.7 us
    psum x1, blocking collectives: 68.5 us -> 34.2 us  [reduce_rows(): owned, small = lax.psum((owned, small), 'rep_hi')]
    unnamed x1 -> x0, blocking collectives: 26.8 us -> none
    all_gather x0 -> x1, blocking collectives: none -> 22.7 us  [on_device(): flat_all = lax.all_gather(flat, SHARD, axis=0, tiled=False)]
    all_gather x2, waiting for transfers between devices: 0.01 us -> 16.2 us  [reduce_rows(): whole = lax.all_gather(owned, 'core', axis=0, tiled=True)]
    convert_element_type x0 -> x4, other arithmetic: none -> 14 us  [the longest x2 10 us: reduce_rows(): halves.astype(jnp.bfloat16)]
    reshape x2, local copies, waits for them, and re-layouts: 20.6 us -> 11.2 us  [reduce_rows(): blocks = partial.reshape(groups, 2, -1, cols)]
  transfers between devices with their start and end apart: 11 -> 12, of which waited for: 7 -> 9; matrix products, arithmetic and copies ran while one was open for 18% -> 23% of each run, Pallas kernels for 0% -> 0%
where the time goes in v2:
time: 738 us; the launch traced here: 730 us
  waiting for transfers between devices  468 us (63%)
  matrix products  67.2 us (9%)
  local copies, waits for them, and re-layouts  61.1 us (8%)
  other arithmetic  60.2 us (8%)
  blocking collectives  56.9 us (8%)
  between operations  15.7 us (2%)
    reduce_scatter x2, waiting for transfers between devices, reduce_rows(): lax.psum_scatter(halves.astype(jnp.bfloat16), SHARD, scatter_dimension=0,...  149 us
    all_gather x2, waiting for transfers between devices, gather_rows(): part = lax.all_gather(mine, SHARD, axis=0, tiled=False)  126 us
    psum x1, waiting for transfers between devices, reduce_rows(): owned, small = lax.psum((owned, small), 'rep_hi')  85.6 us
    unnamed x13, waiting for transfers between devices  37.7 us
    psum x1, blocking collectives, reduce_rows(): owned, small = lax.psum((owned, small), 'rep_hi')  34.2 us
    dot_general x3, matrix products, mixer(): y_intra = jnp.einsum('chij,cjhp->cihp', mixing, scaled_in, precision=HIGH)  30.4 us
    reduce_scatter x2, waiting for transfers between devices, reduce_rows(): halves = lax.psum_scatter(blocks, 'core', scatter_dimension=1, tiled=False)  27.8 us
    all_gather x2, waiting for transfers between devices, gather_rows(): both = lax.all_gather(part, 'core', axis=1, tiled=False)  25.5 us
  transfers between devices with their start and end apart: 12, of which 9 were waited for; matrix products, arithmetic and copies ran while one was open for 23% of the time, Pallas kernels for 0%

profile of v2, /device:TPU:1, one launch (start us, length us, event | category | flops | bytes accessed | tf_op | source)
XLA Modules:
  0.0 729.7 jit_solution(10812523256674741103)
XLA Ops:
  8.8 1.6 copy.95
  11.3 100.5 %all-gather.15.cloned.1.call-done = bf16[512,4384]{1,0:T(8,128)(2,1)} async-done(((bf16[64,4384]{1,0:T(8,128)(2,1)}), bf16[512,4384]{1,0:T(8,128)(2,1)}) %all-gather.15.cloned.1.call-update) | async-done | bytes 4489232 | tf_op jit(solution)/shard_map/all_gather | solution.py:150
  112.6 22.7 %all_gather.33 = f32[8,16,128]{2,1,0:T(8,128)S(1)} all-gather(f32[1,16,128]{2,1,0:T(8,128)S(1)} %pad_bitcast_fusion), channel_id=1, replica_groups=mesh['rep_hi'=8,'core'=2,'shard_0'=4,'shard_1'=2] {'shard_0','shard_1'}, dimensions={0}, use_global_device_ids=true | all-gather | bytes 73728 | tf_op jit(solution)/shard_map/all_gather | solution.py:205
  138.0 2.2 slice_reduce_fusion.3
  141.2 25.8 %all-gather.19.cloned.1.call-done = bf16[1024,1024]{1,0:T(8,128)(2,1)} async-done(((bf16[128,1024]{1,0:T(8,128)(2,1)}), bf16[1024,1024]{1,0:T(8,128)(2,1)}) %all-gather.19.cloned.1.call-update) | async-done | bytes 2097168 | tf_op jit(solution)/shard_map/all_gather | solution.py:150
  167.0 25.5 %all-gather.17.cloned.1.call-done = bf16[8,128,4384]{2,1,0:T(8,128)(2,1)} async-done(((bf16[8,64,4384]{2,1,0:T(8,128)(2,1)}), bf16[8,128,4384]{2,1,0:T(8,128)(2,1)}) %all-gather.17.cloned.1.call-update) | async-done | bytes 8978448 | tf_op jit(solution)/shard_map/all_gather | solution.py:151
  192.5 7.5 %fusion.73 = f32[256,4384]{0,1:T(8,128)S(1)} fusion(bf16[1024,4384]{1,0:T(8,128)(2,1)} %bitcast.178, f32[256,1024]{1,0:T(8,128)S(1)} %copy-done.8, f32[1024]{0:T(1024)S(1)} %slice_bitcast_fusion.1, f32[256]{0:T(256)S(1)} %fusion.66), kind=kOutput, calls=%fused_computation.151 | convolution fusion | flops 2299265024 | bytes 14521344 | tf_op jit(solution)/shard_map/dot_general | solution.py:219
  200.0 2.2 copy-done.2
  203.7 3.7 slice.181
  208.4 1.5 slice.179
  209.9 1.5 slice.177
  211.6 7.5 %fusion.19 = (f32[256,2304]{0,1:T(8,128)S(1)}, f32[256,2304]{0,1:T(8,128)}) fusion(f32[253,2304]{0,1:T(8,128)} %slice.181, f32[2304]{0:T(1024)S(1)} %get-tuple-element.65, pred[256]{0:T(512)(128)(4,1)S(1)} %get-tuple-element.103, f32[254,2304]{0,1:T(8,128)} %slice.179, f32[2304]{0:T(1024)S(1)} %get-tuple-element.66, ...), kind=kLoop, calls=%fused_computation.34 | loop fusion | flops 8847360 | bytes 14147328 | tf_op jit(solution)/shard_map/jvp(jit(silu))/mul | solution.py:110
  220.5 1.8 fusion.45
  223.7 9.2 %fusion.24 = f32[256,32,64]{0,2,1:T(8,128)S(1)} fusion(f32[256,32,64]{0,2,1:T(8,128)S(1)} %bitcast.151, f32[256,32,64]{0,2,1:T(8,128)S(1)} %fusion.45, f32[256,256]{1,0:T(8,128)S(1)} %fusion.53, f32[32,256]{1,0:T(8,128)S(1)} %bitcast_add_fusion.2, pred[256,256]{1,0:T(8,128)(4,1)S(1)} %copy-done.34, f32[32]{0:T(128)S(1)} %copy-done.59, ...), kind=kOutput, calls=%fused_computation.41 | convolution fusion | flops 1619525632 | bytes 6717568 | tf_op jit(solution)/shard_map/jvp(chij,cjhp->cihp)/dot_general | solution.py:132
  232.9 3.1 multiply_reduce_fusion.9
  237.4 4.6 copy.89
  243.3 5.3 multiply_reduce_fusion.5
  249.2 6.8 multiply_reduce_fusion.6
  260.1 3.2 fusion.36
  263.4 13.7 %fusion.6 = (f32[32,256]{1,0:T(8,128)S(1)}, f32[32,256]{1,0:T(8,128)S(1)}, f32[256,256]{1,0:T(8,128)S(1)}) fusion(f32[256,256]{1,0:T(8,128)S(1)} %fusion.53, f32[32,256]{1,0:T(8,128)} %copy-done.37, pred[256,256]{1,0:T(8,128)(4,1)} %fusion.50, f32[32,64,256]{2,1,0:T(8,128)} %bitcast.143, f32[256,32,64]{0,2,1:T(8,128)} %bitcast.152, ...), kind=kOutput, calls=%fused_computation.7 | convolution fusion | flops 1629929472 | bytes 4915200 | tf_op jit(solution)/shard_map/transpose(jvp(chij,cjhp->cihp))/dot_general | solution.py:132
  279.7 7.5 %fusion.25 = (f32[256,32]{0,1:T(8,128)}, f32[1,256,32,64]{1,3,2,0:T(8,128)S(1)}) fusion(f32[1,256,32,64]{1,3,2,0:T(8,128)S(1)} %bitcast.153, f32[256,32]{0,1:T(8,128)S(1)} %copy-done.23, f32[32,64,256]{2,1,0:T(8,128)S(1)} %bitcast.144, f32[256,256]{1,0:T(8,128)S(1)} %fusion.53, f32[32,256]{1,0:T(8,128)S(1)} %copy-done.38, pred[256,256]{1,0:T(8,128)(4,1)S(1)} %copy-done.35), kind=kOutput, calls=%fused_computation.45 | convolution fusion | flops 1618468864 | bytes 6717440 | tf_op jit(solution)/shard_map/transpose(jvp(chij,cjhp->cihp))/dot_general | solution.py:132
  289.6 3.5 multiply_reduce_fusion.4
  293.8 2.5 reduce-window.19
  297.9 5.4 multiply_reduce_fusion.3
  307.9 2.9 fusion.74
  311.0 1.4 copy.87
  312.4 2.0 reshape.572
  314.5 2.5 add_convert_fusion
  317.1 8.1 %multiply_reduce_fusion.10 = (f32[1024]{0:T(1024)S(1)}, f32[256]{0:T(256)S(1)}, f32[256,1024]{1,0:T(8,128)}) fusion(f32[256,1024]{1,0:T(8,128)S(1)} %copy-done.8, f32[256]{0:T(256)S(1)} %fusion.66, f32[1024]{0:T(1024)S(1)} %slice_bitcast_fusion.1, bf16[256,4384]{0,1:T(8,128)(2,1)S(1)} %add_convert_fusion, bf16[1024,4384]{1,0:T(8,128)(2,1)} %bitcast.179), kind=kOutput, calls=%fused_computation.74 | convolution fusion | flops 2300050176 | bytes 13330432 | tf_op jit(solution)/shard_map/dot_general | solution.py:82
  325.4 4.4 fusion.20
  329.8 6.6 copy.88
  336.4 3.8 dynamic_update_slice.6
  340.3 3.8 convert_bitcast_fusion
  344.2 27.7 %reduce-scatter.9.cloned.1.call-done = f32[8,1,64,4480]{3,2,0,1:T(8,128)} async-done(((f32[8,2,64,4480]{3,2,0,1:T(8,128)}), f32[8,1,64,4480]{3,2,0,1:T(8,128)}) %reduce-scatter.9.cloned.1.call-update) | async-done | bytes 9175056 | tf_op jit(solution)/shard_map/reduce_scatter | solution.py:166
  372.0 6.2 bitcast_convert_fusion.2
  378.3 50.5 %reduce-scatter.15.cloned.1.call-done = bf16[1,128,1024]{2,1,0:T(8,128)(2,1)} async-done(((bf16[8,128,1024]{2,1,0:T(8,128)(2,1)}), bf16[1,128,1024]{2,1,0:T(8,128)(2,1)}) %reduce-scatter.15.cloned.1.call-update) | async-done | bytes 262160 | tf_op jit(solution)/shard_map/reduce_scatter | solution.py:167
  428.8 1.8 bitcast_convert_fusion.1
  430.6 98.6 %reduce-scatter.11.cloned.1.call-done = bf16[1,64,4480]{2,1,0:T(8,128)(2,1)} async-done(((bf16[8,64,4480]{2,1,0:T(8,128)(2,1)}), bf16[1,64,4480]{2,1,0:T(8,128)(2,1)}) %reduce-scatter.11.cloned.1.call-update) | async-done | bytes 573456 | tf_op jit(solution)/shard_map/reduce_scatter | solution.py:167
  529.2 2.1 bitcast_convert_fusion
  531.4 1.6 slice.193
  533.1 85.6 %all-reduce.25.cloned.1.call-done = (f32[64,4480]{1,0:T(8,128)}, f32[128,1024]{1,0:T(8,128)}) async-done(((f32[64,4480]{1,0:T(8,128)}, f32[128,1024]{1,0:T(8,128)}), (f32[64,4480]{1,0:T(8,128)}, f32[128,1024]{1,0:T(8,128)})) %all-reduce.25.cloned.1.call-update) | async-done | bytes 1671184 | tf_op jit(solution)/shard_map/psum | solution.py:172
  618.8 37.5 %reduce-scatter.17.cloned.1.call-done = f32[1,20,96]{2,1,0:T(8,128)} async-done(((f32[8,20,96]{2,1,0:T(8,128)}), f32[1,20,96]{2,1,0:T(8,128)}) %reduce-scatter.17.cloned.1.call-update) | async-done | bytes 7696
  656.3 34.2 %psum.22 = f32[20,96]{1,0:T(8,128)S(1)} all-reduce(f32[20,96]{1,0:T(8,128)} %bitcast.174), channel_id=1, replica_groups=mesh['rep_hi'=8,'core'=2,'shard_0'=4,'shard_1'=2] {'rep_hi'}, use_global_device_ids=true, to_apply=%region_30.31 | all-reduce | flops 1920 | bytes 15360 | tf_op jit(solution)/shard_map/psum | solution.py:172
  690.5 2.2 dynamic_update_slice.7
  692.8 2.9 fusion.39
  695.7 2.4 convolution_add_fusion
  698.1 16.2 %all-gather.11.cloned.1.call-done = f32[128,4480]{1,0:T(8,128)} async-done(((f32[64,4480]{1,0:T(8,128)}), f32[128,4480]{1,0:T(8,128)}) %all-gather.11.cloned.1.call-update) | async-done | bytes 2293776 | tf_op jit(solution)/shard_map/all_gather | solution.py:176
  718.4 3.1 copy.90
  (258 shorter events, 36.9 us)
Async XLA Ops:
  7.2 104.6 %all-gather.15.cloned.1.call-start = ((), (), s32[]{:S(2)}) async-start(), calls=%async_computation.11 | async-start | bytes 5160960 | tf_op jit(solution)/shard_map/all_gather | solution.py:150
  10.5 156.5 %all-gather.19.cloned.1.call-start = ((), (), s32[]{:S(2)}) async-start(), calls=%async_computation.13 | async-start | bytes 2359296 | tf_op jit(solution)/shard_map/all_gather | solution.py:150
  11.3 100.7 %copy-start.48 = (f32[288,4]{0,1:T(4,128)S(1)}, f32[288,4]{0,1:T(4,128)}, u32[]{:S(2)}) copy-start(f32[288,4]{0,1:T(4,128)} %param.17) | copy-start | bytes 13828
  11.3 181.2 %all-gather.17.cloned.1.call-start = ((), (), s32[]{:S(2)}) async-start(), calls=%async_computation.12 | async-start | bytes 13762560 | tf_op jit(solution)/shard_map/all_gather | solution.py:151
  111.8 23.5 %copy-start.67 = (s32[1,2]{1,0:T(1,128)S(1)}, s32[1,2]{1,0:T(1,128)}, u32[]{:S(2)}) copy-start(s32[1,2]{1,0:T(1,128)} %param.14) | copy-start | bytes 28
  111.8 26.0 %copy-start.8 = (f32[256,1024]{1,0:T(8,128)S(1)}, f32[256,1024]{1,0:T(8,128)}, u32[]{:S(2)}) copy-start(f32[256,1024]{1,0:T(8,128)} %param.12) | copy-start | bytes 3145732
  111.9 131.4 %all-gather.21.cloned.1.call-start = ((), (), s32[]{:S(2)}) async-start(), calls=%async_computation.14 | async-start | bytes 6291456 | tf_op jit(solution)/shard_map/all_gather | solution.py:151
  136.5 63.5 %copy-start.55 = (f32[32]{0:T(128)}, f32[32]{0:T(128)S(1)}, u32[]{:S(2)}) copy-start(f32[32]{0:T(128)S(1)} %neg.39) | copy-start | bytes 388
  136.5 63.4 %copy-start.57 = (f32[32]{0:T(128)}, f32[32]{0:T(128)S(1)}, u32[]{:S(2)}) copy-start(f32[32]{0:T(128)S(1)} %add.162) | copy-start | bytes 388
  140.2 71.3 %copy-start.26 = (f32[2304]{0:T(1024)}, f32[2304]{0:T(1024)S(1)}, u32[]{:S(2)}) copy-start(f32[2304]{0:T(1024)S(1)} %get-tuple-element.64) | copy-start | bytes 27652
  140.2 71.3 %copy-start.28 = (f32[2304]{0:T(1024)}, f32[2304]{0:T(1024)S(1)}, u32[]{:S(2)}) copy-start(f32[2304]{0:T(1024)S(1)} %get-tuple-element.65) | copy-start | bytes 27652
  140.3 71.3 %copy-start.30 = (f32[2304]{0:T(1024)}, f32[2304]{0:T(1024)S(1)}, u32[]{:S(2)}) copy-start(f32[2304]{0:T(1024)S(1)} %get-tuple-element.67) | copy-start | bytes 27652
  140.3 71.3 %copy-start.32 = (f32[2304]{0:T(1024)}, f32[2304]{0:T(1024)S(1)}, u32[]{:S(2)}) copy-start(f32[2304]{0:T(1024)S(1)} %get-tuple-element.66) | copy-start | bytes 27652
  140.4 71.2 %copy-start.49 = (pred[256]{0:T(512)(128)(4,1)}, pred[256]{0:T(512)(128)(4,1)S(1)}, u32[]{:S(2)}) copy-start(pred[256]{0:T(512)(128)(4,1)S(1)} %get-tuple-element.101) | copy-start | bytes 772
  140.4 71.2 %copy-start.51 = (pred[256]{0:T(512)(128)(4,1)}, pred[256]{0:T(512)(128)(4,1)S(1)}, u32[]{:S(2)}) copy-start(pred[256]{0:T(512)(128)(4,1)S(1)} %get-tuple-element.102) | copy-start | bytes 772
  140.4 71.2 %copy-start.53 = (pred[256]{0:T(512)(128)(4,1)}, pred[256]{0:T(512)(128)(4,1)S(1)}, u32[]{:S(2)}) copy-start(pred[256]{0:T(512)(128)(4,1)S(1)} %get-tuple-element.103) | copy-start | bytes 772
  140.4 79.1 %copy-start.44 = (f32[256]{0:T(256)}, f32[256]{0:T(256)S(1)}, u32[]{:S(2)}) copy-start(f32[256]{0:T(256)S(1)} %get-tuple-element.100) | copy-start | bytes 3076
  167.0 173.4 %reduce-scatter.13.cloned.1.call-start = ((), (), s32[]{:S(2)}) async-start(), calls=%async_computation.8 | async-start | bytes 12582912 | tf_op jit(solution)/shard_map/reduce_scatter | solution.py:166
  203.7 4.7 copy-start.3
  219.3 13.6 %copy-start.17 = (f32[256,2048]{0,1:T(8,128)}, f32[256,2048]{0,1:T(8,128)S(1)}, u32[]{:S(2)}) copy-start(f32[256,2048]{0,1:T(8,128)S(1)} %slice.182) | copy-start | bytes 6291460
  219.3 4.4 copy-start.22
  219.3 4.4 copy-start.34
  219.3 4.4 copy-start.59
  219.5 13.4 %copy-start.20 = (f32[256,32]{0,1:T(8,128)}, f32[256,32]{0,1:T(8,128)S(1)}, u32[]{:S(2)}) copy-start(f32[256,32]{0,1:T(8,128)S(1)} %bitcast_multiply_fusion.4) | copy-start | bytes 98308
  219.5 13.4 %copy-start.37 = (f32[32,256]{1,0:T(8,128)}, f32[32,256]{1,0:T(8,128)S(1)}, u32[]{:S(2)}) copy-start(f32[32,256]{1,0:T(8,128)S(1)} %bitcast_add_fusion.2) | copy-start | bytes 98308
  236.0 7.3 copy-start.41
  241.9 130.1 %reduce-scatter.9.cloned.1.call-start = ((), (), s32[]{:S(2)}) async-start(), calls=%async_computation.5 | async-start | bytes 27525120 | tf_op jit(solution)/shard_map/reduce_scatter | solution.py:166
  249.2 10.9 %copy-start.21 = (f32[256,32]{0,1:T(8,128)S(1)}, f32[256,32]{0,1:T(8,128)}, u32[]{:S(2)}) copy-start(f32[256,32]{0,1:T(8,128)} %copy-done.20) | copy-start | bytes 98308
  263.3 16.3 %copy-start.4 = (f32[256,2048]{0,1:T(8,128)S(1)}, f32[256,2048]{0,1:T(8,128)}, u32[]{:S(2)}) copy-start(f32[256,2048]{0,1:T(8,128)} %get-tuple-element.71) | copy-start | bytes 6291460
  263.3 16.3 %copy-start.18 = (f32[256,2048]{0,1:T(8,128)S(1)}, f32[256,2048]{0,1:T(8,128)}, u32[]{:S(2)}) copy-start(f32[256,2048]{0,1:T(8,128)} %copy-done.17) | copy-start | bytes 6291460
  263.3 16.3 %copy-start.23 = (f32[256,32]{0,1:T(8,128)S(1)}, f32[256,32]{0,1:T(8,128)}, u32[]{:S(2)}) copy-start(f32[256,32]{0,1:T(8,128)} %get-tuple-element.84) | copy-start | bytes 98308
  263.3 16.3 %copy-start.35 = (pred[256,256]{1,0:T(8,128)(4,1)S(1)}, pred[256,256]{1,0:T(8,128)(4,1)}, u32[]{:S(2)}) copy-start(pred[256,256]{1,0:T(8,128)(4,1)} %fusion.50) | copy-start | bytes 196612
  263.4 16.3 %copy-start.38 = (f32[32,256]{1,0:T(8,128)S(1)}, f32[32,256]{1,0:T(8,128)}, u32[]{:S(2)}) copy-start(f32[32,256]{1,0:T(8,128)} %copy-done.37) | copy-start | bytes 98308
  279.7 7.5 %copy-start.36 = (f32[2048]{0:T(1024)S(1)}, f32[2048]{0:T(1024)}, u32[]{:S(2)}) copy-start(f32[2048]{0:T(1024)} %mul.452) | copy-start | bytes 24580
  293.1 4.7 copy-start.50
  293.1 4.7 copy-start.52
  297.9 5.4 copy-start.33
  317.0 8.1 %copy-start.11 = (bf16[256,4384]{0,1:T(8,128)(2,1)}, bf16[256,4384]{0,1:T(8,128)(2,1)S(1)}, u32[]{:S(2)}) copy-start(bf16[256,4384]{0,1:T(8,128)(2,1)S(1)} %add_convert_fusion) | copy-start | bytes 6733828
  317.1 8.1 %copy-start.40 = (f32[8,256]{1,0:T(8,128)S(1)}, f32[8,256]{1,0:T(8,128)}, u32[]{:S(2)}) copy-start(f32[8,256]{1,0:T(8,128)} %reshape.576) | copy-start | bytes 24580
  317.1 8.1 %copy-start.43 = (f32[8,4]{1,0:T(8,128)S(1)}, f32[8,4]{1,0:T(8,128)}, u32[]{:S(2)}) copy-start(f32[8,4]{1,0:T(8,128)} %reshape.575) | copy-start | bytes 388
  340.3 88.5 %reduce-scatter.15.cloned.1.call-start = ((), (), s32[]{:S(2)}) async-start(), calls=%async_computation.9 | async-start | bytes 2359296 | tf_op jit(solution)/shard_map/reduce_scatter | solution.py:167
  344.2 185.0 %reduce-scatter.11.cloned.1.call-start = ((), (), s32[]{:S(2)}) async-start(), calls=%async_computation.6 | async-start | bytes 5160960 | tf_op jit(solution)/shard_map/reduce_scatter | solution.py:167
  378.2 240.5 %all-reduce.25.cloned.1.call-start = ((), (), s32[]{:S(2)}) async-start(), calls=%async_computation.16 | async-start | bytes 3342336 | tf_op jit(solution)/shard_map/psum | solution.py:172
  430.6 262.2 %copy-start.47 = (f32[256]{0:T(256)S(1)}, f32[256]{0:T(256)}, u32[]{:S(2)}) copy-start(f32[256]{0:T(256)} %copy-done.46) | copy-start | bytes 3076
  531.4 124.9 %reduce-scatter.17.cloned.1.call-start = ((), (), s32[]{:S(2)}) async-start(), calls=%async_computation.15 | async-start | bytes 110592
  533.1 165.0 %all-gather.13.cloned.1.call-start = ((), (), s32[]{:S(2)}) async-start(), calls=%async_computation.10 | async-start | bytes 1572864 | tf_op jit(solution)/shard_map/all_gather | solution.py:176
  618.7 95.6 %all-gather.11.cloned.1.call-start = ((), (), s32[]{:S(2)}) async-start(), calls=%async_computation.7 | async-start | bytes 3440640 | tf_op jit(solution)/shard_map/all_gather | solution.py:176
  718.4 4.1 copy-start.1
  (34 other events, 72.9 us)
Sparse Core Ops, SparseCore 0:
  10.6 101.1 all-gather.14
  114.0 52.8 all-gather.18
  168.6 23.8 all-gather.16
  194.0 17.6 all-gather.20
  242.1 20.8 reduce-scatter.12
  340.4 31.5 reduce-scatter.8
  375.1 53.6 reduce-scatter.14
  431.3 97.8 reduce-scatter.10
  532.4 86.2 all-reduce.24
  621.6 34.6 reduce-scatter.16
  658.0 16.1 all-gather.12
  692.8 21.4 all-gather.10

commit v3 on v1

--- a/solution.py
+++ b/solution.py
@@ -157,9 +157,20 @@
     cols = partial.shape[1]
     blocks = partial.reshape(groups, 2, -1, cols)
     halves = lax.psum_scatter(blocks, "core", scatter_dimension=1, tiled=False)
-    owned = lax.psum_scatter(halves, SHARD, scatter_dimension=0, tiled=False)
-    owned = lax.psum(owned, "rep_hi")
+    owned = lax.psum_scatter(halves.astype(jnp.bfloat16), SHARD, scatter_dimension=0, tiled=False)
+    owned = lax.psum(owned.astype(jnp.float32), "rep_hi")
     return lax.all_gather(owned, "core", axis=0, tiled=True)
+
+
+def exchange_sum(values, axes):
+    for axis in axes:
+        size = lax.axis_size(axis)
+        step = 1
+        while step < size:
+            pairs = [(i, i ^ step) for i in range(size)]
+            values = values + lax.ppermute(values, axis, pairs)
+            step *= 2
+    return values
 
 
 def on_device(
@@ -181,7 +192,12 @@
     segment = segment_ids(seq_lengths[0], count)
     smalls = (norm_gain, conv_weight, conv_bias, step_bias, decay_log, skip_gain, gate_gain)
     flat = jnp.concatenate([a.reshape(-1) for a in smalls])
-    flat_all = lax.all_gather(flat, SHARD, axis=0, tiled=False)
+    flat_len = flat.shape[0]
+    place = lax.axis_index(SHARD)
+    spread = jnp.where(
+        (jnp.arange(groups, dtype=jnp.int32) == place)[:, None], flat[None, :], 0.0
+    )
+    flat_all = exchange_sum(spread, ("shard_1", "shard_0"))
     pieces_full = []
     offset = 0
     for a in smalls:
@@ -193,6 +209,7 @@
     normed_f, norm_back = jax.vjp(norm_input, layer_in, norm_full)
     normed = normed_f.astype(jnp.bfloat16)
     in_whole = gather_rows(in_weight)
+    in_whole, out_weight = lax.optimization_barrier((in_whole, out_weight))
     out_whole = gather_rows(out_weight)
     projected = jnp.dot(normed, in_whole, preferred_element_type=jnp.float32)
 
@@ -217,16 +234,16 @@
     gated_grad = back_product(cot_low, out_whole)
     proj_grad, g_convw, g_convb, g_stepb, g_decay, g_skip, g_gategain = mixer_back(gated_grad)
     proj_low = proj_grad.astype(jnp.bfloat16)
-    cols = proj_low.shape[1]
-    wide = -(-cols // 128) * 128
-    proj_wide = jnp.pad(proj_low, ((0, 0), (0, wide - cols)))
-    in_owned = reduce_rows(row_product(normed, proj_wide))[:, :cols]
     normed_grad = back_product(proj_low, in_whole)
     back_in, g_norm = norm_back(normed_grad)
     input_grad = cotangent + back_in
     grads = (g_norm, g_convw, g_convb, g_stepb, g_decay, g_skip, g_gategain)
     small_blocks = jnp.concatenate([g.reshape(groups, -1) for g in grads], axis=1)
-    small_sum = lax.psum(small_blocks, ALL)
+    cols = proj_low.shape[1]
+    wide = -(-cols // 128) * 128
+    proj_wide = jnp.pad(proj_low, ((0, 0), (0, wide - cols)))
+    in_owned = reduce_rows(row_product(normed, proj_wide))[:, :cols]
+    small_sum = exchange_sum(small_blocks, ("shard_1", "shard_0", "core", "rep_hi"))
     mine = lax.dynamic_index_in_dim(small_sum, lax.axis_index(SHARD), axis=0, keepdims=False)
     small_final = []
     offset = 0

time: 835 us -> 652 us (0.78)
  waiting for transfers between devices: 551 us -> 425 us
  blocking collectives: 95.2 us -> 0 us
  starting transfers between devices: 0.69 us -> 21.5 us
  other arithmetic: 35.6 us -> 50.1 us
    reduce_scatter x2, waiting for transfers between devices: 281 us -> 149 us  [reduce_rows(): lax.psum_scatter(halves.astype(jnp.bfloat16), SHARD, scatter_dimension=0,...]
    psum x1 -> x0, blocking collectives: 68.5 us -> none  [on_device(): small_sum = lax.psum(small_blocks, ALL)]
    unnamed x1 -> x0, blocking collectives: 26.8 us -> none
    ppermute x0 -> x10, starting transfers between devices: none -> 20.8 us  [exchange_sum(): values = values + lax.ppermute(values, axis, pairs)]
    ppermute x0 -> x10, waiting for transfers between devices: none -> 15.9 us  [exchange_sum(): values = values + lax.ppermute(values, axis, pairs)]
    convert_element_type x0 -> x4, other arithmetic: none -> 14 us  [the longest x2 10 us: reduce_rows(): halves.astype(jnp.bfloat16)]
    unnamed x158 -> x169, local copies, waits for them, and re-layouts: 17.1 us -> 13.8 us
  transfers between devices with their start and end apart: 11 -> 21, of which waited for: 7 -> 15; matrix products, arithmetic and copies ran while one was open for 18% -> 26% of each run, Pallas kernels for 0% -> 0%
where the time goes in v3:
time: 652 us; the launch traced here: 642 us
  waiting for transfers between devices  425 us (65%)
  matrix products  66.9 us (10%)
  local copies, waits for them, and re-layouts  63.1 us (10%)
  other arithmetic  50.1 us (8%)
  starting transfers between devices  21.5 us (3%)
  between operations  15.5 us (2%)
    reduce_scatter x2, waiting for transfers between devices, reduce_rows(): lax.psum_scatter(halves.astype(jnp.bfloat16), SHARD, scatter_dimension=0,...  149 us
    all_gather x2, waiting for transfers between devices, gather_rows(): part = lax.all_gather(mine, SHARD, axis=0, tiled=False)  122 us
    psum x1, waiting for transfers between devices, reduce_rows(): owned = lax.psum(owned.astype(jnp.float32), 'rep_hi')  87.2 us
    dot_general x3, matrix products, mixer(): y_intra = jnp.einsum('chij,cjhp->cihp', mixing, scaled_in, precision=HIGH)  29.9 us
    reduce_scatter x2, waiting for transfers between devices, reduce_rows(): halves = lax.psum_scatter(blocks, 'core', scatter_dimension=1, tiled=False)  26.3 us
    all_gather x2, waiting for transfers between devices, gather_rows(): both = lax.all_gather(part, 'core', axis=1, tiled=False)  24.8 us
    ppermute x10, starting transfers between devices, exchange_sum(): values = values + lax.ppermute(values, axis, pairs)  20.8 us
    reshape x2, local copies, waits for them, and re-layouts, reduce_rows(): blocks = partial.reshape(groups, 2, -1, cols)  20.6 us
  transfers between devices with their start and end apart: 21, of which 15 were waited for; matrix products, arithmetic and copies ran while one was open for 26% of the time, Pallas kernels for 0%

profile of v3, /device:TPU:1, one launch (start us, length us, event | category | flops | bytes accessed | tf_op | source)
XLA Modules:
  0.0 642.1 jit_solution(2673646134726412609)
XLA Ops:
  8.8 1.6 copy.77
  10.5 101.3 %all-gather.15.cloned.1.call-done = bf16[512,4384]{1,0:T(8,128)(2,1)} async-done(((bf16[64,4384]{1,0:T(8,128)(2,1)}), bf16[512,4384]{1,0:T(8,128)(2,1)}) %all-gather.15.cloned.1.call-update) | async-done | bytes 4489232 | tf_op jit(solution)/shard_map/all_gather | solution.py:150
  113.4 24.8 %all-gather.17.cloned.1.call-done = bf16[8,128,4384]{2,1,0:T(8,128)(2,1)} async-done(((bf16[8,64,4384]{2,1,0:T(8,128)(2,1)}), bf16[8,128,4384]{2,1,0:T(8,128)(2,1)}) %all-gather.17.cloned.1.call-update) | async-done | bytes 8978448 | tf_op jit(solution)/shard_map/all_gather | solution.py:151
  141.9 1.5 collective-permute-done.1
  143.6 3.0 collective-permute-start.2
  146.6 1.6 collective-permute-done.2
  151.0 2.8 slice_reduce_fusion.3
  153.9 7.5 %fusion.74 = f32[256,4384]{0,1:T(8,128)S(1)} fusion(bf16[1024,4384]{1,0:T(8,128)(2,1)} %bitcast.171, f32[256,1024]{1,0:T(8,128)S(1)} %copy-done.12, f32[1024]{0:T(1024)S(1)} %slice_bitcast_fusion.1, f32[256]{0:T(256)S(1)} %fusion.67), kind=kOutput, calls=%fused_computation.159 | convolution fusion | flops 2299265024 | bytes 14521344 | tf_op jit(solution)/shard_map/dot_general | solution.py:214
  161.4 2.1 copy-done.2
  166.1 3.4 slice.178
  169.7 1.5 slice.174
  172.7 20.7 %all-gather.19.cloned.1.call-done = bf16[1024,1024]{1,0:T(8,128)(2,1)} async-done(((bf16[128,1024]{1,0:T(8,128)(2,1)}), bf16[1024,1024]{1,0:T(8,128)(2,1)}) %all-gather.19.cloned.1.call-update) | async-done | bytes 2097168 | tf_op jit(solution)/shard_map/all_gather | solution.py:150
  194.2 7.2 %fusion.19 = (f32[256,2304]{0,1:T(8,128)S(1)}, f32[256,2304]{0,1:T(8,128)}) fusion(f32[253,2304]{0,1:T(8,128)} %slice.178, f32[2304]{0:T(1024)S(1)} %copy-done.39, pred[256]{0:T(512)(128)(4,1)S(1)} %copy-done.63, f32[254,2304]{0,1:T(8,128)S(1)} %slice.176, f32[2304]{0:T(1024)} %get-tuple-element.59, pred[256]{0:T(512)(128)(4,1)S(1)} %copy-done.61, ...), kind=kLoop, calls=%fused_computation.35 | loop fusion | flops 8847360 | bytes 14147328 | tf_op jit(solution)/shard_map/jvp(jit(silu))/mul | solution.py:110
  203.0 1.8 fusion.45
  204.8 9.2 %fusion.24 = f32[256,32,64]{0,2,1:T(8,128)S(1)} fusion(f32[256,32,64]{0,2,1:T(8,128)S(1)} %bitcast.151, f32[256,32,64]{0,2,1:T(8,128)S(1)} %fusion.45, f32[32]{0:T(128)S(1)} %copy-done.70, f32[256,32]{0,1:T(8,128)S(1)} %bitcast_multiply_fusion.4, f32[256,256]{1,0:T(8,128)S(1)} %fusion.53, f32[32,256]{1,0:T(8,128)S(1)} %bitcast_add_fusion.2, ...), kind=kOutput, calls=%fused_computation.42 | convolution fusion | flops 1619525632 | bytes 6717568 | tf_op jit(solution)/shard_map/jvp(chij,cjhp->cihp)/dot_general | solution.py:132
  214.1 3.1 multiply_reduce_fusion.9
  218.6 14.0 %copy.71 = f32[8,2,128,1024]{3,2,0,1:T(8,128)} copy(f32[8,2,128,1024]{3,2,1,0:T(8,128)S(1)} %bitcast.142) | data formatting | bytes 16777216 | tf_op jit(solution)/shard_map/reshape | solution.py:158
  233.4 5.0 multiply_reduce_fusion.5
  238.4 4.2 multiply_reduce_fusion.6
  242.6 12.0 %fusion.6 = (f32[32,256]{1,0:T(8,128)S(1)}, f32[32,256]{1,0:T(8,128)S(1)}, f32[256,256]{1,0:T(8,128)S(1)}) fusion(f32[256,256]{1,0:T(8,128)S(1)} %copy-done.27, f32[32,256]{1,0:T(8,128)S(1)} %copy-done.48, pred[256,256]{1,0:T(8,128)(4,1)S(1)} %copy-done.45, f32[32,64,256]{2,1,0:T(8,128)S(1)} %bitcast.143, f32[256,32,64]{0,2,1:T(8,128)S(1)} %bitcast.153, ...), kind=kOutput, calls=%fused_computation.7 | convolution fusion | flops 1629929472 | bytes 4915200 | tf_op jit(solution)/shard_map/transpose(jvp(chij,cjhp->cihp))/dot_general | solution.py:132
  256.0 3.2 reduce-window.19
  266.5 3.0 fusion.32
  269.6 8.8 %fusion.25 = (f32[256,32]{0,1:T(8,128)S(1)}, f32[1,256,32,64]{1,3,2,0:T(8,128)S(1)}) fusion(f32[1,256,32,64]{1,3,2,0:T(8,128)} %bitcast.152, f32[256,32]{0,1:T(8,128)S(1)} %copy-done.31, f32[32,64,256]{2,1,0:T(8,128)} %bitcast.145, f32[256,256]{1,0:T(8,128)} %copy-done.26, f32[32,256]{1,0:T(8,128)} %copy-done.47, pred[256,256]{1,0:T(8,128)(4,1)} %fusion.50), kind=kOutput, calls=%fused_computation.46 | convolution fusion | flops 1618468864 | bytes 6717440 | tf_op jit(solution)/shard_map/transpose(jvp(chij,cjhp->cihp))/dot_general | solution.py:132
  284.1 2.4 multiply_reduce_fusion.4
  286.6 2.3 multiply_reduce_fusion.3
  292.0 1.8 fusion.75
  294.5 2.8 fusion.20
  297.3 6.6 %copy.70 = f32[8,2,64,4480]{3,2,0,1:T(8,128)} copy(f32[8,2,64,4480]{3,2,1,0:T(8,128)S(1)} %bitcast.139) | data formatting | bytes 36700160 | tf_op jit(solution)/shard_map/reshape | solution.py:158
  304.0 3.8 convert_bitcast_fusion.1
  307.9 26.3 %reduce-scatter.5.cloned.1.call-done = f32[8,1,64,4480]{3,2,0,1:T(8,128)} async-done(((f32[8,2,64,4480]{3,2,0,1:T(8,128)}), f32[8,1,64,4480]{3,2,0,1:T(8,128)}) %reduce-scatter.5.cloned.1.call-update) | async-done | bytes 9175056 | tf_op jit(solution)/shard_map/reduce_scatter | solution.py:159
  334.2 6.2 convert_bitcast_fusion
  340.5 49.9 %reduce-scatter.11.cloned.1.call-done = bf16[1,128,1024]{2,1,0:T(8,128)(2,1)} async-done(((bf16[8,128,1024]{2,1,0:T(8,128)(2,1)}), bf16[1,128,1024]{2,1,0:T(8,128)(2,1)}) %reduce-scatter.11.cloned.1.call-update) | async-done | bytes 262160 | tf_op jit(solution)/shard_map/reduce_scatter | solution.py:160
  390.4 1.8 bitcast_convert_fusion.1
  392.2 98.6 %reduce-scatter.7.cloned.1.call-done = bf16[1,64,4480]{2,1,0:T(8,128)(2,1)} async-done(((bf16[8,64,4480]{2,1,0:T(8,128)(2,1)}), bf16[1,64,4480]{2,1,0:T(8,128)(2,1)}) %reduce-scatter.7.cloned.1.call-update) | async-done | bytes 573456 | tf_op jit(solution)/shard_map/reduce_scatter | solution.py:160
  490.8 2.2 bitcast_convert_fusion
  493.1 87.2 %all-reduce.22.cloned.1.call-done = (f32[64,4480]{1,0:T(8,128)}, f32[128,1024]{1,0:T(8,128)}) async-done(((f32[64,4480]{1,0:T(8,128)}, f32[128,1024]{1,0:T(8,128)}), (f32[64,4480]{1,0:T(8,128)}, f32[128,1024]{1,0:T(8,128)})) %all-reduce.22.cloned.1.call-update) | async-done | bytes 1671184 | tf_op jit(solution)/shard_map/psum | solution.py:161
  580.8 7.9 %multiply_reduce_fusion.10 = (f32[1024]{0:T(1024)S(1)}, f32[256]{0:T(256)S(1)}, f32[256,1024]{1,0:T(8,128)}) fusion(f32[256,1024]{1,0:T(8,128)S(1)} %copy-done.12, f32[256]{0:T(256)S(1)} %copy-done.50, f32[1024]{0:T(1024)S(1)} %slice_bitcast_fusion.1, bf16[256,4384]{0,1:T(8,128)(2,1)} %copy-done.14, bf16[1024,4384]{1,0:T(8,128)(2,1)} %bitcast.172), kind=kOutput, calls=%fused_computation.75 | convolution fusion | flops 2300050176 | bytes 13330432 | tf_op jit(solution)/shard_map/dot_general | solution.py:82
  590.7 2.0 reshape.575
  593.3 2.7 collective-permute-done.3
  597.3 1.8 collective-permute-done.4
  599.1 3.0 collective-permute-start.5
  602.0 1.7 collective-permute-done.5
  603.8 8.9 %collective-permute-start.6 = (f32[8,1836]{1,0:T(8,128)S(1)}, f32[8,1836]{1,0:T(8,128)S(1)}, u32[]{:S(2)}, u32[]{:S(2)}) collective-permute-start(f32[8,1836]{1,0:T(8,128)S(1)} %add.209), channel_id=1, source_target_pairs={{0,8},{8,0},{1,9},{9,1},{2,10},{10,2},{3,11},{11,3},{4,12},{12,4},... | collective-permute-start | bytes 176264 | tf_op jit(solution)/shard_map/ppermute | solution.py:171
  613.7 4.7 convolution_add_fusion
  618.4 1.5 collective-permute-start.8
  619.9 3.2 collective-permute-done.8
  625.2 2.6 collective-permute-done.9
  631.0 3.2 copy.72
  (298 shorter events, 48.1 us)
Async XLA Ops:
  7.2 104.6 %all-gather.15.cloned.1.call-start = ((), (), s32[]{:S(2)}) async-start(), calls=%async_computation.10 | async-start | bytes 5160960 | tf_op jit(solution)/shard_map/all_gather | solution.py:150
  10.5 101.5 %copy-start.58 = (f32[288,4]{0,1:T(4,128)S(1)}, f32[288,4]{0,1:T(4,128)}, u32[]{:S(2)}) copy-start(f32[288,4]{0,1:T(4,128)} %param.17) | copy-start | bytes 13828
  10.5 127.7 %all-gather.17.cloned.1.call-start = ((), (), s32[]{:S(2)}) async-start(), calls=%async_computation.11 | async-start | bytes 13762560 | tf_op jit(solution)/shard_map/all_gather | solution.py:151
  111.8 26.3 %copy-start.33 = (bf16[256,1024]{1,0:T(8,128)(2,1)S(1)}, bf16[256,1024]{1,0:T(8,128)(2,1)}, u32[]{:S(2)}) copy-start(bf16[256,1024]{1,0:T(8,128)(2,1)} %param.23) | copy-start | bytes 1572868
  111.9 29.9 %copy-start.12 = (f32[256,1024]{1,0:T(8,128)S(1)}, f32[256,1024]{1,0:T(8,128)}, u32[]{:S(2)}) copy-start(f32[256,1024]{1,0:T(8,128)} %param.12) | copy-start | bytes 3145732
  111.9 81.5 %all-gather.19.cloned.1.call-start = ((), (), s32[]{:S(2)}) async-start(), calls=%async_computation.12 | async-start | bytes 2359296 | tf_op jit(solution)/shard_map/all_gather | solution.py:150
  112.7 27.6 %collective-permute-start = (f32[8,1836]{1,0:T(8,128)S(1)}, f32[8,1836]{1,0:T(8,128)S(1)}, u32[]{:S(2)}, u32[]{:S(2)}) collective-permute-start(f32[8,1836]{1,0:T(8,128)S(1)} %broadcast_select_fusion.3), channel_id=1, source_target_pairs={{0,1},{1,0},{2,3},{3,2},{4,5},{5,4},{6,7},{7,6},{8,9},{9,8},{10,11... | collective-permute-start | bytes 176264 | tf_op jit(solution)/shard_map/ppermute | solution.py:171
  138.9 94.4 %all-gather.21.cloned.1.call-start = ((), (), s32[]{:S(2)}) async-start(), calls=%async_computation.13 | async-start | bytes 6291456 | tf_op jit(solution)/shard_map/all_gather | solution.py:151
  140.3 53.9 %copy-start.59 = (pred[256]{0:T(512)(128)(4,1)}, pred[256]{0:T(512)(128)(4,1)S(1)}, u32[]{:S(2)}) copy-start(pred[256]{0:T(512)(128)(4,1)S(1)} %get-tuple-element.94) | copy-start | bytes 772
  140.3 62.1 %copy-start.53 = (f32[256]{0:T(256)}, f32[256]{0:T(256)S(1)}, u32[]{:S(2)}) copy-start(f32[256]{0:T(256)S(1)} %get-tuple-element.93) | copy-start | bytes 3076
  140.4 3.1 collective-permute-start.1
  143.6 4.6 collective-permute-start.2
  149.1 12.2 %copy-start.65 = (f32[32]{0:T(128)}, f32[32]{0:T(128)S(1)}, u32[]{:S(2)}) copy-start(f32[32]{0:T(128)S(1)} %add.196) | copy-start | bytes 388
  149.8 11.6 %copy-start.67 = (f32[32]{0:T(128)}, f32[32]{0:T(128)S(1)}, u32[]{:S(2)}) copy-start(f32[32]{0:T(128)S(1)} %neg.39) | copy-start | bytes 388
  169.7 24.5 %copy-start.8 = (f32[254,2304]{0,1:T(8,128)}, f32[254,2304]{0,1:T(8,128)S(1)}, u32[]{:S(2)}) copy-start(f32[254,2304]{0,1:T(8,128)S(1)} %slice.176) | copy-start | bytes 7022596
  169.7 24.5 %copy-start.37 = (f32[2304]{0:T(1024)S(1)}, f32[2304]{0:T(1024)}, u32[]{:S(2)}) copy-start(f32[2304]{0:T(1024)} %get-tuple-element.57) | copy-start | bytes 27652
  169.7 24.5 %copy-start.39 = (f32[2304]{0:T(1024)S(1)}, f32[2304]{0:T(1024)}, u32[]{:S(2)}) copy-start(f32[2304]{0:T(1024)} %get-tuple-element.58) | copy-start | bytes 27652
  169.7 24.5 %copy-start.61 = (pred[256]{0:T(512)(128)(4,1)S(1)}, pred[256]{0:T(512)(128)(4,1)}, u32[]{:S(2)}) copy-start(pred[256]{0:T(512)(128)(4,1)} %get-tuple-element.95) | copy-start | bytes 772
  169.7 24.5 %copy-start.63 = (pred[256]{0:T(512)(128)(4,1)S(1)}, pred[256]{0:T(512)(128)(4,1)}, u32[]{:S(2)}) copy-start(pred[256]{0:T(512)(128)(4,1)} %get-tuple-element.96) | copy-start | bytes 772
  193.5 110.6 %reduce-scatter.9.cloned.1.call-start = ((), (), s32[]{:S(2)}) async-start(), calls=%async_computation.7 | async-start | bytes 12582912 | tf_op jit(solution)/shard_map/reduce_scatter | solution.py:159
  202.2 11.8 %copy-start.22 = (f32[256,2048]{0,1:T(8,128)}, f32[256,2048]{0,1:T(8,128)S(1)}, u32[]{:S(2)}) copy-start(f32[256,2048]{0,1:T(8,128)S(1)} %slice.179) | copy-start | bytes 6291460
  202.4 11.6 %copy-start.28 = (f32[256,32]{0,1:T(8,128)}, f32[256,32]{0,1:T(8,128)S(1)}, u32[]{:S(2)}) copy-start(f32[256,32]{0,1:T(8,128)S(1)} %bitcast_multiply_fusion.4) | copy-start | bytes 98308
  202.5 11.6 %copy-start.47 = (f32[32,256]{1,0:T(8,128)}, f32[32,256]{1,0:T(8,128)S(1)}, u32[]{:S(2)}) copy-start(f32[32,256]{1,0:T(8,128)S(1)} %bitcast_add_fusion.2) | copy-start | bytes 98308
  203.0 11.1 %copy-start.26 = (f32[256,256]{1,0:T(8,128)}, f32[256,256]{1,0:T(8,128)S(1)}, u32[]{:S(2)}) copy-start(f32[256,256]{1,0:T(8,128)S(1)} %fusion.53) | copy-start | bytes 786436
  217.2 21.1 %copy-start.51 = (f32[256]{0:T(256)}, f32[256]{0:T(256)S(1)}, u32[]{:S(2)}) copy-start(f32[256]{0:T(256)S(1)} %fusion.68) | copy-start | bytes 3076
  232.6 101.7 %reduce-scatter.5.cloned.1.call-start = ((), (), s32[]{:S(2)}) async-start(), calls=%async_computation.4 | async-start | bytes 27525120 | tf_op jit(solution)/shard_map/reduce_scatter | solution.py:159
  242.6 12.0 %copy-start.4 = (f32[256,2048]{0,1:T(8,128)}, f32[256,2048]{0,1:T(8,128)S(1)}, u32[]{:S(2)}) copy-start(f32[256,2048]{0,1:T(8,128)S(1)} %get-tuple-element.64) | copy-start | bytes 6291460
  242.6 12.0 %copy-start.19 = (f32[256,32,64]{0,2,1:T(8,128)S(1)}, f32[256,32,64]{0,2,1:T(8,128)}, u32[]{:S(2)}) copy-start(f32[256,32,64]{0,2,1:T(8,128)} %copy-done.18) | copy-start | bytes 6291460
  255.3 14.2 %copy-start.31 = (f32[256,32]{0,1:T(8,128)S(1)}, f32[256,32]{0,1:T(8,128)}, u32[]{:S(2)}) copy-start(f32[256,32]{0,1:T(8,128)} %get-tuple-element.77) | copy-start | bytes 98308
  266.5 11.9 %slice-start = ((s8[4489216]{0:T(1024)(128)(4,1)}), s8[4194304]{0:T(1024)(128)(4,1)S(1)}, s32[]{:S(2)}) async-start(s8[4489216]{0:T(1024)(128)(4,1)} %bitcast.140), calls=%async_computation.15 | async-start | bytes 8388608
  269.6 12.1 %copy-start.5 = (f32[256,2048]{0,1:T(8,128)S(1)}, f32[256,2048]{0,1:T(8,128)}, u32[]{:S(2)}) copy-start(f32[256,2048]{0,1:T(8,128)} %copy-done.4) | copy-start | bytes 6291460
  269.6 12.1 %copy-start.46 = (f32[2048]{0:T(1024)S(1)}, f32[2048]{0:T(1024)}, u32[]{:S(2)}) copy-start(f32[2048]{0:T(1024)} %mul.457) | copy-start | bytes 24580
  304.0 86.4 %reduce-scatter.11.cloned.1.call-start = ((), (), s32[]{:S(2)}) async-start(), calls=%async_computation.8 | async-start | bytes 2359296 | tf_op jit(solution)/shard_map/reduce_scatter | solution.py:160
  307.9 182.9 %reduce-scatter.7.cloned.1.call-start = ((), (), s32[]{:S(2)}) async-start(), calls=%async_computation.5 | async-start | bytes 5160960 | tf_op jit(solution)/shard_map/reduce_scatter | solution.py:160
  340.4 240.3 %copy-start.73 = (f32[32]{0:T(128)S(1)}, f32[32]{0:T(128)}, u32[]{:S(2)}) copy-start(f32[32]{0:T(128)} %get-tuple-element.86) | copy-start | bytes 388
  340.4 239.9 %all-reduce.22.cloned.1.call-start = ((), (), s32[]{:S(2)}) async-start(), calls=%async_computation.14 | async-start | bytes 3342336 | tf_op jit(solution)/shard_map/psum | solution.py:161
  493.0 138.0 %all-gather.13.cloned.1.call-start = ((), (), s32[]{:S(2)}) async-start(), calls=%async_computation.9 | async-start | bytes 1572864 | tf_op jit(solution)/shard_map/all_gather | solution.py:162
  580.4 50.6 %all-gather.11.cloned.1.call-start = ((), (), s32[]{:S(2)}) async-start(), calls=%async_computation.6 | async-start | bytes 3440640 | tf_op jit(solution)/shard_map/all_gather | solution.py:162
  588.7 24.9 %copy-start.52 = (f32[256]{0:T(256)S(1)}, f32[256]{0:T(256)}, u32[]{:S(2)}) copy-start(f32[256]{0:T(256)} %copy-done.51) | copy-start | bytes 3076
  592.8 3.1 collective-permute-start.3
  595.9 3.2 collective-permute-start.4
  599.1 4.7 collective-permute-start.5
  603.8 9.8 %collective-permute-start.6 = (f32[8,1836]{1,0:T(8,128)S(1)}, f32[8,1836]{1,0:T(8,128)S(1)}, u32[]{:S(2)}, u32[]{:S(2)}) collective-permute-start(f32[8,1836]{1,0:T(8,128)S(1)} %add.209), channel_id=1, source_target_pairs={{0,8},{8,0},{1,9},{9,1},{2,10},{10,2},{3,11},{11,3},{4,12},{12,4},... | collective-permute-start | bytes 176264 | tf_op jit(solution)/shard_map/ppermute | solution.py:171
  613.5 10.4 %copy-start.21 = (f32[256,1024]{1,0:T(8,128)S(1)}, f32[256,1024]{1,0:T(8,128)}, u32[]{:S(2)}) copy-start(f32[256,1024]{1,0:T(8,128)} %param.13) | copy-start | bytes 3145732
  613.6 10.4 %copy-start.24 = (f32[256,1024]{1,0:T(8,128)S(1)}, f32[256,1024]{1,0:T(8,128)}, u32[]{:S(2)}) copy-start(f32[256,1024]{1,0:T(8,128)} %get-tuple-element.98) | copy-start | bytes 3145732
  613.6 4.8 collective-permute-start.7
  618.4 4.7 collective-permute-start.8
  623.1 4.7 collective-permute-start.9
  (54 other events, 186.3 us)
Sparse Core Ops, SparseCore 0:
  10.6 101.1 all-gather.14
  113.5 24.6 all-gather.16
  140.4 53.0 all-gather.18
  194.9 16.1 all-gather.20
  232.7 19.2 reduce-scatter.8
  304.1 30.0 reduce-scatter.4
  336.7 53.5 reduce-scatter.10
  392.9 97.8 reduce-scatter.6
  494.0 86.2 all-reduce.21
  581.9 15.0 all-gather.12
  598.8 14.9 all-gather.10

commit v4 on v3

--- a/solution.py
+++ b/solution.py
@@ -142,24 +142,36 @@
     return gated_pre * scaling * gate_gain[None, :]
 
 
+def core_swap(values):
+    return lax.ppermute(values, "core", [(0, 1), (1, 0)])
+
+
 def gather_rows(weight):
     rows = weight.shape[0]
     half = rows // 2
     core = lax.axis_index("core")
     mine = lax.dynamic_slice_in_dim(weight, core * half, half, axis=0)
     part = lax.all_gather(mine, SHARD, axis=0, tiled=False)
-    both = lax.all_gather(part, "core", axis=1, tiled=False)
-    return both.reshape(-1, weight.shape[1])
+    other = core_swap(part)
+    first = jnp.where(core == 0, part, other)
+    second = jnp.where(core == 0, other, part)
+    return jnp.stack([first, second], axis=1).reshape(-1, weight.shape[1])
 
 
 def reduce_rows(partial):
     groups = lax.axis_size(SHARD)
     cols = partial.shape[1]
+    core = lax.axis_index("core")
     blocks = partial.reshape(groups, 2, -1, cols)
-    halves = lax.psum_scatter(blocks, "core", scatter_dimension=1, tiled=False)
+    keep = jnp.where(core == 0, blocks[:, 0], blocks[:, 1])
+    give = jnp.where(core == 0, blocks[:, 1], blocks[:, 0])
+    halves = keep + core_swap(give)
     owned = lax.psum_scatter(halves.astype(jnp.bfloat16), SHARD, scatter_dimension=0, tiled=False)
     owned = lax.psum(owned.astype(jnp.float32), "rep_hi")
-    return lax.all_gather(owned, "core", axis=0, tiled=True)
+    other = core_swap(owned)
+    first = jnp.where(core == 0, owned, other)
+    second = jnp.where(core == 0, other, owned)
+    return jnp.concatenate([first, second], axis=0)
 
 
 def exchange_sum(values, axes):

time: 652 us -> 570 us (0.87)
  waiting for transfers between devices: 425 us -> 343 us
  other arithmetic: 50.1 us -> 79.9 us
  local copies, waits for them, and re-layouts: 63.1 us -> 35.6 us
    psum x1, waiting for transfers between devices: 87.2 us -> 51.8 us  [reduce_rows(): owned = lax.psum(owned.astype(jnp.float32), 'rep_hi')]
    reduce_scatter x2 -> x0, waiting for transfers between devices: 26.3 us -> none  [reduce_rows(): halves = lax.psum_scatter(blocks, 'core', scatter_dimension=1, tiled=False)]
    all_gather x4 -> x0, waiting for transfers between devices: 24.8 us -> none  [the longest x2 24.8 us: gather_rows(): both = lax.all_gather(part, 'core', axis=1, tiled=False)]
    reshape x2 -> x0, local copies, waits for them, and re-layouts: 20.6 us -> none  [reduce_rows(): blocks = partial.reshape(groups, 2, -1, cols)]
    reduce_scatter x2, waiting for transfers between devices: 149 us -> 130 us  [reduce_rows(): lax.psum_scatter(halves.astype(jnp.bfloat16), SHARD, scatter_dimension=0,...]
    ppermute x0 -> x6, waiting for transfers between devices: none -> 16 us  [core_swap(): return lax.ppermute(values, 'core', [(0, 1), (1, 0)])]
    another operation x6 -> x10, other arithmetic: 5.92 us -> 20.3 us  [the longest x4 16.9 us: gather_rows(): return jnp.stack([first, second], axis=1).reshape(-1, weight.shape[1])]
    select_n x0 -> x4, other arithmetic: none -> 13.3 us  [the longest x2 12 us: reduce_rows(): give = jnp.where(core == 0, blocks[:, 1], blocks[:, 0])]
  transfers between devices with their start and end apart: 21 -> 21, of which waited for: 15 -> 14; matrix products, arithmetic and copies ran while one was open for 26% -> 19% of each run, Pallas kernels for 0% -> 0%
where the time goes in v4:
time: 570 us; the launch traced here: 565 us
  waiting for transfers between devices  343 us (60%)
  other arithmetic  79.9 us (14%)
  matrix products  65.4 us (11%)
  local copies, waits for them, and re-layouts  35.6 us (6%)
  starting transfers between devices  25.7 us (5%)
  between operations  15.4 us (3%)
    reduce_scatter x2, waiting for transfers between devices, reduce_rows(): lax.psum_scatter(halves.astype(jnp.bfloat16), SHARD, scatter_dimension=0,...  130 us
    all_gather x2, waiting for transfers between devices, gather_rows(): part = lax.all_gather(mine, SHARD, axis=0, tiled=False)  129 us
    psum x1, waiting for transfers between devices, reduce_rows(): owned = lax.psum(owned.astype(jnp.float32), 'rep_hi')  51.8 us
    dot_general x3, matrix products, mixer(): y_intra = jnp.einsum('chij,cjhp->cihp', mixing, scaled_in, precision=HIGH)  28.8 us
    ppermute x10, waiting for transfers between devices, exchange_sum(): values = values + lax.ppermute(values, axis, pairs)  17.2 us
    ppermute x10, starting transfers between devices, exchange_sum(): values = values + lax.ppermute(values, axis, pairs)  16.9 us
    another operation x4, other arithmetic, gather_rows(): return jnp.stack([first, second], axis=1).reshape(-1, weight.shape[1])  16.9 us
    ppermute x6, waiting for transfers between devices, core_swap(): return lax.ppermute(values, 'core', [(0, 1), (1, 0)])  16 us
  transfers between devices with their start and end apart: 21, of which 14 were waited for; matrix products, arithmetic and copies ran while one was open for 19% of the time, Pallas kernels for 0%

profile of v4, /device:TPU:1, one launch (start us, length us, event | category | flops | bytes accessed | tf_op | source)
XLA Modules:
  0.0 565.2 jit_solution(14343709525989139011)
XLA Ops:
  10.6 101.3 %all-gather.5.cloned.1.call-done = bf16[512,4384]{1,0:T(8,128)(2,1)} async-done(((bf16[64,4384]{1,0:T(8,128)(2,1)}), bf16[512,4384]{1,0:T(8,128)(2,1)}) %all-gather.5.cloned.1.call-update) | async-done | bytes 4489232 | tf_op jit(solution)/shard_map/all_gather | solution.py:154
  113.9 3.0 collective-permute-done
  117.4 2.7 collective-permute-done.1
  120.2 1.8 collective-permute-start.2
  122.0 8.1 %select_bitcast_fusion.2 = (bf16[8,1,64,4384]{3,2,0,1:T(8,128)(2,1)}, bf16[8,1,64,4384]{3,2,0,1:T(8,128)(2,1)}) fusion(bf16[8,64,4384]{2,1,0:T(8,128)(2,1)} %bitcast.196, bf16[8,64,4384]{2,1,0:T(8,128)(2,1)} %collective-permute-done.3, pred[]{:T(512)S(6)} %eq.74), kind=kLoop, calls=%fused_computation.15 | loop fusion | flops 4489216 | bytes 17956864 | tf_op jit(solution)/shard_map/stack | solution.py:158
  130.1 8.2 %pad_maximum_fusion = bf16[8,2,64,4384]{3,2,0,1:T(8,128)(2,1)} fusion(bf16[8,1,64,4384]{3,2,0,1:T(8,128)(2,1)} %get-tuple-element.81, bf16[8,1,64,4384]{3,2,0,1:T(8,128)(2,1)} %get-tuple-element.80), kind=kLoop, calls=%fused_computation.2 | loop fusion | flops 4489216 | bytes 17956864 | tf_op jit(solution)/shard_map/stack | solution.py:158
  138.2 8.1 %copy.71 = bf16[8,2,64,4384]{3,2,1,0:T(8,128)(2,1)} copy(bf16[8,2,64,4384]{3,2,0,1:T(8,128)(2,1)} %pad_maximum_fusion) | data formatting | bytes 17956864 | tf_op jit(solution)/shard_map/stack | solution.py:158
  149.3 2.2 slice_reduce_fusion.3
  151.5 7.5 %fusion.76 = f32[256,4384]{0,1:T(8,128)S(1)} fusion(bf16[1024,4384]{1,0:T(8,128)(2,1)} %bitcast.193, f32[256,1024]{1,0:T(8,128)S(1)} %copy-done.9, f32[1024]{0:T(1024)S(1)} %slice_bitcast_fusion.5, f32[256]{0:T(256)S(1)} %fusion.69), kind=kOutput, calls=%fused_computation.179 | convolution fusion | flops 2299265024 | bytes 14521344 | tf_op jit(solution)/shard_map/dot_general | solution.py:226
  159.1 1.7 slice.198
  160.7 1.9 slice.196
  165.5 7.3 %fusion.21 = (f32[256,2304]{0,1:T(8,128)S(1)}, f32[256,2304]{0,1:T(8,128)}) fusion(f32[253,2304]{0,1:T(8,128)} %slice.198, f32[2304]{0:T(1024)S(1)} %get-tuple-element.58, pred[256]{0:T(512)(128)(4,1)S(1)} %get-tuple-element.104, f32[254,2304]{0,1:T(8,128)} %slice.196, f32[2304]{0:T(1024)S(1)} %get-tuple-element.59, ...), kind=kLoop, calls=%fused_computation.48 | loop fusion | flops 8847360 | bytes 14147328 | tf_op jit(solution)/shard_map/jvp(jit(silu))/mul | solution.py:110
  172.7 27.5 %all-gather.7.cloned.1.call-done = bf16[1024,1024]{1,0:T(8,128)(2,1)} async-done(((bf16[128,1024]{1,0:T(8,128)(2,1)}), bf16[1024,1024]{1,0:T(8,128)(2,1)}) %all-gather.7.cloned.1.call-update) | async-done | bytes 2097168 | tf_op jit(solution)/shard_map/all_gather | solution.py:154
  202.2 1.8 fusion.47
  204.0 9.2 %fusion.26 = f32[256,32,64]{0,2,1:T(8,128)S(1)} fusion(f32[256,32,64]{0,2,1:T(8,128)S(1)} %bitcast.197, f32[256,32,64]{0,2,1:T(8,128)S(1)} %fusion.47, f32[32]{0:T(128)S(1)} %mul.426, f32[256,32]{0,1:T(8,128)S(1)} %bitcast_multiply_fusion.4, f32[256,256]{1,0:T(8,128)S(1)} %fusion.55, f32[32,256]{1,0:T(8,128)S(1)} %bitcast_add_fusion.4, ...), kind=kOutput, calls=%fused_computation.56 | convolution fusion | flops 1619525632 | bytes 6717568 | tf_op jit(solution)/shard_map/jvp(chij,cjhp->cihp)/dot_general | solution.py:132
  216.3 1.9 multiply_reduce_fusion.5
  218.6 3.0 multiply_reduce_fusion.6
  223.5 11.5 %fusion.7 = (f32[32,256]{1,0:T(8,128)S(1)}, f32[32,256]{1,0:T(8,128)S(1)}, f32[256,256]{1,0:T(8,128)S(1)}) fusion(f32[256,256]{1,0:T(8,128)S(1)} %fusion.55, f32[32,256]{1,0:T(8,128)S(1)} %bitcast_add_fusion.4, pred[256,256]{1,0:T(8,128)(4,1)S(1)} %copy-done.30, f32[32,64,256]{2,1,0:T(8,128)S(1)} %bitcast.189, f32[256,32,64]{0,2,1:T(8,128)S(1)} %bitcast.198, ...), kind=kOutput, calls=%fused_computation.13 | convolution fusion | flops 1629929472 | bytes 4915200 | tf_op jit(solution)/shard_map/transpose(jvp(chij,cjhp->cihp))/dot_general | solution.py:132
  235.0 8.1 %fusion.27 = (f32[256,32]{0,1:T(8,128)S(1)}, f32[1,256,32,64]{1,3,2,0:T(8,128)}) fusion(f32[1,256,32,64]{1,3,2,0:T(8,128)S(1)} %bitcast.199, f32[256,32]{0,1:T(8,128)S(1)} %get-tuple-element.77, f32[32,64,256]{2,1,0:T(8,128)S(1)} %bitcast.190, f32[256,256]{1,0:T(8,128)S(1)} %fusion.55, f32[32,256]{1,0:T(8,128)S(1)} %bitcast_add_fusion.4, ...), kind=kOutput, calls=%fused_computation.60 | convolution fusion | flops 1618468864 | bytes 6717440 | tf_op jit(solution)/shard_map/transpose(jvp(chij,cjhp->cihp))/dot_general | solution.py:132
  244.0 2.5 reduce-window.19
  246.9 2.7 bitcast_add_fusion.3
  250.5 2.4 multiply_reduce_fusion.4
  253.0 2.3 multiply_reduce_fusion.3
  258.7 1.8 fusion.77
  261.8 7.8 %fusion.22 = f32[1024,4480]{1,0:T(8,128)} fusion(bf16[256,4384]{0,1:T(8,128)(2,1)S(1)} %add_convert_fusion, f32[256,1024]{1,0:T(8,128)S(1)} %copy-done.10, f32[1024]{0:T(1024)S(1)} %slice_bitcast_fusion.5, f32[256]{0:T(256)S(1)} %copy-done.32), kind=kOutput, calls=%fused_computation.51 | convolution fusion | flops 2349596672 | bytes 21648384 | tf_op jit(solution)/shard_map/dot_general | solution.py:76
  269.6 10.6 %select_bitcast_fusion = f32[8,64,4480]{2,1,0:T(8,128)} fusion(f32[8,2,64,4480]{3,2,1,0:T(8,128)} %bitcast.180, pred[]{:T(512)S(6)} %eq.74), kind=kLoop, calls=%fused_computation.5 | loop fusion | flops 2293760 | bytes 27525120 | tf_op jit(solution)/shard_map/jit(_where)/select_n | solution.py:167
  280.3 2.5 fusion.49
  285.0 15.5 %collective-permute-done.14 = f32[8,128,1024]{2,1,0:T(8,128)S(1)} collective-permute-done((f32[8,128,1024]{2,1,0:T(8,128)S(1)}, f32[8,128,1024]{2,1,0:T(8,128)S(1)}, u32[]{:S(2)}, u32[]{:S(2)}) %collective-permute-start.14) | collective-permute-done | bytes 4194336 | tf_op jit(solution)/shard_map/ppermute | solution.py:146
  300.5 2.5 fusion.8
  303.1 11.9 %fusion = bf16[8,64,4480]{2,1,0:T(8,128)(2,1)} fusion(f32[8,64,4480]{2,1,0:T(8,128)} %collective-permute-done.12, f32[8,2,64,4480]{3,2,1,0:T(8,128)} %bitcast.181, pred[]{:T(512)S(6)} %eq.74), kind=kLoop, calls=%fused_computation.4 | loop fusion | flops 6881280 | bytes 32112640 | tf_op jit(solution)/shard_map/convert_element_type | solution.py:169
  315.2 8.0 %multiply_reduce_fusion.10 = (f32[1024]{0:T(1024)S(1)}, f32[256]{0:T(256)S(1)}, f32[256,1024]{1,0:T(8,128)}) fusion(f32[256,1024]{1,0:T(8,128)S(1)} %copy-done.10, f32[256]{0:T(256)S(1)} %copy-done.32, f32[1024]{0:T(1024)S(1)} %slice_bitcast_fusion.5, bf16[256,4384]{0,1:T(8,128)(2,1)} %copy-done.13, bf16[1024,4384]{1,0:T(8,128)(2,1)} %bitcast.194), kind=kOutput, calls=%fused_computation.91 | convolution fusion | flops 2300050176 | bytes 13330432 | tf_op jit(solution)/shard_map/dot_general | solution.py:82
  323.1 31.2 %reduce-scatter.5.cloned.1.call-done = bf16[1,128,1024]{2,1,0:T(8,128)(2,1)} async-done(((bf16[8,128,1024]{2,1,0:T(8,128)(2,1)}), bf16[1,128,1024]{2,1,0:T(8,128)(2,1)}) %reduce-scatter.5.cloned.1.call-update) | async-done | bytes 262160 | tf_op jit(solution)/shard_map/reduce_scatter | solution.py:169
  354.3 1.8 bitcast_convert_fusion.1
  356.1 98.4 %reduce-scatter.3.cloned.1.call-done = bf16[1,64,4480]{2,1,0:T(8,128)(2,1)} async-done(((bf16[8,64,4480]{2,1,0:T(8,128)(2,1)}), bf16[1,64,4480]{2,1,0:T(8,128)(2,1)}) %reduce-scatter.3.cloned.1.call-update) | async-done | bytes 573456 | tf_op jit(solution)/shard_map/reduce_scatter | solution.py:169
  454.5 2.1 bitcast_convert_fusion
  458.6 2.0 reshape.581
  461.3 2.7 collective-permute-done.5
  464.5 2.6 collective-permute-done.6
  467.1 2.1 collective-permute-start.7
  469.2 3.0 collective-permute-done.7
  472.2 4.0 collective-permute-start.8
  478.4 4.6 convolution_add_fusion
  482.9 2.5 collective-permute-start.10
  485.5 2.2 collective-permute-done.10
  487.7 4.0 collective-permute-start.11
  493.0 51.8 %all-reduce.22.cloned.1.call-done = (f32[64,4480]{1,0:T(8,128)}, f32[128,1024]{1,0:T(8,128)}) async-done(((f32[64,4480]{1,0:T(8,128)}, f32[128,1024]{1,0:T(8,128)}), (f32[64,4480]{1,0:T(8,128)}, f32[128,1024]{1,0:T(8,128)})) %all-reduce.22.cloned.1.call-update) | async-done | bytes 1671184 | tf_op jit(solution)/shard_map/psum | solution.py:170
  544.7 5.3 collective-permute-start.13
  556.3 2.0 copy.86
  (257 shorter events, 40.3 us)
Async XLA Ops:
  7.2 105.6 %copy-start.37 = (f32[288,4]{0,1:T(4,128)S(1)}, f32[288,4]{0,1:T(4,128)}, u32[]{:S(2)}) copy-start(f32[288,4]{0,1:T(4,128)} %param.17) | copy-start | bytes 13828
  7.2 104.6 %all-gather.5.cloned.1.call-start = ((), (), s32[]{:S(2)}) async-start(), calls=%async_computation.4 | async-start | bytes 5160960 | tf_op jit(solution)/shard_map/all_gather | solution.py:154
  8.4 104.6 %copy-start.48 = (f32[288]{0:T(512)S(1)}, f32[288]{0:T(512)}, u32[]{:S(2)}) copy-start(f32[288]{0:T(512)} %param.18) | copy-start | bytes 3460
  8.4 104.6 %copy-start.49 = (f32[256]{0:T(256)S(1)}, f32[256]{0:T(256)}, u32[]{:S(2)}) copy-start(f32[256]{0:T(256)} %param.22) | copy-start | bytes 3076
  8.4 104.6 %copy-start.50 = (f32[128]{0:T(128)S(1)}, f32[128]{0:T(128)}, u32[]{:S(2)}) copy-start(f32[128]{0:T(128)} %param.15) | copy-start | bytes 1540
  8.4 104.6 %copy-start.51 = (f32[4]{0:T(128)S(1)}, f32[4]{0:T(128)}, u32[]{:S(2)}) copy-start(f32[4]{0:T(128)} %param.19) | copy-start | bytes 52
  8.5 104.6 %copy-start.52 = (f32[4]{0:T(128)S(1)}, f32[4]{0:T(128)}, u32[]{:S(2)}) copy-start(f32[4]{0:T(128)} %param.20) | copy-start | bytes 52
  8.5 104.6 %copy-start.53 = (f32[4]{0:T(128)S(1)}, f32[4]{0:T(128)}, u32[]{:S(2)}) copy-start(f32[4]{0:T(128)} %param.21) | copy-start | bytes 52
  8.5 105.0 %copy-start.54 = (s32[1,2]{1,0:T(1,128)S(1)}, s32[1,2]{1,0:T(1,128)}, u32[]{:S(2)}) copy-start(s32[1,2]{1,0:T(1,128)} %param.14) | copy-start | bytes 28
  8.5 108.7 %copy-start.9 = (f32[256,1024]{1,0:T(8,128)S(1)}, f32[256,1024]{1,0:T(8,128)}, u32[]{:S(2)}) copy-start(f32[256,1024]{1,0:T(8,128)} %param.12) | copy-start | bytes 3145732
  10.5 189.7 %all-gather.7.cloned.1.call-start = ((), (), s32[]{:S(2)}) async-start(), calls=%async_computation.5 | async-start | bytes 2359296 | tf_op jit(solution)/shard_map/all_gather | solution.py:154
  111.9 10.1 %collective-permute-start.3 = (bf16[8,64,4384]{2,1,0:T(8,128)(2,1)}, bf16[8,64,4384]{2,1,0:T(8,128)(2,1)}, u32[]{:S(2)}, u32[]{:S(2)}) collective-permute-start(bf16[8,64,4384]{2,1,0:T(8,128)(2,1)} %bitcast.195), channel_id=1, source_target_pairs={{0,8},{8,0},{1,9},{9,1},{2,10},{10,2},{3,11},{11,3},{4,12},{12,4},... | collective-permute-start | bytes 13467656 | tf_op jit(solution)/shard_map/ppermute | solution.py:146
  113.3 3.6 collective-permute-start
  113.8 90.1 %copy-start.29 = (pred[256,256]{1,0:T(8,128)(4,1)}, pred[256,256]{1,0:T(8,128)(4,1)S(1)}, u32[]{:S(2)}) copy-start(pred[256,256]{1,0:T(8,128)(4,1)S(1)} %fusion.52) | copy-start | bytes 196612
  113.9 51.5 %copy-start.38 = (pred[256]{0:T(512)(128)(4,1)}, pred[256]{0:T(512)(128)(4,1)S(1)}, u32[]{:S(2)}) copy-start(pred[256]{0:T(512)(128)(4,1)S(1)} %get-tuple-element.102) | copy-start | bytes 772
  113.9 51.5 %copy-start.40 = (pred[256]{0:T(512)(128)(4,1)}, pred[256]{0:T(512)(128)(4,1)S(1)}, u32[]{:S(2)}) copy-start(pred[256]{0:T(512)(128)(4,1)S(1)} %get-tuple-element.103) | copy-start | bytes 772
  113.9 51.5 %copy-start.42 = (pred[256]{0:T(512)(128)(4,1)}, pred[256]{0:T(512)(128)(4,1)S(1)}, u32[]{:S(2)}) copy-start(pred[256]{0:T(512)(128)(4,1)S(1)} %get-tuple-element.104) | copy-start | bytes 772
  113.9 87.6 %copy-start.33 = (f32[256]{0:T(256)}, f32[256]{0:T(256)S(1)}, u32[]{:S(2)}) copy-start(f32[256]{0:T(256)S(1)} %get-tuple-element.101) | copy-start | bytes 3076
  117.0 3.1 collective-permute-start.1
  117.3 30.0 %copy-start.35 = (f32[256]{0:T(256)}, f32[256]{0:T(256)S(1)}, u32[]{:S(2)}) copy-start(f32[256]{0:T(256)S(1)} %multiply_reduce_fusion.12) | copy-start | bytes 3076
  120.2 27.2 %collective-permute-start.2 = (f32[8,1836]{1,0:T(8,128)S(1)}, f32[8,1836]{1,0:T(8,128)S(1)}, u32[]{:S(2)}, u32[]{:S(2)}) collective-permute-start(f32[8,1836]{1,0:T(8,128)S(1)} %fusion.92), channel_id=1, source_target_pairs={{0,4},{2,6},{4,0},{6,2},{1,5},{3,7},{5,1},{7,3},{8,12},{10,14},{12... | collective-permute-start | bytes 176264 | tf_op jit(solution)/shard_map/ppermute | solution.py:183
  147.1 207.2 %reduce-scatter.5.cloned.1.call-start = ((), (), s32[]{:S(2)}) async-start(), calls=%async_computation.3 | async-start | bytes 2359296 | tf_op jit(solution)/shard_map/reduce_scatter | solution.py:169
  147.7 16.5 %copy-start.44 = (f32[32]{0:T(128)}, f32[32]{0:T(128)S(1)}, u32[]{:S(2)}) copy-start(f32[32]{0:T(128)S(1)} %add.198) | copy-start | bytes 388
  147.9 16.3 %copy-start.46 = (f32[32]{0:T(128)}, f32[32]{0:T(128)S(1)}, u32[]{:S(2)}) copy-start(f32[32]{0:T(128)S(1)} %neg.39) | copy-start | bytes 388
  151.5 13.9 %copy-start.21 = (f32[2304]{0:T(1024)}, f32[2304]{0:T(1024)S(1)}, u32[]{:S(2)}) copy-start(f32[2304]{0:T(1024)S(1)} %get-tuple-element.57) | copy-start | bytes 27652
  151.5 13.9 %copy-start.23 = (f32[2304]{0:T(1024)}, f32[2304]{0:T(1024)S(1)}, u32[]{:S(2)}) copy-start(f32[2304]{0:T(1024)S(1)} %get-tuple-element.58) | copy-start | bytes 27652
  151.5 13.9 %copy-start.25 = (f32[2304]{0:T(1024)}, f32[2304]{0:T(1024)S(1)}, u32[]{:S(2)}) copy-start(f32[2304]{0:T(1024)S(1)} %get-tuple-element.60) | copy-start | bytes 27652
  151.5 13.9 %copy-start.27 = (f32[2304]{0:T(1024)}, f32[2304]{0:T(1024)S(1)}, u32[]{:S(2)}) copy-start(f32[2304]{0:T(1024)S(1)} %get-tuple-element.59) | copy-start | bytes 27652
  172.7 29.4 %copy-start.4 = (f32[256,2304]{0,1:T(8,128)}, f32[256,2304]{0,1:T(8,128)S(1)}, u32[]{:S(2)}) copy-start(f32[256,2304]{0,1:T(8,128)S(1)} %get-tuple-element.78) | copy-start | bytes 7077892
  200.2 13.7 %collective-permute-start.4 = (bf16[8,128,1024]{2,1,0:T(8,128)(2,1)}, bf16[8,128,1024]{2,1,0:T(8,128)(2,1)S(1)}, u32[]{:S(2)}, u32[]{:S(2)}) collective-permute-start(bf16[8,128,1024]{2,1,0:T(8,128)(2,1)} %bitcast.200), channel_id=1, source_target_pairs={{0,8},{8,0},{1,9},{9,1},{2,10},{10,2},{3,11},{11,3},{4,12},{12,4},... | collective-permute-start | bytes 6291464 | tf_op jit(solution)/shard_map/ppermute | solution.py:146
  202.1 11.0 %slice-start = ((s8[4489216]{0:T(1024)(128)(4,1)}), s8[4194304]{0:T(1024)(128)(4,1)S(1)}, s32[]{:S(2)}) async-start(s8[4489216]{0:T(1024)(128)(4,1)} %bitcast.184), calls=%async_computation.7 | async-start | bytes 8388608
  221.6 13.4 %copy-start.3 = (f32[256,2048]{0,1:T(8,128)}, f32[256,2048]{0,1:T(8,128)S(1)}, u32[]{:S(2)}) copy-start(f32[256,2048]{0,1:T(8,128)S(1)} %get-tuple-element.64) | copy-start | bytes 6291460
  280.2 22.9 %collective-permute-start.12 = (f32[8,64,4480]{2,1,0:T(8,128)}, f32[8,64,4480]{2,1,0:T(8,128)}, u32[]{:S(2)}, u32[]{:S(2)}) collective-permute-start(f32[8,64,4480]{2,1,0:T(8,128)} %select_bitcast_fusion), channel_id=1, source_target_pairs={{0,8},{8,0},{1,9},{9,1},{2,10},{10,2},{3,11},{11,3},{4,12},{12,4},... | collective-permute-start | bytes 27525128 | tf_op jit(solution)/shard_map/ppermute | solution.py:146
  284.2 16.4 %collective-permute-start.14 = (f32[8,128,1024]{2,1,0:T(8,128)S(1)}, f32[8,128,1024]{2,1,0:T(8,128)S(1)}, u32[]{:S(2)}, u32[]{:S(2)}) collective-permute-start(f32[8,128,1024]{2,1,0:T(8,128)S(1)} %select_bitcast_fusion.3), channel_id=1, source_target_pairs={{0,8},{8,0},{1,9},{9,1},{2,10},{10,2},{3,11},{11,3},{4,12},{12,4},... | collective-permute-start | bytes 12582920 | tf_op jit(solution)/shard_map/ppermute | solution.py:146
  303.1 151.4 %reduce-scatter.3.cloned.1.call-start = ((), (), s32[]{:S(2)}) async-start(), calls=%async_computation.2 | async-start | bytes 5160960 | tf_op jit(solution)/shard_map/reduce_scatter | solution.py:169
  315.1 229.7 %all-reduce.22.cloned.1.call-start = ((), (), s32[]{:S(2)}) async-start(), calls=%async_computation.6 | async-start | bytes 3342336 | tf_op jit(solution)/shard_map/psum | solution.py:170
  460.8 3.1 collective-permute-start.5
  463.9 3.2 collective-permute-start.6
  467.1 5.1 collective-permute-start.7
  472.2 4.9 collective-permute-start.8
  477.1 14.7 %copy-start.16 = (f32[256,1024]{1,0:T(8,128)S(1)}, f32[256,1024]{1,0:T(8,128)}, u32[]{:S(2)}) copy-start(f32[256,1024]{1,0:T(8,128)} %param.13) | copy-start | bytes 3145732
  477.1 14.7 %copy-start.19 = (f32[256,1024]{1,0:T(8,128)S(1)}, f32[256,1024]{1,0:T(8,128)}, u32[]{:S(2)}) copy-start(f32[256,1024]{1,0:T(8,128)} %get-tuple-element.106) | copy-start | bytes 3145732
  477.1 5.8 %collective-permute-start.9 = (f32[8,1836]{1,0:T(8,128)S(1)}, f32[8,1836]{1,0:T(8,128)S(1)}, u32[]{:S(2)}, u32[]{:S(2)}) collective-permute-start(f32[8,1836]{1,0:T(8,128)S(1)} %add.212), channel_id=1, source_target_pairs={{0,16},{16,0},{32,48},{48,32},{64,80},{80,64},{96,112},{112,96},{1... | collective-permute-start | bytes 176264 | tf_op jit(solution)/shard_map/ppermute | solution.py:183
  482.9 4.8 collective-permute-start.10
  487.7 62.4 %collective-permute-start.11 = (f32[8,1836]{1,0:T(8,128)S(1)}, f32[8,1836]{1,0:T(8,128)S(1)}, u32[]{:S(2)}, u32[]{:S(2)}) collective-permute-start(f32[8,1836]{1,0:T(8,128)S(1)} %add.214), channel_id=1, source_target_pairs={{0,64},{16,80},{32,96},{48,112},{64,0},{80,16},{96,32},{112,48},{1... | collective-permute-start | bytes 176264 | tf_op jit(solution)/shard_map/ppermute | solution.py:183
  544.7 11.2 %copy-start.18 = (f32[64,4480]{1,0:T(8,128)S(1)}, f32[64,4480]{1,0:T(8,128)}, u32[]{:S(2)}) copy-start(f32[64,4480]{1,0:T(8,128)} %get-tuple-element.61) | copy-start | bytes 3440644
  544.7 11.2 %collective-permute-start.13 = (f32[64,4480]{1,0:T(8,128)}, f32[64,4480]{1,0:T(8,128)S(1)}, u32[]{:S(2)}, u32[]{:S(2)}) collective-permute-start(f32[64,4480]{1,0:T(8,128)} %get-tuple-element.61), channel_id=1, source_target_pairs={{0,8},{8,0},{1,9},{9,1},{2,10},{10,2},{3,11},{11,3},{4,12},{12,4},... | collective-permute-start | bytes 3440648 | tf_op jit(solution)/shard_map/ppermute | solution.py:146
  551.6 2.1 collective-permute-start.15
  (32 other events, 102.2 us)
Sparse Core Ops, SparseCore 0:
  10.6 101.1 all-gather.4
  147.2 53.0 all-gather.6
  303.2 51.0 reduce-scatter.4
  356.6 97.8 reduce-scatter.2
  457.1 87.5 all-reduce.21

commit v5 on v4

--- a/solution.py
+++ b/solution.py
@@ -146,32 +146,68 @@
     return lax.ppermute(values, "core", [(0, 1), (1, 0)])
 
 
-def gather_rows(weight):
+def gather_group(block):
+    ring = lax.axis_size("shard_0")
+    y = lax.axis_index("shard_1")
+    z = lax.axis_index("shard_0")
+    other_y = lax.ppermute(block, "shard_1", [(0, 1), (1, 0)])
+    pair = jnp.where(y == 0, jnp.stack([block, other_y]), jnp.stack([other_y, block]))
+    up = [(i, (i + 1) % ring) for i in range(ring)]
+    down = [(i, (i - 1) % ring) for i in range(ring)]
+    from_prev = lax.ppermute(pair, "shard_0", up)
+    from_next = lax.ppermute(pair, "shard_0", down)
+    half = block.shape[0] // 2
+    far_a = lax.ppermute(from_prev[:, :half], "shard_0", up)
+    far_b = lax.ppermute(from_next[:, half:], "shard_0", down)
+    opposite = jnp.concatenate([far_a, far_b], axis=1)
+    ordered = jnp.stack([pair, from_next, opposite, from_prev])
+    doubled = jnp.concatenate([ordered, ordered], axis=0)
+    start = (ring - z) % ring
+    placed = lax.dynamic_slice_in_dim(doubled, start, ring, axis=0)
+    return placed.reshape((ring * 2,) + block.shape)
+
+
+def core_swap(values):
+    return lax.ppermute(values, "core", [(0, 1), (1, 0)])
+
+
+def gather_rows(weight, by_permutes=False):
     rows = weight.shape[0]
     half = rows // 2
     core = lax.axis_index("core")
     mine = lax.dynamic_slice_in_dim(weight, core * half, half, axis=0)
-    part = lax.all_gather(mine, SHARD, axis=0, tiled=False)
+    if by_permutes:
+        part = gather_group(mine)
+    else:
+        part = lax.all_gather(mine, SHARD, axis=0, tiled=False)
     other = core_swap(part)
     first = jnp.where(core == 0, part, other)
     second = jnp.where(core == 0, other, part)
     return jnp.stack([first, second], axis=1).reshape(-1, weight.shape[1])
 
 
-def reduce_rows(partial):
+def reduce_core(partial):
     groups = lax.axis_size(SHARD)
     cols = partial.shape[1]
     core = lax.axis_index("core")
     blocks = partial.reshape(groups, 2, -1, cols)
     keep = jnp.where(core == 0, blocks[:, 0], blocks[:, 1])
     give = jnp.where(core == 0, blocks[:, 1], blocks[:, 0])
-    halves = keep + core_swap(give)
+    return keep + core_swap(give)
+
+
+def reduce_rest(halves):
+    core = lax.axis_index("core")
     owned = lax.psum_scatter(halves.astype(jnp.bfloat16), SHARD, scatter_dimension=0, tiled=False)
     owned = lax.psum(owned.astype(jnp.float32), "rep_hi")
     other = core_swap(owned)
     first = jnp.where(core == 0, owned, other)
     second = jnp.where(core == 0, other, owned)
     return jnp.concatenate([first, second], axis=0)
+
+
+def reduce_rows(partial):
+    return reduce_rest(reduce_core(partial))
 
 
 def exchange_sum(values, axes):
@@ -220,7 +256,7 @@
     norm_full, convw_full, convb_full, stepb_full, decay_full, skip_full, gategain_full = pieces_full
     normed_f, norm_back = jax.vjp(norm_input, layer_in, norm_full)
     normed = normed_f.astype(jnp.bfloat16)
-    in_whole = gather_rows(in_weight)
+    in_whole = gather_rows(in_weight, by_permutes=True)
     in_whole, out_weight = lax.optimization_barrier((in_whole, out_weight))
     out_whole = gather_rows(out_weight)
     projected = jnp.dot(normed, in_whole, preferred_element_type=jnp.float32)
@@ -242,8 +278,10 @@
     branch_out = jnp.dot(gated, out_whole, preferred_element_type=jnp.float32)
     layer_out = layer_in + branch_out
     cot_low = cotangent.astype(jnp.bfloat16)
-    out_owned = reduce_rows(row_product(gated, cot_low))
+    out_halves = reduce_core(row_product(gated, cot_low))
     gated_grad = back_product(cot_low, out_whole)
+    out_halves, gated_grad = lax.optimization_barrier((out_halves, gated_grad))
+    out_owned = reduce_rest(out_halves)
     proj_grad, g_convw, g_convb, g_stepb, g_decay, g_skip, g_gategain = mixer_back(gated_grad)
     proj_low = proj_grad.astype(jnp.bfloat16)
     normed_grad = back_product(proj_low, in_whole)

time: 570 us -> 552 us (0.968)
  waiting for transfers between devices: 343 us -> 273 us
  other arithmetic: 79.9 us -> 98.5 us
  starting transfers between devices: 25.7 us -> 40.9 us
  local copies, waits for them, and re-layouts: 35.6 us -> 50.4 us
    all_gather x2 -> x1, waiting for transfers between devices: 129 us -> 29.1 us  [gather_rows(): part = lax.all_gather(mine, SHARD, axis=0, tiled=False)]
    ppermute x0 -> x5, waiting for transfers between devices: none -> 45.6 us  [the longest x1 22.8 us: gather_group(): from_prev = lax.ppermute(pair, 'shard_0', up)]
    reduce_scatter x2, waiting for transfers between devices: 130 us -> 115 us  [reduce_rest(): lax.psum_scatter(halves.astype(jnp.bfloat16), SHARD, scatter_dimension=0,...]
    ppermute x0 -> x5, starting transfers between devices: none -> 9.02 us  [the longest x1 2.72 us: gather_group(): far_b = lax.ppermute(from_next[:, half:], 'shard_0', down)]
    add x0 -> x1, other arithmetic: none -> 7.2 us  [reduce_core(): return keep + core_swap(give)]
    unnamed x124 -> x163, local copies, waits for them, and re-layouts: 9.81 us -> 16.1 us
    select_n x4 -> x5, other arithmetic: 13.3 us -> 16.6 us  [the longest x2 14 us: reduce_core(): give = jnp.where(core == 0, blocks[:, 1], blocks[:, 0])]
    convert_element_type x4 -> x3, other arithmetic: 18.4 us -> 15.8 us  [the longest x1 11.9 us: reduce_rest(): halves.astype(jnp.bfloat16)]
  transfers between devices with their start and end apart: 21 -> 25, of which waited for: 14 -> 17; matrix products, arithmetic and copies ran while one was open for 19% -> 14% of each run, Pallas kernels for 0% -> 0%
where the time goes in v5:
time: 552 us; the launch traced here: 546 us
  waiting for transfers between devices  273 us (49%)
  other arithmetic  98.5 us (18%)
  matrix products  67.4 us (12%)
  local copies, waits for them, and re-layouts  50.4 us (9%)
  starting transfers between devices  40.9 us (7%)
  between operations  15.5 us (3%)
    reduce_scatter x2, waiting for transfers between devices, reduce_rest(): lax.psum_scatter(halves.astype(jnp.bfloat16), SHARD, scatter_dimension=0,...  115 us
    psum x1, waiting for transfers between devices, reduce_rest(): owned = lax.psum(owned.astype(jnp.float32), 'rep_hi')  51.8 us
    dot_general x3, matrix products, mixer(): y_intra = jnp.einsum('chij,cjhp->cihp', mixing, scaled_in, precision=HIGH)  32.5 us
    all_gather x1, waiting for transfers between devices, gather_rows(): part = lax.all_gather(mine, SHARD, axis=0, tiled=False)  29.1 us
    ppermute x1, waiting for transfers between devices, gather_group(): from_prev = lax.ppermute(pair, 'shard_0', up)  22.8 us
    another operation x4, other arithmetic, gather_rows(): return jnp.stack([first, second], axis=1).reshape(-1, weight.shape[1])  19.1 us
    ppermute x10, starting transfers between devices, exchange_sum(): values = values + lax.ppermute(values, axis, pairs)  18.9 us
    ppermute x10, waiting for transfers between devices, exchange_sum(): values = values + lax.ppermute(values, axis, pairs)  17.1 us
  transfers between devices with their start and end apart: 25, of which 17 were waited for; matrix products, arithmetic and copies ran while one was open for 14% of the time, Pallas kernels for 0%

profile of v5, /device:TPU:1, one launch (start us, length us, event | category | flops | bytes accessed | tf_op | source)
XLA Modules:
  0.0 546.2 jit_solution(374880517827054285)
XLA Ops:
  9.8 2.2 collective-permute-start.3
  12.0 12.3 %collective-permute-done.3 = bf16[64,4384]{1,0:T(8,128)(2,1)S(1)} collective-permute-done((bf16[64,4384]{1,0:T(8,128)(2,1)S(1)}, bf16[64,4384]{1,0:T(8,128)(2,1)S(1)}, u32[]{:S(2)}, u32[]{:S(2)}) %collective-permute-start.3) | collective-permute-done | bytes 561184 | tf_op jit(solution)/shard_map/ppermute | solution.py:153
  28.3 2.1 collective-permute-start.4
  31.9 22.8 %collective-permute-done.5 = bf16[2,64,4384]{2,1,0:T(8,128)(2,1)S(1)} collective-permute-done((bf16[2,64,4384]{2,1,0:T(8,128)(2,1)}, bf16[2,64,4384]{2,1,0:T(8,128)(2,1)S(1)}, u32[]{:S(2)}, u32[]{:S(2)}) %collective-permute-start.5) | collective-permute-done | bytes 1122336 | tf_op jit(solution)/shard_map/ppermute | solution.py:157
  54.8 2.7 collective-permute-start.7
  57.7 10.5 %collective-permute-done.6 = bf16[2,32,4384]{2,1,0:T(8,128)(2,1)S(1)} collective-permute-done((bf16[2,32,4384]{2,1,0:T(8,128)(2,1)S(1)}, bf16[2,32,4384]{2,1,0:T(8,128)(2,1)S(1)}, u32[]{:S(2)}, u32[]{:S(2)}) %collective-permute-start.6) | collective-permute-done | bytes 561184 | tf_op jit(solution)/shard_map/ppermute | solution.py:160
  69.4 2.4 constant_dynamic-slice_fusion.1
  71.8 3.1 collective-permute-start.8
  79.4 2.9 collective-permute-done.1
  82.4 2.8 collective-permute-start.2
  89.4 2.2 slice_reduce_fusion.3
  91.7 8.1 %select_bitcast_fusion.2 = (bf16[8,1,64,4384]{3,2,0,1:T(8,128)(2,1)}, bf16[8,1,64,4384]{3,2,0,1:T(8,128)(2,1)}) fusion(bf16[8,64,4384]{2,1,0:T(8,128)(2,1)} %collective-permute-done.8, pred[]{:T(512)S(6)} %eq.79, bf16[4,2,64,4384]{3,2,1,0:T(8,128)(2,1)} %constant_dynamic-slice_fusion.1), kind=kLoop, calls=%fused_computation.15 | loop fusion | flops 4489216 | bytes 17956864 | tf_op jit(solution)/shard_map/stack | solution.py:186
  99.8 8.2 %pad_maximum_fusion = bf16[8,2,64,4384]{3,2,0,1:T(8,128)(2,1)} fusion(bf16[8,1,64,4384]{3,2,0,1:T(8,128)(2,1)} %get-tuple-element.96, bf16[8,1,64,4384]{3,2,0,1:T(8,128)(2,1)} %get-tuple-element.95), kind=kLoop, calls=%fused_computation.2 | loop fusion | flops 4489216 | bytes 17956864 | tf_op jit(solution)/shard_map/stack | solution.py:186
  108.0 8.0 %copy.88 = bf16[8,2,64,4384]{3,2,1,0:T(8,128)(2,1)} copy(bf16[8,2,64,4384]{3,2,0,1:T(8,128)(2,1)} %pad_maximum_fusion) | data formatting | bytes 17956864 | tf_op jit(solution)/shard_map/stack | solution.py:186
  116.0 7.5 %fusion.79 = f32[256,4384]{0,1:T(8,128)S(1)} fusion(bf16[1024,4384]{1,0:T(8,128)(2,1)} %bitcast.210, f32[256,1024]{1,0:T(8,128)S(1)} %copy-done.15, f32[1024]{0:T(1024)S(1)} %slice_bitcast_fusion.5, f32[256]{0:T(256)S(1)} %fusion.72), kind=kOutput, calls=%fused_computation.190 | convolution fusion | flops 2299265024 | bytes 14521344 | tf_op jit(solution)/shard_map/dot_general | solution.py:262
  133.8 4.9 fusion.20
  145.7 11.8 %fusion.25 = f32[256,32,64]{0,2,1:T(8,128)S(1)} fusion(f32[256,32,64]{0,2,1:T(8,128)} %bitcast.215, f32[256,32,64]{0,2,1:T(8,128)S(1)} %fusion.48, f32[32]{0:T(128)} %mul.426, f32[256,32]{0,1:T(8,128)S(1)} %bitcast_multiply_fusion.4, f32[256,256]{1,0:T(8,128)S(1)} %fusion.58, f32[32,256]{1,0:T(8,128)S(1)} %bitcast_add_fusion.4, ...), kind=kOutput, calls=%fused_computation.55 | convolution fusion | flops 1619525632 | bytes 6717568 | tf_op jit(solution)/shard_map/jvp(chij,cjhp->cihp)/dot_general | solution.py:132
  157.5 3.1 multiply_reduce_fusion.9
  162.5 3.4 select_bitcast_fusion.3
  167.1 3.1 collective-permute-start.10
  170.1 29.1 %all-gather.3.cloned.1.call-done = bf16[1024,1024]{1,0:T(8,128)(2,1)} async-done(((bf16[128,1024]{1,0:T(8,128)(2,1)}), bf16[1024,1024]{1,0:T(8,128)(2,1)}) %all-gather.3.cloned.1.call-update) | async-done | bytes 2097168 | tf_op jit(solution)/shard_map/all_gather | solution.py:182
  203.0 7.2 %bitcast_add_fusion.1 = bf16[8,128,1024]{2,1,0:T(8,128)(2,1)} fusion(f32[8,128,1024]{2,1,0:T(8,128)} %collective-permute-done.10, f32[8,2,128,1024]{3,2,1,0:T(8,128)} %bitcast.199, pred[]{:T(512)S(6)} %eq.79), kind=kLoop, calls=%fused_computation.20 | loop fusion | flops 3145728 | bytes 14680065 | tf_op jit(solution)/shard_map/add | solution.py:196
  210.2 2.5 select_bitcast_fusion.5
  217.2 4.8 multiply_reduce_fusion.6
  224.3 11.9 %fusion.7 = (f32[32,256]{1,0:T(8,128)S(1)}, f32[32,256]{1,0:T(8,128)S(1)}, f32[256,256]{1,0:T(8,128)S(1)}) fusion(f32[256,256]{1,0:T(8,128)S(1)} %fusion.58, f32[32,256]{1,0:T(8,128)S(1)} %copy-done.48, pred[256,256]{1,0:T(8,128)(4,1)S(1)} %copy-done.43, f32[32,64,256]{2,1,0:T(8,128)S(1)} %bitcast.205, f32[256,32,64]{0,2,1:T(8,128)S(1)} %bitcast.216, ...), kind=kOutput, calls=%fused_computation.13 | convolution fusion | flops 1629929472 | bytes 4915200 | tf_op jit(solution)/shard_map/transpose(jvp(chij,cjhp->cihp))/dot_general | solution.py:132
  236.3 8.8 %fusion.26 = (f32[256,32]{0,1:T(8,128)}, f32[1,256,32,64]{1,3,2,0:T(8,128)}) fusion(f32[1,256,32,64]{1,3,2,0:T(8,128)S(1)} %bitcast.217, f32[256,32]{0,1:T(8,128)S(1)} %copy-done.31, f32[32,64,256]{2,1,0:T(8,128)S(1)} %bitcast.206, f32[256,256]{1,0:T(8,128)S(1)} %fusion.58, f32[32,256]{1,0:T(8,128)S(1)} %copy-done.48, pred[256,256]{1,0:T(8,128)(4,1)S(1)} %copy-done.43), kind=kOutput, calls=%fused_computation.59 | convolution fusion | flops 1618468864 | bytes 6717440 | tf_op jit(solution)/shard_map/transpose(jvp(chij,cjhp->cihp))/dot_general | solution.py:132
  245.9 2.5 reduce-window.19
  250.7 2.7 bitcast_add_fusion.3
  254.4 2.8 multiply_reduce_fusion.4
  257.2 2.3 multiply_reduce_fusion.3
  265.0 7.9 %fusion.21 = f32[1024,4480]{1,0:T(8,128)} fusion(bf16[256,4384]{0,1:T(8,128)(2,1)S(1)} %add_convert_fusion, f32[256,1024]{1,0:T(8,128)S(1)} %copy-done.15, f32[1024]{0:T(1024)S(1)} %slice_bitcast_fusion.5, f32[256]{0:T(256)S(1)} %fusion.72), kind=kOutput, calls=%fused_computation.50 | convolution fusion | flops 2349596672 | bytes 21648384 | tf_op jit(solution)/shard_map/dot_general | solution.py:76
  272.9 10.6 %select_bitcast_fusion = f32[8,64,4480]{2,1,0:T(8,128)} fusion(f32[8,2,64,4480]{3,2,1,0:T(8,128)} %bitcast.196, pred[]{:T(512)S(6)} %eq.79), kind=kLoop, calls=%fused_computation.5 | loop fusion | flops 2293760 | bytes 27525120 | tf_op jit(solution)/shard_map/jit(_where)/select_n | solution.py:195
  283.6 14.5 %collective-permute-done.18 = f32[8,64,4480]{2,1,0:T(8,128)} collective-permute-done((f32[8,64,4480]{2,1,0:T(8,128)}, f32[8,64,4480]{2,1,0:T(8,128)}, u32[]{:S(2)}, u32[]{:S(2)}) %collective-permute-start.18) | collective-permute-done | bytes 9175072 | tf_op jit(solution)/shard_map/ppermute | solution.py:171
  298.1 11.9 %fusion = bf16[8,64,4480]{2,1,0:T(8,128)(2,1)} fusion(f32[8,64,4480]{2,1,0:T(8,128)} %collective-permute-done.18, f32[8,2,64,4480]{3,2,1,0:T(8,128)} %bitcast.197, pred[]{:T(512)S(6)} %eq.79), kind=kLoop, calls=%fused_computation.4 | loop fusion | flops 6881280 | bytes 32112640 | tf_op jit(solution)/shard_map/convert_element_type | solution.py:201
  310.8 8.0 %multiply_reduce_fusion.10 = (f32[1024]{0:T(1024)S(1)}, f32[256]{0:T(256)S(1)}, f32[256,1024]{1,0:T(8,128)}) fusion(f32[256,1024]{1,0:T(8,128)S(1)} %copy-done.15, f32[256]{0:T(256)S(1)} %fusion.72, f32[1024]{0:T(1024)S(1)} %slice_bitcast_fusion.5, bf16[256,4384]{0,1:T(8,128)(2,1)} %copy-done.20, bf16[1024,4384]{1,0:T(8,128)(2,1)} %bitcast.211), kind=kOutput, calls=%fused_computation.97 | convolution fusion | flops 2300050176 | bytes 13330432 | tf_op jit(solution)/shard_map/dot_general | solution.py:82
  318.8 16.3 %reduce-scatter.5.cloned.1.call-done = bf16[1,128,1024]{2,1,0:T(8,128)(2,1)} async-done(((bf16[8,128,1024]{2,1,0:T(8,128)(2,1)}), bf16[1,128,1024]{2,1,0:T(8,128)(2,1)}) %reduce-scatter.5.cloned.1.call-update) | async-done | bytes 262160 | tf_op jit(solution)/shard_map/reduce_scatter | solution.py:201
  336.9 98.5 %reduce-scatter.3.cloned.1.call-done = bf16[1,64,4480]{2,1,0:T(8,128)(2,1)} async-done(((bf16[8,64,4480]{2,1,0:T(8,128)(2,1)}), bf16[1,64,4480]{2,1,0:T(8,128)(2,1)}) %reduce-scatter.3.cloned.1.call-update) | async-done | bytes 573456 | tf_op jit(solution)/shard_map/reduce_scatter | solution.py:201
  435.4 2.2 bitcast_convert_fusion
  442.2 2.7 collective-permute-done.11
  445.4 2.7 collective-permute-done.12
  450.2 3.0 collective-permute-done.13
  453.1 4.0 collective-permute-start.14
  459.3 4.6 convolution_add_fusion
  463.9 2.5 collective-permute-start.16
  466.4 2.2 collective-permute-done.16
  468.7 4.0 collective-permute-start.17
  473.9 51.8 %all-reduce.22.cloned.1.call-done = (f32[64,4480]{1,0:T(8,128)}, f32[128,1024]{1,0:T(8,128)}) async-done(((f32[64,4480]{1,0:T(8,128)}, f32[128,1024]{1,0:T(8,128)}), (f32[64,4480]{1,0:T(8,128)}, f32[128,1024]{1,0:T(8,128)})) %all-reduce.22.cloned.1.call-update) | async-done | bytes 1671184 | tf_op jit(solution)/shard_map/psum | solution.py:202
  525.7 5.3 collective-permute-start.19
  (312 shorter events, 79.3 us)
Async XLA Ops:
  7.2 192.1 %all-gather.3.cloned.1.call-start = ((), (), s32[]{:S(2)}) async-start(), calls=%async_computation.4 | async-start | bytes 2359296 | tf_op jit(solution)/shard_map/all_gather | solution.py:182
  9.8 14.5 %collective-permute-start.3 = (bf16[64,4384]{1,0:T(8,128)(2,1)S(1)}, bf16[64,4384]{1,0:T(8,128)(2,1)S(1)}, u32[]{:S(2)}, u32[]{:S(2)}) collective-permute-start(bf16[64,4384]{1,0:T(8,128)(2,1)S(1)} %copy.108), channel_id=1, source_target_pairs={{0,1},{1,0},{2,3},{3,2},{4,5},{5,4},{6,7},{7,6},{8,9},{9,8},{10,11... | collective-permute-start | bytes 1683464 | tf_op jit(solution)/shard_map/ppermute | solution.py:153
  26.4 28.3 %collective-permute-start.5 = (bf16[2,64,4384]{2,1,0:T(8,128)(2,1)}, bf16[2,64,4384]{2,1,0:T(8,128)(2,1)S(1)}, u32[]{:S(2)}, u32[]{:S(2)}) collective-permute-start(bf16[2,64,4384]{2,1,0:T(8,128)(2,1)} %maximum_select_fusion.1), channel_id=1, source_target_pairs={{0,2},{2,4},{4,6},{6,0},{1,3},{3,5},{5,7},{7,1},{8,10},{10,12},{12... | collective-permute-start | bytes 3366920 | tf_op jit(solution)/shard_map/ppermute | solution.py:157
  28.3 26.5 %collective-permute-start.4 = (bf16[2,64,4384]{2,1,0:T(8,128)(2,1)}, bf16[2,64,4384]{2,1,0:T(8,128)(2,1)S(1)}, u32[]{:S(2)}, u32[]{:S(2)}) collective-permute-start(bf16[2,64,4384]{2,1,0:T(8,128)(2,1)} %maximum_select_fusion.1), channel_id=1, source_target_pairs={{0,6},{2,0},{4,2},{6,4},{1,7},{3,1},{5,3},{7,5},{8,14},{10,8},{12,... | collective-permute-start | bytes 3366920 | tf_op jit(solution)/shard_map/ppermute | solution.py:158
  54.7 13.6 %collective-permute-start.6 = (bf16[2,32,4384]{2,1,0:T(8,128)(2,1)S(1)}, bf16[2,32,4384]{2,1,0:T(8,128)(2,1)S(1)}, u32[]{:S(2)}, u32[]{:S(2)}) collective-permute-start(bf16[2,32,4384]{2,1,0:T(8,128)(2,1)S(1)} %slice.200), channel_id=1, source_target_pairs={{0,2},{2,4},{4,6},{6,0},{1,3},{3,5},{5,7},{7,1},{8,10},{10,12},{12... | collective-permute-start | bytes 1683464 | tf_op jit(solution)/shard_map/ppermute | solution.py:160
  54.8 13.4 %collective-permute-start.7 = (bf16[2,32,4384]{2,1,0:T(8,128)(2,1)S(1)}, bf16[2,32,4384]{2,1,0:T(8,128)(2,1)S(1)}, u32[]{:S(2)}, u32[]{:S(2)}) collective-permute-start(bf16[2,32,4384]{2,1,0:T(8,128)(2,1)S(1)} %slice.201), channel_id=1, source_target_pairs={{0,6},{2,0},{4,2},{6,4},{1,7},{3,1},{5,3},{7,5},{8,14},{10,8},{12,... | collective-permute-start | bytes 1683464 | tf_op jit(solution)/shard_map/ppermute | solution.py:161
  57.7 10.9 %copy-start.27 = (bf16[64,4384]{1,0:T(8,128)(2,1)S(1)}, bf16[64,4384]{1,0:T(8,128)(2,1)}, u32[]{:S(2)}) copy-start(bf16[64,4384]{1,0:T(8,128)(2,1)} %copy-done.26) | copy-start | bytes 1683460
  69.4 7.4 %copy-start.74 = (s32[1,2]{1,0:T(1,128)S(1)}, s32[1,2]{1,0:T(1,128)}, u32[]{:S(2)}) copy-start(s32[1,2]{1,0:T(1,128)} %param.14) | copy-start | bytes 28
  69.4 9.8 %copy-start.15 = (f32[256,1024]{1,0:T(8,128)S(1)}, f32[256,1024]{1,0:T(8,128)}, u32[]{:S(2)}) copy-start(f32[256,1024]{1,0:T(8,128)} %param.12) | copy-start | bytes 3145732
  71.8 19.9 %collective-permute-start.8 = (bf16[8,64,4384]{2,1,0:T(8,128)(2,1)}, bf16[8,64,4384]{2,1,0:T(8,128)(2,1)}, u32[]{:S(2)}, u32[]{:S(2)}) collective-permute-start(bf16[8,64,4384]{2,1,0:T(8,128)(2,1)} %bitcast.8), channel_id=1, source_target_pairs={{0,8},{8,0},{1,9},{9,1},{2,10},{10,2},{3,11},{11,3},{4,12},{12,4},... | collective-permute-start | bytes 13467656 | tf_op jit(solution)/shard_map/ppermute | solution.py:171
  75.5 3.6 collective-permute-start
  78.3 53.7 %copy-start.57 = (pred[256]{0:T(512)(128)(4,1)}, pred[256]{0:T(512)(128)(4,1)S(1)}, u32[]{:S(2)}) copy-start(pred[256]{0:T(512)(128)(4,1)S(1)} %get-tuple-element.117) | copy-start | bytes 772
  78.3 53.7 %copy-start.59 = (pred[256]{0:T(512)(128)(4,1)}, pred[256]{0:T(512)(128)(4,1)S(1)}, u32[]{:S(2)}) copy-start(pred[256]{0:T(512)(128)(4,1)S(1)} %get-tuple-element.118) | copy-start | bytes 772
  78.4 53.7 %copy-start.61 = (pred[256]{0:T(512)(128)(4,1)}, pred[256]{0:T(512)(128)(4,1)S(1)}, u32[]{:S(2)}) copy-start(pred[256]{0:T(512)(128)(4,1)S(1)} %get-tuple-element.119) | copy-start | bytes 772
  79.2 3.1 collective-permute-start.1
  79.4 12.3 %copy-start.52 = (f32[256]{0:T(256)}, f32[256]{0:T(256)S(1)}, u32[]{:S(2)}) copy-start(f32[256]{0:T(256)S(1)} %multiply_reduce_fusion.12) | copy-start | bytes 3076
  82.4 4.8 collective-permute-start.2
  87.5 36.0 %copy-start.63 = (f32[32]{0:T(128)}, f32[32]{0:T(128)S(1)}, u32[]{:S(2)}) copy-start(f32[32]{0:T(128)S(1)} %add.207) | copy-start | bytes 388
  88.2 35.3 %copy-start.65 = (f32[32]{0:T(128)}, f32[32]{0:T(128)S(1)}, u32[]{:S(2)}) copy-start(f32[32]{0:T(128)S(1)} %neg.39) | copy-start | bytes 388
  91.7 40.4 %copy-start.35 = (f32[2304]{0:T(1024)}, f32[2304]{0:T(1024)S(1)}, u32[]{:S(2)}) copy-start(f32[2304]{0:T(1024)S(1)} %get-tuple-element.72) | copy-start | bytes 27652
  91.7 40.4 %copy-start.37 = (f32[2304]{0:T(1024)}, f32[2304]{0:T(1024)S(1)}, u32[]{:S(2)}) copy-start(f32[2304]{0:T(1024)S(1)} %get-tuple-element.73) | copy-start | bytes 27652
  91.7 40.4 %copy-start.39 = (f32[2304]{0:T(1024)}, f32[2304]{0:T(1024)S(1)}, u32[]{:S(2)}) copy-start(f32[2304]{0:T(1024)S(1)} %get-tuple-element.75) | copy-start | bytes 27652
  91.7 40.4 %copy-start.41 = (f32[2304]{0:T(1024)}, f32[2304]{0:T(1024)S(1)}, u32[]{:S(2)}) copy-start(f32[2304]{0:T(1024)S(1)} %get-tuple-element.74) | copy-start | bytes 27652
  143.2 191.9 %reduce-scatter.5.cloned.1.call-start = ((), (), s32[]{:S(2)}) async-start(), calls=%async_computation.3 | async-start | bytes 2359296 | tf_op jit(solution)/shard_map/reduce_scatter | solution.py:201
  144.8 12.7 %copy-start.47 = (f32[32,256]{1,0:T(8,128)}, f32[32,256]{1,0:T(8,128)S(1)}, u32[]{:S(2)}) copy-start(f32[32,256]{1,0:T(8,128)S(1)} %bitcast_add_fusion.4) | copy-start | bytes 98308
  167.1 36.0 %collective-permute-start.10 = (f32[8,128,1024]{2,1,0:T(8,128)}, f32[8,128,1024]{2,1,0:T(8,128)}, u32[]{:S(2)}, u32[]{:S(2)}) collective-permute-start(f32[8,128,1024]{2,1,0:T(8,128)} %select_bitcast_fusion.3), channel_id=1, source_target_pairs={{0,8},{8,0},{1,9},{9,1},{2,10},{10,2},{3,11},{11,3},{4,12},{12,4},... | collective-permute-start | bytes 12582920 | tf_op jit(solution)/shard_map/ppermute | solution.py:171
  199.3 11.0 %collective-permute-start.9 = (bf16[8,128,1024]{2,1,0:T(8,128)(2,1)}, bf16[8,128,1024]{2,1,0:T(8,128)(2,1)}, u32[]{:S(2)}, u32[]{:S(2)}) collective-permute-start(bf16[8,128,1024]{2,1,0:T(8,128)(2,1)} %bitcast.218), channel_id=1, source_target_pairs={{0,8},{8,0},{1,9},{9,1},{2,10},{10,2},{3,11},{11,3},{4,12},{12,4},... | collective-permute-start | bytes 6291464 | tf_op jit(solution)/shard_map/ppermute | solution.py:171
  222.0 14.3 %copy-start.6 = (f32[256,2048]{0,1:T(8,128)}, f32[256,2048]{0,1:T(8,128)S(1)}, u32[]{:S(2)}) copy-start(f32[256,2048]{0,1:T(8,128)S(1)} %get-tuple-element.79) | copy-start | bytes 6291460
  236.3 9.5 %copy-start.51 = (f32[256]{0:T(256)S(1)}, f32[256]{0:T(256)}, u32[]{:S(2)}) copy-start(f32[256]{0:T(256)} %get-tuple-element.116) | copy-start | bytes 3076
  265.0 7.9 %copy-start.20 = (bf16[256,4384]{0,1:T(8,128)(2,1)}, bf16[256,4384]{0,1:T(8,128)(2,1)S(1)}, u32[]{:S(2)}) copy-start(bf16[256,4384]{0,1:T(8,128)(2,1)S(1)} %add_convert_fusion) | copy-start | bytes 6733828
  283.5 14.6 %collective-permute-start.18 = (f32[8,64,4480]{2,1,0:T(8,128)}, f32[8,64,4480]{2,1,0:T(8,128)}, u32[]{:S(2)}, u32[]{:S(2)}) collective-permute-start(f32[8,64,4480]{2,1,0:T(8,128)} %select_bitcast_fusion), channel_id=1, source_target_pairs={{0,8},{8,0},{1,9},{9,1},{2,10},{10,2},{3,11},{11,3},{4,12},{12,4},... | collective-permute-start | bytes 27525128 | tf_op jit(solution)/shard_map/ppermute | solution.py:171
  283.5 151.9 %reduce-scatter.3.cloned.1.call-start = ((), (), s32[]{:S(2)}) async-start(), calls=%async_computation.2 | async-start | bytes 5160960 | tf_op jit(solution)/shard_map/reduce_scatter | solution.py:201
  310.0 215.7 %all-reduce.22.cloned.1.call-start = ((), (), s32[]{:S(2)}) async-start(), calls=%async_computation.5 | async-start | bytes 3342336 | tf_op jit(solution)/shard_map/psum | solution.py:202
  318.8 118.9 %copy-start.46 = (f32[2048]{0:T(1024)S(1)}, f32[2048]{0:T(1024)}, u32[]{:S(2)}) copy-start(f32[2048]{0:T(1024)} %get-tuple-element.66) | copy-start | bytes 24580
  318.8 118.9 %copy-start.45 = (f32[2048]{0:T(1024)S(1)}, f32[2048]{0:T(1024)}, u32[]{:S(2)}) copy-start(f32[2048]{0:T(1024)} %get-tuple-element.78) | copy-start | bytes 24580
  441.8 3.1 collective-permute-start.11
  444.9 3.2 collective-permute-start.12
  448.1 5.1 collective-permute-start.13
  453.1 4.9 collective-permute-start.14
  458.0 8.4 %copy-start.53 = (f32[256]{0:T(256)S(1)}, f32[256]{0:T(256)}, u32[]{:S(2)}) copy-start(f32[256]{0:T(256)} %copy-done.52) | copy-start | bytes 3076
  458.0 14.6 %copy-start.18 = (f32[256,1024]{1,0:T(8,128)S(1)}, f32[256,1024]{1,0:T(8,128)}, u32[]{:S(2)}) copy-start(f32[256,1024]{1,0:T(8,128)} %param.13) | copy-start | bytes 3145732
  458.0 14.6 %copy-start.30 = (f32[256,1024]{1,0:T(8,128)S(1)}, f32[256,1024]{1,0:T(8,128)}, u32[]{:S(2)}) copy-start(f32[256,1024]{1,0:T(8,128)} %get-tuple-element.120) | copy-start | bytes 3145732
  458.1 5.8 %collective-permute-start.15 = (f32[8,1836]{1,0:T(8,128)S(1)}, f32[8,1836]{1,0:T(8,128)S(1)}, u32[]{:S(2)}, u32[]{:S(2)}) collective-permute-start(f32[8,1836]{1,0:T(8,128)S(1)} %add.222), channel_id=1, source_target_pairs={{0,16},{16,0},{32,48},{48,32},{64,80},{80,64},{96,112},{112,96},{1... | collective-permute-start | bytes 176264 | tf_op jit(solution)/shard_map/ppermute | solution.py:219
  463.9 4.8 collective-permute-start.16
  468.7 62.3 %collective-permute-start.17 = (f32[8,1836]{1,0:T(8,128)S(1)}, f32[8,1836]{1,0:T(8,128)S(1)}, u32[]{:S(2)}, u32[]{:S(2)}) collective-permute-start(f32[8,1836]{1,0:T(8,128)S(1)} %add.224), channel_id=1, source_target_pairs={{0,64},{16,80},{32,96},{48,112},{64,0},{80,16},{96,32},{112,48},{1... | collective-permute-start | bytes 176264 | tf_op jit(solution)/shard_map/ppermute | solution.py:219
  525.7 11.2 %copy-start.29 = (f32[64,4480]{1,0:T(8,128)S(1)}, f32[64,4480]{1,0:T(8,128)}, u32[]{:S(2)}) copy-start(f32[64,4480]{1,0:T(8,128)} %get-tuple-element.76) | copy-start | bytes 3440644
  525.7 11.2 %collective-permute-start.19 = (f32[64,4480]{1,0:T(8,128)}, f32[64,4480]{1,0:T(8,128)S(1)}, u32[]{:S(2)}, u32[]{:S(2)}) collective-permute-start(f32[64,4480]{1,0:T(8,128)} %get-tuple-element.76), channel_id=1, source_target_pairs={{0,8},{8,0},{1,9},{9,1},{2,10},{10,2},{3,11},{11,3},{4,12},{12,4},... | collective-permute-start | bytes 3440648 | tf_op jit(solution)/shard_map/ppermute | solution.py:171
  532.6 2.1 collective-permute-start.20
  (54 other events, 153.6 us)
Sparse Core Ops, SparseCore 0:
  143.3 55.9 all-gather.2
  283.7 51.4 reduce-scatter.4
  337.6 97.7 reduce-scatter.2
  438.0 87.5 all-reduce.21

commit v6 on v5

--- a/solution.py
+++ b/solution.py
@@ -142,6 +142,33 @@
     return gated_pre * scaling * gate_gain[None, :]
 
 
+def reduce_group(halves):
+    ring = lax.axis_size("shard_0")
+    y = lax.axis_index("shard_1")
+    z = lax.axis_index("shard_0")
+    rows, cols = halves.shape[1], halves.shape[2]
+    blocks = halves.reshape(ring, 2, rows, cols)
+    doubled = jnp.concatenate([blocks, blocks], axis=0)
+    rel = lax.dynamic_slice_in_dim(doubled, z, ring, axis=0)
+    up = [(i, (i + 1) % ring) for i in range(ring)]
+    down = [(i, (i - 1) % ring) for i in range(ring)]
+    half = rows // 2
+    low = lambda a: a.astype(jnp.bfloat16)
+    acc_up = lax.ppermute(low(rel[3][:, :half]), "shard_0", up)
+    acc_dn = lax.ppermute(low(rel[1][:, half:]), "shard_0", down)
+    acc_up = lax.ppermute(low(acc_up + rel[2][:, :half]), "shard_0", up)
+    acc_dn = lax.ppermute(low(acc_dn + rel[2][:, half:]), "shard_0", down)
+    acc_up = lax.ppermute(low(acc_up + rel[1][:, :half]), "shard_0", up)
+    acc_dn = lax.ppermute(low(acc_dn + rel[3][:, half:]), "shard_0", down)
+    zsum = jnp.concatenate(
+        [acc_up.astype(jnp.float32) + rel[0][:, :half], acc_dn.astype(jnp.float32) + rel[0][:, half:]],
+        axis=1,
+    )
+    keep = lax.dynamic_index_in_dim(zsum, y, axis=0, keepdims=False)
+    give = lax.dynamic_index_in_dim(zsum, 1 - y, axis=0, keepdims=False)
+    return keep + lax.ppermute(low(give), "shard_1", [(0, 1), (1, 0)]).astype(jnp.float32)
+
+
 def core_swap(values):
     return lax.ppermute(values, "core", [(0, 1), (1, 0)])
 
@@ -196,18 +223,20 @@
     return keep + core_swap(give)
 
 
-def reduce_rest(halves):
+def reduce_rest(halves, wait_for=None):
     core = lax.axis_index("core")
-    owned = lax.psum_scatter(halves.astype(jnp.bfloat16), SHARD, scatter_dimension=0, tiled=False)
-    owned = lax.psum(owned.astype(jnp.float32), "rep_hi")
+    owned = reduce_group(halves)
+    if wait_for is not None:
+        owned, wait_for = lax.optimization_barrier((owned, wait_for))
+    owned = lax.psum(owned, "rep_hi")
     other = core_swap(owned)
     first = jnp.where(core == 0, owned, other)
     second = jnp.where(core == 0, other, owned)
     return jnp.concatenate([first, second], axis=0)
 
 
-def reduce_rows(partial):
-    return reduce_rest(reduce_core(partial))
+def reduce_rows(partial, wait_for=None):
+    return reduce_rest(reduce_core(partial), wait_for)
 
 
 def exchange_sum(values, axes):
@@ -292,7 +321,7 @@
     cols = proj_low.shape[1]
     wide = -(-cols // 128) * 128
     proj_wide = jnp.pad(proj_low, ((0, 0), (0, wide - cols)))
-    in_owned = reduce_rows(row_product(normed, proj_wide))[:, :cols]
+    in_owned = reduce_rows(row_product(normed, proj_wide), out_owned)[:, :cols]
     small_sum = exchange_sum(small_blocks, ("shard_1", "shard_0", "core", "rep_hi"))
     mine = lax.dynamic_index_in_dim(small_sum, lax.axis_index(SHARD), axis=0, keepdims=False)
     small_final = []

time: 552 us -> 592 us (1.072)
  other arithmetic: 98.5 us -> 130 us
  waiting for transfers between devices: 273 us -> 255 us
  local copies, waits for them, and re-layouts: 50.4 us -> 64.4 us
  starting transfers between devices: 40.9 us -> 53.6 us
    reduce_scatter x2 -> x0, waiting for transfers between devices: 115 us -> none  [reduce_rest(): lax.psum_scatter(halves.astype(jnp.bfloat16), SHARD, scatter_dimension=0,...]
    psum x1 -> x2, waiting for transfers between devices: 51.8 us -> 119 us  [reduce_rest(): owned = lax.psum(owned, 'rep_hi')]
    ppermute x0 -> x14, waiting for transfers between devices: none -> 43.9 us  [the longest x2 15.9 us: reduce_group(): acc_up = lax.ppermute(low(acc_up + rel[1][:, :half]), 'shard_0', up)]
    ppermute x6, waiting for transfers between devices: 15 us -> 0.02 us  [core_swap(): return lax.ppermute(values, 'core', [(0, 1), (1, 0)])]
    add x1 -> x2, other arithmetic: 7.2 us -> 22.1 us  [reduce_core(): return keep + core_swap(give)]
    concatenate x0 -> x2, other arithmetic: none -> 11.4 us  [reduce_group(): doubled = jnp.concatenate([blocks, blocks], axis=0)]
    ppermute x0 -> x14, starting transfers between devices: none -> 10.5 us  [the longest x2 3.35 us: reduce_group(): acc_dn = lax.ppermute(low(acc_dn + rel[3][:, half:]), 'shard_0', down)]
    add x0 -> x4, other arithmetic: none -> 7.65 us  [the longest x2 4.12 us: reduce_group(): keep + lax.ppermute(low(give), 'shard_1', [(0, 1), (1, 0)]).astype(jnp.fl...]
  transfers between devices with their start and end apart: 25 -> 38, of which waited for: 17 -> 23; matrix products, arithmetic and copies ran while one was open for 14% -> 20% of each run, Pallas kernels for 0% -> 0%
where the time goes in v6:
time: 592 us; the launch traced here: 586 us
  waiting for transfers between devices  255 us (43%)
  other arithmetic  130 us (22%)
  matrix products  66.8 us (11%)
  local copies, waits for them, and re-layouts  64.4 us (11%)
  starting transfers between devices  53.6 us (9%)
  between operations  15.5 us (3%)
    psum x2, waiting for transfers between devices, reduce_rest(): owned = lax.psum(owned, 'rep_hi')  119 us
    dot_general x3, matrix products, mixer(): y_intra = jnp.einsum('chij,cjhp->cihp', mixing, scaled_in, precision=HIGH)  32.6 us
    all_gather x1, waiting for transfers between devices, gather_rows(): part = lax.all_gather(mine, SHARD, axis=0, tiled=False)  29 us
    ppermute x1, waiting for transfers between devices, gather_group(): from_prev = lax.ppermute(pair, 'shard_0', up)  22.8 us
    add x2, other arithmetic, reduce_core(): return keep + core_swap(give)  22.1 us
    ppermute x6, starting transfers between devices, core_swap(): return lax.ppermute(values, 'core', [(0, 1), (1, 0)])  19.3 us
    another operation x4, other arithmetic, gather_rows(): return jnp.stack([first, second], axis=1).reshape(-1, weight.shape[1])  18.8 us
    ppermute x10, waiting for transfers between devices, exchange_sum(): values = values + lax.ppermute(values, axis, pairs)  17.9 us
  transfers between devices with their start and end apart: 38, of which 23 were waited for; matrix products, arithmetic and copies ran while one was open for 20% of the time, Pallas kernels for 0%

profile of v6, /device:TPU:1, one launch (start us, length us, event | category | flops | bytes accessed | tf_op | source)
XLA Modules:
  0.0 585.6 jit_solution(7869188572535177079)
XLA Ops:
  12.0 12.3 %collective-permute-done.3 = bf16[64,4384]{1,0:T(8,128)(2,1)S(1)} collective-permute-done((bf16[64,4384]{1,0:T(8,128)(2,1)S(1)}, bf16[64,4384]{1,0:T(8,128)(2,1)S(1)}, u32[]{:S(2)}, u32[]{:S(2)}) %collective-permute-start.3) | collective-permute-done | bytes 561184 | tf_op jit(solution)/shard_map/ppermute | solution.py:180
  31.8 22.8 %collective-permute-done.5 = bf16[2,64,4384]{2,1,0:T(8,128)(2,1)S(1)} collective-permute-done((bf16[2,64,4384]{2,1,0:T(8,128)(2,1)}, bf16[2,64,4384]{2,1,0:T(8,128)(2,1)S(1)}, u32[]{:S(2)}, u32[]{:S(2)}) %collective-permute-start.5) | collective-permute-done | bytes 1122336 | tf_op jit(solution)/shard_map/ppermute | solution.py:184
  54.8 2.7 collective-permute-start.7
  57.7 10.5 %collective-permute-done.6 = bf16[2,32,4384]{2,1,0:T(8,128)(2,1)S(1)} collective-permute-done((bf16[2,32,4384]{2,1,0:T(8,128)(2,1)S(1)}, bf16[2,32,4384]{2,1,0:T(8,128)(2,1)S(1)}, u32[]{:S(2)}, u32[]{:S(2)}) %collective-permute-start.6) | collective-permute-done | bytes 561184 | tf_op jit(solution)/shard_map/ppermute | solution.py:187
  71.9 3.1 collective-permute-start.8
  79.4 2.9 collective-permute-done.1
  82.4 2.7 collective-permute-start.2
  91.7 8.0 %select_bitcast_fusion.2 = (bf16[8,1,64,4384]{3,2,0,1:T(8,128)(2,1)}, bf16[8,1,64,4384]{3,2,0,1:T(8,128)(2,1)}) fusion(bf16[8,64,4384]{2,1,0:T(8,128)(2,1)} %collective-permute-done.8, pred[]{:T(512)S(6)} %eq.79, bf16[4,2,64,4384]{3,2,1,0:T(8,128)(2,1)} %constant_dynamic-slice_fusion.1), kind=kLoop, calls=%fused_computation.19 | loop fusion | flops 4489216 | bytes 17956864 | tf_op jit(solution)/shard_map/stack | solution.py:213
  99.8 8.2 %pad_maximum_fusion = bf16[8,2,64,4384]{3,2,0,1:T(8,128)(2,1)} fusion(bf16[8,1,64,4384]{3,2,0,1:T(8,128)(2,1)} %get-tuple-element.100, bf16[8,1,64,4384]{3,2,0,1:T(8,128)(2,1)} %get-tuple-element.99), kind=kLoop, calls=%fused_computation.3 | loop fusion | flops 4489216 | bytes 17956864 | tf_op jit(solution)/shard_map/stack | solution.py:213
  108.0 8.0 %copy.107 = bf16[8,2,64,4384]{3,2,1,0:T(8,128)(2,1)} copy(bf16[8,2,64,4384]{3,2,0,1:T(8,128)(2,1)} %pad_maximum_fusion) | data formatting | bytes 17956864 | tf_op jit(solution)/shard_map/stack | solution.py:213
  116.0 7.5 %fusion.104 = f32[256,4384]{0,1:T(8,128)S(1)} fusion(bf16[1024,4384]{1,0:T(8,128)(2,1)} %bitcast.238, f32[256,1024]{1,0:T(8,128)S(1)} %copy-done.15, f32[1024]{0:T(1024)S(1)} %slice_bitcast_fusion.9, f32[256]{0:T(256)S(1)} %fusion.97), kind=kOutput, calls=%fused_computation.245 | convolution fusion | flops 2299265024 | bytes 14521344 | tf_op jit(solution)/shard_map/dot_general | solution.py:291
  133.6 4.9 fusion.25
  145.5 11.9 %fusion.30 = f32[256,32,64]{0,2,1:T(8,128)S(1)} fusion(f32[256,32,64]{0,2,1:T(8,128)} %bitcast.243, f32[256,32,64]{0,2,1:T(8,128)S(1)} %fusion.72, f32[32]{0:T(128)} %mul.426, f32[256,32]{0,1:T(8,128)S(1)} %bitcast_multiply_fusion.4, f32[256,256]{1,0:T(8,128)S(1)} %fusion.83, f32[32,256]{1,0:T(8,128)S(1)} %bitcast_add_fusion.2, ...), kind=kOutput, calls=%fused_computation.68 | convolution fusion | flops 1619525632 | bytes 6717568 | tf_op jit(solution)/shard_map/jvp(chij,cjhp->cihp)/dot_general | solution.py:132
  157.5 3.1 multiply_reduce_fusion.9
  162.5 3.4 select_bitcast_fusion.3
  167.0 3.1 collective-permute-start.10
  170.1 29.0 %all-gather.3.cloned.1.call-done = bf16[1024,1024]{1,0:T(8,128)(2,1)} async-done(((bf16[128,1024]{1,0:T(8,128)(2,1)}), bf16[1024,1024]{1,0:T(8,128)(2,1)}) %all-gather.3.cloned.1.call-update) | async-done | bytes 2097168 | tf_op jit(solution)/shard_map/all_gather | solution.py:209
  203.2 8.8 %fusion.12 = f32[8,128,1024]{2,1,0:T(8,128)} fusion(f32[8,128,1024]{2,1,0:T(8,128)} %collective-permute-done.10, f32[8,2,128,1024]{3,2,1,0:T(8,128)} %bitcast.225, pred[]{:T(512)S(6)} %eq.79), kind=kLoop, calls=%fused_computation.25 | loop fusion | flops 2097152 | bytes 16777216 | tf_op jit(solution)/shard_map/add | solution.py:223
  218.5 4.9 multiply_reduce_fusion.6
  225.7 11.9 %fusion.9 = (f32[32,256]{1,0:T(8,128)S(1)}, f32[32,256]{1,0:T(8,128)S(1)}, f32[256,256]{1,0:T(8,128)S(1)}) fusion(f32[256,256]{1,0:T(8,128)S(1)} %fusion.83, f32[32,256]{1,0:T(8,128)S(1)} %copy-done.66, pred[256,256]{1,0:T(8,128)(4,1)S(1)} %copy-done.55, f32[32,64,256]{2,1,0:T(8,128)S(1)} %bitcast.232, f32[256,32,64]{0,2,1:T(8,128)S(1)} %bitcast.244, ...), kind=kOutput, calls=%fused_computation.17 | convolution fusion | flops 1629929472 | bytes 4915200 | tf_op jit(solution)/shard_map/transpose(jvp(chij,cjhp->cihp))/dot_general | solution.py:132
  237.7 8.8 %fusion.31 = (f32[256,32]{0,1:T(8,128)}, f32[1,256,32,64]{1,3,2,0:T(8,128)}) fusion(f32[1,256,32,64]{1,3,2,0:T(8,128)S(1)} %bitcast.245, f32[256,32]{0,1:T(8,128)S(1)} %copy-done.43, f32[32,64,256]{2,1,0:T(8,128)S(1)} %bitcast.233, f32[256,256]{1,0:T(8,128)S(1)} %fusion.83, f32[32,256]{1,0:T(8,128)S(1)} %copy-done.66, pred[256,256]{1,0:T(8,128)(4,1)S(1)} %copy-done.55), kind=kOutput, calls=%fused_computation.72 | convolution fusion | flops 1618468864 | bytes 6717440 | tf_op jit(solution)/shard_map/transpose(jvp(chij,cjhp->cihp))/dot_general | solution.py:132
  247.3 2.5 reduce-window.19
  252.1 2.7 bitcast_add_fusion.1
  255.8 2.8 multiply_reduce_fusion.4
  258.6 2.9 multiply_reduce_fusion.3
  268.1 7.8 %fusion.26 = f32[1024,4480]{1,0:T(8,128)} fusion(bf16[256,4384]{0,1:T(8,128)(2,1)S(1)} %add_convert_fusion, f32[256,1024]{1,0:T(8,128)S(1)} %copy-done.15, f32[1024]{0:T(1024)S(1)} %slice_bitcast_fusion.9, f32[256]{0:T(256)S(1)} %fusion.97), kind=kOutput, calls=%fused_computation.63 | convolution fusion | flops 2349596672 | bytes 21648384 | tf_op jit(solution)/shard_map/dot_general | solution.py:76
  275.9 10.6 %select_bitcast_fusion = f32[8,64,4480]{2,1,0:T(8,128)} fusion(f32[8,2,64,4480]{3,2,1,0:T(8,128)} %bitcast.222, pred[]{:T(512)S(6)} %eq.79), kind=kLoop, calls=%fused_computation.7 | loop fusion | flops 2293760 | bytes 27525120 | tf_op jit(solution)/shard_map/jit(_where)/select_n | solution.py:222
  286.6 3.2 fusion.10
  292.6 5.9 %collective-permute-done.29 = bf16[2,64,1024]{2,1,0:T(8,128)(2,1)S(1)} collective-permute-done((bf16[2,64,1024]{2,1,0:T(8,128)(2,1)S(1)}, bf16[2,64,1024]{2,1,0:T(8,128)(2,1)S(1)}, u32[]{:S(2)}, u32[]{:S(2)}) %collective-permute-start.29) | collective-permute-done | bytes 262176 | tf_op jit(solution)/shard_map/ppermute | solution.py:158
  302.7 4.5 collective-permute-done.30
  309.8 13.3 %fusion.2 = f32[8,64,4480]{2,1,0:T(8,128)} fusion(f32[8,64,4480]{2,1,0:T(8,128)} %collective-permute-done.18, f32[8,2,64,4480]{3,2,1,0:T(8,128)} %bitcast.223, pred[]{:T(512)S(6)} %eq.79), kind=kLoop, calls=%fused_computation.6 | loop fusion | flops 4587520 | bytes 36700160 | tf_op jit(solution)/shard_map/add | solution.py:223
  323.1 8.2 %fusion = f32[4,2,64,4480]{3,2,1,0:T(8,128)} fusion(s32[]{:T(128)S(6)} %select_n.224, f32[4,2,64,4480]{3,2,1,0:T(8,128)} %bitcast.230), kind=kLoop, calls=%fused_computation.2 | loop fusion | flops 2293760 | bytes 18350084 | tf_op jit(solution)/shard_map/concatenate | solution.py:151
  331.3 6.4 %slice_bitcast_fusion.3 = (f32[2,64,4480]{2,1,0:T(8,128)S(1)}, f32[2,64,4480]{2,1,0:T(8,128)S(1)}, f32[2,64,4480]{2,1,0:T(8,128)}, f32[2,64,4480]{2,1,0:T(8,128)}) fusion(f32[4,2,64,4480]{3,2,1,0:T(8,128)} %fusion), kind=kLoop, calls=%fused_computation.62 | loop fusion | bytes 18350080 | tf_op jit(solution)/shard_map/squeeze | solution.py:157
  343.4 15.9 %collective-permute-done.28 = bf16[2,64,1024]{2,1,0:T(8,128)(2,1)} collective-permute-done((bf16[2,64,1024]{2,1,0:T(8,128)(2,1)}, bf16[2,64,1024]{2,1,0:T(8,128)(2,1)}, u32[]{:S(2)}, u32[]{:S(2)}) %collective-permute-start.28) | collective-permute-done | bytes 262176 | tf_op jit(solution)/shard_map/ppermute | solution.py:161
  360.8 2.8 fusion.44
  378.7 3.7 collective-permute-done.20
  383.3 7.4 %multiply_reduce_fusion.10 = (f32[1024]{0:T(1024)S(1)}, f32[256]{0:T(256)S(1)}, f32[256,1024]{1,0:T(8,128)}) fusion(f32[256,1024]{1,0:T(8,128)S(1)} %copy-done.15, f32[256]{0:T(256)S(1)} %fusion.97, f32[1024]{0:T(1024)S(1)} %slice_bitcast_fusion.9, bf16[256,4384]{0,1:T(8,128)(2,1)S(1)} %copy-done.25, bf16[1024,4384]{1,0:T(8,128)(2,1)} %bitcast.239), kind=kOutput, calls=%fused_computation.135 | convolution fusion | flops 2300050176 | bytes 13330432 | tf_op jit(solution)/shard_map/dot_general | solution.py:82
  390.7 64.5 %all-reduce.22.cloned.1.call-done = f32[128,1024]{1,0:T(8,128)} async-done(((f32[128,1024]{1,0:T(8,128)}), f32[128,1024]{1,0:T(8,128)}) %all-reduce.22.cloned.1.call-update) | async-done | bytes 524304 | tf_op jit(solution)/shard_map/psum | solution.py:231
  455.3 6.1 %collective-permute-start.33 = (f32[128,1024]{1,0:T(8,128)}, f32[128,1024]{1,0:T(8,128)}, u32[]{:S(2)}, u32[]{:S(2)}) collective-permute-start(f32[128,1024]{1,0:T(8,128)} %all-reduce.22.cloned.1.call-done), channel_id=1, source_target_pairs={{0,8},{8,0},{1,9},{9,1},{2,10},{10,2},{3,11},{11,3},{4,12},{12,4},... | collective-permute-start | bytes 1572872 | tf_op jit(solution)/shard_map/ppermute | solution.py:198
  472.5 8.0 %collective-permute-done.25 = bf16[64,4480]{1,0:T(8,128)(2,1)} collective-permute-done((bf16[64,4480]{1,0:T(8,128)(2,1)}, bf16[64,4480]{1,0:T(8,128)(2,1)}, u32[]{:S(2)}, u32[]{:S(2)}) %collective-permute-start.25) | collective-permute-done | bytes 573472 | tf_op jit(solution)/shard_map/ppermute | solution.py:169
  483.3 2.8 collective-permute-done.11
  489.2 2.9 collective-permute-start.13
  494.4 3.8 collective-permute-start.14
  499.2 4.6 convolution_add_fusion
  505.4 4.0 collective-permute-done.16
  510.4 54.5 %all-reduce.24.cloned.1.call-done = f32[64,4480]{1,0:T(8,128)} async-done(((f32[64,4480]{1,0:T(8,128)}), f32[64,4480]{1,0:T(8,128)}) %all-reduce.24.cloned.1.call-update) | async-done | bytes 1146896 | tf_op jit(solution)/shard_map/psum | solution.py:231
  564.9 5.6 collective-permute-start.34
  570.5 2.8 fusion.50
  (395 shorter events, 131.3 us)
Async XLA Ops:
  7.2 191.9 %all-gather.3.cloned.1.call-start = ((), (), s32[]{:S(2)}) async-start(), calls=%async_computation.2 | async-start | bytes 2359296 | tf_op jit(solution)/shard_map/all_gather | solution.py:209
  9.8 14.5 %collective-permute-start.3 = (bf16[64,4384]{1,0:T(8,128)(2,1)S(1)}, bf16[64,4384]{1,0:T(8,128)(2,1)S(1)}, u32[]{:S(2)}, u32[]{:S(2)}) collective-permute-start(bf16[64,4384]{1,0:T(8,128)(2,1)S(1)} %copy.131), channel_id=1, source_target_pairs={{0,1},{1,0},{2,3},{3,2},{4,5},{5,4},{6,7},{7,6},{8,9},{9,8},{10,11... | collective-permute-start | bytes 1683464 | tf_op jit(solution)/shard_map/ppermute | solution.py:180
  26.4 28.3 %collective-permute-start.5 = (bf16[2,64,4384]{2,1,0:T(8,128)(2,1)}, bf16[2,64,4384]{2,1,0:T(8,128)(2,1)S(1)}, u32[]{:S(2)}, u32[]{:S(2)}) collective-permute-start(bf16[2,64,4384]{2,1,0:T(8,128)(2,1)} %maximum_select_fusion.1), channel_id=1, source_target_pairs={{0,2},{2,4},{4,6},{6,0},{1,3},{3,5},{5,7},{7,1},{8,10},{10,12},{12... | collective-permute-start | bytes 3366920 | tf_op jit(solution)/shard_map/ppermute | solution.py:184
  28.3 26.5 %collective-permute-start.4 = (bf16[2,64,4384]{2,1,0:T(8,128)(2,1)}, bf16[2,64,4384]{2,1,0:T(8,128)(2,1)S(1)}, u32[]{:S(2)}, u32[]{:S(2)}) collective-permute-start(bf16[2,64,4384]{2,1,0:T(8,128)(2,1)} %maximum_select_fusion.1), channel_id=1, source_target_pairs={{0,6},{2,0},{4,2},{6,4},{1,7},{3,1},{5,3},{7,5},{8,14},{10,8},{12,... | collective-permute-start | bytes 3366920 | tf_op jit(solution)/shard_map/ppermute | solution.py:185
  54.7 13.6 %collective-permute-start.6 = (bf16[2,32,4384]{2,1,0:T(8,128)(2,1)S(1)}, bf16[2,32,4384]{2,1,0:T(8,128)(2,1)S(1)}, u32[]{:S(2)}, u32[]{:S(2)}) collective-permute-start(bf16[2,32,4384]{2,1,0:T(8,128)(2,1)S(1)} %slice.308), channel_id=1, source_target_pairs={{0,2},{2,4},{4,6},{6,0},{1,3},{3,5},{5,7},{7,1},{8,10},{10,12},{12... | collective-permute-start | bytes 1683464 | tf_op jit(solution)/shard_map/ppermute | solution.py:187
  54.8 13.4 %collective-permute-start.7 = (bf16[2,32,4384]{2,1,0:T(8,128)(2,1)S(1)}, bf16[2,32,4384]{2,1,0:T(8,128)(2,1)S(1)}, u32[]{:S(2)}, u32[]{:S(2)}) collective-permute-start(bf16[2,32,4384]{2,1,0:T(8,128)(2,1)S(1)} %slice.309), channel_id=1, source_target_pairs={{0,6},{2,0},{4,2},{6,4},{1,7},{3,1},{5,3},{7,5},{8,14},{10,8},{12,... | collective-permute-start | bytes 1683464 | tf_op jit(solution)/shard_map/ppermute | solution.py:188
  71.9 19.9 %collective-permute-start.8 = (bf16[8,64,4384]{2,1,0:T(8,128)(2,1)}, bf16[8,64,4384]{2,1,0:T(8,128)(2,1)}, u32[]{:S(2)}, u32[]{:S(2)}) collective-permute-start(bf16[8,64,4384]{2,1,0:T(8,128)(2,1)} %bitcast.8), channel_id=1, source_target_pairs={{0,8},{8,0},{1,9},{9,1},{2,10},{10,2},{3,11},{11,3},{4,12},{12,4},... | collective-permute-start | bytes 13467656 | tf_op jit(solution)/shard_map/ppermute | solution.py:198
  75.5 3.6 collective-permute-start
  78.4 53.5 %copy-start.75 = (pred[256]{0:T(512)(128)(4,1)}, pred[256]{0:T(512)(128)(4,1)S(1)}, u32[]{:S(2)}) copy-start(pred[256]{0:T(512)(128)(4,1)S(1)} %get-tuple-element.133) | copy-start | bytes 772
  78.4 53.5 %copy-start.77 = (pred[256]{0:T(512)(128)(4,1)}, pred[256]{0:T(512)(128)(4,1)S(1)}, u32[]{:S(2)}) copy-start(pred[256]{0:T(512)(128)(4,1)S(1)} %get-tuple-element.134) | copy-start | bytes 772
  78.4 53.5 %copy-start.79 = (pred[256]{0:T(512)(128)(4,1)}, pred[256]{0:T(512)(128)(4,1)S(1)}, u32[]{:S(2)}) copy-start(pred[256]{0:T(512)(128)(4,1)S(1)} %get-tuple-element.135) | copy-start | bytes 772
  79.2 3.1 collective-permute-start.1
  82.4 4.8 collective-permute-start.2
  87.5 35.9 %copy-start.81 = (f32[32]{0:T(128)}, f32[32]{0:T(128)S(1)}, u32[]{:S(2)}) copy-start(f32[32]{0:T(128)S(1)} %add.260) | copy-start | bytes 388
  88.2 35.3 %copy-start.83 = (f32[32]{0:T(128)}, f32[32]{0:T(128)S(1)}, u32[]{:S(2)}) copy-start(f32[32]{0:T(128)S(1)} %neg.39) | copy-start | bytes 388
  91.7 40.2 %copy-start.47 = (f32[2304]{0:T(1024)}, f32[2304]{0:T(1024)S(1)}, u32[]{:S(2)}) copy-start(f32[2304]{0:T(1024)S(1)} %get-tuple-element.74) | copy-start | bytes 27652
  91.7 40.2 %copy-start.49 = (f32[2304]{0:T(1024)}, f32[2304]{0:T(1024)S(1)}, u32[]{:S(2)}) copy-start(f32[2304]{0:T(1024)S(1)} %get-tuple-element.75) | copy-start | bytes 27652
  91.7 40.2 %copy-start.51 = (f32[2304]{0:T(1024)}, f32[2304]{0:T(1024)S(1)}, u32[]{:S(2)}) copy-start(f32[2304]{0:T(1024)S(1)} %get-tuple-element.77) | copy-start | bytes 27652
  91.7 40.2 %copy-start.53 = (f32[2304]{0:T(1024)}, f32[2304]{0:T(1024)S(1)}, u32[]{:S(2)}) copy-start(f32[2304]{0:T(1024)S(1)} %get-tuple-element.76) | copy-start | bytes 27652
  143.0 312.2 %all-reduce.22.cloned.1.call-start = ((), (), s32[]{:S(2)}) async-start(), calls=%async_computation | async-start | bytes 1048576 | tf_op jit(solution)/shard_map/psum | solution.py:231
  167.0 36.1 %collective-permute-start.10 = (f32[8,128,1024]{2,1,0:T(8,128)}, f32[8,128,1024]{2,1,0:T(8,128)}, u32[]{:S(2)}, u32[]{:S(2)}) collective-permute-start(f32[8,128,1024]{2,1,0:T(8,128)} %select_bitcast_fusion.3), channel_id=1, source_target_pairs={{0,8},{8,0},{1,9},{9,1},{2,10},{10,2},{3,11},{11,3},{4,12},{12,4},... | collective-permute-start | bytes 12582920 | tf_op jit(solution)/shard_map/ppermute | solution.py:198
  199.1 12.9 %collective-permute-start.9 = (bf16[8,128,1024]{2,1,0:T(8,128)(2,1)}, bf16[8,128,1024]{2,1,0:T(8,128)(2,1)}, u32[]{:S(2)}, u32[]{:S(2)}) collective-permute-start(bf16[8,128,1024]{2,1,0:T(8,128)(2,1)} %bitcast.246), channel_id=1, source_target_pairs={{0,8},{8,0},{1,9},{9,1},{2,10},{10,2},{3,11},{11,3},{4,12},{12,4},... | collective-permute-start | bytes 6291464 | tf_op jit(solution)/shard_map/ppermute | solution.py:198
  286.5 23.3 %collective-permute-start.18 = (f32[8,64,4480]{2,1,0:T(8,128)}, f32[8,64,4480]{2,1,0:T(8,128)}, u32[]{:S(2)}, u32[]{:S(2)}) collective-permute-start(f32[8,64,4480]{2,1,0:T(8,128)} %select_bitcast_fusion), channel_id=1, source_target_pairs={{0,8},{8,0},{1,9},{9,1},{2,10},{10,2},{3,11},{11,3},{4,12},{12,4},... | collective-permute-start | bytes 27525128 | tf_op jit(solution)/shard_map/ppermute | solution.py:198
  291.1 7.5 %collective-permute-start.29 = (bf16[2,64,1024]{2,1,0:T(8,128)(2,1)S(1)}, bf16[2,64,1024]{2,1,0:T(8,128)(2,1)S(1)}, u32[]{:S(2)}, u32[]{:S(2)}) collective-permute-start(bf16[2,64,1024]{2,1,0:T(8,128)(2,1)S(1)} %slice.460), channel_id=1, source_target_pairs={{0,6},{2,0},{4,2},{6,4},{1,7},{3,1},{5,3},{7,5},{8,14},{10,8},{12,... | collective-permute-start | bytes 786440 | tf_op jit(solution)/shard_map/ppermute | solution.py:158
  291.9 8.3 %collective-permute-start.26 = (bf16[2,64,1024]{2,1,0:T(8,128)(2,1)S(1)}, bf16[2,64,1024]{2,1,0:T(8,128)(2,1)S(1)}, u32[]{:S(2)}, u32[]{:S(2)}) collective-permute-start(bf16[2,64,1024]{2,1,0:T(8,128)(2,1)S(1)} %slice.461), channel_id=1, source_target_pairs={{0,2},{2,4},{4,6},{6,0},{1,3},{3,5},{5,7},{7,1},{8,10},{10,12},{12... | collective-permute-start | bytes 786440 | tf_op jit(solution)/shard_map/ppermute | solution.py:157
  301.0 6.1 %collective-permute-start.30 = (bf16[2,64,1024]{2,1,0:T(8,128)(2,1)S(1)}, bf16[2,64,1024]{2,1,0:T(8,128)(2,1)S(1)}, u32[]{:S(2)}, u32[]{:S(2)}) collective-permute-start(bf16[2,64,1024]{2,1,0:T(8,128)(2,1)S(1)} %get-tuple-element.123), channel_id=1, source_target_pairs={{0,6},{2,0},{4,2},{6,4},{1,7},{3,1},{5,3},{7,5},{8,14},{10,8},{12,... | collective-permute-start | bytes 786440 | tf_op jit(solution)/shard_map/ppermute | solution.py:160
  301.4 40.3 %collective-permute-start.27 = (bf16[2,64,1024]{2,1,0:T(8,128)(2,1)}, bf16[2,64,1024]{2,1,0:T(8,128)(2,1)}, u32[]{:S(2)}, u32[]{:S(2)}) collective-permute-start(bf16[2,64,1024]{2,1,0:T(8,128)(2,1)} %get-tuple-element.124), channel_id=1, source_target_pairs={{0,2},{2,4},{4,6},{6,0},{1,3},{3,5},{5,7},{7,1},{8,10},{10,12},{12... | collective-permute-start | bytes 786440 | tf_op jit(solution)/shard_map/ppermute | solution.py:159
  307.9 35.4 %collective-permute-start.31 = (bf16[2,64,1024]{2,1,0:T(8,128)(2,1)}, bf16[2,64,1024]{2,1,0:T(8,128)(2,1)S(1)}, u32[]{:S(2)}, u32[]{:S(2)}) collective-permute-start(bf16[2,64,1024]{2,1,0:T(8,128)(2,1)} %fusion.67), channel_id=1, source_target_pairs={{0,6},{2,0},{4,2},{6,4},{1,7},{3,1},{5,3},{7,5},{8,14},{10,8},{12,... | collective-permute-start | bytes 786440 | tf_op jit(solution)/shard_map/ppermute | solution.py:162
  340.2 20.6 %collective-permute-start.22 = (bf16[2,32,4480]{2,1,0:T(8,128)(2,1)}, bf16[2,32,4480]{2,1,0:T(8,128)(2,1)}, u32[]{:S(2)}, u32[]{:S(2)}) collective-permute-start(bf16[2,32,4480]{2,1,0:T(8,128)(2,1)} %slice.458), channel_id=1, source_target_pairs={{0,6},{2,0},{4,2},{6,4},{1,7},{3,1},{5,3},{7,5},{8,14},{10,8},{12,... | collective-permute-start | bytes 1720328 | tf_op jit(solution)/shard_map/ppermute | solution.py:158
  340.2 20.5 %collective-permute-start.19 = (bf16[2,32,4480]{2,1,0:T(8,128)(2,1)}, bf16[2,32,4480]{2,1,0:T(8,128)(2,1)}, u32[]{:S(2)}, u32[]{:S(2)}) collective-permute-start(bf16[2,32,4480]{2,1,0:T(8,128)(2,1)} %slice.459), channel_id=1, source_target_pairs={{0,2},{2,4},{4,6},{6,0},{1,3},{3,5},{5,7},{7,1},{8,10},{10,12},{12... | collective-permute-start | bytes 1720328 | tf_op jit(solution)/shard_map/ppermute | solution.py:157
  343.3 16.0 %collective-permute-start.28 = (bf16[2,64,1024]{2,1,0:T(8,128)(2,1)}, bf16[2,64,1024]{2,1,0:T(8,128)(2,1)}, u32[]{:S(2)}, u32[]{:S(2)}) collective-permute-start(bf16[2,64,1024]{2,1,0:T(8,128)(2,1)} %fusion.69), channel_id=1, source_target_pairs={{0,2},{2,4},{4,6},{6,0},{1,3},{3,5},{5,7},{7,1},{8,10},{10,12},{12... | collective-permute-start | bytes 786440 | tf_op jit(solution)/shard_map/ppermute | solution.py:161
  343.3 17.4 %copy-start.23 = (f32[2,64,4480]{2,1,0:T(8,128)S(1)}, f32[2,64,4480]{2,1,0:T(8,128)}, u32[]{:S(2)}) copy-start(f32[2,64,4480]{2,1,0:T(8,128)} %get-tuple-element.97) | copy-start | bytes 6881284
  363.6 11.3 %collective-permute-start.23 = (bf16[2,32,4480]{2,1,0:T(8,128)(2,1)}, bf16[2,32,4480]{2,1,0:T(8,128)(2,1)}, u32[]{:S(2)}, u32[]{:S(2)}) collective-permute-start(bf16[2,32,4480]{2,1,0:T(8,128)(2,1)} %get-tuple-element.115), channel_id=1, source_target_pairs={{0,6},{2,0},{4,2},{6,4},{1,7},{3,1},{5,3},{7,5},{8,14},{10,8},{12,... | collective-permute-start | bytes 1720328 | tf_op jit(solution)/shard_map/ppermute | solution.py:160
  363.6 5.4 collective-permute-start.32
  371.0 193.9 %all-reduce.24.cloned.1.call-start = ((), (), s32[]{:S(2)}) async-start(), calls=%async_computation.1 | async-start | bytes 2293760 | tf_op jit(solution)/shard_map/psum | solution.py:231
  371.1 11.3 %collective-permute-start.20 = (bf16[2,32,4480]{2,1,0:T(8,128)(2,1)}, bf16[2,32,4480]{2,1,0:T(8,128)(2,1)S(1)}, u32[]{:S(2)}, u32[]{:S(2)}) collective-permute-start(bf16[2,32,4480]{2,1,0:T(8,128)(2,1)} %get-tuple-element.116), channel_id=1, source_target_pairs={{0,2},{2,4},{4,6},{6,0},{1,3},{3,5},{5,7},{7,1},{8,10},{10,12},{12... | collective-permute-start | bytes 1720328 | tf_op jit(solution)/shard_map/ppermute | solution.py:159
  377.2 84.2 %collective-permute-start.24 = (bf16[2,32,4480]{2,1,0:T(8,128)(2,1)}, bf16[2,32,4480]{2,1,0:T(8,128)(2,1)}, u32[]{:S(2)}, u32[]{:S(2)}) collective-permute-start(bf16[2,32,4480]{2,1,0:T(8,128)(2,1)} %fusion.43), channel_id=1, source_target_pairs={{0,6},{2,0},{4,2},{6,4},{1,7},{3,1},{5,3},{7,5},{8,14},{10,8},{12,... | collective-permute-start | bytes 1720328 | tf_op jit(solution)/shard_map/ppermute | solution.py:162
  383.3 78.1 %collective-permute-start.21 = (bf16[2,32,4480]{2,1,0:T(8,128)(2,1)}, bf16[2,32,4480]{2,1,0:T(8,128)(2,1)}, u32[]{:S(2)}, u32[]{:S(2)}) collective-permute-start(bf16[2,32,4480]{2,1,0:T(8,128)(2,1)} %fusion.45), channel_id=1, source_target_pairs={{0,2},{2,4},{4,6},{6,0},{1,3},{3,5},{5,7},{7,1},{8,10},{10,12},{12... | collective-permute-start | bytes 1720328 | tf_op jit(solution)/shard_map/ppermute | solution.py:161
  455.3 14.8 %collective-permute-start.33 = (f32[128,1024]{1,0:T(8,128)}, f32[128,1024]{1,0:T(8,128)}, u32[]{:S(2)}, u32[]{:S(2)}) collective-permute-start(f32[128,1024]{1,0:T(8,128)} %all-reduce.22.cloned.1.call-done), channel_id=1, source_target_pairs={{0,8},{8,0},{1,9},{9,1},{2,10},{10,2},{3,11},{11,3},{4,12},{12,4},... | collective-permute-start | bytes 1572872 | tf_op jit(solution)/shard_map/ppermute | solution.py:198
  465.4 15.1 %collective-permute-start.25 = (bf16[64,4480]{1,0:T(8,128)(2,1)}, bf16[64,4480]{1,0:T(8,128)(2,1)}, u32[]{:S(2)}, u32[]{:S(2)}) collective-permute-start(bf16[64,4480]{1,0:T(8,128)(2,1)} %fusion.61), channel_id=1, source_target_pairs={{0,1},{1,0},{2,3},{3,2},{4,5},{5,4},{6,7},{7,6},{8,9},{9,8},{10,11... | collective-permute-start | bytes 1720328 | tf_op jit(solution)/shard_map/ppermute | solution.py:169
  482.9 3.1 collective-permute-start.11
  486.0 3.2 collective-permute-start.12
  489.2 5.2 collective-permute-start.13
  494.4 4.7 collective-permute-start.14
  499.1 5.2 collective-permute-start.15
  504.3 5.1 collective-permute-start.16
  509.4 63.9 %collective-permute-start.17 = (f32[8,1836]{1,0:T(8,128)S(1)}, f32[8,1836]{1,0:T(8,128)S(1)}, u32[]{:S(2)}, u32[]{:S(2)}) collective-permute-start(f32[8,1836]{1,0:T(8,128)S(1)} %add.277), channel_id=1, source_target_pairs={{0,64},{16,80},{32,96},{48,112},{64,0},{80,16},{96,32},{112,48},{1... | collective-permute-start | bytes 176264 | tf_op jit(solution)/shard_map/ppermute | solution.py:248
  564.9 11.6 %collective-permute-start.34 = (f32[64,4480]{1,0:T(8,128)}, f32[64,4480]{1,0:T(8,128)S(1)}, u32[]{:S(2)}, u32[]{:S(2)}) collective-permute-start(f32[64,4480]{1,0:T(8,128)} %all-reduce.24.cloned.1.call-done), channel_id=1, source_target_pairs={{0,8},{8,0},{1,9},{9,1},{2,10},{10,2},{3,11},{11,3},{4,12},{12,4},... | collective-permute-start | bytes 3440648 | tf_op jit(solution)/shard_map/ppermute | solution.py:198
  (87 other events, 379.1 us)
Sparse Core Ops, SparseCore 0:
  143.1 55.9 all-gather.2
  371.1 84.0 all-reduce.21
  482.9 82.0 all-reduce.23

commit v7 on v6

--- a/solution.py
+++ b/solution.py
@@ -321,7 +321,7 @@
     cols = proj_low.shape[1]
     wide = -(-cols // 128) * 128
     proj_wide = jnp.pad(proj_low, ((0, 0), (0, wide - cols)))
-    in_owned = reduce_rows(row_product(normed, proj_wide), out_owned)[:, :cols]
+    in_owned = reduce_rows(row_product(normed, proj_wide))[:, :cols]
     small_sum = exchange_sum(small_blocks, ("shard_1", "shard_0", "core", "rep_hi"))
     mine = lax.dynamic_index_in_dim(small_sum, lax.axis_index(SHARD), axis=0, keepdims=False)
     small_final = []

time: 592 us -> 524 us (0.89)
  waiting for transfers between devices: 255 us -> 202 us
  other arithmetic: 130 us -> 122 us
    psum x2 -> x1, waiting for transfers between devices: 119 us -> 50.9 us  [reduce_rest(): owned = lax.psum(owned, 'rep_hi')]
    ppermute x2, waiting for transfers between devices: 15.9 us -> 3.42 us  [reduce_group(): acc_up = lax.ppermute(low(acc_up + rel[1][:, :half]), 'shard_0', up)]
    ppermute x2, waiting for transfers between devices: 9.9 us -> 0.01 us  [reduce_group(): lax.ppermute(low(give), 'shard_1', [(0, 1), (1, 0)]).astype(jnp.float32)]
    ppermute x6, waiting for transfers between devices: 0.02 us -> 9.36 us  [core_swap(): return lax.ppermute(values, 'core', [(0, 1), (1, 0)])]
    ppermute x2, waiting for transfers between devices: 5.92 us -> 15 us  [reduce_group(): acc_dn = lax.ppermute(low(rel[1][:, half:]), 'shard_0', down)]
    ppermute x2, waiting for transfers between devices: 6.78 us -> 13.4 us  [reduce_group(): acc_dn = lax.ppermute(low(acc_dn + rel[2][:, half:]), 'shard_0', down)]
    convert_element_type x8, other arithmetic: 10.2 us -> 3.84 us  [reduce_group(): low = lambda a: a.astype(jnp.bfloat16)]
    ppermute x6, starting transfers between devices: 19.3 us -> 12.9 us  [core_swap(): return lax.ppermute(values, 'core', [(0, 1), (1, 0)])]
  transfers between devices with their start and end apart: 38 -> 37, of which waited for: 23 -> 22; matrix products, arithmetic and copies ran while one was open for 20% -> 16% of each run, Pallas kernels for 0% -> 0%
where the time goes in v7:
time: 524 us; the launch traced here: 518 us
  waiting for transfers between devices  202 us (39%)
  other arithmetic  122 us (23%)
  matrix products  67.4 us (13%)
  local copies, waits for them, and re-layouts  60.9 us (12%)
  starting transfers between devices  50.7 us (10%)
  between operations  15.8 us (3%)
    psum x1, waiting for transfers between devices, reduce_rest(): owned = lax.psum(owned, 'rep_hi')  50.9 us
    dot_general x3, matrix products, mixer(): y_intra = jnp.einsum('chij,cjhp->cihp', mixing, scaled_in, precision=HIGH)  32.6 us
    all_gather x1, waiting for transfers between devices, gather_rows(): part = lax.all_gather(mine, SHARD, axis=0, tiled=False)  29.1 us
    ppermute x1, waiting for transfers between devices, gather_group(): from_prev = lax.ppermute(pair, 'shard_0', up)  22.7 us
    add x2, other arithmetic, reduce_core(): return keep + core_swap(give)  22.3 us
    ppermute x10, waiting for transfers between devices, exchange_sum(): values = values + lax.ppermute(values, axis, pairs)  20.9 us
    another operation x4, other arithmetic, gather_rows(): return jnp.stack([first, second], axis=1).reshape(-1, weight.shape[1])  18.8 us
    ppermute x10, starting transfers between devices, exchange_sum(): values = values + lax.ppermute(values, axis, pairs)  18.5 us
  transfers between devices with their start and end apart: 37, of which 22 were waited for; matrix products, arithmetic and copies ran while one was open for 16% of the time, Pallas kernels for 0%

profile of v7, /device:TPU:1, one launch (start us, length us, event | category | flops | bytes accessed | tf_op | source)
XLA Modules:
  0.0 518.1 jit_solution(3027361201502290386)
XLA Ops:
  12.0 12.3 %collective-permute-done.3 = bf16[64,4384]{1,0:T(8,128)(2,1)S(1)} collective-permute-done((bf16[64,4384]{1,0:T(8,128)(2,1)S(1)}, bf16[64,4384]{1,0:T(8,128)(2,1)S(1)}, u32[]{:S(2)}, u32[]{:S(2)}) %collective-permute-start.3) | collective-permute-done | bytes 561184 | tf_op jit(solution)/shard_map/ppermute | solution.py:180
  31.9 22.7 %collective-permute-done.5 = bf16[2,64,4384]{2,1,0:T(8,128)(2,1)S(1)} collective-permute-done((bf16[2,64,4384]{2,1,0:T(8,128)(2,1)}, bf16[2,64,4384]{2,1,0:T(8,128)(2,1)S(1)}, u32[]{:S(2)}, u32[]{:S(2)}) %collective-permute-start.5) | collective-permute-done | bytes 1122336 | tf_op jit(solution)/shard_map/ppermute | solution.py:184
  54.8 2.7 collective-permute-start.7
  57.7 10.5 %collective-permute-done.6 = bf16[2,32,4384]{2,1,0:T(8,128)(2,1)S(1)} collective-permute-done((bf16[2,32,4384]{2,1,0:T(8,128)(2,1)S(1)}, bf16[2,32,4384]{2,1,0:T(8,128)(2,1)S(1)}, u32[]{:S(2)}, u32[]{:S(2)}) %collective-permute-start.6) | collective-permute-done | bytes 561184 | tf_op jit(solution)/shard_map/ppermute | solution.py:187
  71.9 3.1 collective-permute-start.8
  79.4 2.9 collective-permute-done.1
  82.4 2.7 collective-permute-start.2
  91.7 8.1 %select_bitcast_fusion.2 = (bf16[8,1,64,4384]{3,2,0,1:T(8,128)(2,1)}, bf16[8,1,64,4384]{3,2,0,1:T(8,128)(2,1)}) fusion(bf16[8,64,4384]{2,1,0:T(8,128)(2,1)} %collective-permute-done.8, pred[]{:T(512)S(6)} %eq.79, bf16[4,2,64,4384]{3,2,1,0:T(8,128)(2,1)} %constant_dynamic-slice_fusion.1), kind=kLoop, calls=%fused_computation.19 | loop fusion | flops 4489216 | bytes 17956864 | tf_op jit(solution)/shard_map/stack | solution.py:213
  99.8 8.2 %pad_maximum_fusion = bf16[8,2,64,4384]{3,2,0,1:T(8,128)(2,1)} fusion(bf16[8,1,64,4384]{3,2,0,1:T(8,128)(2,1)} %get-tuple-element.100, bf16[8,1,64,4384]{3,2,0,1:T(8,128)(2,1)} %get-tuple-element.99), kind=kLoop, calls=%fused_computation.3 | loop fusion | flops 4489216 | bytes 17956864 | tf_op jit(solution)/shard_map/stack | solution.py:213
  108.0 8.0 %copy.107 = bf16[8,2,64,4384]{3,2,1,0:T(8,128)(2,1)} copy(bf16[8,2,64,4384]{3,2,0,1:T(8,128)(2,1)} %pad_maximum_fusion) | data formatting | bytes 17956864 | tf_op jit(solution)/shard_map/stack | solution.py:213
  116.0 7.5 %fusion.104 = f32[256,4384]{0,1:T(8,128)S(1)} fusion(bf16[1024,4384]{1,0:T(8,128)(2,1)} %bitcast.238, f32[256,1024]{1,0:T(8,128)S(1)} %copy-done.15, f32[1024]{0:T(1024)S(1)} %slice_bitcast_fusion.9, f32[256]{0:T(256)S(1)} %fusion.97), kind=kOutput, calls=%fused_computation.245 | convolution fusion | flops 2299265024 | bytes 14521344 | tf_op jit(solution)/shard_map/dot_general | solution.py:291
  133.7 4.9 fusion.25
  145.5 11.9 %fusion.30 = f32[256,32,64]{0,2,1:T(8,128)S(1)} fusion(f32[256,32,64]{0,2,1:T(8,128)} %bitcast.243, f32[256,32,64]{0,2,1:T(8,128)S(1)} %fusion.72, f32[32]{0:T(128)} %mul.426, f32[256,32]{0,1:T(8,128)S(1)} %bitcast_multiply_fusion.4, f32[256,256]{1,0:T(8,128)S(1)} %fusion.83, f32[32,256]{1,0:T(8,128)S(1)} %bitcast_add_fusion.2, ...), kind=kOutput, calls=%fused_computation.68 | convolution fusion | flops 1619525632 | bytes 6717568 | tf_op jit(solution)/shard_map/jvp(chij,cjhp->cihp)/dot_general | solution.py:132
  157.5 3.1 multiply_reduce_fusion.9
  162.4 3.4 select_bitcast_fusion.3
  167.0 3.1 collective-permute-start.10
  170.1 29.1 %all-gather.3.cloned.1.call-done = bf16[1024,1024]{1,0:T(8,128)(2,1)} async-done(((bf16[128,1024]{1,0:T(8,128)(2,1)}), bf16[1024,1024]{1,0:T(8,128)(2,1)}) %all-gather.3.cloned.1.call-update) | async-done | bytes 2097168 | tf_op jit(solution)/shard_map/all_gather | solution.py:209
  203.2 8.8 %fusion.12 = f32[8,128,1024]{2,1,0:T(8,128)} fusion(f32[8,128,1024]{2,1,0:T(8,128)} %collective-permute-done.10, f32[8,2,128,1024]{3,2,1,0:T(8,128)} %bitcast.225, pred[]{:T(512)S(6)} %eq.79), kind=kLoop, calls=%fused_computation.25 | loop fusion | flops 2097152 | bytes 16777216 | tf_op jit(solution)/shard_map/add | solution.py:223
  218.5 4.8 multiply_reduce_fusion.6
  225.7 11.9 %fusion.9 = (f32[32,256]{1,0:T(8,128)S(1)}, f32[32,256]{1,0:T(8,128)S(1)}, f32[256,256]{1,0:T(8,128)S(1)}) fusion(f32[256,256]{1,0:T(8,128)S(1)} %fusion.83, f32[32,256]{1,0:T(8,128)S(1)} %copy-done.59, pred[256,256]{1,0:T(8,128)(4,1)S(1)} %copy-done.47, f32[32,64,256]{2,1,0:T(8,128)S(1)} %bitcast.232, f32[256,32,64]{0,2,1:T(8,128)S(1)} %bitcast.244, ...), kind=kOutput, calls=%fused_computation.17 | convolution fusion | flops 1629929472 | bytes 4915200 | tf_op jit(solution)/shard_map/transpose(jvp(chij,cjhp->cihp))/dot_general | solution.py:132
  237.7 8.8 %fusion.31 = (f32[256,32]{0,1:T(8,128)}, f32[1,256,32,64]{1,3,2,0:T(8,128)}) fusion(f32[1,256,32,64]{1,3,2,0:T(8,128)S(1)} %bitcast.245, f32[256,32]{0,1:T(8,128)S(1)} %copy-done.35, f32[32,64,256]{2,1,0:T(8,128)S(1)} %bitcast.233, f32[256,256]{1,0:T(8,128)S(1)} %fusion.83, f32[32,256]{1,0:T(8,128)S(1)} %copy-done.59, pred[256,256]{1,0:T(8,128)(4,1)S(1)} %copy-done.47), kind=kOutput, calls=%fused_computation.72 | convolution fusion | flops 1618468864 | bytes 6717440 | tf_op jit(solution)/shard_map/transpose(jvp(chij,cjhp->cihp))/dot_general | solution.py:132
  247.3 2.5 reduce-window.19
  252.1 2.7 bitcast_add_fusion.1
  255.8 2.8 multiply_reduce_fusion.4
  258.6 2.9 multiply_reduce_fusion.3
  268.1 7.9 %fusion.26 = f32[1024,4480]{1,0:T(8,128)} fusion(bf16[256,4384]{0,1:T(8,128)(2,1)S(1)} %add_convert_fusion, f32[256,1024]{1,0:T(8,128)S(1)} %copy-done.15, f32[1024]{0:T(1024)S(1)} %slice_bitcast_fusion.9, f32[256]{0:T(256)S(1)} %fusion.97), kind=kOutput, calls=%fused_computation.63 | convolution fusion | flops 2349596672 | bytes 21648384 | tf_op jit(solution)/shard_map/dot_general | solution.py:76
  275.9 10.6 %select_bitcast_fusion = f32[8,64,4480]{2,1,0:T(8,128)} fusion(f32[8,2,64,4480]{3,2,1,0:T(8,128)} %bitcast.222, pred[]{:T(512)S(6)} %eq.79), kind=kLoop, calls=%fused_computation.7 | loop fusion | flops 2293760 | bytes 27525120 | tf_op jit(solution)/shard_map/jit(_where)/select_n | solution.py:222
  286.6 5.7 %fusion.10 = f32[4,2,128,1024]{3,2,1,0:T(8,128)} fusion(s32[]{:T(128)S(6)} %select_n.224, f32[4,2,128,1024]{3,2,1,0:T(8,128)} %bitcast.234), kind=kLoop, calls=%fused_computation.21 | loop fusion | flops 1048576 | bytes 8388612 | tf_op jit(solution)/shard_map/concatenate | solution.py:151
  292.3 8.9 %collective-permute-done.18 = f32[8,64,4480]{2,1,0:T(8,128)} collective-permute-done((f32[8,64,4480]{2,1,0:T(8,128)}, f32[8,64,4480]{2,1,0:T(8,128)}, u32[]{:S(2)}, u32[]{:S(2)}) %collective-permute-start.18) | collective-permute-done | bytes 9175072 | tf_op jit(solution)/shard_map/ppermute | solution.py:198
  301.2 13.5 %fusion.2 = f32[8,64,4480]{2,1,0:T(8,128)} fusion(f32[8,64,4480]{2,1,0:T(8,128)} %collective-permute-done.18, f32[8,2,64,4480]{3,2,1,0:T(8,128)} %bitcast.223, pred[]{:T(512)S(6)} %eq.79), kind=kLoop, calls=%fused_computation.6 | loop fusion | flops 4587520 | bytes 36700160 | tf_op jit(solution)/shard_map/add | solution.py:223
  314.7 8.2 %fusion = f32[4,2,64,4480]{3,2,1,0:T(8,128)} fusion(s32[]{:T(128)S(6)} %select_n.224, f32[4,2,64,4480]{3,2,1,0:T(8,128)} %bitcast.230), kind=kLoop, calls=%fused_computation.2 | loop fusion | flops 2293760 | bytes 18350084 | tf_op jit(solution)/shard_map/concatenate | solution.py:151
  322.9 5.8 %slice_bitcast_fusion.3 = (f32[2,64,4480]{2,1,0:T(8,128)S(1)}, f32[2,64,4480]{2,1,0:T(8,128)S(1)}, f32[2,64,4480]{2,1,0:T(8,128)S(1)}, f32[2,64,4480]{2,1,0:T(8,128)}) fusion(f32[4,2,64,4480]{3,2,1,0:T(8,128)} %fusion), kind=kLoop, calls=%fused_computation.62 | loop fusion | bytes 18350080 | tf_op jit(solution)/shard_map/squeeze | solution.py:157
  334.0 15.0 %collective-permute-done.30 = bf16[2,64,1024]{2,1,0:T(8,128)(2,1)S(1)} collective-permute-done((bf16[2,64,1024]{2,1,0:T(8,128)(2,1)S(1)}, bf16[2,64,1024]{2,1,0:T(8,128)(2,1)S(1)}, u32[]{:S(2)}, u32[]{:S(2)}) %collective-permute-start.30) | collective-permute-done | bytes 262176 | tf_op jit(solution)/shard_map/ppermute | solution.py:158
  352.9 4.5 collective-permute-done.31
  360.9 8.9 %collective-permute-done.23 = bf16[2,32,4480]{2,1,0:T(8,128)(2,1)S(1)} collective-permute-done((bf16[2,32,4480]{2,1,0:T(8,128)(2,1)S(1)}, bf16[2,32,4480]{2,1,0:T(8,128)(2,1)S(1)}, u32[]{:S(2)}, u32[]{:S(2)}) %collective-permute-start.23) | collective-permute-done | bytes 573472 | tf_op jit(solution)/shard_map/ppermute | solution.py:160
  372.5 6.3 %collective-permute-done.20 = bf16[2,32,4480]{2,1,0:T(8,128)(2,1)S(1)} collective-permute-done((bf16[2,32,4480]{2,1,0:T(8,128)(2,1)S(1)}, bf16[2,32,4480]{2,1,0:T(8,128)(2,1)S(1)}, u32[]{:S(2)}, u32[]{:S(2)}) %collective-permute-start.20) | collective-permute-done | bytes 573472 | tf_op jit(solution)/shard_map/ppermute | solution.py:159
  381.7 6.0 %collective-permute-done.24 = bf16[2,32,4480]{2,1,0:T(8,128)(2,1)} collective-permute-done((bf16[2,32,4480]{2,1,0:T(8,128)(2,1)}, bf16[2,32,4480]{2,1,0:T(8,128)(2,1)}, u32[]{:S(2)}, u32[]{:S(2)}) %collective-permute-start.24) | collective-permute-done | bytes 573472 | tf_op jit(solution)/shard_map/ppermute | solution.py:162
  387.7 3.4 collective-permute-done.21
  394.3 7.9 %multiply_reduce_fusion.10 = (f32[1024]{0:T(1024)}, f32[256]{0:T(256)}, f32[256,1024]{1,0:T(8,128)}) fusion(f32[256,1024]{1,0:T(8,128)S(1)} %copy-done.15, f32[256]{0:T(256)S(1)} %fusion.97, f32[1024]{0:T(1024)S(1)} %slice_bitcast_fusion.9, bf16[256,4384]{0,1:T(8,128)(2,1)S(1)} %copy-done.23, bf16[1024,4384]{1,0:T(8,128)(2,1)} %bitcast.239), kind=kOutput, calls=%fused_computation.135 | convolution fusion | flops 2300050176 | bytes 13330432 | tf_op jit(solution)/shard_map/dot_general | solution.py:82
  411.3 2.7 collective-permute-done.11
  414.2 3.1 collective-permute-done.12
  417.3 4.6 collective-permute-done.13
  421.9 9.0 %collective-permute-start.14 = (f32[8,1836]{1,0:T(8,128)S(1)}, f32[8,1836]{1,0:T(8,128)S(1)}, u32[]{:S(2)}, u32[]{:S(2)}) collective-permute-start(f32[8,1836]{1,0:T(8,128)S(1)} %add.274), channel_id=1, source_target_pairs={{0,8},{8,0},{1,9},{9,1},{2,10},{10,2},{3,11},{11,3},{4,12},{12,4},... | collective-permute-start | bytes 176264 | tf_op jit(solution)/shard_map/ppermute | solution.py:248
  433.1 4.6 convolution_add_fusion
  437.7 2.5 collective-permute-start.16
  440.2 4.0 collective-permute-done.16
  446.6 50.9 %all-reduce.22.cloned.1.call-done = (f32[64,4480]{1,0:T(8,128)}, f32[128,1024]{1,0:T(8,128)}) async-done(((f32[64,4480]{1,0:T(8,128)}, f32[128,1024]{1,0:T(8,128)}), (f32[64,4480]{1,0:T(8,128)}, f32[128,1024]{1,0:T(8,128)})) %all-reduce.22.cloned.1.call-update) | async-done | bytes 1671184 | tf_op jit(solution)/shard_map/psum | solution.py:231
  497.5 5.3 %collective-permute-start.26 = (f32[64,4480]{1,0:T(8,128)}, f32[64,4480]{1,0:T(8,128)S(1)}, u32[]{:S(2)}, u32[]{:S(2)}) collective-permute-start(f32[64,4480]{1,0:T(8,128)} %get-tuple-element.76), channel_id=1, source_target_pairs={{0,8},{8,0},{1,9},{9,1},{2,10},{10,2},{3,11},{11,3},{4,12},{12,4},... | collective-permute-start | bytes 3440648 | tf_op jit(solution)/shard_map/ppermute | solution.py:198
  (382 shorter events, 113.6 us)
Async XLA Ops:
  7.2 191.9 %all-gather.3.cloned.1.call-start = ((), (), s32[]{:S(2)}) async-start(), calls=%async_computation | async-start | bytes 2359296 | tf_op jit(solution)/shard_map/all_gather | solution.py:209
  9.8 14.5 %collective-permute-start.3 = (bf16[64,4384]{1,0:T(8,128)(2,1)S(1)}, bf16[64,4384]{1,0:T(8,128)(2,1)S(1)}, u32[]{:S(2)}, u32[]{:S(2)}) collective-permute-start(bf16[64,4384]{1,0:T(8,128)(2,1)S(1)} %copy.131), channel_id=1, source_target_pairs={{0,1},{1,0},{2,3},{3,2},{4,5},{5,4},{6,7},{7,6},{8,9},{9,8},{10,11... | collective-permute-start | bytes 1683464 | tf_op jit(solution)/shard_map/ppermute | solution.py:180
  26.4 28.3 %collective-permute-start.5 = (bf16[2,64,4384]{2,1,0:T(8,128)(2,1)}, bf16[2,64,4384]{2,1,0:T(8,128)(2,1)S(1)}, u32[]{:S(2)}, u32[]{:S(2)}) collective-permute-start(bf16[2,64,4384]{2,1,0:T(8,128)(2,1)} %maximum_select_fusion.1), channel_id=1, source_target_pairs={{0,2},{2,4},{4,6},{6,0},{1,3},{3,5},{5,7},{7,1},{8,10},{10,12},{12... | collective-permute-start | bytes 3366920 | tf_op jit(solution)/shard_map/ppermute | solution.py:184
  28.3 26.5 %collective-permute-start.4 = (bf16[2,64,4384]{2,1,0:T(8,128)(2,1)}, bf16[2,64,4384]{2,1,0:T(8,128)(2,1)S(1)}, u32[]{:S(2)}, u32[]{:S(2)}) collective-permute-start(bf16[2,64,4384]{2,1,0:T(8,128)(2,1)} %maximum_select_fusion.1), channel_id=1, source_target_pairs={{0,6},{2,0},{4,2},{6,4},{1,7},{3,1},{5,3},{7,5},{8,14},{10,8},{12,... | collective-permute-start | bytes 3366920 | tf_op jit(solution)/shard_map/ppermute | solution.py:185
  54.7 13.6 %collective-permute-start.6 = (bf16[2,32,4384]{2,1,0:T(8,128)(2,1)S(1)}, bf16[2,32,4384]{2,1,0:T(8,128)(2,1)S(1)}, u32[]{:S(2)}, u32[]{:S(2)}) collective-permute-start(bf16[2,32,4384]{2,1,0:T(8,128)(2,1)S(1)} %slice.308), channel_id=1, source_target_pairs={{0,2},{2,4},{4,6},{6,0},{1,3},{3,5},{5,7},{7,1},{8,10},{10,12},{12... | collective-permute-start | bytes 1683464 | tf_op jit(solution)/shard_map/ppermute | solution.py:187
  54.8 13.4 %collective-permute-start.7 = (bf16[2,32,4384]{2,1,0:T(8,128)(2,1)S(1)}, bf16[2,32,4384]{2,1,0:T(8,128)(2,1)S(1)}, u32[]{:S(2)}, u32[]{:S(2)}) collective-permute-start(bf16[2,32,4384]{2,1,0:T(8,128)(2,1)S(1)} %slice.309), channel_id=1, source_target_pairs={{0,6},{2,0},{4,2},{6,4},{1,7},{3,1},{5,3},{7,5},{8,14},{10,8},{12,... | collective-permute-start | bytes 1683464 | tf_op jit(solution)/shard_map/ppermute | solution.py:188
  71.9 19.9 %collective-permute-start.8 = (bf16[8,64,4384]{2,1,0:T(8,128)(2,1)}, bf16[8,64,4384]{2,1,0:T(8,128)(2,1)}, u32[]{:S(2)}, u32[]{:S(2)}) collective-permute-start(bf16[8,64,4384]{2,1,0:T(8,128)(2,1)} %bitcast.8), channel_id=1, source_target_pairs={{0,8},{8,0},{1,9},{9,1},{2,10},{10,2},{3,11},{11,3},{4,12},{12,4},... | collective-permute-start | bytes 13467656 | tf_op jit(solution)/shard_map/ppermute | solution.py:198
  75.5 3.6 collective-permute-start
  78.4 53.5 %copy-start.68 = (pred[256]{0:T(512)(128)(4,1)}, pred[256]{0:T(512)(128)(4,1)S(1)}, u32[]{:S(2)}) copy-start(pred[256]{0:T(512)(128)(4,1)S(1)} %get-tuple-element.133) | copy-start | bytes 772
  78.4 53.6 %copy-start.70 = (pred[256]{0:T(512)(128)(4,1)}, pred[256]{0:T(512)(128)(4,1)S(1)}, u32[]{:S(2)}) copy-start(pred[256]{0:T(512)(128)(4,1)S(1)} %get-tuple-element.134) | copy-start | bytes 772
  78.4 53.6 %copy-start.72 = (pred[256]{0:T(512)(128)(4,1)}, pred[256]{0:T(512)(128)(4,1)S(1)}, u32[]{:S(2)}) copy-start(pred[256]{0:T(512)(128)(4,1)S(1)} %get-tuple-element.135) | copy-start | bytes 772
  79.2 3.1 collective-permute-start.1
  82.4 4.8 collective-permute-start.2
  87.5 36.0 %copy-start.74 = (f32[32]{0:T(128)}, f32[32]{0:T(128)S(1)}, u32[]{:S(2)}) copy-start(f32[32]{0:T(128)S(1)} %add.260) | copy-start | bytes 388
  88.2 35.3 %copy-start.76 = (f32[32]{0:T(128)}, f32[32]{0:T(128)S(1)}, u32[]{:S(2)}) copy-start(f32[32]{0:T(128)S(1)} %neg.39) | copy-start | bytes 388
  91.7 40.3 %copy-start.39 = (f32[2304]{0:T(1024)}, f32[2304]{0:T(1024)S(1)}, u32[]{:S(2)}) copy-start(f32[2304]{0:T(1024)S(1)} %get-tuple-element.72) | copy-start | bytes 27652
  91.7 40.3 %copy-start.41 = (f32[2304]{0:T(1024)}, f32[2304]{0:T(1024)S(1)}, u32[]{:S(2)}) copy-start(f32[2304]{0:T(1024)S(1)} %get-tuple-element.73) | copy-start | bytes 27652
  91.7 40.3 %copy-start.43 = (f32[2304]{0:T(1024)}, f32[2304]{0:T(1024)S(1)}, u32[]{:S(2)}) copy-start(f32[2304]{0:T(1024)S(1)} %get-tuple-element.75) | copy-start | bytes 27652
  91.7 40.3 %copy-start.45 = (f32[2304]{0:T(1024)}, f32[2304]{0:T(1024)S(1)}, u32[]{:S(2)}) copy-start(f32[2304]{0:T(1024)S(1)} %get-tuple-element.74) | copy-start | bytes 27652
  143.1 354.4 %all-reduce.22.cloned.1.call-start = ((), (), s32[]{:S(2)}) async-start(), calls=%async_computation.1 | async-start | bytes 3342336 | tf_op jit(solution)/shard_map/psum | solution.py:231
  167.0 36.2 %collective-permute-start.10 = (f32[8,128,1024]{2,1,0:T(8,128)}, f32[8,128,1024]{2,1,0:T(8,128)}, u32[]{:S(2)}, u32[]{:S(2)}) collective-permute-start(f32[8,128,1024]{2,1,0:T(8,128)} %select_bitcast_fusion.3), channel_id=1, source_target_pairs={{0,8},{8,0},{1,9},{9,1},{2,10},{10,2},{3,11},{11,3},{4,12},{12,4},... | collective-permute-start | bytes 12582920 | tf_op jit(solution)/shard_map/ppermute | solution.py:198
  199.1 12.8 %collective-permute-start.9 = (bf16[8,128,1024]{2,1,0:T(8,128)(2,1)}, bf16[8,128,1024]{2,1,0:T(8,128)(2,1)}, u32[]{:S(2)}, u32[]{:S(2)}) collective-permute-start(bf16[8,128,1024]{2,1,0:T(8,128)(2,1)} %bitcast.246), channel_id=1, source_target_pairs={{0,8},{8,0},{1,9},{9,1},{2,10},{10,2},{3,11},{11,3},{4,12},{12,4},... | collective-permute-start | bytes 6291464 | tf_op jit(solution)/shard_map/ppermute | solution.py:198
  223.4 14.3 %copy-start.6 = (f32[256,2048]{0,1:T(8,128)}, f32[256,2048]{0,1:T(8,128)S(1)}, u32[]{:S(2)}) copy-start(f32[256,2048]{0,1:T(8,128)S(1)} %get-tuple-element.79) | copy-start | bytes 6291460
  286.6 14.6 %collective-permute-start.18 = (f32[8,64,4480]{2,1,0:T(8,128)}, f32[8,64,4480]{2,1,0:T(8,128)}, u32[]{:S(2)}, u32[]{:S(2)}) collective-permute-start(f32[8,64,4480]{2,1,0:T(8,128)} %select_bitcast_fusion), channel_id=1, source_target_pairs={{0,8},{8,0},{1,9},{9,1},{2,10},{10,2},{3,11},{11,3},{4,12},{12,4},... | collective-permute-start | bytes 27525128 | tf_op jit(solution)/shard_map/ppermute | solution.py:198
  328.9 22.3 %collective-permute-start.22 = (bf16[2,32,4480]{2,1,0:T(8,128)(2,1)S(1)}, bf16[2,32,4480]{2,1,0:T(8,128)(2,1)S(1)}, u32[]{:S(2)}, u32[]{:S(2)}) collective-permute-start(bf16[2,32,4480]{2,1,0:T(8,128)(2,1)S(1)} %slice.458), channel_id=1, source_target_pairs={{0,6},{2,0},{4,2},{6,4},{1,7},{3,1},{5,3},{7,5},{8,14},{10,8},{12,... | collective-permute-start | bytes 1720328 | tf_op jit(solution)/shard_map/ppermute | solution.py:158
  329.7 21.5 %collective-permute-start.19 = (bf16[2,32,4480]{2,1,0:T(8,128)(2,1)S(1)}, bf16[2,32,4480]{2,1,0:T(8,128)(2,1)S(1)}, u32[]{:S(2)}, u32[]{:S(2)}) collective-permute-start(bf16[2,32,4480]{2,1,0:T(8,128)(2,1)S(1)} %slice.459), channel_id=1, source_target_pairs={{0,2},{2,4},{4,6},{6,0},{1,3},{3,5},{5,7},{7,1},{8,10},{10,12},{12... | collective-permute-start | bytes 1720328 | tf_op jit(solution)/shard_map/ppermute | solution.py:157
  332.0 17.0 %collective-permute-start.30 = (bf16[2,64,1024]{2,1,0:T(8,128)(2,1)S(1)}, bf16[2,64,1024]{2,1,0:T(8,128)(2,1)S(1)}, u32[]{:S(2)}, u32[]{:S(2)}) collective-permute-start(bf16[2,64,1024]{2,1,0:T(8,128)(2,1)S(1)} %slice.460), channel_id=1, source_target_pairs={{0,6},{2,0},{4,2},{6,4},{1,7},{3,1},{5,3},{7,5},{8,14},{10,8},{12,... | collective-permute-start | bytes 786440 | tf_op jit(solution)/shard_map/ppermute | solution.py:158
  334.0 16.6 %collective-permute-start.27 = (bf16[2,64,1024]{2,1,0:T(8,128)(2,1)S(1)}, bf16[2,64,1024]{2,1,0:T(8,128)(2,1)S(1)}, u32[]{:S(2)}, u32[]{:S(2)}) collective-permute-start(bf16[2,64,1024]{2,1,0:T(8,128)(2,1)S(1)} %slice.461), channel_id=1, source_target_pairs={{0,2},{2,4},{4,6},{6,0},{1,3},{3,5},{5,7},{7,1},{8,10},{10,12},{12... | collective-permute-start | bytes 786440 | tf_op jit(solution)/shard_map/ppermute | solution.py:157
  350.8 6.6 %collective-permute-start.31 = (bf16[2,64,1024]{2,1,0:T(8,128)(2,1)S(1)}, bf16[2,64,1024]{2,1,0:T(8,128)(2,1)S(1)}, u32[]{:S(2)}, u32[]{:S(2)}) collective-permute-start(bf16[2,64,1024]{2,1,0:T(8,128)(2,1)S(1)} %get-tuple-element.123), channel_id=1, source_target_pairs={{0,6},{2,0},{4,2},{6,4},{1,7},{3,1},{5,3},{7,5},{8,14},{10,8},{12,... | collective-permute-start | bytes 786440 | tf_op jit(solution)/shard_map/ppermute | solution.py:160
  351.4 18.4 %collective-permute-start.23 = (bf16[2,32,4480]{2,1,0:T(8,128)(2,1)S(1)}, bf16[2,32,4480]{2,1,0:T(8,128)(2,1)S(1)}, u32[]{:S(2)}, u32[]{:S(2)}) collective-permute-start(bf16[2,32,4480]{2,1,0:T(8,128)(2,1)S(1)} %get-tuple-element.115), channel_id=1, source_target_pairs={{0,6},{2,0},{4,2},{6,4},{1,7},{3,1},{5,3},{7,5},{8,14},{10,8},{12,... | collective-permute-start | bytes 1720328 | tf_op jit(solution)/shard_map/ppermute | solution.py:160
  351.6 8.5 %collective-permute-start.28 = (bf16[2,64,1024]{2,1,0:T(8,128)(2,1)S(1)}, bf16[2,64,1024]{2,1,0:T(8,128)(2,1)S(1)}, u32[]{:S(2)}, u32[]{:S(2)}) collective-permute-start(bf16[2,64,1024]{2,1,0:T(8,128)(2,1)S(1)} %get-tuple-element.124), channel_id=1, source_target_pairs={{0,2},{2,4},{4,6},{6,0},{1,3},{3,5},{5,7},{7,1},{8,10},{10,12},{12... | collective-permute-start | bytes 786440 | tf_op jit(solution)/shard_map/ppermute | solution.py:159
  358.2 21.4 %collective-permute-start.32 = (bf16[2,64,1024]{2,1,0:T(8,128)(2,1)}, bf16[2,64,1024]{2,1,0:T(8,128)(2,1)S(1)}, u32[]{:S(2)}, u32[]{:S(2)}) collective-permute-start(bf16[2,64,1024]{2,1,0:T(8,128)(2,1)} %fusion.67), channel_id=1, source_target_pairs={{0,6},{2,0},{4,2},{6,4},{1,7},{3,1},{5,3},{7,5},{8,14},{10,8},{12,... | collective-permute-start | bytes 786440 | tf_op jit(solution)/shard_map/ppermute | solution.py:162
  360.8 18.8 %collective-permute-start.29 = (bf16[2,64,1024]{2,1,0:T(8,128)(2,1)}, bf16[2,64,1024]{2,1,0:T(8,128)(2,1)}, u32[]{:S(2)}, u32[]{:S(2)}) collective-permute-start(bf16[2,64,1024]{2,1,0:T(8,128)(2,1)} %fusion.69), channel_id=1, source_target_pairs={{0,2},{2,4},{4,6},{6,0},{1,3},{3,5},{5,7},{7,1},{8,10},{10,12},{12... | collective-permute-start | bytes 786440 | tf_op jit(solution)/shard_map/ppermute | solution.py:161
  360.8 17.9 %collective-permute-start.20 = (bf16[2,32,4480]{2,1,0:T(8,128)(2,1)S(1)}, bf16[2,32,4480]{2,1,0:T(8,128)(2,1)S(1)}, u32[]{:S(2)}, u32[]{:S(2)}) collective-permute-start(bf16[2,32,4480]{2,1,0:T(8,128)(2,1)S(1)} %get-tuple-element.116), channel_id=1, source_target_pairs={{0,2},{2,4},{4,6},{6,0},{1,3},{3,5},{5,7},{7,1},{8,10},{10,12},{12... | collective-permute-start | bytes 1720328 | tf_op jit(solution)/shard_map/ppermute | solution.py:159
  370.7 17.0 %collective-permute-start.24 = (bf16[2,32,4480]{2,1,0:T(8,128)(2,1)}, bf16[2,32,4480]{2,1,0:T(8,128)(2,1)}, u32[]{:S(2)}, u32[]{:S(2)}) collective-permute-start(bf16[2,32,4480]{2,1,0:T(8,128)(2,1)} %fusion.43), channel_id=1, source_target_pairs={{0,6},{2,0},{4,2},{6,4},{1,7},{3,1},{5,3},{7,5},{8,14},{10,8},{12,... | collective-permute-start | bytes 1720328 | tf_op jit(solution)/shard_map/ppermute | solution.py:162
  379.7 11.5 %collective-permute-start.21 = (bf16[2,32,4480]{2,1,0:T(8,128)(2,1)}, bf16[2,32,4480]{2,1,0:T(8,128)(2,1)}, u32[]{:S(2)}, u32[]{:S(2)}) collective-permute-start(bf16[2,32,4480]{2,1,0:T(8,128)(2,1)} %fusion.45), channel_id=1, source_target_pairs={{0,2},{2,4},{4,6},{6,0},{1,3},{3,5},{5,7},{7,1},{8,10},{10,12},{12... | collective-permute-start | bytes 1720328 | tf_op jit(solution)/shard_map/ppermute | solution.py:161
  381.3 23.3 %collective-permute-start.33 = (bf16[128,1024]{1,0:T(8,128)(2,1)S(1)}, bf16[128,1024]{1,0:T(8,128)(2,1)S(1)}, u32[]{:S(2)}, u32[]{:S(2)}) collective-permute-start(bf16[128,1024]{1,0:T(8,128)(2,1)S(1)} %fusion.74), channel_id=1, source_target_pairs={{0,1},{1,0},{2,3},{3,2},{4,5},{5,4},{6,7},{7,6},{8,9},{9,8},{10,11... | collective-permute-start | bytes 786440 | tf_op jit(solution)/shard_map/ppermute | solution.py:169
  392.7 12.8 %collective-permute-start.25 = (bf16[64,4480]{1,0:T(8,128)(2,1)S(1)}, bf16[64,4480]{1,0:T(8,128)(2,1)S(1)}, u32[]{:S(2)}, u32[]{:S(2)}) collective-permute-start(bf16[64,4480]{1,0:T(8,128)(2,1)S(1)} %fusion.61), channel_id=1, source_target_pairs={{0,1},{1,0},{2,3},{3,2},{4,5},{5,4},{6,7},{7,6},{8,9},{9,8},{10,11... | collective-permute-start | bytes 1720328 | tf_op jit(solution)/shard_map/ppermute | solution.py:169
  411.0 3.1 collective-permute-start.11
  414.1 3.2 collective-permute-start.12
  417.2 4.7 collective-permute-start.13
  421.9 9.9 %collective-permute-start.14 = (f32[8,1836]{1,0:T(8,128)S(1)}, f32[8,1836]{1,0:T(8,128)S(1)}, u32[]{:S(2)}, u32[]{:S(2)}) collective-permute-start(f32[8,1836]{1,0:T(8,128)S(1)} %add.274), channel_id=1, source_target_pairs={{0,8},{8,0},{1,9},{9,1},{2,10},{10,2},{3,11},{11,3},{4,12},{12,4},... | collective-permute-start | bytes 176264 | tf_op jit(solution)/shard_map/ppermute | solution.py:248
  431.8 13.5 %copy-start.19 = (f32[256,1024]{1,0:T(8,128)S(1)}, f32[256,1024]{1,0:T(8,128)}, u32[]{:S(2)}) copy-start(f32[256,1024]{1,0:T(8,128)} %param.13) | copy-start | bytes 3145732
  431.8 5.9 %collective-permute-start.15 = (f32[8,1836]{1,0:T(8,128)S(1)}, f32[8,1836]{1,0:T(8,128)S(1)}, u32[]{:S(2)}, u32[]{:S(2)}) collective-permute-start(f32[8,1836]{1,0:T(8,128)S(1)} %add.275), channel_id=1, source_target_pairs={{0,16},{16,0},{32,48},{48,32},{64,80},{80,64},{96,112},{112,96},{1... | collective-permute-start | bytes 176264 | tf_op jit(solution)/shard_map/ppermute | solution.py:248
  437.7 6.5 %collective-permute-start.16 = (f32[8,1836]{1,0:T(8,128)S(1)}, f32[8,1836]{1,0:T(8,128)S(1)}, u32[]{:S(2)}, u32[]{:S(2)}) collective-permute-start(f32[8,1836]{1,0:T(8,128)S(1)} %add.276), channel_id=1, source_target_pairs={{0,32},{16,48},{32,0},{48,16},{64,96},{80,112},{96,64},{112,80},{1... | collective-permute-start | bytes 176264 | tf_op jit(solution)/shard_map/ppermute | solution.py:248
  444.2 58.6 %collective-permute-start.17 = (f32[8,1836]{1,0:T(8,128)S(1)}, f32[8,1836]{1,0:T(8,128)S(1)}, u32[]{:S(2)}, u32[]{:S(2)}) collective-permute-start(f32[8,1836]{1,0:T(8,128)S(1)} %add.277), channel_id=1, source_target_pairs={{0,64},{16,80},{32,96},{48,112},{64,0},{80,16},{96,32},{112,48},{1... | collective-permute-start | bytes 176264 | tf_op jit(solution)/shard_map/ppermute | solution.py:248
  497.5 11.2 %collective-permute-start.26 = (f32[64,4480]{1,0:T(8,128)}, f32[64,4480]{1,0:T(8,128)S(1)}, u32[]{:S(2)}, u32[]{:S(2)}) collective-permute-start(f32[64,4480]{1,0:T(8,128)} %get-tuple-element.76), channel_id=1, source_target_pairs={{0,8},{8,0},{1,9},{9,1},{2,10},{10,2},{3,11},{11,3},{4,12},{12,4},... | collective-permute-start | bytes 3440648 | tf_op jit(solution)/shard_map/ppermute | solution.py:198
  504.4 2.1 collective-permute-start.34
  (81 other events, 352.9 us)
Sparse Core Ops, SparseCore 0:
  143.2 55.9 all-gather.2
  406.8 90.5 all-reduce.21

commit v8 on v7

--- a/solution.py
+++ b/solution.py
@@ -169,6 +169,46 @@
     return keep + lax.ppermute(low(give), "shard_1", [(0, 1), (1, 0)]).astype(jnp.float32)
 
 
+def allreduce_rep(values):
+    ring = 4
+    size = lax.axis_size("rep_hi")
+    index = lax.axis_index("rep_hi")
+    x = index % ring
+    up = [(i, (i // ring) * ring + (i % ring + 1) % ring) for i in range(size)]
+    down = [(i, (i // ring) * ring + (i % ring - 1) % ring) for i in range(size)]
+    rows = values.shape[0]
+    chunks = values.reshape(ring, rows // ring, values.shape[1])
+    doubled = jnp.concatenate([chunks, chunks], axis=0)
+    rel = lax.dynamic_slice_in_dim(doubled, x, ring, axis=0)
+    half = rows // ring // 2
+    a = lax.ppermute(rel[2][:half], "rep_hi", up)
+    b = lax.ppermute(rel[2][half:], "rep_hi", down)
+    up_msg = jnp.concatenate([a + rel[1][:half], rel[1][half:]], axis=0)
+    down_msg = jnp.concatenate([rel[3][:half], b + rel[3][half:]], axis=0)
+    mine = rel[0] + lax.ppermute(up_msg, "rep_hi", up) + lax.ppermute(down_msg, "rep_hi", down)
+    step = ring
+    while step < size:
+        mine = mine + lax.ppermute(mine, "rep_hi", [(i, i ^ step) for i in range(size)])
+        step *= 2
+    from_prev = lax.ppermute(mine, "rep_hi", up)
+    from_next = lax.ppermute(mine, "rep_hi", down)
+    far_a = lax.ppermute(from_prev[:half], "rep_hi", up)
+    far_b = lax.ppermute(from_next[half:], "rep_hi", down)
+    opposite = jnp.concatenate([far_a, far_b], axis=0)
+    ordered = jnp.stack([mine, from_next, opposite, from_prev])
+    doubled = jnp.concatenate([ordered, ordered], axis=0)
+    placed = lax.dynamic_slice_in_dim(doubled, (ring - x) % ring, ring, axis=0)
+    return placed.reshape(values.shape)
+
+
+def core_join(owned):
+    core = lax.axis_index("core")
+    other = core_swap(owned)
+    first = jnp.where(core == 0, owned, other)
+    second = jnp.where(core == 0, other, owned)
+    return jnp.concatenate([first, second], axis=0)
+
+
 def core_swap(values):
     return lax.ppermute(values, "core", [(0, 1), (1, 0)])
 
@@ -286,7 +326,6 @@
     normed_f, norm_back = jax.vjp(norm_input, layer_in, norm_full)
     normed = normed_f.astype(jnp.bfloat16)
     in_whole = gather_rows(in_weight, by_permutes=True)
-    in_whole, out_weight = lax.optimization_barrier((in_whole, out_weight))
     out_whole = gather_rows(out_weight)
     projected = jnp.dot(normed, in_whole, preferred_element_type=jnp.float32)
 
@@ -310,7 +349,7 @@
     out_halves = reduce_core(row_product(gated, cot_low))
     gated_grad = back_product(cot_low, out_whole)
     out_halves, gated_grad = lax.optimization_barrier((out_halves, gated_grad))
-    out_owned = reduce_rest(out_halves)
+    out_group = reduce_group(out_halves)
     proj_grad, g_convw, g_convb, g_stepb, g_decay, g_skip, g_gategain = mixer_back(gated_grad)
     proj_low = proj_grad.astype(jnp.bfloat16)
     normed_grad = back_product(proj_low, in_whole)
@@ -321,7 +360,13 @@
     cols = proj_low.shape[1]
     wide = -(-cols // 128) * 128
     proj_wide = jnp.pad(proj_low, ((0, 0), (0, wide - cols)))
-    in_owned = reduce_rows(row_product(normed, proj_wide))[:, :cols]
+    in_group = reduce_group(reduce_core(row_product(normed, proj_wide)))
+    in_shape, out_shape = in_group.shape, out_group.shape
+    joined = jnp.concatenate([in_group.reshape(-1, 128), out_group.reshape(-1, 128)], axis=0)
+    joined = allreduce_rep(joined)
+    split_at = in_group.size // 128
+    in_owned = core_join(joined[:split_at].reshape(in_shape))[:, :cols]
+    out_owned = core_join(joined[split_at:].reshape(out_shape))
     small_sum = exchange_sum(small_blocks, ("shard_1", "shard_0", "core", "rep_hi"))
     mine = lax.dynamic_index_in_dim(small_sum, lax.axis_index(SHARD), axis=0, keepdims=False)
     small_final = []

time: 524 us -> 514 us (0.981)
  waiting for transfers between devices: 202 us -> 175 us
  starting transfers between devices: 50.7 us -> 64.2 us
    psum x1 -> x0, waiting for transfers between devices: 50.9 us -> none  [reduce_rest(): owned = lax.psum(owned, 'rep_hi')]
    all_gather x1, waiting for transfers between devices: 29.1 us -> 0.01 us  [gather_rows(): part = lax.all_gather(mine, SHARD, axis=0, tiled=False)]
    ppermute x2, waiting for transfers between devices: 0.01 us -> 15.7 us  [reduce_group(): lax.ppermute(low(give), 'shard_1', [(0, 1), (1, 0)]).astype(jnp.float32)]
    ppermute x2, waiting for transfers between devices: 3.42 us -> 18.4 us  [reduce_group(): acc_up = lax.ppermute(low(acc_up + rel[1][:, :half]), 'shard_0', up)]
    ppermute x6, waiting for transfers between devices: 9.36 us -> 23.8 us  [core_swap(): return lax.ppermute(values, 'core', [(0, 1), (1, 0)])]
    ppermute x0 -> x9, starting transfers between devices: none -> 13 us  [the longest x1 2.82 us: allreduce_rep(): lax.ppermute(mine, 'rep_hi', [(i, i ^ step) for i in range(size)])]
    ppermute x0 -> x9, waiting for transfers between devices: none -> 8.31 us  [the longest x1 5.23 us: allreduce_rep(): lax.ppermute(mine, 'rep_hi', [(i, i ^ step) for i in range(size)])]
    reshape x0 -> x4, local copies, waits for them, and re-layouts: none -> 6.9 us  [the longest x1 2.52 us: on_device(): in_owned = core_join(joined[:split_at].reshape(in_shape))[:, :cols]]
  transfers between devices with their start and end apart: 37 -> 45, of which waited for: 22 -> 22; matrix products, arithmetic and copies ran while one was open for 16% -> 24% of each run, Pallas kernels for 0% -> 0%
where the time goes in v8:
time: 514 us; the launch traced here: 508 us
  waiting for transfers between devices  175 us (34%)
  other arithmetic  122 us (24%)
  matrix products  66.1 us (13%)
  local copies, waits for them, and re-layouts  64.8 us (13%)
  starting transfers between devices  64.2 us (12%)
  between operations  16 us (3%)
    dot_general x3, matrix products, mixer(): y_intra = jnp.einsum('chij,cjhp->cihp', mixing, scaled_in, precision=HIGH)  30.7 us
    ppermute x10, waiting for transfers between devices, exchange_sum(): values = values + lax.ppermute(values, axis, pairs)  24.4 us
    ppermute x6, waiting for transfers between devices, core_swap(): return lax.ppermute(values, 'core', [(0, 1), (1, 0)])  23.8 us
    ppermute x1, waiting for transfers between devices, gather_group(): from_prev = lax.ppermute(pair, 'shard_0', up)  22.7 us
    another operation x4, other arithmetic, gather_rows(): return jnp.stack([first, second], axis=1).reshape(-1, weight.shape[1])  19.4 us
    add x2, other arithmetic, reduce_core(): return keep + core_swap(give)  18.7 us
    ppermute x2, waiting for transfers between devices, reduce_group(): acc_up = lax.ppermute(low(acc_up + rel[1][:, :half]), 'shard_0', up)  18.4 us
    unnamed x203, local copies, waits for them, and re-layouts  18 us
  transfers between devices with their start and end apart: 45, of which 22 were waited for; matrix products, arithmetic and copies ran while one was open for 24% of the time, Pallas kernels for 0%

profile of v8, /device:TPU:1, one launch (start us, length us, event | category | flops | bytes accessed | tf_op | source)
XLA Modules:
  0.0 508.0 jit_solution(6504520436463504035)
XLA Ops:
  12.0 12.3 %collective-permute-done.3 = bf16[64,4384]{1,0:T(8,128)(2,1)S(1)} collective-permute-done((bf16[64,4384]{1,0:T(8,128)(2,1)S(1)}, bf16[64,4384]{1,0:T(8,128)(2,1)S(1)}, u32[]{:S(2)}, u32[]{:S(2)}) %collective-permute-start.3) | collective-permute-done | bytes 561184 | tf_op jit(solution)/shard_map/ppermute | solution.py:220
  31.9 22.7 %collective-permute-done.5 = bf16[2,64,4384]{2,1,0:T(8,128)(2,1)S(1)} collective-permute-done((bf16[2,64,4384]{2,1,0:T(8,128)(2,1)}, bf16[2,64,4384]{2,1,0:T(8,128)(2,1)S(1)}, u32[]{:S(2)}, u32[]{:S(2)}) %collective-permute-start.5) | collective-permute-done | bytes 1122336 | tf_op jit(solution)/shard_map/ppermute | solution.py:224
  57.7 10.5 %collective-permute-done.6 = bf16[2,32,4384]{2,1,0:T(8,128)(2,1)S(1)} collective-permute-done((bf16[2,32,4384]{2,1,0:T(8,128)(2,1)S(1)}, bf16[2,32,4384]{2,1,0:T(8,128)(2,1)S(1)}, u32[]{:S(2)}, u32[]{:S(2)}) %collective-permute-start.6) | collective-permute-done | bytes 561184 | tf_op jit(solution)/shard_map/ppermute | solution.py:227
  71.9 3.1 collective-permute-start.8
  79.5 2.9 collective-permute-done.1
  82.4 2.7 collective-permute-start.2
  90.1 2.8 slice_reduce_fusion.3
  92.9 8.1 %select_bitcast_fusion.2 = (bf16[8,1,64,4384]{3,2,0,1:T(8,128)(2,1)}, bf16[8,1,64,4384]{3,2,0,1:T(8,128)(2,1)}) fusion(bf16[8,64,4384]{2,1,0:T(8,128)(2,1)} %collective-permute-done.8, pred[]{:T(512)S(6)} %eq.81, bf16[4,2,64,4384]{3,2,1,0:T(8,128)(2,1)} %constant_dynamic-slice_fusion.2), kind=kLoop, calls=%fused_computation.19 | loop fusion | flops 4489216 | bytes 17956864 | tf_op jit(solution)/shard_map/stack | solution.py:253
  101.1 8.2 %pad_maximum_fusion = bf16[8,2,64,4384]{3,2,0,1:T(8,128)(2,1)} fusion(bf16[8,1,64,4384]{3,2,0,1:T(8,128)(2,1)} %get-tuple-element.85, bf16[8,1,64,4384]{3,2,0,1:T(8,128)(2,1)} %get-tuple-element.84), kind=kLoop, calls=%fused_computation.3 | loop fusion | flops 4489216 | bytes 17956864 | tf_op jit(solution)/shard_map/stack | solution.py:253
  109.3 8.1 %copy.83 = bf16[8,2,64,4384]{3,2,1,0:T(8,128)(2,1)} copy(bf16[8,2,64,4384]{3,2,0,1:T(8,128)(2,1)} %pad_maximum_fusion) | data formatting | bytes 17956864 | tf_op jit(solution)/shard_map/stack | solution.py:253
  117.4 7.5 %fusion.111 = f32[256,4384]{0,1:T(8,128)S(1)} fusion(bf16[1024,4384]{1,0:T(8,128)(2,1)} %bitcast.279, f32[256,1024]{1,0:T(8,128)S(1)} %copy-done.15, f32[1024]{0:T(1024)S(1)} %slice_bitcast_fusion.16, f32[256]{0:T(256)S(1)} %fusion.104), kind=kOutput, calls=%fused_computation.272 | convolution fusion | flops 2299265024 | bytes 14521344 | tf_op jit(solution)/shard_map/dot_general | solution.py:330
  133.7 5.3 %fusion.25 = (f32[256,2304]{0,1:T(8,128)S(1)}, f32[256,2304]{0,1:T(8,128)}) fusion(f32[253,2304]{0,1:T(8,128)S(1)} %slice.396, f32[2304]{0:T(1024)S(1)} %copy-done.46, pred[256]{0:T(512)(128)(4,1)S(1)} %copy-done.74, f32[254,2304]{0,1:T(8,128)S(1)} %slice.394, f32[2304]{0:T(1024)S(1)} %copy-done.50, pred[256]{0:T(512)(128)(4,1)S(1)} %copy-done.72, ...), kind=kLoop, calls=%fused_computation.58 | loop fusion | flops 8847360 | bytes 14147328 | tf_op jit(solution)/shard_map/jvp(jit(silu))/mul | solution.py:110
  145.8 10.0 %fusion.30 = f32[256,32,64]{0,2,1:T(8,128)S(1)} fusion(f32[256,32,64]{0,2,1:T(8,128)S(1)} %bitcast.287, f32[256,32,64]{0,2,1:T(8,128)S(1)} %fusion.73, f32[32]{0:T(128)} %mul.426, f32[256,32]{0,1:T(8,128)S(1)} %bitcast_multiply_fusion.4, f32[256,256]{1,0:T(8,128)S(1)} %copy-done.41, f32[32,256]{1,0:T(8,128)S(1)} %bitcast_add_fusion.2, ...), kind=kOutput, calls=%fused_computation.70 | convolution fusion | flops 1619525632 | bytes 6717568 | tf_op jit(solution)/shard_map/jvp(chij,cjhp->cihp)/dot_general | solution.py:132
  155.8 3.1 multiply_reduce_fusion.9
  160.2 3.6 select_bitcast_fusion.3
  164.7 3.0 collective-permute-start.10
  168.5 9.4 %collective-permute-done.9 = bf16[8,128,1024]{2,1,0:T(8,128)(2,1)} collective-permute-done((bf16[8,128,1024]{2,1,0:T(8,128)(2,1)}, bf16[8,128,1024]{2,1,0:T(8,128)(2,1)}, u32[]{:S(2)}, u32[]{:S(2)}) %collective-permute-start.9) | collective-permute-done | bytes 2097184 | tf_op jit(solution)/shard_map/ppermute | solution.py:238
  184.8 5.4 %fusion.12 = f32[8,128,1024]{2,1,0:T(8,128)} fusion(f32[8,128,1024]{2,1,0:T(8,128)} %collective-permute-done.10, f32[8,2,128,1024]{3,2,1,0:T(8,128)S(1)} %bitcast.266, pred[]{:T(512)S(6)} %eq.81), kind=kLoop, calls=%fused_computation.25 | loop fusion | flops 2097152 | bytes 16777216 | tf_op jit(solution)/shard_map/add | solution.py:263
  191.8 4.9 multiply_reduce_fusion.6
  199.1 12.0 %fusion.9 = (f32[32,256]{1,0:T(8,128)S(1)}, f32[32,256]{1,0:T(8,128)S(1)}, f32[256,256]{1,0:T(8,128)S(1)}) fusion(f32[256,256]{1,0:T(8,128)S(1)} %copy-done.42, f32[32,256]{1,0:T(8,128)S(1)} %copy-done.61, pred[256,256]{1,0:T(8,128)(4,1)S(1)} %copy-done.53, f32[32,64,256]{2,1,0:T(8,128)S(1)} %bitcast.273, f32[256,32,64]{0,2,1:T(8,128)S(1)} %bitcast.288, ...), kind=kOutput, calls=%fused_computation.17 | convolution fusion | flops 1629929472 | bytes 4915200 | tf_op jit(solution)/shard_map/transpose(jvp(chij,cjhp->cihp))/dot_general | solution.py:132
  211.1 8.8 %fusion.31 = (f32[256,32]{0,1:T(8,128)}, f32[1,256,32,64]{1,3,2,0:T(8,128)}) fusion(f32[1,256,32,64]{1,3,2,0:T(8,128)S(1)} %bitcast.289, f32[256,32]{0,1:T(8,128)S(1)} %get-tuple-element.77, f32[32,64,256]{2,1,0:T(8,128)S(1)} %bitcast.274, f32[256,256]{1,0:T(8,128)S(1)} %copy-done.42, f32[32,256]{1,0:T(8,128)S(1)} %copy-done.61, ...), kind=kOutput, calls=%fused_computation.74 | convolution fusion | flops 1618468864 | bytes 6717440 | tf_op jit(solution)/shard_map/transpose(jvp(chij,cjhp->cihp))/dot_general | solution.py:132
  227.2 2.8 multiply_reduce_fusion.4
  230.1 2.9 multiply_reduce_fusion.3
  239.3 7.8 %fusion.26 = f32[1024,4480]{1,0:T(8,128)} fusion(bf16[256,4384]{0,1:T(8,128)(2,1)S(1)} %add_convert_fusion, f32[256,1024]{1,0:T(8,128)S(1)} %copy-done.15, f32[1024]{0:T(1024)S(1)} %slice_bitcast_fusion.16, f32[256]{0:T(256)S(1)} %copy-done.64), kind=kOutput, calls=%fused_computation.65 | convolution fusion | flops 2349596672 | bytes 21648384 | tf_op jit(solution)/shard_map/dot_general | solution.py:76
  247.2 10.7 %select_bitcast_fusion = f32[8,64,4480]{2,1,0:T(8,128)} fusion(f32[8,2,64,4480]{3,2,1,0:T(8,128)} %bitcast.261, pred[]{:T(512)S(6)} %eq.81), kind=kLoop, calls=%fused_computation.7 | loop fusion | flops 2293760 | bytes 27525120 | tf_op jit(solution)/shard_map/jit(_where)/select_n | solution.py:262
  258.2 14.3 %collective-permute-done.18 = f32[8,64,4480]{2,1,0:T(8,128)} collective-permute-done((f32[8,64,4480]{2,1,0:T(8,128)}, f32[8,64,4480]{2,1,0:T(8,128)}, u32[]{:S(2)}, u32[]{:S(2)}) %collective-permute-start.18) | collective-permute-done | bytes 9175072 | tf_op jit(solution)/shard_map/ppermute | solution.py:238
  272.4 13.3 %fusion.2 = f32[8,64,4480]{2,1,0:T(8,128)} fusion(f32[8,64,4480]{2,1,0:T(8,128)} %collective-permute-done.18, f32[8,2,64,4480]{3,2,1,0:T(8,128)} %bitcast.262, pred[]{:T(512)S(6)} %eq.81), kind=kLoop, calls=%fused_computation.6 | loop fusion | flops 4587520 | bytes 36700160 | tf_op jit(solution)/shard_map/add | solution.py:263
  285.8 8.2 %fusion = f32[4,2,64,4480]{3,2,1,0:T(8,128)} fusion(s32[]{:T(128)S(6)} %select_n.238, f32[4,2,64,4480]{3,2,1,0:T(8,128)} %bitcast.271), kind=kLoop, calls=%fused_computation.2 | loop fusion | flops 2293760 | bytes 18350084 | tf_op jit(solution)/shard_map/concatenate | solution.py:151
  294.0 5.8 %slice_bitcast_fusion.3 = (f32[2,64,4480]{2,1,0:T(8,128)S(1)}, f32[2,64,4480]{2,1,0:T(8,128)S(1)}, f32[2,64,4480]{2,1,0:T(8,128)S(1)}, f32[2,64,4480]{2,1,0:T(8,128)}) fusion(f32[4,2,64,4480]{3,2,1,0:T(8,128)} %fusion), kind=kLoop, calls=%fused_computation.64 | loop fusion | bytes 18350080 | tf_op jit(solution)/shard_map/squeeze | solution.py:157
  300.0 2.9 collective-permute-start.22
  308.2 6.7 %collective-permute-done.22 = bf16[2,32,4480]{2,1,0:T(8,128)(2,1)S(1)} collective-permute-done((bf16[2,32,4480]{2,1,0:T(8,128)(2,1)S(1)}, bf16[2,32,4480]{2,1,0:T(8,128)(2,1)S(1)}, u32[]{:S(2)}, u32[]{:S(2)}) %collective-permute-start.22) | collective-permute-done | bytes 573472 | tf_op jit(solution)/shard_map/ppermute | solution.py:158
  314.8 3.2 collective-permute-done.19
  320.5 3.2 collective-permute-done.26
  325.4 13.0 %collective-permute-done.30 = bf16[2,64,1024]{2,1,0:T(8,128)(2,1)S(1)} collective-permute-done((bf16[2,64,1024]{2,1,0:T(8,128)(2,1)S(1)}, bf16[2,64,1024]{2,1,0:T(8,128)(2,1)S(1)}, u32[]{:S(2)}, u32[]{:S(2)}) %collective-permute-start.30) | collective-permute-done | bytes 262176 | tf_op jit(solution)/shard_map/ppermute | solution.py:160
  339.1 3.4 collective-permute-start.31
  346.1 10.6 %collective-permute-done.20 = bf16[2,32,4480]{2,1,0:T(8,128)(2,1)S(1)} collective-permute-done((bf16[2,32,4480]{2,1,0:T(8,128)(2,1)S(1)}, bf16[2,32,4480]{2,1,0:T(8,128)(2,1)S(1)}, u32[]{:S(2)}, u32[]{:S(2)}) %collective-permute-start.20) | collective-permute-done | bytes 573472 | tf_op jit(solution)/shard_map/ppermute | solution.py:159
  358.4 18.4 %collective-permute-done.28 = bf16[2,64,1024]{2,1,0:T(8,128)(2,1)} collective-permute-done((bf16[2,64,1024]{2,1,0:T(8,128)(2,1)}, bf16[2,64,1024]{2,1,0:T(8,128)(2,1)}, u32[]{:S(2)}, u32[]{:S(2)}) %collective-permute-start.28) | collective-permute-done | bytes 262176 | tf_op jit(solution)/shard_map/ppermute | solution.py:161
  384.2 15.7 %collective-permute-done.32 = bf16[128,1024]{1,0:T(8,128)(2,1)} collective-permute-done((bf16[128,1024]{1,0:T(8,128)(2,1)S(1)}, bf16[128,1024]{1,0:T(8,128)(2,1)}, u32[]{:S(2)}, u32[]{:S(2)}) %collective-permute-start.32) | collective-permute-done | bytes 262176 | tf_op jit(solution)/shard_map/ppermute | solution.py:169
  413.4 7.3 %multiply_reduce_fusion.10 = (f32[1024]{0:T(1024)S(1)}, f32[256]{0:T(256)S(1)}, f32[256,1024]{1,0:T(8,128)}) fusion(f32[256,1024]{1,0:T(8,128)S(1)} %copy-done.15, f32[256]{0:T(256)S(1)} %copy-done.64, f32[1024]{0:T(1024)S(1)} %slice_bitcast_fusion.16, bf16[256,4384]{0,1:T(8,128)(2,1)S(1)} %copy-done.25, bf16[1024,4384]{1,0:T(8,128)(2,1)} %bitcast.280), kind=kOutput, calls=%fused_computation.139 | convolution fusion | flops 2300050176 | bytes 13330432 | tf_op jit(solution)/shard_map/dot_general | solution.py:82
  432.8 3.5 collective-permute-done.12
  436.4 5.2 %collective-permute-done.13 = f32[8,1836]{1,0:T(8,128)S(1)} collective-permute-done((f32[8,1836]{1,0:T(8,128)S(1)}, f32[8,1836]{1,0:T(8,128)S(1)}, u32[]{:S(2)}, u32[]{:S(2)}) %collective-permute-start.13) | collective-permute-done | bytes 58784 | tf_op jit(solution)/shard_map/ppermute | solution.py:288
  441.6 7.0 %collective-permute-start.14 = (f32[8,1836]{1,0:T(8,128)S(1)}, f32[8,1836]{1,0:T(8,128)S(1)}, u32[]{:S(2)}, u32[]{:S(2)}) collective-permute-start(f32[8,1836]{1,0:T(8,128)S(1)} %add.297), channel_id=1, source_target_pairs={{0,8},{8,0},{1,9},{9,1},{2,10},{10,2},{3,11},{11,3},{4,12},{12,4},... | collective-permute-start | bytes 176264 | tf_op jit(solution)/shard_map/ppermute | solution.py:288
  449.9 2.8 collective-permute-start.37
  452.7 4.7 convolution_add_fusion
  457.5 5.2 %collective-permute-done.37 = f32[816,128]{1,0:T(8,128)S(1)} collective-permute-done((f32[816,128]{1,0:T(8,128)S(1)}, f32[816,128]{1,0:T(8,128)S(1)}, u32[]{:S(2)}, u32[]{:S(2)}) %collective-permute-start.37) | collective-permute-done | bytes 417824 | tf_op jit(solution)/shard_map/ppermute | solution.py:191
  468.0 8.5 %collective-permute-done.16 = f32[8,1836]{1,0:T(8,128)S(1)} collective-permute-done((f32[8,1836]{1,0:T(8,128)S(1)}, f32[8,1836]{1,0:T(8,128)S(1)}, u32[]{:S(2)}, u32[]{:S(2)}) %collective-permute-start.16) | collective-permute-done | bytes 58784 | tf_op jit(solution)/shard_map/ppermute | solution.py:288
  482.1 3.1 collective-permute-done.40
  489.1 3.5 collective-permute-start.42
  (428 shorter events, 143.8 us)
Async XLA Ops:
  7.2 160.6 %all-gather.3.cloned.1.call-start = ((), (), s32[]{:S(2)}) async-start(), calls=%async_computation | async-start | bytes 2359296 | tf_op jit(solution)/shard_map/all_gather | solution.py:249
  9.8 14.5 %collective-permute-start.3 = (bf16[64,4384]{1,0:T(8,128)(2,1)S(1)}, bf16[64,4384]{1,0:T(8,128)(2,1)S(1)}, u32[]{:S(2)}, u32[]{:S(2)}) collective-permute-start(bf16[64,4384]{1,0:T(8,128)(2,1)S(1)} %copy.107), channel_id=1, source_target_pairs={{0,1},{1,0},{2,3},{3,2},{4,5},{5,4},{6,7},{7,6},{8,9},{9,8},{10,11... | collective-permute-start | bytes 1683464 | tf_op jit(solution)/shard_map/ppermute | solution.py:220
  26.4 28.3 %collective-permute-start.5 = (bf16[2,64,4384]{2,1,0:T(8,128)(2,1)}, bf16[2,64,4384]{2,1,0:T(8,128)(2,1)S(1)}, u32[]{:S(2)}, u32[]{:S(2)}) collective-permute-start(bf16[2,64,4384]{2,1,0:T(8,128)(2,1)} %maximum_select_fusion.1), channel_id=1, source_target_pairs={{0,2},{2,4},{4,6},{6,0},{1,3},{3,5},{5,7},{7,1},{8,10},{10,12},{12... | collective-permute-start | bytes 3366920 | tf_op jit(solution)/shard_map/ppermute | solution.py:224
  28.3 26.5 %collective-permute-start.4 = (bf16[2,64,4384]{2,1,0:T(8,128)(2,1)}, bf16[2,64,4384]{2,1,0:T(8,128)(2,1)S(1)}, u32[]{:S(2)}, u32[]{:S(2)}) collective-permute-start(bf16[2,64,4384]{2,1,0:T(8,128)(2,1)} %maximum_select_fusion.1), channel_id=1, source_target_pairs={{0,6},{2,0},{4,2},{6,4},{1,7},{3,1},{5,3},{7,5},{8,14},{10,8},{12,... | collective-permute-start | bytes 3366920 | tf_op jit(solution)/shard_map/ppermute | solution.py:225
  54.7 13.6 %collective-permute-start.6 = (bf16[2,32,4384]{2,1,0:T(8,128)(2,1)S(1)}, bf16[2,32,4384]{2,1,0:T(8,128)(2,1)S(1)}, u32[]{:S(2)}, u32[]{:S(2)}) collective-permute-start(bf16[2,32,4384]{2,1,0:T(8,128)(2,1)S(1)} %slice.388), channel_id=1, source_target_pairs={{0,2},{2,4},{4,6},{6,0},{1,3},{3,5},{5,7},{7,1},{8,10},{10,12},{12... | collective-permute-start | bytes 1683464 | tf_op jit(solution)/shard_map/ppermute | solution.py:227
  54.8 13.4 %collective-permute-start.7 = (bf16[2,32,4384]{2,1,0:T(8,128)(2,1)S(1)}, bf16[2,32,4384]{2,1,0:T(8,128)(2,1)S(1)}, u32[]{:S(2)}, u32[]{:S(2)}) collective-permute-start(bf16[2,32,4384]{2,1,0:T(8,128)(2,1)S(1)} %slice.389), channel_id=1, source_target_pairs={{0,6},{2,0},{4,2},{6,4},{1,7},{3,1},{5,3},{7,5},{8,14},{10,8},{12,... | collective-permute-start | bytes 1683464 | tf_op jit(solution)/shard_map/ppermute | solution.py:228
  71.9 21.1 %collective-permute-start.8 = (bf16[8,64,4384]{2,1,0:T(8,128)(2,1)}, bf16[8,64,4384]{2,1,0:T(8,128)(2,1)}, u32[]{:S(2)}, u32[]{:S(2)}) collective-permute-start(bf16[8,64,4384]{2,1,0:T(8,128)(2,1)} %bitcast.8), channel_id=1, source_target_pairs={{0,8},{8,0},{1,9},{9,1},{2,10},{10,2},{3,11},{11,3},{4,12},{12,4},... | collective-permute-start | bytes 13467656 | tf_op jit(solution)/shard_map/ppermute | solution.py:238
  75.5 3.7 collective-permute-start
  79.2 64.7 %copy-start.65 = (f32[256]{0:T(256)}, f32[256]{0:T(256)S(1)}, u32[]{:S(2)}) copy-start(f32[256]{0:T(256)S(1)} %get-tuple-element.123) | copy-start | bytes 3076
  79.3 3.1 collective-permute-start.1
  82.4 4.8 collective-permute-start.2
  88.2 36.7 %copy-start.76 = (f32[32]{0:T(128)}, f32[32]{0:T(128)S(1)}, u32[]{:S(2)}) copy-start(f32[32]{0:T(128)S(1)} %add.283) | copy-start | bytes 388
  88.9 36.0 %copy-start.78 = (f32[32]{0:T(128)}, f32[32]{0:T(128)S(1)}, u32[]{:S(2)}) copy-start(f32[32]{0:T(128)S(1)} %neg.39) | copy-start | bytes 388
  164.7 18.4 %collective-permute-start.10 = (f32[8,128,1024]{2,1,0:T(8,128)}, f32[8,128,1024]{2,1,0:T(8,128)}, u32[]{:S(2)}, u32[]{:S(2)}) collective-permute-start(f32[8,128,1024]{2,1,0:T(8,128)} %select_bitcast_fusion.3), channel_id=1, source_target_pairs={{0,8},{8,0},{1,9},{9,1},{2,10},{10,2},{3,11},{11,3},{4,12},{12,4},... | collective-permute-start | bytes 12582920 | tf_op jit(solution)/shard_map/ppermute | solution.py:238
  167.8 10.1 %collective-permute-start.9 = (bf16[8,128,1024]{2,1,0:T(8,128)(2,1)}, bf16[8,128,1024]{2,1,0:T(8,128)(2,1)}, u32[]{:S(2)}, u32[]{:S(2)}) collective-permute-start(bf16[8,128,1024]{2,1,0:T(8,128)(2,1)} %bitcast.290), channel_id=1, source_target_pairs={{0,8},{8,0},{1,9},{9,1},{2,10},{10,2},{3,11},{11,3},{4,12},{12,4},... | collective-permute-start | bytes 6291464 | tf_op jit(solution)/shard_map/ppermute | solution.py:238
  257.8 14.6 %collective-permute-start.18 = (f32[8,64,4480]{2,1,0:T(8,128)}, f32[8,64,4480]{2,1,0:T(8,128)}, u32[]{:S(2)}, u32[]{:S(2)}) collective-permute-start(f32[8,64,4480]{2,1,0:T(8,128)} %select_bitcast_fusion), channel_id=1, source_target_pairs={{0,8},{8,0},{1,9},{9,1},{2,10},{10,2},{3,11},{11,3},{4,12},{12,4},... | collective-permute-start | bytes 27525128 | tf_op jit(solution)/shard_map/ppermute | solution.py:238
  300.0 14.9 %collective-permute-start.22 = (bf16[2,32,4480]{2,1,0:T(8,128)(2,1)S(1)}, bf16[2,32,4480]{2,1,0:T(8,128)(2,1)S(1)}, u32[]{:S(2)}, u32[]{:S(2)}) collective-permute-start(bf16[2,32,4480]{2,1,0:T(8,128)(2,1)S(1)} %slice.564), channel_id=1, source_target_pairs={{0,6},{2,0},{4,2},{6,4},{1,7},{3,1},{5,3},{7,5},{8,14},{10,8},{12,... | collective-permute-start | bytes 1720328 | tf_op jit(solution)/shard_map/ppermute | solution.py:158
  302.9 15.2 %collective-permute-start.19 = (bf16[2,32,4480]{2,1,0:T(8,128)(2,1)S(1)}, bf16[2,32,4480]{2,1,0:T(8,128)(2,1)S(1)}, u32[]{:S(2)}, u32[]{:S(2)}) collective-permute-start(bf16[2,32,4480]{2,1,0:T(8,128)(2,1)S(1)} %slice.565), channel_id=1, source_target_pairs={{0,2},{2,4},{4,6},{6,0},{1,3},{3,5},{5,7},{7,1},{8,10},{10,12},{12... | collective-permute-start | bytes 1720328 | tf_op jit(solution)/shard_map/ppermute | solution.py:157
  305.5 15.0 %collective-permute-start.29 = (bf16[2,64,1024]{2,1,0:T(8,128)(2,1)S(1)}, bf16[2,64,1024]{2,1,0:T(8,128)(2,1)S(1)}, u32[]{:S(2)}, u32[]{:S(2)}) collective-permute-start(bf16[2,64,1024]{2,1,0:T(8,128)(2,1)S(1)} %slice.566), channel_id=1, source_target_pairs={{0,6},{2,0},{4,2},{6,4},{1,7},{3,1},{5,3},{7,5},{8,14},{10,8},{12,... | collective-permute-start | bytes 786440 | tf_op jit(solution)/shard_map/ppermute | solution.py:158
  308.2 15.5 %collective-permute-start.26 = (bf16[2,64,1024]{2,1,0:T(8,128)(2,1)S(1)}, bf16[2,64,1024]{2,1,0:T(8,128)(2,1)S(1)}, u32[]{:S(2)}, u32[]{:S(2)}) collective-permute-start(bf16[2,64,1024]{2,1,0:T(8,128)(2,1)S(1)} %slice.567), channel_id=1, source_target_pairs={{0,2},{2,4},{4,6},{6,0},{1,3},{3,5},{5,7},{7,1},{8,10},{10,12},{12... | collective-permute-start | bytes 786440 | tf_op jit(solution)/shard_map/ppermute | solution.py:157
  318.3 24.3 %collective-permute-start.23 = (bf16[2,32,4480]{2,1,0:T(8,128)(2,1)S(1)}, bf16[2,32,4480]{2,1,0:T(8,128)(2,1)S(1)}, u32[]{:S(2)}, u32[]{:S(2)}) collective-permute-start(bf16[2,32,4480]{2,1,0:T(8,128)(2,1)S(1)} %get-tuple-element.100), channel_id=1, source_target_pairs={{0,6},{2,0},{4,2},{6,4},{1,7},{3,1},{5,3},{7,5},{8,14},{10,8},{12,... | collective-permute-start | bytes 1720328 | tf_op jit(solution)/shard_map/ppermute | solution.py:160
  323.9 14.5 %collective-permute-start.30 = (bf16[2,64,1024]{2,1,0:T(8,128)(2,1)S(1)}, bf16[2,64,1024]{2,1,0:T(8,128)(2,1)S(1)}, u32[]{:S(2)}, u32[]{:S(2)}) collective-permute-start(bf16[2,64,1024]{2,1,0:T(8,128)(2,1)S(1)} %get-tuple-element.114), channel_id=1, source_target_pairs={{0,6},{2,0},{4,2},{6,4},{1,7},{3,1},{5,3},{7,5},{8,14},{10,8},{12,... | collective-permute-start | bytes 786440 | tf_op jit(solution)/shard_map/ppermute | solution.py:160
  324.1 33.6 %collective-permute-start.27 = (bf16[2,64,1024]{2,1,0:T(8,128)(2,1)S(1)}, bf16[2,64,1024]{2,1,0:T(8,128)(2,1)S(1)}, u32[]{:S(2)}, u32[]{:S(2)}) collective-permute-start(bf16[2,64,1024]{2,1,0:T(8,128)(2,1)S(1)} %get-tuple-element.115), channel_id=1, source_target_pairs={{0,2},{2,4},{4,6},{6,0},{1,3},{3,5},{5,7},{7,1},{8,10},{10,12},{12... | collective-permute-start | bytes 786440 | tf_op jit(solution)/shard_map/ppermute | solution.py:159
  339.1 19.3 %collective-permute-start.31 = (bf16[2,64,1024]{2,1,0:T(8,128)(2,1)}, bf16[2,64,1024]{2,1,0:T(8,128)(2,1)S(1)}, u32[]{:S(2)}, u32[]{:S(2)}) collective-permute-start(bf16[2,64,1024]{2,1,0:T(8,128)(2,1)} %fusion.68), channel_id=1, source_target_pairs={{0,6},{2,0},{4,2},{6,4},{1,7},{3,1},{5,3},{7,5},{8,14},{10,8},{12,... | collective-permute-start | bytes 786440 | tf_op jit(solution)/shard_map/ppermute | solution.py:162
  342.5 14.2 %collective-permute-start.20 = (bf16[2,32,4480]{2,1,0:T(8,128)(2,1)S(1)}, bf16[2,32,4480]{2,1,0:T(8,128)(2,1)S(1)}, u32[]{:S(2)}, u32[]{:S(2)}) collective-permute-start(bf16[2,32,4480]{2,1,0:T(8,128)(2,1)S(1)} %get-tuple-element.101), channel_id=1, source_target_pairs={{0,2},{2,4},{4,6},{6,0},{1,3},{3,5},{5,7},{7,1},{8,10},{10,12},{12... | collective-permute-start | bytes 1720328 | tf_op jit(solution)/shard_map/ppermute | solution.py:159
  343.5 34.8 %collective-permute-start.24 = (bf16[2,32,4480]{2,1,0:T(8,128)(2,1)}, bf16[2,32,4480]{2,1,0:T(8,128)(2,1)}, u32[]{:S(2)}, u32[]{:S(2)}) collective-permute-start(bf16[2,32,4480]{2,1,0:T(8,128)(2,1)} %fusion.44), channel_id=1, source_target_pairs={{0,6},{2,0},{4,2},{6,4},{1,7},{3,1},{5,3},{7,5},{8,14},{10,8},{12,... | collective-permute-start | bytes 1720328 | tf_op jit(solution)/shard_map/ppermute | solution.py:162
  357.7 20.7 %collective-permute-start.21 = (bf16[2,32,4480]{2,1,0:T(8,128)(2,1)}, bf16[2,32,4480]{2,1,0:T(8,128)(2,1)}, u32[]{:S(2)}, u32[]{:S(2)}) collective-permute-start(bf16[2,32,4480]{2,1,0:T(8,128)(2,1)} %fusion.46), channel_id=1, source_target_pairs={{0,2},{2,4},{4,6},{6,0},{1,3},{3,5},{5,7},{7,1},{8,10},{10,12},{12... | collective-permute-start | bytes 1720328 | tf_op jit(solution)/shard_map/ppermute | solution.py:161
  358.4 18.4 %collective-permute-start.28 = (bf16[2,64,1024]{2,1,0:T(8,128)(2,1)}, bf16[2,64,1024]{2,1,0:T(8,128)(2,1)}, u32[]{:S(2)}, u32[]{:S(2)}) collective-permute-start(bf16[2,64,1024]{2,1,0:T(8,128)(2,1)} %fusion.70), channel_id=1, source_target_pairs={{0,2},{2,4},{4,6},{6,0},{1,3},{3,5},{5,7},{7,1},{8,10},{10,12},{12... | collective-permute-start | bytes 786440 | tf_op jit(solution)/shard_map/ppermute | solution.py:161
  382.0 21.8 %collective-permute-start.25 = (bf16[64,4480]{1,0:T(8,128)(2,1)}, bf16[64,4480]{1,0:T(8,128)(2,1)}, u32[]{:S(2)}, u32[]{:S(2)}) collective-permute-start(bf16[64,4480]{1,0:T(8,128)(2,1)} %fusion.62), channel_id=1, source_target_pairs={{0,1},{1,0},{2,3},{3,2},{4,5},{5,4},{6,7},{7,6},{8,9},{9,8},{10,11... | collective-permute-start | bytes 1720328 | tf_op jit(solution)/shard_map/ppermute | solution.py:169
  384.1 15.9 %collective-permute-start.32 = (bf16[128,1024]{1,0:T(8,128)(2,1)S(1)}, bf16[128,1024]{1,0:T(8,128)(2,1)}, u32[]{:S(2)}, u32[]{:S(2)}) collective-permute-start(bf16[128,1024]{1,0:T(8,128)(2,1)S(1)} %fusion.79), channel_id=1, source_target_pairs={{0,1},{1,0},{2,3},{3,2},{4,5},{5,4},{6,7},{7,6},{8,9},{9,8},{10,11... | collective-permute-start | bytes 786440 | tf_op jit(solution)/shard_map/ppermute | solution.py:169
  410.6 10.2 %collective-permute-start.33 = (f32[408,128]{1,0:T(8,128)S(1)}, f32[408,128]{1,0:T(8,128)S(1)}, u32[]{:S(2)}, u32[]{:S(2)}) collective-permute-start(f32[408,128]{1,0:T(8,128)S(1)} %get-tuple-element.106), channel_id=1, source_target_pairs={{0,16},{16,32},{32,48},{48,0},{64,80},{80,96},{96,112},{112,64},{1... | collective-permute-start | bytes 626696 | tf_op jit(solution)/shard_map/ppermute | solution.py:184
  412.0 8.8 %collective-permute-start.35 = (f32[408,128]{1,0:T(8,128)S(1)}, f32[408,128]{1,0:T(8,128)S(1)}, u32[]{:S(2)}, u32[]{:S(2)}) collective-permute-start(f32[408,128]{1,0:T(8,128)S(1)} %get-tuple-element.107), channel_id=1, source_target_pairs={{0,48},{16,0},{32,16},{48,32},{64,112},{80,64},{96,80},{112,96},{1... | collective-permute-start | bytes 626696 | tf_op jit(solution)/shard_map/ppermute | solution.py:185
  421.7 26.9 %collective-permute-start.36 = (f32[816,128]{1,0:T(8,128)}, f32[816,128]{1,0:T(8,128)}, u32[]{:S(2)}, u32[]{:S(2)}) collective-permute-start(f32[816,128]{1,0:T(8,128)} %pad_maximum_fusion.6), channel_id=1, source_target_pairs={{0,48},{16,0},{32,16},{48,32},{64,112},{80,64},{96,80},{112,96},{1... | collective-permute-start | bytes 1253384 | tf_op jit(solution)/shard_map/ppermute | solution.py:188
  424.3 24.2 %collective-permute-start.34 = (f32[816,128]{1,0:T(8,128)}, f32[816,128]{1,0:T(8,128)}, u32[]{:S(2)}, u32[]{:S(2)}) collective-permute-start(f32[816,128]{1,0:T(8,128)} %pad_maximum_fusion.5), channel_id=1, source_target_pairs={{0,16},{16,32},{32,48},{48,0},{64,80},{80,96},{96,112},{112,64},{1... | collective-permute-start | bytes 1253384 | tf_op jit(solution)/shard_map/ppermute | solution.py:188
  429.2 3.5 collective-permute-start.11
  432.7 3.6 collective-permute-start.12
  436.3 5.3 %collective-permute-start.13 = (f32[8,1836]{1,0:T(8,128)S(1)}, f32[8,1836]{1,0:T(8,128)S(1)}, u32[]{:S(2)}, u32[]{:S(2)}) collective-permute-start(f32[8,1836]{1,0:T(8,128)S(1)} %add.296), channel_id=1, source_target_pairs={{0,4},{2,6},{4,0},{6,2},{1,5},{3,7},{5,1},{7,3},{8,12},{10,14},{12... | collective-permute-start | bytes 176264 | tf_op jit(solution)/shard_map/ppermute | solution.py:288
  441.6 15.8 %collective-permute-start.14 = (f32[8,1836]{1,0:T(8,128)S(1)}, f32[8,1836]{1,0:T(8,128)S(1)}, u32[]{:S(2)}, u32[]{:S(2)}) collective-permute-start(f32[8,1836]{1,0:T(8,128)S(1)} %add.297), channel_id=1, source_target_pairs={{0,8},{8,0},{1,9},{9,1},{2,10},{10,2},{3,11},{11,3},{4,12},{12,4},... | collective-permute-start | bytes 176264 | tf_op jit(solution)/shard_map/ppermute | solution.py:288
  449.9 12.8 %collective-permute-start.37 = (f32[816,128]{1,0:T(8,128)S(1)}, f32[816,128]{1,0:T(8,128)S(1)}, u32[]{:S(2)}, u32[]{:S(2)}) collective-permute-start(f32[816,128]{1,0:T(8,128)S(1)} %fusion.76), channel_id=1, source_target_pairs={{0,64},{16,80},{32,96},{48,112},{64,0},{80,16},{96,32},{112,48},{1... | collective-permute-start | bytes 1253384 | tf_op jit(solution)/shard_map/ppermute | solution.py:191
  457.4 8.2 %collective-permute-start.15 = (f32[8,1836]{1,0:T(8,128)S(1)}, f32[8,1836]{1,0:T(8,128)S(1)}, u32[]{:S(2)}, u32[]{:S(2)}) collective-permute-start(f32[8,1836]{1,0:T(8,128)S(1)} %add.298), channel_id=1, source_target_pairs={{0,16},{16,0},{32,48},{48,32},{64,80},{80,64},{96,112},{112,96},{1... | collective-permute-start | bytes 176264 | tf_op jit(solution)/shard_map/ppermute | solution.py:288
  462.8 16.4 %collective-permute-start.39 = (f32[816,128]{1,0:T(8,128)S(1)}, f32[816,128]{1,0:T(8,128)S(1)}, u32[]{:S(2)}, u32[]{:S(2)}) collective-permute-start(f32[816,128]{1,0:T(8,128)S(1)} %get-tuple-element.62), channel_id=1, source_target_pairs={{0,16},{16,32},{32,48},{48,0},{64,80},{80,96},{96,112},{112,64},{1... | collective-permute-start | bytes 1253384 | tf_op jit(solution)/shard_map/ppermute | solution.py:193
  462.9 16.9 %collective-permute-start.38 = (f32[816,128]{1,0:T(8,128)S(1)}, f32[816,128]{1,0:T(8,128)S(1)}, u32[]{:S(2)}, u32[]{:S(2)}) collective-permute-start(f32[816,128]{1,0:T(8,128)S(1)} %get-tuple-element.62), channel_id=1, source_target_pairs={{0,48},{16,0},{32,16},{48,32},{64,112},{80,64},{96,80},{112,96},{1... | collective-permute-start | bytes 1253384 | tf_op jit(solution)/shard_map/ppermute | solution.py:194
  465.6 11.0 %collective-permute-start.16 = (f32[8,1836]{1,0:T(8,128)S(1)}, f32[8,1836]{1,0:T(8,128)S(1)}, u32[]{:S(2)}, u32[]{:S(2)}) collective-permute-start(f32[8,1836]{1,0:T(8,128)S(1)} %add.299), channel_id=1, source_target_pairs={{0,32},{16,48},{32,0},{48,16},{64,96},{80,112},{96,64},{112,80},{1... | collective-permute-start | bytes 176264 | tf_op jit(solution)/shard_map/ppermute | solution.py:288
  476.5 16.0 %collective-permute-start.17 = (f32[8,1836]{1,0:T(8,128)S(1)}, f32[8,1836]{1,0:T(8,128)S(1)}, u32[]{:S(2)}, u32[]{:S(2)}) collective-permute-start(f32[8,1836]{1,0:T(8,128)S(1)} %add.300), channel_id=1, source_target_pairs={{0,64},{16,80},{32,96},{48,112},{64,0},{80,16},{96,32},{112,48},{1... | collective-permute-start | bytes 176264 | tf_op jit(solution)/shard_map/ppermute | solution.py:288
  479.2 5.9 %collective-permute-start.40 = (f32[408,128]{1,0:T(8,128)S(1)}, f32[408,128]{1,0:T(8,128)S(1)}, u32[]{:S(2)}, u32[]{:S(2)}) collective-permute-start(f32[408,128]{1,0:T(8,128)S(1)} %slice.444), channel_id=1, source_target_pairs={{0,16},{16,32},{32,48},{48,0},{64,80},{80,96},{96,112},{112,64},{1... | collective-permute-start | bytes 626696 | tf_op jit(solution)/shard_map/ppermute | solution.py:195
  479.9 5.3 %collective-permute-start.41 = (f32[408,128]{1,0:T(8,128)S(1)}, f32[408,128]{1,0:T(8,128)S(1)}, u32[]{:S(2)}, u32[]{:S(2)}) collective-permute-start(f32[408,128]{1,0:T(8,128)S(1)} %slice.445), channel_id=1, source_target_pairs={{0,48},{16,0},{32,16},{48,32},{64,112},{80,64},{96,80},{112,96},{1... | collective-permute-start | bytes 626696 | tf_op jit(solution)/shard_map/ppermute | solution.py:196
  489.1 8.3 %collective-permute-start.42 = (f32[64,4480]{1,0:T(8,128)}, f32[64,4480]{1,0:T(8,128)}, u32[]{:S(2)}, u32[]{:S(2)}) collective-permute-start(f32[64,4480]{1,0:T(8,128)} %reshape.685), channel_id=1, source_target_pairs={{0,8},{8,0},{1,9},{9,1},{2,10},{10,2},{3,11},{11,3},{4,12},{12,4},... | collective-permute-start | bytes 3440648 | tf_op jit(solution)/shard_map/ppermute | solution.py:238
  494.2 2.0 collective-permute-start.43
  (92 other events, 463.0 us)
Sparse Core Ops, SparseCore 0:
  77.7 52.8 all-gather.2

commit v9 on v8

--- a/solution.py
+++ b/solution.py
@@ -142,31 +142,39 @@
     return gated_pre * scaling * gate_gain[None, :]
 
 
-def reduce_group(halves):
+def reduce_group(halves, small=None):
     ring = lax.axis_size("shard_0")
     y = lax.axis_index("shard_1")
     z = lax.axis_index("shard_0")
-    rows, cols = halves.shape[1], halves.shape[2]
-    blocks = halves.reshape(ring, 2, rows, cols)
-    doubled = jnp.concatenate([blocks, blocks], axis=0)
-    rel = lax.dynamic_slice_in_dim(doubled, z, ring, axis=0)
     up = [(i, (i + 1) % ring) for i in range(ring)]
     down = [(i, (i - 1) % ring) for i in range(ring)]
-    half = rows // 2
-    low = lambda a: a.astype(jnp.bfloat16)
-    acc_up = lax.ppermute(low(rel[3][:, :half]), "shard_0", up)
-    acc_dn = lax.ppermute(low(rel[1][:, half:]), "shard_0", down)
-    acc_up = lax.ppermute(low(acc_up + rel[2][:, :half]), "shard_0", up)
-    acc_dn = lax.ppermute(low(acc_dn + rel[2][:, half:]), "shard_0", down)
-    acc_up = lax.ppermute(low(acc_up + rel[1][:, :half]), "shard_0", up)
-    acc_dn = lax.ppermute(low(acc_dn + rel[3][:, half:]), "shard_0", down)
-    zsum = jnp.concatenate(
-        [acc_up.astype(jnp.float32) + rel[0][:, :half], acc_dn.astype(jnp.float32) + rel[0][:, half:]],
-        axis=1,
-    )
-    keep = lax.dynamic_index_in_dim(zsum, y, axis=0, keepdims=False)
-    give = lax.dynamic_index_in_dim(zsum, 1 - y, axis=0, keepdims=False)
-    return keep + lax.ppermute(low(give), "shard_1", [(0, 1), (1, 0)]).astype(jnp.float32)
+    items = [(halves, jnp.bfloat16)] + ([] if small is None else [(small, jnp.float32)])
+    rels, halfs = [], []
+    for values, _ in items:
+        blocks = values.reshape((ring, 2) + values.shape[1:])
+        doubled = jnp.concatenate([blocks, blocks], axis=0)
+        rels.append(lax.dynamic_slice_in_dim(doubled, z, ring, axis=0))
+        halfs.append(values.shape[1] // 2)
+
+    def send(parts, pairs):
+        return [lax.ppermute(p.astype(w), "shard_0", pairs) for p, (_, w) in zip(parts, items)]
+
+    acc_up = send([r[3][:, :h] for r, h in zip(rels, halfs)], up)
+    acc_dn = send([r[1][:, h:] for r, h in zip(rels, halfs)], down)
+    acc_up = send([a + r[2][:, :h] for a, r, h in zip(acc_up, rels, halfs)], up)
+    acc_dn = send([a + r[2][:, h:] for a, r, h in zip(acc_dn, rels, halfs)], down)
+    acc_up = send([a + r[1][:, :h] for a, r, h in zip(acc_up, rels, halfs)], up)
+    acc_dn = send([a + r[3][:, h:] for a, r, h in zip(acc_dn, rels, halfs)], down)
+    results = []
+    for au, ad, r, h, (_, w) in zip(acc_up, acc_dn, rels, halfs, items):
+        zsum = jnp.concatenate(
+            [au.astype(jnp.float32) + r[0][:, :h], ad.astype(jnp.float32) + r[0][:, h:]], axis=1
+        )
+        keep = lax.dynamic_index_in_dim(zsum, y, axis=0, keepdims=False)
+        give = lax.dynamic_index_in_dim(zsum, 1 - y, axis=0, keepdims=False)
+        got = lax.ppermute(give.astype(w), "shard_1", [(0, 1), (1, 0)])
+        results.append(keep + got.astype(jnp.float32))
+    return results[0] if small is None else results
 
 
 def allreduce_rep(values):
@@ -357,18 +365,30 @@
     input_grad = cotangent + back_in
     grads = (g_norm, g_convw, g_convb, g_stepb, g_decay, g_skip, g_gategain)
     small_blocks = jnp.concatenate([g.reshape(groups, -1) for g in grads], axis=1)
+    small_len = small_blocks.shape[1]
+    small_rows = -(-small_len // 2048) * 16
+    small_blocks = jnp.pad(small_blocks, ((0, 0), (0, small_rows * 128 - small_len)))
+    small_blocks = small_blocks.reshape(groups, small_rows, 128)
+    small_blocks = small_blocks + core_swap(small_blocks)
     cols = proj_low.shape[1]
     wide = -(-cols // 128) * 128
     proj_wide = jnp.pad(proj_low, ((0, 0), (0, wide - cols)))
-    in_group = reduce_group(reduce_core(row_product(normed, proj_wide)))
+    in_group, small_group = reduce_group(
+        reduce_core(row_product(normed, proj_wide)), small_blocks
+    )
     in_shape, out_shape = in_group.shape, out_group.shape
-    joined = jnp.concatenate([in_group.reshape(-1, 128), out_group.reshape(-1, 128)], axis=0)
+    big_rows = (in_group.size + out_group.size) // 128
+    tail_rows = -(-(big_rows + small_group.shape[0]) // 64) * 64 - big_rows
+    small_group = jnp.pad(small_group, ((0, tail_rows - small_group.shape[0]), (0, 0)))
+    joined = jnp.concatenate(
+        [in_group.reshape(-1, 128), out_group.reshape(-1, 128), small_group], axis=0
+    )
     joined = allreduce_rep(joined)
     split_at = in_group.size // 128
+    split_out = split_at + out_group.size // 128
     in_owned = core_join(joined[:split_at].reshape(in_shape))[:, :cols]
-    out_owned = core_join(joined[split_at:].reshape(out_shape))
-    small_sum = exchange_sum(small_blocks, ("shard_1", "shard_0", "core", "rep_hi"))
-    mine = lax.dynamic_index_in_dim(small_sum, lax.axis_index(SHARD), axis=0, keepdims=False)
+    out_owned = core_join(joined[split_at:split_out].reshape(out_shape))
+    mine = joined[split_out:].reshape(-1)[:small_len]
     small_final = []
     offset = 0
     for g in grads:

time: 514 us -> 487 us (0.947)
  waiting for transfers between devices: 175 us -> 131 us
  local copies, waits for them, and re-layouts: 64.8 us -> 74.2 us
  starting transfers between devices: 64.2 us -> 72.5 us
    ppermute x14 -> x21, waiting for transfers between devices: 72.8 us -> 45.7 us  [the longest x18 36.7 us: send(): lax.ppermute(p.astype(w), 'shard_0', pairs)]
    ppermute x10 -> x3, waiting for transfers between devices: 24.4 us -> 6.03 us  [exchange_sum(): values = values + lax.ppermute(values, axis, pairs)]
    ppermute x6 -> x7, waiting for transfers between devices: 23.8 us -> 9.4 us  [core_swap(): return lax.ppermute(values, 'core', [(0, 1), (1, 0)])]
    ppermute x10 -> x3, starting transfers between devices: 16.4 us -> 4.08 us  [exchange_sum(): values = values + lax.ppermute(values, axis, pairs)]
    ppermute x6 -> x7, starting transfers between devices: 10.1 us -> 21 us  [core_swap(): return lax.ppermute(values, 'core', [(0, 1), (1, 0)])]
    ppermute x14 -> x21, starting transfers between devices: 15.8 us -> 24.6 us  [the longest x18 20.4 us: send(): lax.ppermute(p.astype(w), 'shard_0', pairs)]
    ppermute x1, waiting for transfers between devices: 0.01 us -> 5.76 us  [allreduce_rep(): lax.ppermute(up_msg, 'rep_hi', up)]
    concatenate x2 -> x3, other arithmetic: 9.3 us -> 11.5 us  [reduce_group(): doubled = jnp.concatenate([blocks, blocks], axis=0)]
  transfers between devices with their start and end apart: 45 -> 46, of which waited for: 22 -> 20; matrix products, arithmetic and copies ran while one was open for 24% -> 31% of each run, Pallas kernels for 0% -> 0%
where the time goes in v9:
time: 487 us; the launch traced here: 481 us
  waiting for transfers between devices  131 us (27%)
  other arithmetic  119 us (24%)
  local copies, waits for them, and re-layouts  74.2 us (15%)
  starting transfers between devices  72.5 us (15%)
  matrix products  67.6 us (14%)
  between operations  16.1 us (3%)
    ppermute x18, waiting for transfers between devices, send(): lax.ppermute(p.astype(w), 'shard_0', pairs)  36.7 us
    dot_general x3, matrix products, mixer(): y_intra = jnp.einsum('chij,cjhp->cihp', mixing, scaled_in, precision=HIGH)  30.2 us
    ppermute x1, waiting for transfers between devices, gather_group(): from_prev = lax.ppermute(pair, 'shard_0', up)  22.7 us
    unnamed x203, local copies, waits for them, and re-layouts  22.6 us
    ppermute x7, starting transfers between devices, core_swap(): return lax.ppermute(values, 'core', [(0, 1), (1, 0)])  21 us
    ppermute x18, starting transfers between devices, send(): lax.ppermute(p.astype(w), 'shard_0', pairs)  20.4 us
    another operation x4, other arithmetic, gather_rows(): return jnp.stack([first, second], axis=1).reshape(-1, weight.shape[1])  19.4 us
    add x2, other arithmetic, reduce_core(): return keep + core_swap(give)  19.2 us
  transfers between devices with their start and end apart: 46, of which 20 were waited for; matrix products, arithmetic and copies ran while one was open for 31% of the time, Pallas kernels for 0%

profile of v9, /device:TPU:1, one launch (start us, length us, event | category | flops | bytes accessed | tf_op | source)
XLA Modules:
  0.0 481.1 jit_solution(12918609368612634559)
XLA Ops:
  12.0 12.3 %collective-permute-done.3 = bf16[64,4384]{1,0:T(8,128)(2,1)S(1)} collective-permute-done((bf16[64,4384]{1,0:T(8,128)(2,1)S(1)}, bf16[64,4384]{1,0:T(8,128)(2,1)S(1)}, u32[]{:S(2)}, u32[]{:S(2)}) %collective-permute-start.3) | collective-permute-done | bytes 561184 | tf_op jit(solution)/shard_map/ppermute | solution.py:228
  31.8 22.7 %collective-permute-done.5 = bf16[2,64,4384]{2,1,0:T(8,128)(2,1)S(1)} collective-permute-done((bf16[2,64,4384]{2,1,0:T(8,128)(2,1)}, bf16[2,64,4384]{2,1,0:T(8,128)(2,1)S(1)}, u32[]{:S(2)}, u32[]{:S(2)}) %collective-permute-start.5) | collective-permute-done | bytes 1122336 | tf_op jit(solution)/shard_map/ppermute | solution.py:232
  57.7 10.5 %collective-permute-done.6 = bf16[2,32,4384]{2,1,0:T(8,128)(2,1)S(1)} collective-permute-done((bf16[2,32,4384]{2,1,0:T(8,128)(2,1)S(1)}, bf16[2,32,4384]{2,1,0:T(8,128)(2,1)S(1)}, u32[]{:S(2)}, u32[]{:S(2)}) %collective-permute-start.6) | collective-permute-done | bytes 561184 | tf_op jit(solution)/shard_map/ppermute | solution.py:235
  71.8 3.1 collective-permute-start.8
  79.4 2.9 collective-permute-done.1
  82.3 2.7 collective-permute-start.2
  91.2 8.1 %select_bitcast_fusion.2 = (bf16[8,1,64,4384]{3,2,0,1:T(8,128)(2,1)}, bf16[8,1,64,4384]{3,2,0,1:T(8,128)(2,1)}) fusion(bf16[8,64,4384]{2,1,0:T(8,128)(2,1)} %collective-permute-done.8, pred[]{:T(512)S(6)} %eq.81, bf16[4,2,64,4384]{3,2,1,0:T(8,128)(2,1)} %constant_dynamic-slice_fusion.2), kind=kLoop, calls=%fused_computation.19 | loop fusion | flops 4489216 | bytes 17956864 | tf_op jit(solution)/shard_map/stack | solution.py:261
  99.3 8.2 %pad_maximum_fusion = bf16[8,2,64,4384]{3,2,0,1:T(8,128)(2,1)} fusion(bf16[8,1,64,4384]{3,2,0,1:T(8,128)(2,1)} %get-tuple-element.85, bf16[8,1,64,4384]{3,2,0,1:T(8,128)(2,1)} %get-tuple-element.84), kind=kLoop, calls=%fused_computation.3 | loop fusion | flops 4489216 | bytes 17956864 | tf_op jit(solution)/shard_map/stack | solution.py:261
  107.6 8.0 %copy.89 = bf16[8,2,64,4384]{3,2,1,0:T(8,128)(2,1)} copy(bf16[8,2,64,4384]{3,2,0,1:T(8,128)(2,1)} %pad_maximum_fusion) | data formatting | bytes 17956864 | tf_op jit(solution)/shard_map/stack | solution.py:261
  115.6 7.5 %fusion.115 = f32[256,4384]{0,1:T(8,128)S(1)} fusion(bf16[1024,4384]{1,0:T(8,128)(2,1)} %bitcast.295, f32[256,1024]{1,0:T(8,128)S(1)} %copy-done.15, f32[1024]{0:T(1024)S(1)} %slice_bitcast_fusion.21, f32[256]{0:T(256)S(1)} %fusion.107), kind=kOutput, calls=%fused_computation.289 | convolution fusion | flops 2299265024 | bytes 14521344 | tf_op jit(solution)/shard_map/dot_general | solution.py:338
  131.3 5.3 %fusion.25 = (f32[256,2304]{0,1:T(8,128)S(1)}, f32[256,2304]{0,1:T(8,128)}) fusion(f32[253,2304]{0,1:T(8,128)S(1)} %slice.446, f32[2304]{0:T(1024)S(1)} %get-tuple-element.58, pred[256]{0:T(512)(128)(4,1)S(1)} %get-tuple-element.136, f32[254,2304]{0,1:T(8,128)S(1)} %slice.444, f32[2304]{0:T(1024)S(1)} %get-tuple-element.59, ...), kind=kLoop, calls=%fused_computation.58 | loop fusion | flops 8847360 | bytes 14147328 | tf_op jit(solution)/shard_map/jvp(jit(silu))/mul | solution.py:110
  139.9 2.8 fusion.73
  144.1 10.1 %fusion.30 = f32[256,32,64]{0,2,1:T(8,128)S(1)} fusion(f32[256,32,64]{0,2,1:T(8,128)S(1)} %bitcast.306, f32[256,32,64]{0,2,1:T(8,128)S(1)} %fusion.73, f32[32]{0:T(128)S(1)} %mul.425, f32[256,32]{0,1:T(8,128)S(1)} %bitcast_multiply_fusion.4, f32[256,256]{1,0:T(8,128)} %fusion.90, f32[32,256]{1,0:T(8,128)S(1)} %bitcast_add_fusion.2, ...), kind=kOutput, calls=%fused_computation.70 | convolution fusion | flops 1619525632 | bytes 6717568 | tf_op jit(solution)/shard_map/jvp(chij,cjhp->cihp)/dot_general | solution.py:132
  154.2 3.1 multiply_reduce_fusion.9
  158.6 3.6 select_bitcast_fusion.3
  163.2 3.1 collective-permute-start.10
  167.0 9.4 %collective-permute-done.9 = bf16[8,128,1024]{2,1,0:T(8,128)(2,1)} collective-permute-done((bf16[8,128,1024]{2,1,0:T(8,128)(2,1)}, bf16[8,128,1024]{2,1,0:T(8,128)(2,1)}, u32[]{:S(2)}, u32[]{:S(2)}) %collective-permute-start.9) | collective-permute-done | bytes 2097184 | tf_op jit(solution)/shard_map/ppermute | solution.py:246
  183.3 5.9 %fusion.12 = f32[8,128,1024]{2,1,0:T(8,128)} fusion(f32[8,128,1024]{2,1,0:T(8,128)} %collective-permute-done.10, f32[8,2,128,1024]{3,2,1,0:T(8,128)S(1)} %bitcast.282, pred[]{:T(512)S(6)} %eq.81), kind=kLoop, calls=%fused_computation.25 | loop fusion | flops 2097152 | bytes 16777216 | tf_op jit(solution)/shard_map/add | solution.py:271
  190.9 4.6 multiply_reduce_fusion.6
  197.9 11.4 %fusion.9 = (f32[32,256]{1,0:T(8,128)S(1)}, f32[32,256]{1,0:T(8,128)S(1)}, f32[256,256]{1,0:T(8,128)S(1)}) fusion(f32[256,256]{1,0:T(8,128)S(1)} %copy-done.47, f32[32,256]{1,0:T(8,128)S(1)} %copy-done.66, pred[256,256]{1,0:T(8,128)(4,1)S(1)} %copy-done.61, f32[32,64,256]{2,1,0:T(8,128)S(1)} %bitcast.289, f32[256,32,64]{0,2,1:T(8,128)S(1)} %bitcast.307, ...), kind=kOutput, calls=%fused_computation.17 | convolution fusion | flops 1629929472 | bytes 4915200 | tf_op jit(solution)/shard_map/transpose(jvp(chij,cjhp->cihp))/dot_general | solution.py:132
  209.3 8.7 %fusion.31 = (f32[256,32]{0,1:T(8,128)}, f32[1,256,32,64]{1,3,2,0:T(8,128)}) fusion(f32[1,256,32,64]{1,3,2,0:T(8,128)S(1)} %bitcast.308, f32[256,32]{0,1:T(8,128)S(1)} %copy-done.49, f32[32,64,256]{2,1,0:T(8,128)S(1)} %bitcast.290, f32[256,256]{1,0:T(8,128)S(1)} %copy-done.47, f32[32,256]{1,0:T(8,128)S(1)} %copy-done.66, pred[256,256]{1,0:T(8,128)(4,1)S(1)} %copy-done.61), kind=kOutput, calls=%fused_computation.74 | convolution fusion | flops 1618468864 | bytes 6717440 | tf_op jit(solution)/shard_map/transpose(jvp(chij,cjhp->cihp))/dot_general | solution.py:132
  226.7 2.8 multiply_reduce_fusion.4
  237.2 7.9 %fusion.26 = f32[1024,4480]{1,0:T(8,128)} fusion(bf16[256,4384]{0,1:T(8,128)(2,1)S(1)} %add_convert_fusion, f32[256,1024]{1,0:T(8,128)S(1)} %copy-done.15, f32[1024]{0:T(1024)S(1)} %slice_bitcast_fusion.21, f32[256]{0:T(256)S(1)} %fusion.107), kind=kOutput, calls=%fused_computation.65 | convolution fusion | flops 2349596672 | bytes 21648384 | tf_op jit(solution)/shard_map/dot_general | solution.py:76
  245.1 10.7 %select_bitcast_fusion = f32[8,64,4480]{2,1,0:T(8,128)} fusion(f32[8,2,64,4480]{3,2,1,0:T(8,128)} %bitcast.277, pred[]{:T(512)S(6)} %eq.81), kind=kLoop, calls=%fused_computation.7 | loop fusion | flops 2293760 | bytes 27525120 | tf_op jit(solution)/shard_map/jit(_where)/select_n | solution.py:270
  260.5 8.5 %multiply_reduce_fusion.10 = (f32[1024]{0:T(1024)S(1)}, f32[256]{0:T(256)}, f32[256,1024]{1,0:T(8,128)}) fusion(f32[256,1024]{1,0:T(8,128)S(1)} %copy-done.15, f32[256]{0:T(256)S(1)} %fusion.107, f32[1024]{0:T(1024)S(1)} %slice_bitcast_fusion.21, bf16[256,4384]{0,1:T(8,128)(2,1)} %copy-done.23, bf16[1024,4384]{1,0:T(8,128)(2,1)} %bitcast.296), kind=kOutput, calls=%fused_computation.140 | convolution fusion | flops 2300050176 | bytes 13330432 | tf_op jit(solution)/shard_map/dot_general | solution.py:82
  269.3 3.2 fusion.10
  276.5 2.8 collective-permute-start.22
  279.5 2.7 collective-permute-start.30
  282.2 13.3 %fusion.2 = f32[8,64,4480]{2,1,0:T(8,128)} fusion(f32[8,64,4480]{2,1,0:T(8,128)} %collective-permute-done.11, f32[8,2,64,4480]{3,2,1,0:T(8,128)} %bitcast.278, pred[]{:T(512)S(6)} %eq.81), kind=kLoop, calls=%fused_computation.6 | loop fusion | flops 4587520 | bytes 36700160 | tf_op jit(solution)/shard_map/add | solution.py:271
  295.5 8.2 %fusion = f32[4,2,64,4480]{3,2,1,0:T(8,128)} fusion(s32[]{:T(128)S(6)} %select_n.236, f32[4,2,64,4480]{3,2,1,0:T(8,128)} %bitcast.287), kind=kLoop, calls=%fused_computation.2 | loop fusion | flops 2293760 | bytes 18350084 | tf_op jit(solution)/shard_map/concatenate | solution.py:155
  303.8 6.4 %slice_bitcast_fusion.3 = (f32[2,64,4480]{2,1,0:T(8,128)S(1)}, f32[2,64,4480]{2,1,0:T(8,128)S(1)}, f32[2,64,4480]{2,1,0:T(8,128)}, f32[2,64,4480]{2,1,0:T(8,128)}) fusion(f32[4,2,64,4480]{3,2,1,0:T(8,128)} %fusion), kind=kLoop, calls=%fused_computation.64 | loop fusion | bytes 18350080 | tf_op jit(solution)/shard_map/squeeze | solution.py:162
  315.4 10.9 %collective-permute-done.31 = f32[2,8,128]{2,0,1:T(2,128)S(1)} collective-permute-done((f32[2,8,128]{2,0,1:T(2,128)S(1)}, f32[2,8,128]{2,0,1:T(2,128)S(1)}, u32[]{:S(2)}, u32[]{:S(2)}) %collective-permute-start.31) | collective-permute-done | bytes 8224 | tf_op jit(solution)/shard_map/ppermute | solution.py:160
  329.4 2.9 collective-permute-start.23
  340.5 7.6 %collective-permute-done.16 = bf16[2,32,4480]{2,1,0:T(8,128)(2,1)S(1)} collective-permute-done((bf16[2,32,4480]{2,1,0:T(8,128)(2,1)S(1)}, bf16[2,32,4480]{2,1,0:T(8,128)(2,1)S(1)}, u32[]{:S(2)}, u32[]{:S(2)}) %collective-permute-start.16) | collective-permute-done | bytes 573472 | tf_op jit(solution)/shard_map/ppermute | solution.py:160
  348.5 10.0 %collective-permute-done.13 = bf16[2,32,4480]{2,1,0:T(8,128)(2,1)S(1)} collective-permute-done((bf16[2,32,4480]{2,1,0:T(8,128)(2,1)S(1)}, bf16[2,32,4480]{2,1,0:T(8,128)(2,1)S(1)}, u32[]{:S(2)}, u32[]{:S(2)}) %collective-permute-start.13) | collective-permute-done | bytes 573472 | tf_op jit(solution)/shard_map/ppermute | solution.py:160
  362.6 4.4 collective-permute-done.17
  367.1 3.8 collective-permute-done.14
  375.1 9.0 %collective-permute-done.33 = f32[16,128]{1,0:T(8,128)S(1)} collective-permute-done((f32[16,128]{1,0:T(8,128)S(1)}, f32[16,128]{1,0:T(8,128)S(1)}, u32[]{:S(2)}, u32[]{:S(2)}) %collective-permute-start.33) | collective-permute-done | bytes 8224 | tf_op jit(solution)/shard_map/ppermute | solution.py:175
  397.5 3.2 collective-permute-done.34
  403.7 5.0 %collective-permute-done.37 = f32[832,128]{1,0:T(8,128)S(1)} collective-permute-done((f32[832,128]{1,0:T(8,128)S(1)}, f32[832,128]{1,0:T(8,128)S(1)}, u32[]{:S(2)}, u32[]{:S(2)}) %collective-permute-start.37) | collective-permute-done | bytes 426016 | tf_op jit(solution)/shard_map/ppermute | solution.py:196
  408.6 5.8 %collective-permute-done.35 = f32[832,128]{1,0:T(8,128)S(1)} collective-permute-done((f32[832,128]{1,0:T(8,128)S(1)}, f32[832,128]{1,0:T(8,128)S(1)}, u32[]{:S(2)}, u32[]{:S(2)}) %collective-permute-start.35) | collective-permute-done | bytes 426016 | tf_op jit(solution)/shard_map/ppermute | solution.py:196
  415.2 2.8 collective-permute-start.38
  418.0 6.0 %collective-permute-done.38 = f32[832,128]{1,0:T(8,128)} collective-permute-done((f32[832,128]{1,0:T(8,128)}, f32[832,128]{1,0:T(8,128)}, u32[]{:S(2)}, u32[]{:S(2)}) %collective-permute-start.38) | collective-permute-done | bytes 426016 | tf_op jit(solution)/shard_map/ppermute | solution.py:199
  428.0 4.5 convolution_add_fusion
  434.0 2.7 collective-permute-start.42
  436.8 3.1 collective-permute-done.41
  445.0 14.0 %collective-permute-start.43 = (f32[64,4480]{1,0:T(8,128)}, f32[64,4480]{1,0:T(8,128)}, u32[]{:S(2)}, u32[]{:S(2)}) collective-permute-start(f32[64,4480]{1,0:T(8,128)} %reshape.690), channel_id=1, source_target_pairs={{0,8},{8,0},{1,9},{9,1},{2,10},{10,2},{3,11},{11,3},{4,12},{12,4},... | collective-permute-start | bytes 3440648 | tf_op jit(solution)/shard_map/ppermute | solution.py:246
  471.1 3.0 copy.111
  (436 shorter events, 145.6 us)
Async XLA Ops:
  7.2 159.1 %all-gather.3.cloned.1.call-start = ((), (), s32[]{:S(2)}) async-start(), calls=%async_computation | async-start | bytes 2359296 | tf_op jit(solution)/shard_map/all_gather | solution.py:257
  9.8 14.5 %collective-permute-start.3 = (bf16[64,4384]{1,0:T(8,128)(2,1)S(1)}, bf16[64,4384]{1,0:T(8,128)(2,1)S(1)}, u32[]{:S(2)}, u32[]{:S(2)}) collective-permute-start(bf16[64,4384]{1,0:T(8,128)(2,1)S(1)} %copy.116), channel_id=1, source_target_pairs={{0,1},{1,0},{2,3},{3,2},{4,5},{5,4},{6,7},{7,6},{8,9},{9,8},{10,11... | collective-permute-start | bytes 1683464 | tf_op jit(solution)/shard_map/ppermute | solution.py:228
  26.3 28.3 %collective-permute-start.5 = (bf16[2,64,4384]{2,1,0:T(8,128)(2,1)}, bf16[2,64,4384]{2,1,0:T(8,128)(2,1)S(1)}, u32[]{:S(2)}, u32[]{:S(2)}) collective-permute-start(bf16[2,64,4384]{2,1,0:T(8,128)(2,1)} %maximum_select_fusion.1), channel_id=1, source_target_pairs={{0,2},{2,4},{4,6},{6,0},{1,3},{3,5},{5,7},{7,1},{8,10},{10,12},{12... | collective-permute-start | bytes 3366920 | tf_op jit(solution)/shard_map/ppermute | solution.py:232
  28.2 26.5 %collective-permute-start.4 = (bf16[2,64,4384]{2,1,0:T(8,128)(2,1)}, bf16[2,64,4384]{2,1,0:T(8,128)(2,1)S(1)}, u32[]{:S(2)}, u32[]{:S(2)}) collective-permute-start(bf16[2,64,4384]{2,1,0:T(8,128)(2,1)} %maximum_select_fusion.1), channel_id=1, source_target_pairs={{0,6},{2,0},{4,2},{6,4},{1,7},{3,1},{5,3},{7,5},{8,14},{10,8},{12,... | collective-permute-start | bytes 3366920 | tf_op jit(solution)/shard_map/ppermute | solution.py:233
  54.6 13.6 %collective-permute-start.6 = (bf16[2,32,4384]{2,1,0:T(8,128)(2,1)S(1)}, bf16[2,32,4384]{2,1,0:T(8,128)(2,1)S(1)}, u32[]{:S(2)}, u32[]{:S(2)}) collective-permute-start(bf16[2,32,4384]{2,1,0:T(8,128)(2,1)S(1)} %slice.438), channel_id=1, source_target_pairs={{0,2},{2,4},{4,6},{6,0},{1,3},{3,5},{5,7},{7,1},{8,10},{10,12},{12... | collective-permute-start | bytes 1683464 | tf_op jit(solution)/shard_map/ppermute | solution.py:235
  54.8 13.4 %collective-permute-start.7 = (bf16[2,32,4384]{2,1,0:T(8,128)(2,1)S(1)}, bf16[2,32,4384]{2,1,0:T(8,128)(2,1)S(1)}, u32[]{:S(2)}, u32[]{:S(2)}) collective-permute-start(bf16[2,32,4384]{2,1,0:T(8,128)(2,1)S(1)} %slice.439), channel_id=1, source_target_pairs={{0,6},{2,0},{4,2},{6,4},{1,7},{3,1},{5,3},{7,5},{8,14},{10,8},{12,... | collective-permute-start | bytes 1683464 | tf_op jit(solution)/shard_map/ppermute | solution.py:236
  71.8 19.4 %collective-permute-start.8 = (bf16[8,64,4384]{2,1,0:T(8,128)(2,1)}, bf16[8,64,4384]{2,1,0:T(8,128)(2,1)}, u32[]{:S(2)}, u32[]{:S(2)}) collective-permute-start(bf16[8,64,4384]{2,1,0:T(8,128)(2,1)} %bitcast.8), channel_id=1, source_target_pairs={{0,8},{8,0},{1,9},{9,1},{2,10},{10,2},{3,11},{11,3},{4,12},{12,4},... | collective-permute-start | bytes 13467656 | tf_op jit(solution)/shard_map/ppermute | solution.py:246
  75.4 3.6 collective-permute-start
  77.9 64.8 %copy-start.60 = (pred[256,256]{1,0:T(8,128)(4,1)}, pred[256,256]{1,0:T(8,128)(4,1)S(1)}, u32[]{:S(2)}) copy-start(pred[256,256]{1,0:T(8,128)(4,1)S(1)} %fusion.83) | copy-start | bytes 196612
  78.0 61.9 %copy-start.68 = (f32[256]{0:T(256)}, f32[256]{0:T(256)S(1)}, u32[]{:S(2)}) copy-start(f32[256]{0:T(256)S(1)} %get-tuple-element.133) | copy-start | bytes 3076
  79.2 3.1 collective-permute-start.1
  82.3 4.8 %collective-permute-start.2 = (f32[8,1836]{1,0:T(8,128)S(1)}, f32[8,1836]{1,0:T(8,128)S(1)}, u32[]{:S(2)}, u32[]{:S(2)}) collective-permute-start(f32[8,1836]{1,0:T(8,128)S(1)} %fusion.132), channel_id=1, source_target_pairs={{0,4},{2,6},{4,0},{6,2},{1,5},{3,7},{5,1},{7,3},{8,12},{10,14},{12... | collective-permute-start | bytes 176264 | tf_op jit(solution)/shard_map/ppermute | solution.py:296
  163.2 18.5 %collective-permute-start.10 = (f32[8,128,1024]{2,1,0:T(8,128)}, f32[8,128,1024]{2,1,0:T(8,128)}, u32[]{:S(2)}, u32[]{:S(2)}) collective-permute-start(f32[8,128,1024]{2,1,0:T(8,128)} %select_bitcast_fusion.3), channel_id=1, source_target_pairs={{0,8},{8,0},{1,9},{9,1},{2,10},{10,2},{3,11},{11,3},{4,12},{12,4},... | collective-permute-start | bytes 12582920 | tf_op jit(solution)/shard_map/ppermute | solution.py:246
  166.3 10.1 %collective-permute-start.9 = (bf16[8,128,1024]{2,1,0:T(8,128)(2,1)}, bf16[8,128,1024]{2,1,0:T(8,128)(2,1)}, u32[]{:S(2)}, u32[]{:S(2)}) collective-permute-start(bf16[8,128,1024]{2,1,0:T(8,128)(2,1)} %bitcast.309), channel_id=1, source_target_pairs={{0,8},{8,0},{1,9},{9,1},{2,10},{10,2},{3,11},{11,3},{4,12},{12,4},... | collective-permute-start | bytes 6291464 | tf_op jit(solution)/shard_map/ppermute | solution.py:246
  255.8 26.4 %collective-permute-start.11 = (f32[8,64,4480]{2,1,0:T(8,128)}, f32[8,64,4480]{2,1,0:T(8,128)}, u32[]{:S(2)}, u32[]{:S(2)}) collective-permute-start(f32[8,64,4480]{2,1,0:T(8,128)} %select_bitcast_fusion), channel_id=1, source_target_pairs={{0,8},{8,0},{1,9},{9,1},{2,10},{10,2},{3,11},{11,3},{4,12},{12,4},... | collective-permute-start | bytes 27525128 | tf_op jit(solution)/shard_map/ppermute | solution.py:246
  269.1 10.3 %collective-permute-start.26 = (f32[8,16,128]{2,0,1:T(8,128)S(1)}, f32[8,16,128]{2,0,1:T(8,128)S(1)}, u32[]{:S(2)}, u32[]{:S(2)}) collective-permute-start(f32[8,16,128]{2,0,1:T(8,128)S(1)} %pad_bitcast_fusion), channel_id=1, source_target_pairs={{0,8},{8,0},{1,9},{9,1},{2,10},{10,2},{3,11},{11,3},{4,12},{12,4},... | collective-permute-start | bytes 196616 | tf_op jit(solution)/shard_map/ppermute | solution.py:246
  276.5 51.4 %collective-permute-start.22 = (bf16[2,64,1024]{2,1,0:T(8,128)(2,1)}, bf16[2,64,1024]{2,1,0:T(8,128)(2,1)}, u32[]{:S(2)}, u32[]{:S(2)}) collective-permute-start(bf16[2,64,1024]{2,1,0:T(8,128)(2,1)} %slice.635), channel_id=1, source_target_pairs={{0,6},{2,0},{4,2},{6,4},{1,7},{3,1},{5,3},{7,5},{8,14},{10,8},{12,... | collective-permute-start | bytes 786440 | tf_op jit(solution)/shard_map/ppermute | solution.py:160
  279.3 48.6 %collective-permute-start.19 = (bf16[2,64,1024]{2,1,0:T(8,128)(2,1)}, bf16[2,64,1024]{2,1,0:T(8,128)(2,1)}, u32[]{:S(2)}, u32[]{:S(2)}) collective-permute-start(bf16[2,64,1024]{2,1,0:T(8,128)(2,1)} %slice.636), channel_id=1, source_target_pairs={{0,2},{2,4},{4,6},{6,0},{1,3},{3,5},{5,7},{7,1},{8,10},{10,12},{12... | collective-permute-start | bytes 786440 | tf_op jit(solution)/shard_map/ppermute | solution.py:160
  279.5 34.6 %collective-permute-start.30 = (f32[2,8,128]{2,0,1:T(2,128)S(1)}, f32[2,8,128]{2,0,1:T(2,128)S(1)}, u32[]{:S(2)}, u32[]{:S(2)}) collective-permute-start(f32[2,8,128]{2,0,1:T(2,128)S(1)} %slice.494), channel_id=1, source_target_pairs={{0,6},{2,0},{4,2},{6,4},{1,7},{3,1},{5,3},{7,5},{8,14},{10,8},{12,... | collective-permute-start | bytes 24584 | tf_op jit(solution)/shard_map/ppermute | solution.py:160
  312.6 19.8 %collective-permute-start.15 = (bf16[2,32,4480]{2,1,0:T(8,128)(2,1)}, bf16[2,32,4480]{2,1,0:T(8,128)(2,1)}, u32[]{:S(2)}, u32[]{:S(2)}) collective-permute-start(bf16[2,32,4480]{2,1,0:T(8,128)(2,1)} %slice.633), channel_id=1, source_target_pairs={{0,6},{2,0},{4,2},{6,4},{1,7},{3,1},{5,3},{7,5},{8,14},{10,8},{12,... | collective-permute-start | bytes 1720328 | tf_op jit(solution)/shard_map/ppermute | solution.py:160
  312.7 19.7 %collective-permute-start.12 = (bf16[2,32,4480]{2,1,0:T(8,128)(2,1)}, bf16[2,32,4480]{2,1,0:T(8,128)(2,1)}, u32[]{:S(2)}, u32[]{:S(2)}) collective-permute-start(bf16[2,32,4480]{2,1,0:T(8,128)(2,1)} %slice.634), channel_id=1, source_target_pairs={{0,2},{2,4},{4,6},{6,0},{1,3},{3,5},{5,7},{7,1},{8,10},{10,12},{12... | collective-permute-start | bytes 1720328 | tf_op jit(solution)/shard_map/ppermute | solution.py:160
  314.1 12.3 %collective-permute-start.31 = (f32[2,8,128]{2,0,1:T(2,128)S(1)}, f32[2,8,128]{2,0,1:T(2,128)S(1)}, u32[]{:S(2)}, u32[]{:S(2)}) collective-permute-start(f32[2,8,128]{2,0,1:T(2,128)S(1)} %slice_add_fusion.15), channel_id=1, source_target_pairs={{0,6},{2,0},{4,2},{6,4},{1,7},{3,1},{5,3},{7,5},{8,14},{10,8},{12,... | collective-permute-start | bytes 24584 | tf_op jit(solution)/shard_map/ppermute | solution.py:160
  326.4 48.6 %collective-permute-start.32 = (f32[2,8,128]{2,0,1:T(2,128)S(1)}, f32[2,8,128]{2,0,1:T(2,128)S(1)}, u32[]{:S(2)}, u32[]{:S(2)}) collective-permute-start(f32[2,8,128]{2,0,1:T(2,128)S(1)} %get-tuple-element.131), channel_id=1, source_target_pairs={{0,6},{2,0},{4,2},{6,4},{1,7},{3,1},{5,3},{7,5},{8,14},{10,8},{12,... | collective-permute-start | bytes 24584 | tf_op jit(solution)/shard_map/ppermute | solution.py:160
  327.9 9.5 %collective-permute-start.27 = (f32[2,8,128]{2,0,1:T(2,128)S(1)}, f32[2,8,128]{2,0,1:T(2,128)S(1)}, u32[]{:S(2)}, u32[]{:S(2)}) collective-permute-start(f32[2,8,128]{2,0,1:T(2,128)S(1)} %get-tuple-element.132), channel_id=1, source_target_pairs={{0,2},{2,4},{4,6},{6,0},{1,3},{3,5},{5,7},{7,1},{8,10},{10,12},{12... | collective-permute-start | bytes 24584 | tf_op jit(solution)/shard_map/ppermute | solution.py:160
  329.4 8.1 %collective-permute-start.23 = (bf16[2,64,1024]{2,1,0:T(8,128)(2,1)S(1)}, bf16[2,64,1024]{2,1,0:T(8,128)(2,1)S(1)}, u32[]{:S(2)}, u32[]{:S(2)}) collective-permute-start(bf16[2,64,1024]{2,1,0:T(8,128)(2,1)S(1)} %get-tuple-element.114), channel_id=1, source_target_pairs={{0,6},{2,0},{4,2},{6,4},{1,7},{3,1},{5,3},{7,5},{8,14},{10,8},{12,... | collective-permute-start | bytes 786440 | tf_op jit(solution)/shard_map/ppermute | solution.py:160
  332.4 8.0 %collective-permute-start.20 = (bf16[2,64,1024]{2,1,0:T(8,128)(2,1)S(1)}, bf16[2,64,1024]{2,1,0:T(8,128)(2,1)S(1)}, u32[]{:S(2)}, u32[]{:S(2)}) collective-permute-start(bf16[2,64,1024]{2,1,0:T(8,128)(2,1)S(1)} %get-tuple-element.115), channel_id=1, source_target_pairs={{0,2},{2,4},{4,6},{6,0},{1,3},{3,5},{5,7},{7,1},{8,10},{10,12},{12... | collective-permute-start | bytes 786440 | tf_op jit(solution)/shard_map/ppermute | solution.py:160
  334.7 13.4 %collective-permute-start.16 = (bf16[2,32,4480]{2,1,0:T(8,128)(2,1)S(1)}, bf16[2,32,4480]{2,1,0:T(8,128)(2,1)S(1)}, u32[]{:S(2)}, u32[]{:S(2)}) collective-permute-start(bf16[2,32,4480]{2,1,0:T(8,128)(2,1)S(1)} %get-tuple-element.100), channel_id=1, source_target_pairs={{0,6},{2,0},{4,2},{6,4},{1,7},{3,1},{5,3},{7,5},{8,14},{10,8},{12,... | collective-permute-start | bytes 1720328 | tf_op jit(solution)/shard_map/ppermute | solution.py:160
  337.4 22.7 %collective-permute-start.28 = (f32[2,8,128]{2,0,1:T(2,128)S(1)}, f32[2,8,128]{2,0,1:T(2,128)S(1)}, u32[]{:S(2)}, u32[]{:S(2)}) collective-permute-start(f32[2,8,128]{2,0,1:T(2,128)S(1)} %slice_add_fusion.18), channel_id=1, source_target_pairs={{0,2},{2,4},{4,6},{6,0},{1,3},{3,5},{5,7},{7,1},{8,10},{10,12},{12... | collective-permute-start | bytes 24584 | tf_op jit(solution)/shard_map/ppermute | solution.py:160
  337.6 22.6 %collective-permute-start.24 = (bf16[2,64,1024]{2,1,0:T(8,128)(2,1)S(1)}, bf16[2,64,1024]{2,1,0:T(8,128)(2,1)S(1)}, u32[]{:S(2)}, u32[]{:S(2)}) collective-permute-start(bf16[2,64,1024]{2,1,0:T(8,128)(2,1)S(1)} %fusion.68), channel_id=1, source_target_pairs={{0,6},{2,0},{4,2},{6,4},{1,7},{3,1},{5,3},{7,5},{8,14},{10,8},{12,... | collective-permute-start | bytes 786440 | tf_op jit(solution)/shard_map/ppermute | solution.py:160
  340.4 19.9 %collective-permute-start.21 = (bf16[2,64,1024]{2,1,0:T(8,128)(2,1)S(1)}, bf16[2,64,1024]{2,1,0:T(8,128)(2,1)S(1)}, u32[]{:S(2)}, u32[]{:S(2)}) collective-permute-start(bf16[2,64,1024]{2,1,0:T(8,128)(2,1)S(1)} %fusion.70), channel_id=1, source_target_pairs={{0,2},{2,4},{4,6},{6,0},{1,3},{3,5},{5,7},{7,1},{8,10},{10,12},{12... | collective-permute-start | bytes 786440 | tf_op jit(solution)/shard_map/ppermute | solution.py:160
  348.1 10.4 %collective-permute-start.13 = (bf16[2,32,4480]{2,1,0:T(8,128)(2,1)S(1)}, bf16[2,32,4480]{2,1,0:T(8,128)(2,1)S(1)}, u32[]{:S(2)}, u32[]{:S(2)}) collective-permute-start(bf16[2,32,4480]{2,1,0:T(8,128)(2,1)S(1)} %get-tuple-element.101), channel_id=1, source_target_pairs={{0,2},{2,4},{4,6},{6,0},{1,3},{3,5},{5,7},{7,1},{8,10},{10,12},{12... | collective-permute-start | bytes 1720328 | tf_op jit(solution)/shard_map/ppermute | solution.py:160
  358.5 8.6 %collective-permute-start.17 = (bf16[2,32,4480]{2,1,0:T(8,128)(2,1)S(1)}, bf16[2,32,4480]{2,1,0:T(8,128)(2,1)S(1)}, u32[]{:S(2)}, u32[]{:S(2)}) collective-permute-start(bf16[2,32,4480]{2,1,0:T(8,128)(2,1)S(1)} %fusion.44), channel_id=1, source_target_pairs={{0,6},{2,0},{4,2},{6,4},{1,7},{3,1},{5,3},{7,5},{8,14},{10,8},{12,... | collective-permute-start | bytes 1720328 | tf_op jit(solution)/shard_map/ppermute | solution.py:160
  360.1 10.7 %collective-permute-start.14 = (bf16[2,32,4480]{2,1,0:T(8,128)(2,1)S(1)}, bf16[2,32,4480]{2,1,0:T(8,128)(2,1)S(1)}, u32[]{:S(2)}, u32[]{:S(2)}) collective-permute-start(bf16[2,32,4480]{2,1,0:T(8,128)(2,1)S(1)} %fusion.46), channel_id=1, source_target_pairs={{0,2},{2,4},{4,6},{6,0},{1,3},{3,5},{5,7},{7,1},{8,10},{10,12},{12... | collective-permute-start | bytes 1720328 | tf_op jit(solution)/shard_map/ppermute | solution.py:160
  360.2 14.7 %collective-permute-start.29 = (f32[2,8,128]{2,0,1:T(2,128)S(1)}, f32[2,8,128]{2,0,1:T(2,128)S(1)}, u32[]{:S(2)}, u32[]{:S(2)}) collective-permute-start(f32[2,8,128]{2,0,1:T(2,128)S(1)} %slice_add_fusion.17), channel_id=1, source_target_pairs={{0,2},{2,4},{4,6},{6,0},{1,3},{3,5},{5,7},{7,1},{8,10},{10,12},{12... | collective-permute-start | bytes 24584 | tf_op jit(solution)/shard_map/ppermute | solution.py:160
  360.6 23.5 %collective-permute-start.25 = (bf16[128,1024]{1,0:T(8,128)(2,1)S(1)}, bf16[128,1024]{1,0:T(8,128)(2,1)}, u32[]{:S(2)}, u32[]{:S(2)}) collective-permute-start(bf16[128,1024]{1,0:T(8,128)(2,1)S(1)} %fusion.79), channel_id=1, source_target_pairs={{0,1},{1,0},{2,3},{3,2},{4,5},{5,4},{6,7},{7,6},{8,9},{9,8},{10,11... | collective-permute-start | bytes 786440 | tf_op jit(solution)/shard_map/ppermute | solution.py:175
  372.9 15.0 %collective-permute-start.18 = (bf16[64,4480]{1,0:T(8,128)(2,1)}, bf16[64,4480]{1,0:T(8,128)(2,1)}, u32[]{:S(2)}, u32[]{:S(2)}) collective-permute-start(bf16[64,4480]{1,0:T(8,128)(2,1)} %fusion.62), channel_id=1, source_target_pairs={{0,1},{1,0},{2,3},{3,2},{4,5},{5,4},{6,7},{7,6},{8,9},{9,8},{10,11... | collective-permute-start | bytes 1720328 | tf_op jit(solution)/shard_map/ppermute | solution.py:175
  375.0 9.1 %collective-permute-start.33 = (f32[16,128]{1,0:T(8,128)S(1)}, f32[16,128]{1,0:T(8,128)S(1)}, u32[]{:S(2)}, u32[]{:S(2)}) collective-permute-start(f32[16,128]{1,0:T(8,128)S(1)} %bitcast.326), channel_id=1, source_target_pairs={{0,1},{1,0},{2,3},{3,2},{4,5},{5,4},{6,7},{7,6},{8,9},{9,8},{10,11... | collective-permute-start | bytes 24584 | tf_op jit(solution)/shard_map/ppermute | solution.py:175
  394.8 6.0 %collective-permute-start.34 = (f32[416,128]{1,0:T(8,128)S(1)}, f32[416,128]{1,0:T(8,128)S(1)}, u32[]{:S(2)}, u32[]{:S(2)}) collective-permute-start(f32[416,128]{1,0:T(8,128)S(1)} %get-tuple-element.106), channel_id=1, source_target_pairs={{0,16},{16,32},{32,48},{48,0},{64,80},{80,96},{96,112},{112,64},{1... | collective-permute-start | bytes 638984 | tf_op jit(solution)/shard_map/ppermute | solution.py:192
  396.1 4.7 collective-permute-start.36
  400.9 7.7 %collective-permute-start.37 = (f32[832,128]{1,0:T(8,128)S(1)}, f32[832,128]{1,0:T(8,128)S(1)}, u32[]{:S(2)}, u32[]{:S(2)}) collective-permute-start(f32[832,128]{1,0:T(8,128)S(1)} %pad_maximum_fusion.5), channel_id=1, source_target_pairs={{0,48},{16,0},{32,16},{48,32},{64,112},{80,64},{96,80},{112,96},{1... | collective-permute-start | bytes 1277960 | tf_op jit(solution)/shard_map/ppermute | solution.py:196
  403.6 10.8 %collective-permute-start.35 = (f32[832,128]{1,0:T(8,128)S(1)}, f32[832,128]{1,0:T(8,128)S(1)}, u32[]{:S(2)}, u32[]{:S(2)}) collective-permute-start(f32[832,128]{1,0:T(8,128)S(1)} %pad_maximum_fusion.4), channel_id=1, source_target_pairs={{0,16},{16,32},{32,48},{48,0},{64,80},{80,96},{96,112},{112,64},{1... | collective-permute-start | bytes 1277960 | tf_op jit(solution)/shard_map/ppermute | solution.py:196
  415.2 8.8 %collective-permute-start.38 = (f32[832,128]{1,0:T(8,128)}, f32[832,128]{1,0:T(8,128)}, u32[]{:S(2)}, u32[]{:S(2)}) collective-permute-start(f32[832,128]{1,0:T(8,128)} %fusion.76), channel_id=1, source_target_pairs={{0,64},{16,80},{32,96},{48,112},{64,0},{80,16},{96,32},{112,48},{1... | collective-permute-start | bytes 1277960 | tf_op jit(solution)/shard_map/ppermute | solution.py:199
  425.3 8.7 %collective-permute-start.40 = (f32[832,128]{1,0:T(8,128)S(1)}, f32[832,128]{1,0:T(8,128)S(1)}, u32[]{:S(2)}, u32[]{:S(2)}) collective-permute-start(f32[832,128]{1,0:T(8,128)S(1)} %get-tuple-element.62), channel_id=1, source_target_pairs={{0,16},{16,32},{32,48},{48,0},{64,80},{80,96},{96,112},{112,64},{1... | collective-permute-start | bytes 1277960 | tf_op jit(solution)/shard_map/ppermute | solution.py:201
  425.3 8.7 %collective-permute-start.39 = (f32[832,128]{1,0:T(8,128)S(1)}, f32[832,128]{1,0:T(8,128)S(1)}, u32[]{:S(2)}, u32[]{:S(2)}) collective-permute-start(f32[832,128]{1,0:T(8,128)S(1)} %get-tuple-element.62), channel_id=1, source_target_pairs={{0,48},{16,0},{32,16},{48,32},{64,112},{80,64},{96,80},{112,96},{1... | collective-permute-start | bytes 1277960 | tf_op jit(solution)/shard_map/ppermute | solution.py:202
  433.9 6.0 %collective-permute-start.41 = (f32[416,128]{1,0:T(8,128)S(1)}, f32[416,128]{1,0:T(8,128)S(1)}, u32[]{:S(2)}, u32[]{:S(2)}) collective-permute-start(f32[416,128]{1,0:T(8,128)S(1)} %slice.505), channel_id=1, source_target_pairs={{0,16},{16,32},{32,48},{48,0},{64,80},{80,96},{96,112},{112,64},{1... | collective-permute-start | bytes 638984 | tf_op jit(solution)/shard_map/ppermute | solution.py:203
  434.0 5.9 %collective-permute-start.42 = (f32[416,128]{1,0:T(8,128)S(1)}, f32[416,128]{1,0:T(8,128)S(1)}, u32[]{:S(2)}, u32[]{:S(2)}) collective-permute-start(f32[416,128]{1,0:T(8,128)S(1)} %slice.506), channel_id=1, source_target_pairs={{0,48},{16,0},{32,16},{48,32},{64,112},{80,64},{96,80},{112,96},{1... | collective-permute-start | bytes 638984 | tf_op jit(solution)/shard_map/ppermute | solution.py:204
  445.0 23.1 %collective-permute-start.43 = (f32[64,4480]{1,0:T(8,128)}, f32[64,4480]{1,0:T(8,128)}, u32[]{:S(2)}, u32[]{:S(2)}) collective-permute-start(f32[64,4480]{1,0:T(8,128)} %reshape.690), channel_id=1, source_target_pairs={{0,8},{8,0},{1,9},{9,1},{2,10},{10,2},{3,11},{11,3},{4,12},{12,4},... | collective-permute-start | bytes 3440648 | tf_op jit(solution)/shard_map/ppermute | solution.py:246
  461.5 5.5 %collective-permute-start.44 = (f32[128,1024]{1,0:T(8,128)S(1)}, f32[128,1024]{1,0:T(8,128)S(1)}, u32[]{:S(2)}, u32[]{:S(2)}) collective-permute-start(f32[128,1024]{1,0:T(8,128)S(1)} %reshape.692), channel_id=1, source_target_pairs={{0,8},{8,0},{1,9},{9,1},{2,10},{10,2},{3,11},{11,3},{4,12},{12,4},... | collective-permute-start | bytes 1572872 | tf_op jit(solution)/shard_map/ppermute | solution.py:246
  (93 other events, 845.9 us)
Sparse Core Ops, SparseCore 0:
  77.6 52.8 all-gather.2

commit v10 on v9

--- a/solution.py
+++ b/solution.py
@@ -256,9 +256,37 @@
     else:
         part = lax.all_gather(mine, SHARD, axis=0, tiled=False)
     other = core_swap(part)
-    first = jnp.where(core == 0, part, other)
-    second = jnp.where(core == 0, other, part)
-    return jnp.stack([first, second], axis=1).reshape(-1, weight.shape[1])
+    return part.reshape(-1, weight.shape[1]), other.reshape(-1, weight.shape[1])
+
+
+def split_cols(values, groups):
+    core = lax.axis_index("core")
+    blocks = values.reshape(values.shape[0], groups, 2, -1)
+    own = lax.dynamic_index_in_dim(blocks, core, axis=2, keepdims=False)
+    other = lax.dynamic_index_in_dim(blocks, 1 - core, axis=2, keepdims=False)
+    return own.reshape(values.shape[0], -1), other.reshape(values.shape[0], -1)
+
+
+def join_cols(own, other, groups):
+    core = lax.axis_index("core")
+    count = own.shape[0]
+    pair = jnp.stack([own.reshape(count, groups, -1), other.reshape(count, groups, -1)], axis=2)
+    doubled = jnp.concatenate([pair, pair], axis=2)
+    placed = lax.dynamic_slice_in_dim(doubled, core, 2, axis=2)
+    return placed.reshape(count, -1)
+
+
+def halves_product(left, halves, groups):
+    own_l, other_l = split_cols(left, groups)
+    own_w, other_w = halves
+    return jnp.dot(own_l, own_w, preferred_element_type=jnp.float32) + jnp.dot(
+        other_l, other_w, preferred_element_type=jnp.float32
+    )
+
+
+def halves_back(left, halves, groups):
+    own_w, other_w = halves
+    return join_cols(back_product(left, own_w), back_product(left, other_w), groups)
 
 
 def reduce_core(partial):
@@ -266,8 +294,8 @@
     cols = partial.shape[1]
     core = lax.axis_index("core")
     blocks = partial.reshape(groups, 2, -1, cols)
-    keep = jnp.where(core == 0, blocks[:, 0], blocks[:, 1])
-    give = jnp.where(core == 0, blocks[:, 1], blocks[:, 0])
+    keep = lax.dynamic_index_in_dim(blocks, core, axis=1, keepdims=False)
+    give = lax.dynamic_index_in_dim(blocks, 1 - core, axis=1, keepdims=False)
     return keep + core_swap(give)
 
 
@@ -335,7 +363,7 @@
     normed = normed_f.astype(jnp.bfloat16)
     in_whole = gather_rows(in_weight, by_permutes=True)
     out_whole = gather_rows(out_weight)
-    projected = jnp.dot(normed, in_whole, preferred_element_type=jnp.float32)
+    projected = halves_product(normed, in_whole, groups)
 
     def bound_mixer(proj_arg, cw_arg, cb_arg, sb_arg, dl_arg, sk_arg, gg_arg):
         return mixer(proj_arg, segment, cw_arg, cb_arg, sb_arg, dl_arg, sk_arg, gg_arg)
@@ -351,16 +379,16 @@
         gategain_full,
     )
     gated = gated_f.astype(jnp.bfloat16)
-    branch_out = jnp.dot(gated, out_whole, preferred_element_type=jnp.float32)
+    branch_out = halves_product(gated, out_whole, groups)
     layer_out = layer_in + branch_out
     cot_low = cotangent.astype(jnp.bfloat16)
     out_halves = reduce_core(row_product(gated, cot_low))
-    gated_grad = back_product(cot_low, out_whole)
+    gated_grad = halves_back(cot_low, out_whole, groups)
     out_halves, gated_grad = lax.optimization_barrier((out_halves, gated_grad))
     out_group = reduce_group(out_halves)
     proj_grad, g_convw, g_convb, g_stepb, g_decay, g_skip, g_gategain = mixer_back(gated_grad)
     proj_low = proj_grad.astype(jnp.bfloat16)
-    normed_grad = back_product(proj_low, in_whole)
+    normed_grad = halves_back(proj_low, in_whole, groups)
     back_in, g_norm = norm_back(normed_grad)
     input_grad = cotangent + back_in
     grads = (g_norm, g_convw, g_convb, g_stepb, g_decay, g_skip, g_gategain)

time: 487 us -> 458 us (0.940)
  other arithmetic: 119 us -> 86.2 us
  waiting for transfers between devices: 131 us -> 121 us
  local copies, waits for them, and re-layouts: 74.2 us -> 81.4 us
    another operation x10 -> x6, other arithmetic: 22.8 us -> 3.54 us  [the longest x4 19.4 us: gather_rows(): return jnp.stack([first, second], axis=1).reshape(-1, weight.shape[1])]
    select_n x2 -> x0, other arithmetic: 14.3 us -> none  [reduce_core(): give = jnp.where(core == 0, blocks[:, 1], blocks[:, 0])]
    squeeze x0 -> x2, local copies, waits for them, and re-layouts: none -> 10.5 us  [reduce_core(): give = lax.dynamic_index_in_dim(blocks, 1 - core, axis=1, keepdims=False)]
    another operation x13 -> x12, local copies, waits for them, and re-layouts: 9.97 us -> 4.44 us  [the longest x1 8.02 us: gather_rows(): return jnp.stack([first, second], axis=1).reshape(-1, weight.shape[1])]
    ppermute x7, waiting for transfers between devices: 9.4 us -> 4.26 us  [core_swap(): return lax.ppermute(values, 'core', [(0, 1), (1, 0)])]
    dot_general x2 -> x4, matrix products: 9.83 us -> 12.7 us  [back_product(): lax.dot_general(left, right, (((1,), (1,)), ((), ())), preferred_element_...]
    unnamed x203 -> x218, local copies, waits for them, and re-layouts: 22.6 us -> 25.2 us
    dot_general x2 -> x4, matrix products: 12 us -> 12.5 us  [the longest x2 7.52 us: halves_product(): jnp.dot(other_l, other_w, preferred_element_type=jnp.float32)]
  transfers between devices with their start and end apart: 46 -> 46, of which waited for: 20 -> 20; matrix products, arithmetic and copies ran while one was open for 31% -> 30% of each run, Pallas kernels for 0% -> 0%
where the time goes in v10:
time: 458 us; the launch traced here: 451 us
  waiting for transfers between devices  121 us (26%)
  other arithmetic  86.2 us (19%)
  local copies, waits for them, and re-layouts  81.4 us (18%)
  starting transfers between devices  75.1 us (16%)
  matrix products  70.9 us (15%)
  between operations  16.4 us (4%)
    ppermute x18, waiting for transfers between devices, send(): lax.ppermute(p.astype(w), 'shard_0', pairs)  37.6 us
    dot_general x3, matrix products, mixer(): y_intra = jnp.einsum('chij,cjhp->cihp', mixing, scaled_in, precision=HIGH)  32.6 us
    unnamed x218, local copies, waits for them, and re-layouts  25.2 us
    ppermute x7, starting transfers between devices, core_swap(): return lax.ppermute(values, 'core', [(0, 1), (1, 0)])  23.4 us
    ppermute x1, waiting for transfers between devices, gather_group(): from_prev = lax.ppermute(pair, 'shard_0', up)  22.7 us
    ppermute x18, starting transfers between devices, send(): lax.ppermute(p.astype(w), 'shard_0', pairs)  20.2 us
    add x2, other arithmetic, reduce_core(): return keep + core_swap(give)  16 us
    dot_general x4, matrix products, back_product(): lax.dot_general(left, right, (((1,), (1,)), ((), ())), preferred_element_...  12.7 us
  transfers between devices with their start and end apart: 46, of which 20 were waited for; matrix products, arithmetic and copies ran while one was open for 30% of the time, Pallas kernels for 0%

profile of v10, /device:TPU:1, one launch (start us, length us, event | category | flops | bytes accessed | tf_op | source)
XLA Modules:
  0.0 451.4 jit_solution(11867109565638739128)
XLA Ops:
  12.0 12.3 %collective-permute-done.3 = bf16[64,4384]{1,0:T(8,128)(2,1)S(1)} collective-permute-done((bf16[64,4384]{1,0:T(8,128)(2,1)S(1)}, bf16[64,4384]{1,0:T(8,128)(2,1)S(1)}, u32[]{:S(2)}, u32[]{:S(2)}) %collective-permute-start.3) | collective-permute-done | bytes 561184 | tf_op jit(solution)/shard_map/ppermute | solution.py:228
  31.9 22.7 %collective-permute-done.5 = bf16[2,64,4384]{2,1,0:T(8,128)(2,1)S(1)} collective-permute-done((bf16[2,64,4384]{2,1,0:T(8,128)(2,1)}, bf16[2,64,4384]{2,1,0:T(8,128)(2,1)S(1)}, u32[]{:S(2)}, u32[]{:S(2)}) %collective-permute-start.5) | collective-permute-done | bytes 1122336 | tf_op jit(solution)/shard_map/ppermute | solution.py:232
  54.8 2.7 collective-permute-start.7
  57.7 10.5 %collective-permute-done.6 = bf16[2,32,4384]{2,1,0:T(8,128)(2,1)S(1)} collective-permute-done((bf16[2,32,4384]{2,1,0:T(8,128)(2,1)S(1)}, bf16[2,32,4384]{2,1,0:T(8,128)(2,1)S(1)}, u32[]{:S(2)}, u32[]{:S(2)}) %collective-permute-start.6) | collective-permute-done | bytes 561184 | tf_op jit(solution)/shard_map/ppermute | solution.py:235
  71.9 3.1 collective-permute-start.8
  79.4 2.9 collective-permute-done.1
  82.4 2.7 collective-permute-start.2
  92.8 4.2 fusion.139
  97.0 4.2 convolution_add_fusion
  111.5 4.9 %fusion.21 = (f32[256,2304]{0,1:T(8,128)S(1)}, f32[256,2304]{0,1:T(8,128)}) fusion(f32[253,2304]{0,1:T(8,128)S(1)} %slice.426, f32[2304]{0:T(1024)S(1)} %get-tuple-element.58, pred[256]{0:T(512)(128)(4,1)S(1)} %get-tuple-element.136, f32[254,2304]{0,1:T(8,128)S(1)} %slice.424, f32[2304]{0:T(1024)S(1)} %get-tuple-element.59, ...), kind=kLoop, calls=%fused_computation.54 | loop fusion | flops 8847360 | bytes 14147328 | tf_op jit(solution)/shard_map/jvp(jit(silu))/mul | solution.py:110
  123.4 11.9 %fusion.33 = f32[256,32,64]{0,2,1:T(8,128)S(1)} fusion(f32[256,32,64]{0,2,1:T(8,128)} %bitcast.318, f32[256,32,64]{0,2,1:T(8,128)S(1)} %fusion.87, f32[32]{0:T(128)} %mul.425, f32[256,32]{0,1:T(8,128)S(1)} %bitcast_multiply_fusion.6, f32[256,256]{1,0:T(8,128)S(1)} %fusion.101, f32[32,256]{1,0:T(8,128)S(1)} %bitcast_add_fusion.4, ...), kind=kOutput, calls=%fused_computation.77 | convolution fusion | flops 1619525632 | bytes 6717568 | tf_op jit(solution)/shard_map/jvp(chij,cjhp->cihp)/dot_general | solution.py:132
  135.3 3.1 multiply_reduce_fusion.9
  146.4 3.0 collective-permute-start.10
  152.5 2.8 fusion.123
  155.3 4.2 collective-permute-done.9
  162.6 5.3 %bitcast_add_fusion.1 = f32[8,128,1024]{2,1,0:T(8,128)} fusion(f32[8,128,1024]{2,1,0:T(8,128)} %collective-permute-done.10, f32[8,2,128,1024]{3,2,1,0:T(8,128)S(1)} %bitcast.293, s32[]{:T(128)S(6)} %select_n.161), kind=kLoop, calls=%fused_computation.22 | loop fusion | flops 1048576 | bytes 12582916 | tf_op jit(solution)/shard_map/add | solution.py:299
  169.5 5.1 %multiply_reduce_fusion.6 = (f32[2048]{0:T(1024)}, f32[256,2048]{0,1:T(8,128)S(1)}, f32[256,2048]{0,1:T(8,128)}) fusion(f32[256,2304]{0,1:T(8,128)S(1)} %copy-done.7, f32[256,4384]{0,1:T(8,128)} %copy-done.2, f32[256,2048]{0,1:T(8,128)} %copy-done.5, f32[256]{0:T(256)S(1)} %multiply_multiply_fusion.1, f32[256]{0:T(256)S(1)} %copy-done.72, ...), kind=kLoop, calls=%fused_computation.85 | loop fusion | flops 9959424 | bytes 14698496 | tf_op jit(solution)/shard_map/transpose(jvp())/reduce_sum | solution.py:139
  176.5 12.0 %fusion.7 = (f32[32,256]{1,0:T(8,128)S(1)}, f32[32,256]{1,0:T(8,128)S(1)}, f32[256,256]{1,0:T(8,128)S(1)}) fusion(f32[256,256]{1,0:T(8,128)S(1)} %fusion.101, f32[32,256]{1,0:T(8,128)S(1)} %copy-done.67, pred[256,256]{1,0:T(8,128)(4,1)S(1)} %copy-done.61, f32[32,64,256]{2,1,0:T(8,128)S(1)} %bitcast.296, f32[256,32,64]{0,2,1:T(8,128)S(1)} %bitcast.319, ...), kind=kOutput, calls=%fused_computation.15 | convolution fusion | flops 1629929472 | bytes 4915200 | tf_op jit(solution)/shard_map/transpose(jvp(chij,cjhp->cihp))/dot_general | solution.py:132
  188.5 8.8 %fusion.34 = (f32[256,32]{0,1:T(8,128)}, f32[1,256,32,64]{1,3,2,0:T(8,128)}) fusion(f32[1,256,32,64]{1,3,2,0:T(8,128)S(1)} %bitcast.320, f32[256,32]{0,1:T(8,128)S(1)} %copy-done.49, f32[32,64,256]{2,1,0:T(8,128)S(1)} %bitcast.297, f32[256,256]{1,0:T(8,128)S(1)} %fusion.101, f32[32,256]{1,0:T(8,128)S(1)} %copy-done.67, pred[256,256]{1,0:T(8,128)(4,1)S(1)} %copy-done.61), kind=kOutput, calls=%fused_computation.81 | convolution fusion | flops 1618468864 | bytes 6717440 | tf_op jit(solution)/shard_map/transpose(jvp(chij,cjhp->cihp))/dot_general | solution.py:132
  205.9 2.8 multiply_reduce_fusion.4
  217.3 7.7 %fusion.22 = f32[1024,4480]{1,0:T(8,128)} fusion(bf16[256,1024]{0,1:T(8,128)(2,1)S(1)} %copy-done.39, bf16[256,4384]{0,1:T(8,128)(2,1)S(1)} %add_convert_fusion), kind=kOutput, calls=%fused_computation.61 | convolution fusion | flops 2348810240 | bytes 21118976 | tf_op jit(solution)/shard_map/dot_general | solution.py:76
  225.1 7.9 %dynamic-slice_bitcast_fusion = f32[8,64,4480]{2,1,0:T(8,128)} fusion(f32[8,2,64,4480]{3,2,1,0:T(8,128)} %bitcast.288, s32[]{:T(128)S(6)} %select_n.169), kind=kLoop, calls=%fused_computation.4 | loop fusion | bytes 18350084 | tf_op jit(solution)/shard_map/jit(dynamic_index_in_dim)/squeeze | solution.py:298
  234.2 3.7 fusion.43
  237.9 3.7 fusion.46
  244.0 3.2 fusion.8
  251.3 2.8 collective-permute-start.22
  254.2 2.7 collective-permute-start.30
  257.0 10.7 %bitcast_add_fusion = f32[8,64,4480]{2,1,0:T(8,128)} fusion(f32[8,64,4480]{2,1,0:T(8,128)} %collective-permute-done.11, f32[8,2,64,4480]{3,2,1,0:T(8,128)} %bitcast.289, s32[]{:T(128)S(6)} %select_n.161), kind=kLoop, calls=%fused_computation.3 | loop fusion | flops 2293760 | bytes 27525124 | tf_op jit(solution)/shard_map/add | solution.py:299
  267.7 8.2 %fusion = f32[4,2,64,4480]{3,2,1,0:T(8,128)} fusion(s32[]{:T(128)S(6)} %select_n.183, f32[4,2,64,4480]{3,2,1,0:T(8,128)} %bitcast.294), kind=kLoop, calls=%fused_computation.2 | loop fusion | flops 2293760 | bytes 18350084 | tf_op jit(solution)/shard_map/concatenate | solution.py:155
  276.0 5.7 %slice_bitcast_fusion.3 = (f32[2,64,4480]{2,1,0:T(8,128)S(1)}, f32[2,64,4480]{2,1,0:T(8,128)S(1)}, f32[2,64,4480]{2,1,0:T(8,128)S(1)}, f32[2,64,4480]{2,1,0:T(8,128)}) fusion(f32[4,2,64,4480]{3,2,1,0:T(8,128)} %fusion), kind=kLoop, calls=%fused_computation.60 | loop fusion | bytes 18350080 | tf_op jit(solution)/shard_map/squeeze | solution.py:162
  286.9 10.8 %collective-permute-done.31 = f32[2,8,128]{2,0,1:T(2,128)S(1)} collective-permute-done((f32[2,8,128]{2,0,1:T(2,128)S(1)}, f32[2,8,128]{2,0,1:T(2,128)S(1)}, u32[]{:S(2)}, u32[]{:S(2)}) %collective-permute-start.31) | collective-permute-done | bytes 8224 | tf_op jit(solution)/shard_map/ppermute | solution.py:160
  301.1 2.7 collective-permute-start.23
  305.5 2.7 collective-permute-start.16
  308.4 2.7 collective-permute-start.24
  311.3 8.9 %collective-permute-done.16 = bf16[2,32,4480]{2,1,0:T(8,128)(2,1)S(1)} collective-permute-done((bf16[2,32,4480]{2,1,0:T(8,128)(2,1)S(1)}, bf16[2,32,4480]{2,1,0:T(8,128)(2,1)S(1)}, u32[]{:S(2)}, u32[]{:S(2)}) %collective-permute-start.16) | collective-permute-done | bytes 573472 | tf_op jit(solution)/shard_map/ppermute | solution.py:160
  320.4 11.5 %collective-permute-done.13 = bf16[2,32,4480]{2,1,0:T(8,128)(2,1)S(1)} collective-permute-done((bf16[2,32,4480]{2,1,0:T(8,128)(2,1)S(1)}, bf16[2,32,4480]{2,1,0:T(8,128)(2,1)S(1)}, u32[]{:S(2)}, u32[]{:S(2)}) %collective-permute-start.13) | collective-permute-done | bytes 573472 | tf_op jit(solution)/shard_map/ppermute | solution.py:160
  336.8 4.1 collective-permute-done.17
  346.4 8.9 %collective-permute-done.33 = f32[16,128]{1,0:T(8,128)S(1)} collective-permute-done((f32[16,128]{1,0:T(8,128)S(1)}, f32[16,128]{1,0:T(8,128)S(1)}, u32[]{:S(2)}, u32[]{:S(2)}) %collective-permute-start.33) | collective-permute-done | bytes 8224 | tf_op jit(solution)/shard_map/ppermute | solution.py:175
  366.1 3.2 collective-permute-done.34
  375.0 5.2 %collective-permute-done.37 = f32[832,128]{1,0:T(8,128)} collective-permute-done((f32[832,128]{1,0:T(8,128)}, f32[832,128]{1,0:T(8,128)}, u32[]{:S(2)}, u32[]{:S(2)}) %collective-permute-start.37) | collective-permute-done | bytes 426016 | tf_op jit(solution)/shard_map/ppermute | solution.py:196
  380.2 3.1 collective-permute-done.35
  384.6 2.8 collective-permute-start.38
  389.5 3.7 collective-permute-done.38
  393.3 2.7 collective-permute-start.39
  396.0 3.3 fusion.42
  401.6 3.2 collective-permute-start.42
  404.9 2.6 collective-permute-done.41
  411.8 16.0 %collective-permute-start.43 = (f32[64,4480]{1,0:T(8,128)S(1)}, f32[64,4480]{1,0:T(8,128)}, u32[]{:S(2)}, u32[]{:S(2)}) collective-permute-start(f32[64,4480]{1,0:T(8,128)S(1)} %reshape.732), channel_id=1, source_target_pairs={{0,8},{8,0},{1,9},{9,1},{2,10},{10,2},{3,11},{11,3},{4,12},{12,4},... | collective-permute-start | bytes 3440648 | tf_op jit(solution)/shard_map/ppermute | solution.py:246
  (458 shorter events, 151.0 us)
Async XLA Ops:
  7.2 142.2 %all-gather.3.cloned.1.call-start = ((), (), s32[]{:S(2)}) async-start(), calls=%async_computation | async-start | bytes 2359296 | tf_op jit(solution)/shard_map/all_gather | solution.py:257
  9.8 14.5 %collective-permute-start.3 = (bf16[64,4384]{1,0:T(8,128)(2,1)S(1)}, bf16[64,4384]{1,0:T(8,128)(2,1)S(1)}, u32[]{:S(2)}, u32[]{:S(2)}) collective-permute-start(bf16[64,4384]{1,0:T(8,128)(2,1)S(1)} %copy.115), channel_id=1, source_target_pairs={{0,1},{1,0},{2,3},{3,2},{4,5},{5,4},{6,7},{7,6},{8,9},{9,8},{10,11... | collective-permute-start | bytes 1683464 | tf_op jit(solution)/shard_map/ppermute | solution.py:228
  26.4 28.3 %collective-permute-start.5 = (bf16[2,64,4384]{2,1,0:T(8,128)(2,1)}, bf16[2,64,4384]{2,1,0:T(8,128)(2,1)S(1)}, u32[]{:S(2)}, u32[]{:S(2)}) collective-permute-start(bf16[2,64,4384]{2,1,0:T(8,128)(2,1)} %maximum_select_fusion.1), channel_id=1, source_target_pairs={{0,2},{2,4},{4,6},{6,0},{1,3},{3,5},{5,7},{7,1},{8,10},{10,12},{12... | collective-permute-start | bytes 3366920 | tf_op jit(solution)/shard_map/ppermute | solution.py:232
  28.3 26.5 %collective-permute-start.4 = (bf16[2,64,4384]{2,1,0:T(8,128)(2,1)}, bf16[2,64,4384]{2,1,0:T(8,128)(2,1)S(1)}, u32[]{:S(2)}, u32[]{:S(2)}) collective-permute-start(bf16[2,64,4384]{2,1,0:T(8,128)(2,1)} %maximum_select_fusion.1), channel_id=1, source_target_pairs={{0,6},{2,0},{4,2},{6,4},{1,7},{3,1},{5,3},{7,5},{8,14},{10,8},{12,... | collective-permute-start | bytes 3366920 | tf_op jit(solution)/shard_map/ppermute | solution.py:233
  54.7 13.6 %collective-permute-start.6 = (bf16[2,32,4384]{2,1,0:T(8,128)(2,1)S(1)}, bf16[2,32,4384]{2,1,0:T(8,128)(2,1)S(1)}, u32[]{:S(2)}, u32[]{:S(2)}) collective-permute-start(bf16[2,32,4384]{2,1,0:T(8,128)(2,1)S(1)} %slice.418), channel_id=1, source_target_pairs={{0,2},{2,4},{4,6},{6,0},{1,3},{3,5},{5,7},{7,1},{8,10},{10,12},{12... | collective-permute-start | bytes 1683464 | tf_op jit(solution)/shard_map/ppermute | solution.py:235
  54.8 13.4 %collective-permute-start.7 = (bf16[2,32,4384]{2,1,0:T(8,128)(2,1)S(1)}, bf16[2,32,4384]{2,1,0:T(8,128)(2,1)S(1)}, u32[]{:S(2)}, u32[]{:S(2)}) collective-permute-start(bf16[2,32,4384]{2,1,0:T(8,128)(2,1)S(1)} %slice.419), channel_id=1, source_target_pairs={{0,6},{2,0},{4,2},{6,4},{1,7},{3,1},{5,3},{7,5},{8,14},{10,8},{12,... | collective-permute-start | bytes 1683464 | tf_op jit(solution)/shard_map/ppermute | solution.py:236
  71.9 21.0 %collective-permute-start.8 = (bf16[8,64,4384]{2,1,0:T(8,128)(2,1)}, bf16[8,64,4384]{2,1,0:T(8,128)(2,1)}, u32[]{:S(2)}, u32[]{:S(2)}) collective-permute-start(bf16[8,64,4384]{2,1,0:T(8,128)(2,1)} %bitcast.12), channel_id=1, source_target_pairs={{0,8},{8,0},{1,9},{9,1},{2,10},{10,2},{3,11},{11,3},{4,12},{12,4},... | collective-permute-start | bytes 13467656 | tf_op jit(solution)/shard_map/ppermute | solution.py:246
  75.5 3.7 collective-permute-start
  79.1 30.6 %copy-start.81 = (pred[256]{0:T(512)(128)(4,1)}, pred[256]{0:T(512)(128)(4,1)S(1)}, u32[]{:S(2)}) copy-start(pred[256]{0:T(512)(128)(4,1)S(1)} %get-tuple-element.135) | copy-start | bytes 772
  79.1 30.6 %copy-start.83 = (pred[256]{0:T(512)(128)(4,1)}, pred[256]{0:T(512)(128)(4,1)S(1)}, u32[]{:S(2)}) copy-start(pred[256]{0:T(512)(128)(4,1)S(1)} %get-tuple-element.136) | copy-start | bytes 772
  79.2 3.1 collective-permute-start.1
  82.4 4.8 %collective-permute-start.2 = (f32[8,1836]{1,0:T(8,128)S(1)}, f32[8,1836]{1,0:T(8,128)S(1)}, u32[]{:S(2)}, u32[]{:S(2)}) collective-permute-start(f32[8,1836]{1,0:T(8,128)S(1)} %fusion.159), channel_id=1, source_target_pairs={{0,4},{2,6},{4,0},{6,2},{1,5},{3,7},{5,1},{7,3},{8,12},{10,14},{12... | collective-permute-start | bytes 176264 | tf_op jit(solution)/shard_map/ppermute | solution.py:324
  146.4 16.1 %collective-permute-start.10 = (f32[8,128,1024]{2,1,0:T(8,128)}, f32[8,128,1024]{2,1,0:T(8,128)}, u32[]{:S(2)}, u32[]{:S(2)}) collective-permute-start(f32[8,128,1024]{2,1,0:T(8,128)} %dynamic-slice_bitcast_fusion.1), channel_id=1, source_target_pairs={{0,8},{8,0},{1,9},{9,1},{2,10},{10,2},{3,11},{11,3},{4,12},{12,4},... | collective-permute-start | bytes 12582920 | tf_op jit(solution)/shard_map/ppermute | solution.py:246
  149.4 10.1 %collective-permute-start.9 = (bf16[8,128,1024]{2,1,0:T(8,128)(2,1)}, bf16[8,128,1024]{2,1,0:T(8,128)(2,1)}, u32[]{:S(2)}, u32[]{:S(2)}) collective-permute-start(bf16[8,128,1024]{2,1,0:T(8,128)(2,1)} %bitcast.301), channel_id=1, source_target_pairs={{0,8},{8,0},{1,9},{9,1},{2,10},{10,2},{3,11},{11,3},{4,12},{12,4},... | collective-permute-start | bytes 6291464 | tf_op jit(solution)/shard_map/ppermute | solution.py:246
  233.0 24.0 %collective-permute-start.11 = (f32[8,64,4480]{2,1,0:T(8,128)}, f32[8,64,4480]{2,1,0:T(8,128)}, u32[]{:S(2)}, u32[]{:S(2)}) collective-permute-start(f32[8,64,4480]{2,1,0:T(8,128)} %dynamic-slice_bitcast_fusion), channel_id=1, source_target_pairs={{0,8},{8,0},{1,9},{9,1},{2,10},{10,2},{3,11},{11,3},{4,12},{12,4},... | collective-permute-start | bytes 27525128 | tf_op jit(solution)/shard_map/ppermute | solution.py:246
  243.8 10.3 %collective-permute-start.26 = (f32[8,16,128]{2,0,1:T(8,128)S(1)}, f32[8,16,128]{2,0,1:T(8,128)S(1)}, u32[]{:S(2)}, u32[]{:S(2)}) collective-permute-start(f32[8,16,128]{2,0,1:T(8,128)S(1)} %pad_bitcast_fusion), channel_id=1, source_target_pairs={{0,8},{8,0},{1,9},{9,1},{2,10},{10,2},{3,11},{11,3},{4,12},{12,4},... | collective-permute-start | bytes 196616 | tf_op jit(solution)/shard_map/ppermute | solution.py:246
  251.3 48.0 %collective-permute-start.22 = (bf16[2,64,1024]{2,1,0:T(8,128)(2,1)}, bf16[2,64,1024]{2,1,0:T(8,128)(2,1)}, u32[]{:S(2)}, u32[]{:S(2)}) collective-permute-start(bf16[2,64,1024]{2,1,0:T(8,128)(2,1)} %slice.603), channel_id=1, source_target_pairs={{0,6},{2,0},{4,2},{6,4},{1,7},{3,1},{5,3},{7,5},{8,14},{10,8},{12,... | collective-permute-start | bytes 786440 | tf_op jit(solution)/shard_map/ppermute | solution.py:160
  254.1 45.5 %collective-permute-start.19 = (bf16[2,64,1024]{2,1,0:T(8,128)(2,1)}, bf16[2,64,1024]{2,1,0:T(8,128)(2,1)}, u32[]{:S(2)}, u32[]{:S(2)}) collective-permute-start(bf16[2,64,1024]{2,1,0:T(8,128)(2,1)} %slice.604), channel_id=1, source_target_pairs={{0,2},{2,4},{4,6},{6,0},{1,3},{3,5},{5,7},{7,1},{8,10},{10,12},{12... | collective-permute-start | bytes 786440 | tf_op jit(solution)/shard_map/ppermute | solution.py:160
  254.2 31.3 %collective-permute-start.30 = (f32[2,8,128]{2,0,1:T(2,128)S(1)}, f32[2,8,128]{2,0,1:T(2,128)S(1)}, u32[]{:S(2)}, u32[]{:S(2)}) collective-permute-start(f32[2,8,128]{2,0,1:T(2,128)S(1)} %slice.470), channel_id=1, source_target_pairs={{0,6},{2,0},{4,2},{6,4},{1,7},{3,1},{5,3},{7,5},{8,14},{10,8},{12,... | collective-permute-start | bytes 24584 | tf_op jit(solution)/shard_map/ppermute | solution.py:160
  284.1 19.7 %collective-permute-start.15 = (bf16[2,32,4480]{2,1,0:T(8,128)(2,1)}, bf16[2,32,4480]{2,1,0:T(8,128)(2,1)}, u32[]{:S(2)}, u32[]{:S(2)}) collective-permute-start(bf16[2,32,4480]{2,1,0:T(8,128)(2,1)} %slice.601), channel_id=1, source_target_pairs={{0,6},{2,0},{4,2},{6,4},{1,7},{3,1},{5,3},{7,5},{8,14},{10,8},{12,... | collective-permute-start | bytes 1720328 | tf_op jit(solution)/shard_map/ppermute | solution.py:160
  284.2 19.6 %collective-permute-start.12 = (bf16[2,32,4480]{2,1,0:T(8,128)(2,1)}, bf16[2,32,4480]{2,1,0:T(8,128)(2,1)}, u32[]{:S(2)}, u32[]{:S(2)}) collective-permute-start(bf16[2,32,4480]{2,1,0:T(8,128)(2,1)} %slice.602), channel_id=1, source_target_pairs={{0,2},{2,4},{4,6},{6,0},{1,3},{3,5},{5,7},{7,1},{8,10},{10,12},{12... | collective-permute-start | bytes 1720328 | tf_op jit(solution)/shard_map/ppermute | solution.py:160
  285.6 12.2 %collective-permute-start.31 = (f32[2,8,128]{2,0,1:T(2,128)S(1)}, f32[2,8,128]{2,0,1:T(2,128)S(1)}, u32[]{:S(2)}, u32[]{:S(2)}) collective-permute-start(f32[2,8,128]{2,0,1:T(2,128)S(1)} %slice_add_fusion.15), channel_id=1, source_target_pairs={{0,6},{2,0},{4,2},{6,4},{1,7},{3,1},{5,3},{7,5},{8,14},{10,8},{12,... | collective-permute-start | bytes 24584 | tf_op jit(solution)/shard_map/ppermute | solution.py:160
  297.8 48.5 %collective-permute-start.32 = (f32[2,8,128]{2,0,1:T(2,128)S(1)}, f32[2,8,128]{2,0,1:T(2,128)S(1)}, u32[]{:S(2)}, u32[]{:S(2)}) collective-permute-start(f32[2,8,128]{2,0,1:T(2,128)S(1)} %get-tuple-element.131), channel_id=1, source_target_pairs={{0,6},{2,0},{4,2},{6,4},{1,7},{3,1},{5,3},{7,5},{8,14},{10,8},{12,... | collective-permute-start | bytes 24584 | tf_op jit(solution)/shard_map/ppermute | solution.py:160
  299.3 8.9 %collective-permute-start.27 = (f32[2,8,128]{2,0,1:T(2,128)S(1)}, f32[2,8,128]{2,0,1:T(2,128)S(1)}, u32[]{:S(2)}, u32[]{:S(2)}) collective-permute-start(f32[2,8,128]{2,0,1:T(2,128)S(1)} %get-tuple-element.132), channel_id=1, source_target_pairs={{0,2},{2,4},{4,6},{6,0},{1,3},{3,5},{5,7},{7,1},{8,10},{10,12},{12... | collective-permute-start | bytes 24584 | tf_op jit(solution)/shard_map/ppermute | solution.py:160
  301.1 7.2 %collective-permute-start.23 = (bf16[2,64,1024]{2,1,0:T(8,128)(2,1)S(1)}, bf16[2,64,1024]{2,1,0:T(8,128)(2,1)S(1)}, u32[]{:S(2)}, u32[]{:S(2)}) collective-permute-start(bf16[2,64,1024]{2,1,0:T(8,128)(2,1)S(1)} %get-tuple-element.110), channel_id=1, source_target_pairs={{0,6},{2,0},{4,2},{6,4},{1,7},{3,1},{5,3},{7,5},{8,14},{10,8},{12,... | collective-permute-start | bytes 786440 | tf_op jit(solution)/shard_map/ppermute | solution.py:160
  303.8 7.3 %collective-permute-start.20 = (bf16[2,64,1024]{2,1,0:T(8,128)(2,1)S(1)}, bf16[2,64,1024]{2,1,0:T(8,128)(2,1)S(1)}, u32[]{:S(2)}, u32[]{:S(2)}) collective-permute-start(bf16[2,64,1024]{2,1,0:T(8,128)(2,1)S(1)} %get-tuple-element.111), channel_id=1, source_target_pairs={{0,2},{2,4},{4,6},{6,0},{1,3},{3,5},{5,7},{7,1},{8,10},{10,12},{12... | collective-permute-start | bytes 786440 | tf_op jit(solution)/shard_map/ppermute | solution.py:160
  305.5 14.7 %collective-permute-start.16 = (bf16[2,32,4480]{2,1,0:T(8,128)(2,1)S(1)}, bf16[2,32,4480]{2,1,0:T(8,128)(2,1)S(1)}, u32[]{:S(2)}, u32[]{:S(2)}) collective-permute-start(bf16[2,32,4480]{2,1,0:T(8,128)(2,1)S(1)} %get-tuple-element.96), channel_id=1, source_target_pairs={{0,6},{2,0},{4,2},{6,4},{1,7},{3,1},{5,3},{7,5},{8,14},{10,8},{12,... | collective-permute-start | bytes 1720328 | tf_op jit(solution)/shard_map/ppermute | solution.py:160
  308.2 25.0 %collective-permute-start.28 = (f32[2,8,128]{2,0,1:T(2,128)S(1)}, f32[2,8,128]{2,0,1:T(2,128)S(1)}, u32[]{:S(2)}, u32[]{:S(2)}) collective-permute-start(f32[2,8,128]{2,0,1:T(2,128)S(1)} %slice_add_fusion.18), channel_id=1, source_target_pairs={{0,2},{2,4},{4,6},{6,0},{1,3},{3,5},{5,7},{7,1},{8,10},{10,12},{12... | collective-permute-start | bytes 24584 | tf_op jit(solution)/shard_map/ppermute | solution.py:160
  308.4 25.2 %collective-permute-start.24 = (bf16[2,64,1024]{2,1,0:T(8,128)(2,1)S(1)}, bf16[2,64,1024]{2,1,0:T(8,128)(2,1)S(1)}, u32[]{:S(2)}, u32[]{:S(2)}) collective-permute-start(bf16[2,64,1024]{2,1,0:T(8,128)(2,1)S(1)} %fusion.82), channel_id=1, source_target_pairs={{0,6},{2,0},{4,2},{6,4},{1,7},{3,1},{5,3},{7,5},{8,14},{10,8},{12,... | collective-permute-start | bytes 786440 | tf_op jit(solution)/shard_map/ppermute | solution.py:160
  311.2 22.5 %collective-permute-start.21 = (bf16[2,64,1024]{2,1,0:T(8,128)(2,1)S(1)}, bf16[2,64,1024]{2,1,0:T(8,128)(2,1)S(1)}, u32[]{:S(2)}, u32[]{:S(2)}) collective-permute-start(bf16[2,64,1024]{2,1,0:T(8,128)(2,1)S(1)} %fusion.84), channel_id=1, source_target_pairs={{0,2},{2,4},{4,6},{6,0},{1,3},{3,5},{5,7},{7,1},{8,10},{10,12},{12... | collective-permute-start | bytes 786440 | tf_op jit(solution)/shard_map/ppermute | solution.py:160
  320.2 11.7 %collective-permute-start.13 = (bf16[2,32,4480]{2,1,0:T(8,128)(2,1)S(1)}, bf16[2,32,4480]{2,1,0:T(8,128)(2,1)S(1)}, u32[]{:S(2)}, u32[]{:S(2)}) collective-permute-start(bf16[2,32,4480]{2,1,0:T(8,128)(2,1)S(1)} %get-tuple-element.97), channel_id=1, source_target_pairs={{0,2},{2,4},{4,6},{6,0},{1,3},{3,5},{5,7},{7,1},{8,10},{10,12},{12... | collective-permute-start | bytes 1720328 | tf_op jit(solution)/shard_map/ppermute | solution.py:160
  331.9 9.0 %collective-permute-start.17 = (bf16[2,32,4480]{2,1,0:T(8,128)(2,1)S(1)}, bf16[2,32,4480]{2,1,0:T(8,128)(2,1)S(1)}, u32[]{:S(2)}, u32[]{:S(2)}) collective-permute-start(bf16[2,32,4480]{2,1,0:T(8,128)(2,1)S(1)} %fusion.54), channel_id=1, source_target_pairs={{0,6},{2,0},{4,2},{6,4},{1,7},{3,1},{5,3},{7,5},{8,14},{10,8},{12,... | collective-permute-start | bytes 1720328 | tf_op jit(solution)/shard_map/ppermute | solution.py:160
  333.2 9.8 %collective-permute-start.14 = (bf16[2,32,4480]{2,1,0:T(8,128)(2,1)S(1)}, bf16[2,32,4480]{2,1,0:T(8,128)(2,1)S(1)}, u32[]{:S(2)}, u32[]{:S(2)}) collective-permute-start(bf16[2,32,4480]{2,1,0:T(8,128)(2,1)S(1)} %fusion.56), channel_id=1, source_target_pairs={{0,2},{2,4},{4,6},{6,0},{1,3},{3,5},{5,7},{7,1},{8,10},{10,12},{12... | collective-permute-start | bytes 1720328 | tf_op jit(solution)/shard_map/ppermute | solution.py:160
  333.6 12.7 %collective-permute-start.29 = (f32[2,8,128]{2,0,1:T(2,128)S(1)}, f32[2,8,128]{2,0,1:T(2,128)S(1)}, u32[]{:S(2)}, u32[]{:S(2)}) collective-permute-start(f32[2,8,128]{2,0,1:T(2,128)S(1)} %slice_add_fusion.17), channel_id=1, source_target_pairs={{0,2},{2,4},{4,6},{6,0},{1,3},{3,5},{5,7},{7,1},{8,10},{10,12},{12... | collective-permute-start | bytes 24584 | tf_op jit(solution)/shard_map/ppermute | solution.py:160
  334.7 20.7 %collective-permute-start.25 = (bf16[128,1024]{1,0:T(8,128)(2,1)}, bf16[128,1024]{1,0:T(8,128)(2,1)}, u32[]{:S(2)}, u32[]{:S(2)}) collective-permute-start(bf16[128,1024]{1,0:T(8,128)(2,1)} %fusion.93), channel_id=1, source_target_pairs={{0,1},{1,0},{2,3},{3,2},{4,5},{5,4},{6,7},{7,6},{8,9},{9,8},{10,11... | collective-permute-start | bytes 786440 | tf_op jit(solution)/shard_map/ppermute | solution.py:175
  344.2 15.1 %collective-permute-start.18 = (bf16[64,4480]{1,0:T(8,128)(2,1)}, bf16[64,4480]{1,0:T(8,128)(2,1)}, u32[]{:S(2)}, u32[]{:S(2)}) collective-permute-start(bf16[64,4480]{1,0:T(8,128)(2,1)} %fusion.76), channel_id=1, source_target_pairs={{0,1},{1,0},{2,3},{3,2},{4,5},{5,4},{6,7},{7,6},{8,9},{9,8},{10,11... | collective-permute-start | bytes 1720328 | tf_op jit(solution)/shard_map/ppermute | solution.py:175
  346.3 9.1 %collective-permute-start.33 = (f32[16,128]{1,0:T(8,128)S(1)}, f32[16,128]{1,0:T(8,128)S(1)}, u32[]{:S(2)}, u32[]{:S(2)}) collective-permute-start(f32[16,128]{1,0:T(8,128)S(1)} %bitcast.340), channel_id=1, source_target_pairs={{0,1},{1,0},{2,3},{3,2},{4,5},{5,4},{6,7},{7,6},{8,9},{9,8},{10,11... | collective-permute-start | bytes 24584 | tf_op jit(solution)/shard_map/ppermute | solution.py:175
  363.4 6.0 %collective-permute-start.34 = (f32[416,128]{1,0:T(8,128)S(1)}, f32[416,128]{1,0:T(8,128)S(1)}, u32[]{:S(2)}, u32[]{:S(2)}) collective-permute-start(f32[416,128]{1,0:T(8,128)S(1)} %get-tuple-element.102), channel_id=1, source_target_pairs={{0,16},{16,32},{32,48},{48,0},{64,80},{80,96},{96,112},{112,64},{1... | collective-permute-start | bytes 638984 | tf_op jit(solution)/shard_map/ppermute | solution.py:192
  364.7 4.7 %collective-permute-start.36 = (f32[416,128]{1,0:T(8,128)S(1)}, f32[416,128]{1,0:T(8,128)S(1)}, u32[]{:S(2)}, u32[]{:S(2)}) collective-permute-start(f32[416,128]{1,0:T(8,128)S(1)} %get-tuple-element.103), channel_id=1, source_target_pairs={{0,48},{16,0},{32,16},{48,32},{64,112},{80,64},{96,80},{112,96},{1... | collective-permute-start | bytes 638984 | tf_op jit(solution)/shard_map/ppermute | solution.py:193
  370.3 9.9 %collective-permute-start.37 = (f32[832,128]{1,0:T(8,128)}, f32[832,128]{1,0:T(8,128)}, u32[]{:S(2)}, u32[]{:S(2)}) collective-permute-start(f32[832,128]{1,0:T(8,128)} %pad_maximum_fusion.3), channel_id=1, source_target_pairs={{0,48},{16,0},{32,16},{48,32},{64,112},{80,64},{96,80},{112,96},{1... | collective-permute-start | bytes 1277960 | tf_op jit(solution)/shard_map/ppermute | solution.py:196
  373.7 9.6 %collective-permute-start.35 = (f32[832,128]{1,0:T(8,128)}, f32[832,128]{1,0:T(8,128)}, u32[]{:S(2)}, u32[]{:S(2)}) collective-permute-start(f32[832,128]{1,0:T(8,128)} %pad_maximum_fusion.2), channel_id=1, source_target_pairs={{0,16},{16,32},{32,48},{48,0},{64,80},{80,96},{96,112},{112,64},{1... | collective-permute-start | bytes 1277960 | tf_op jit(solution)/shard_map/ppermute | solution.py:196
  384.6 8.6 %collective-permute-start.38 = (f32[832,128]{1,0:T(8,128)S(1)}, f32[832,128]{1,0:T(8,128)S(1)}, u32[]{:S(2)}, u32[]{:S(2)}) collective-permute-start(f32[832,128]{1,0:T(8,128)S(1)} %fusion.90), channel_id=1, source_target_pairs={{0,64},{16,80},{32,96},{48,112},{64,0},{80,16},{96,32},{112,48},{1... | collective-permute-start | bytes 1277960 | tf_op jit(solution)/shard_map/ppermute | solution.py:199
  393.2 8.3 %collective-permute-start.40 = (f32[832,128]{1,0:T(8,128)S(1)}, f32[832,128]{1,0:T(8,128)S(1)}, u32[]{:S(2)}, u32[]{:S(2)}) collective-permute-start(f32[832,128]{1,0:T(8,128)S(1)} %get-tuple-element.62), channel_id=1, source_target_pairs={{0,16},{16,32},{32,48},{48,0},{64,80},{80,96},{96,112},{112,64},{1... | collective-permute-start | bytes 1277960 | tf_op jit(solution)/shard_map/ppermute | solution.py:201
  393.3 8.3 %collective-permute-start.39 = (f32[832,128]{1,0:T(8,128)S(1)}, f32[832,128]{1,0:T(8,128)S(1)}, u32[]{:S(2)}, u32[]{:S(2)}) collective-permute-start(f32[832,128]{1,0:T(8,128)S(1)} %get-tuple-element.62), channel_id=1, source_target_pairs={{0,48},{16,0},{32,16},{48,32},{64,112},{80,64},{96,80},{112,96},{1... | collective-permute-start | bytes 1277960 | tf_op jit(solution)/shard_map/ppermute | solution.py:202
  401.5 6.0 %collective-permute-start.41 = (f32[416,128]{1,0:T(8,128)S(1)}, f32[416,128]{1,0:T(8,128)S(1)}, u32[]{:S(2)}, u32[]{:S(2)}) collective-permute-start(f32[416,128]{1,0:T(8,128)S(1)} %slice.481), channel_id=1, source_target_pairs={{0,16},{16,32},{32,48},{48,0},{64,80},{80,96},{96,112},{112,64},{1... | collective-permute-start | bytes 638984 | tf_op jit(solution)/shard_map/ppermute | solution.py:203
  401.6 6.0 %collective-permute-start.42 = (f32[416,128]{1,0:T(8,128)S(1)}, f32[416,128]{1,0:T(8,128)S(1)}, u32[]{:S(2)}, u32[]{:S(2)}) collective-permute-start(f32[416,128]{1,0:T(8,128)S(1)} %slice.482), channel_id=1, source_target_pairs={{0,48},{16,0},{32,16},{48,32},{64,112},{80,64},{96,80},{112,96},{1... | collective-permute-start | bytes 638984 | tf_op jit(solution)/shard_map/ppermute | solution.py:204
  411.8 28.7 %collective-permute-start.43 = (f32[64,4480]{1,0:T(8,128)S(1)}, f32[64,4480]{1,0:T(8,128)}, u32[]{:S(2)}, u32[]{:S(2)}) collective-permute-start(f32[64,4480]{1,0:T(8,128)S(1)} %reshape.732), channel_id=1, source_target_pairs={{0,8},{8,0},{1,9},{9,1},{2,10},{10,2},{3,11},{11,3},{4,12},{12,4},... | collective-permute-start | bytes 3440648 | tf_op jit(solution)/shard_map/ppermute | solution.py:246
  433.9 5.4 %collective-permute-start.44 = (f32[128,1024]{1,0:T(8,128)S(1)}, f32[128,1024]{1,0:T(8,128)S(1)}, u32[]{:S(2)}, u32[]{:S(2)}) collective-permute-start(f32[128,1024]{1,0:T(8,128)S(1)} %reshape.734), channel_id=1, source_target_pairs={{0,8},{8,0},{1,9},{9,1},{2,10},{10,2},{3,11},{11,3},{4,12},{12,4},... | collective-permute-start | bytes 1572872 | tf_op jit(solution)/shard_map/ppermute | solution.py:246
  (99 other events, 597.1 us)
Sparse Core Ops, SparseCore 0:
  77.7 52.8 all-gather.2

commit v11 on v10

--- a/solution.py
+++ b/solution.py
@@ -221,25 +221,38 @@
     return lax.ppermute(values, "core", [(0, 1), (1, 0)])
 
 
-def gather_group(block):
+def gather_group(block, sibling):
     ring = lax.axis_size("shard_0")
     y = lax.axis_index("shard_1")
     z = lax.axis_index("shard_0")
-    other_y = lax.ppermute(block, "shard_1", [(0, 1), (1, 0)])
-    pair = jnp.where(y == 0, jnp.stack([block, other_y]), jnp.stack([other_y, block]))
     up = [(i, (i + 1) % ring) for i in range(ring)]
     down = [(i, (i - 1) % ring) for i in range(ring)]
+    half = block.shape[0] // 2
+
+    def place(own, got):
+        return jnp.where(y == 0, jnp.stack([own, got]), jnp.stack([got, own]))
+
+    def arrange(pair, from_next, opposite, from_prev):
+        ordered = jnp.stack([pair, from_next, opposite, from_prev])
+        doubled = jnp.concatenate([ordered, ordered], axis=0)
+        placed = lax.dynamic_slice_in_dim(doubled, (ring - z) % ring, ring, axis=0)
+        return placed.reshape((ring * 2,) + block.shape)
+
+    other_y = lax.ppermute(block, "shard_1", [(0, 1), (1, 0)])
+    pair = place(block, other_y)
     from_prev = lax.ppermute(pair, "shard_0", up)
     from_next = lax.ppermute(pair, "shard_0", down)
-    half = block.shape[0] // 2
+    pair_s = place(sibling, core_swap(other_y))
     far_a = lax.ppermute(from_prev[:, :half], "shard_0", up)
     far_b = lax.ppermute(from_next[:, half:], "shard_0", down)
+    from_prev_s = core_swap(from_prev)
+    from_next_s = core_swap(from_next)
     opposite = jnp.concatenate([far_a, far_b], axis=1)
-    ordered = jnp.stack([pair, from_next, opposite, from_prev])
-    doubled = jnp.concatenate([ordered, ordered], axis=0)
-    start = (ring - z) % ring
-    placed = lax.dynamic_slice_in_dim(doubled, start, ring, axis=0)
-    return placed.reshape((ring * 2,) + block.shape)
+    opposite_s = core_swap(opposite)
+    return (
+        arrange(pair, from_next, opposite, from_prev),
+        arrange(pair_s, from_next_s, opposite_s, from_prev_s),
+    )
 
 
 def core_swap(values):
@@ -252,10 +265,11 @@
     core = lax.axis_index("core")
     mine = lax.dynamic_slice_in_dim(weight, core * half, half, axis=0)
     if by_permutes:
-        part = gather_group(mine)
+        sibling = lax.dynamic_slice_in_dim(weight, (1 - core) * half, half, axis=0)
+        part, other = gather_group(mine, sibling)
     else:
         part = lax.all_gather(mine, SHARD, axis=0, tiled=False)
-    other = core_swap(part)
+        other = core_swap(part)
     return part.reshape(-1, weight.shape[1]), other.reshape(-1, weight.shape[1])
 
 

time: 458 us -> 454 us (level)
  matrix products: 70.9 us -> 60.8 us
  local copies, waits for them, and re-layouts: 81.4 us -> 88.8 us
  starting transfers between devices: 75.1 us -> 80.4 us
  waiting for transfers between devices: 121 us -> 116 us
    ppermute x1, waiting for transfers between devices: 12.3 us -> 1.71 us  [gather_group(): other_y = lax.ppermute(block, 'shard_1', [(0, 1), (1, 0)])]
    unnamed x218 -> x144, local copies, waits for them, and re-layouts: 25.2 us -> 35.1 us
    ppermute x1, waiting for transfers between devices: 22.7 us -> 31.3 us  [gather_group(): from_prev = lax.ppermute(pair, 'shard_0', up)]
    ppermute x7 -> x10, starting transfers between devices: 23.4 us -> 28.8 us  [core_swap(): return lax.ppermute(values, 'core', [(0, 1), (1, 0)])]
    ppermute x1, waiting for transfers between devices: 10.5 us -> 5.19 us  [gather_group(): far_a = lax.ppermute(from_prev[:, :half], 'shard_0', up)]
    dynamic_slice x2 -> x4, local copies, waits for them, and re-layouts: 2.5 us -> 7.62 us  [the longest x2 4.65 us: gather_rows(): sibling = lax.dynamic_slice_in_dim(weight, (1 - core) * half, half, axis=0)]
    dot_general x2, matrix products: 8.99 us -> 3.9 us  [row_product(): lax.dot_general(left, right, (((0,), (0,)), ((), ())), preferred_element_...]
  transfers between devices with their start and end apart: 46 -> 49, of which waited for: 20 -> 17; matrix products, arithmetic and copies ran while one was open for 30% -> 32% of each run, Pallas kernels for 0% -> 0%
where the time goes in v11:
time: 454 us; the launch traced here: 446 us
  waiting for transfers between devices  116 us (26%)
  local copies, waits for them, and re-layouts  88.8 us (20%)
  other arithmetic  83.7 us (18%)
  starting transfers between devices  80.4 us (18%)
  matrix products  60.8 us (13%)
  between operations  15.9 us (4%)
    ppermute x18, waiting for transfers between devices, send(): lax.ppermute(p.astype(w), 'shard_0', pairs)  39.5 us
    unnamed x144, local copies, waits for them, and re-layouts  35.1 us
    ppermute x1, waiting for transfers between devices, gather_group(): from_prev = lax.ppermute(pair, 'shard_0', up)  31.3 us
    dot_general x3, matrix products, mixer(): y_intra = jnp.einsum('chij,cjhp->cihp', mixing, scaled_in, precision=HIGH)  31.1 us
    ppermute x10, starting transfers between devices, core_swap(): return lax.ppermute(values, 'core', [(0, 1), (1, 0)])  28.8 us
    ppermute x18, starting transfers between devices, send(): lax.ppermute(p.astype(w), 'shard_0', pairs)  20.6 us
    add x2, other arithmetic, reduce_core(): return keep + core_swap(give)  16.1 us
    dot_general x4, matrix products, back_product(): lax.dot_general(left, right, (((1,), (1,)), ((), ())), preferred_element_...  13.4 us
  transfers between devices with their start and end apart: 49, of which 17 were waited for; matrix products, arithmetic and copies ran while one was open for 32% of the time, Pallas kernels for 0%

profile of v11, /device:TPU:1, one launch (start us, length us, event | category | flops | bytes accessed | tf_op | source)
XLA Modules:
  0.0 445.8 jit_solution(9889875745430045831)
XLA Ops:
  21.0 3.5 collective-permute-start.2
  37.1 2.9 collective-permute-start.4
  40.0 5.1 %collective-permute-start.8 = (bf16[64,4384]{1,0:T(8,128)(2,1)}, bf16[64,4384]{1,0:T(8,128)(2,1)S(1)}, u32[]{:S(2)}, u32[]{:S(2)}) collective-permute-start(bf16[64,4384]{1,0:T(8,128)(2,1)} %collective-permute-done.3), channel_id=1, source_target_pairs={{0,8},{8,0},{1,9},{9,1},{2,10},{10,2},{3,11},{11,3},{4,12},{12,4},... | collective-permute-start | bytes 1683464 | tf_op jit(solution)/shard_map/ppermute | solution.py:259
  47.8 31.3 %collective-permute-done.5 = bf16[2,64,4384]{2,1,0:T(8,128)(2,1)S(1)} collective-permute-done((bf16[2,64,4384]{2,1,0:T(8,128)(2,1)S(1)}, bf16[2,64,4384]{2,1,0:T(8,128)(2,1)S(1)}, u32[]{:S(2)}, u32[]{:S(2)}) %collective-permute-start.5) | collective-permute-done | bytes 1122336 | tf_op jit(solution)/shard_map/ppermute | solution.py:243
  79.3 2.7 collective-permute-start.7
  82.0 3.6 collective-permute-start.11
  86.7 5.2 %collective-permute-done.6 = bf16[2,32,4384]{2,1,0:T(8,128)(2,1)S(1)} collective-permute-done((bf16[2,32,4384]{2,1,0:T(8,128)(2,1)S(1)}, bf16[2,32,4384]{2,1,0:T(8,128)(2,1)S(1)}, u32[]{:S(2)}, u32[]{:S(2)}) %collective-permute-start.6) | collective-permute-done | bytes 561184 | tf_op jit(solution)/shard_map/ppermute | solution.py:246
  92.0 4.2 collective-permute-start.10
  121.4 4.8 %fusion.21 = (f32[256,2304]{0,1:T(8,128)S(1)}, f32[256,2304]{0,1:T(8,128)}) fusion(f32[253,2304]{0,1:T(8,128)S(1)} %slice.426, f32[2304]{0:T(1024)S(1)} %get-tuple-element.58, pred[256]{0:T(512)(128)(4,1)S(1)} %get-tuple-element.138, f32[254,2304]{0,1:T(8,128)S(1)} %slice.424, f32[2304]{0:T(1024)S(1)} %get-tuple-element.59, ...), kind=kLoop, calls=%fused_computation.54 | loop fusion | flops 8847360 | bytes 14147328 | tf_op jit(solution)/shard_map/jvp(jit(silu))/mul | solution.py:110
  130.5 11.6 %fusion.33 = f32[256,32,64]{0,2,1:T(8,128)S(1)} fusion(f32[256,32,64]{0,2,1:T(8,128)} %bitcast.332, f32[256,32,64]{0,2,1:T(8,128)S(1)} %fusion.85, f32[32]{0:T(128)S(1)} %mul.429, f32[256,32]{0,1:T(8,128)S(1)} %bitcast_multiply_fusion.6, f32[256,256]{1,0:T(8,128)S(1)} %fusion.101, f32[32,256]{1,0:T(8,128)S(1)} %bitcast_add_fusion.4, ...), kind=kOutput, calls=%fused_computation.77 | convolution fusion | flops 1619525632 | bytes 6717568 | tf_op jit(solution)/shard_map/jvp(chij,cjhp->cihp)/dot_general | solution.py:132
  142.2 3.1 multiply_reduce_fusion.9
  148.5 2.6 dynamic-slice_bitcast_fusion.1
  154.0 2.8 fusion.123
  156.8 6.9 %collective-permute-done.12 = bf16[8,128,1024]{2,1,0:T(8,128)(2,1)} collective-permute-done((bf16[8,128,1024]{2,1,0:T(8,128)(2,1)}, bf16[8,128,1024]{2,1,0:T(8,128)(2,1)}, u32[]{:S(2)}, u32[]{:S(2)}) %collective-permute-start.12) | collective-permute-done | bytes 2097184 | tf_op jit(solution)/shard_map/ppermute | solution.py:259
  166.7 5.3 %bitcast_add_fusion.1 = f32[8,128,1024]{2,1,0:T(8,128)} fusion(f32[8,128,1024]{2,1,0:T(8,128)} %collective-permute-done.13, f32[8,2,128,1024]{3,2,1,0:T(8,128)S(1)} %bitcast.302, s32[]{:T(128)S(6)} %select_n.178), kind=kLoop, calls=%fused_computation.22 | loop fusion | flops 1048576 | bytes 12582916 | tf_op jit(solution)/shard_map/add | solution.py:313
  173.6 4.4 multiply_reduce_fusion.6
  179.9 11.4 %fusion.7 = (f32[32,256]{1,0:T(8,128)S(1)}, f32[32,256]{1,0:T(8,128)S(1)}, f32[256,256]{1,0:T(8,128)S(1)}) fusion(f32[256,256]{1,0:T(8,128)S(1)} %fusion.101, f32[32,256]{1,0:T(8,128)S(1)} %bitcast_add_fusion.4, pred[256,256]{1,0:T(8,128)(4,1)S(1)} %copy-done.52, f32[32,64,256]{2,1,0:T(8,128)S(1)} %bitcast.305, f32[256,32,64]{0,2,1:T(8,128)S(1)} %bitcast.333, ...), kind=kOutput, calls=%fused_computation.15 | convolution fusion | flops 1629929472 | bytes 4915200 | tf_op jit(solution)/shard_map/transpose(jvp(chij,cjhp->cihp))/dot_general | solution.py:132
  191.2 8.1 %fusion.34 = (f32[256,32]{0,1:T(8,128)S(1)}, f32[1,256,32,64]{1,3,2,0:T(8,128)}) fusion(f32[1,256,32,64]{1,3,2,0:T(8,128)S(1)} %bitcast.334, f32[256,32]{0,1:T(8,128)S(1)} %get-tuple-element.77, f32[32,64,256]{2,1,0:T(8,128)S(1)} %bitcast.306, f32[256,256]{1,0:T(8,128)S(1)} %fusion.101, f32[32,256]{1,0:T(8,128)S(1)} %bitcast_add_fusion.4, ...), kind=kOutput, calls=%fused_computation.81 | convolution fusion | flops 1618468864 | bytes 6717440 | tf_op jit(solution)/shard_map/transpose(jvp(chij,cjhp->cihp))/dot_general | solution.py:132
  216.0 2.7 fusion.22
  218.7 4.6 %dynamic-slice_bitcast_fusion = f32[8,64,4480]{2,1,0:T(8,128)} fusion(f32[8,2,64,4480]{3,2,1,0:T(8,128)S(1)} %bitcast.297, s32[]{:T(128)S(6)} %select_n.186), kind=kLoop, calls=%fused_computation.4 | loop fusion | bytes 18350084 | tf_op jit(solution)/shard_map/jit(dynamic_index_in_dim)/squeeze | solution.py:312
  223.3 4.4 copy-done.4
  228.8 4.5 %fusion.46 = f32[256,8,1,64]{0,3,1,2:T(8,128)S(1)} fusion(bf16[8,64,4384]{2,1,0:T(8,128)(2,1)} %bitcast.312, bf16[256,4384]{0,1:T(8,128)(2,1)} %copy-done.31), kind=kOutput, calls=%fused_computation.108 | convolution fusion | flops 1149239296 | bytes 7258112 | tf_op jit(solution)/shard_map/dot_general | solution.py:82
  233.4 3.7 fusion.43
  242.0 3.2 fusion.8
  247.8 2.8 collective-permute-start.25
  250.7 2.7 collective-permute-start.33
  253.5 10.8 %bitcast_add_fusion = f32[8,64,4480]{2,1,0:T(8,128)} fusion(f32[8,64,4480]{2,1,0:T(8,128)} %collective-permute-done.14, f32[8,2,64,4480]{3,2,1,0:T(8,128)} %bitcast.298, s32[]{:T(128)S(6)} %select_n.178), kind=kLoop, calls=%fused_computation.3 | loop fusion | flops 2293760 | bytes 27525124 | tf_op jit(solution)/shard_map/add | solution.py:313
  264.3 8.2 %fusion = f32[4,2,64,4480]{3,2,1,0:T(8,128)} fusion(s32[]{:T(128)S(6)} %select_n.202, f32[4,2,64,4480]{3,2,1,0:T(8,128)} %bitcast.303), kind=kLoop, calls=%fused_computation.2 | loop fusion | flops 2293760 | bytes 18350084 | tf_op jit(solution)/shard_map/concatenate | solution.py:155
  272.5 6.4 %slice_bitcast_fusion.3 = (f32[2,64,4480]{2,1,0:T(8,128)S(1)}, f32[2,64,4480]{2,1,0:T(8,128)S(1)}, f32[2,64,4480]{2,1,0:T(8,128)}, f32[2,64,4480]{2,1,0:T(8,128)}) fusion(f32[4,2,64,4480]{3,2,1,0:T(8,128)} %fusion), kind=kLoop, calls=%fused_computation.60 | loop fusion | bytes 18350080 | tf_op jit(solution)/shard_map/squeeze | solution.py:162
  284.2 11.3 %collective-permute-done.34 = f32[2,8,128]{2,0,1:T(2,128)S(1)} collective-permute-done((f32[2,8,128]{2,0,1:T(2,128)S(1)}, f32[2,8,128]{2,0,1:T(2,128)S(1)}, u32[]{:S(2)}, u32[]{:S(2)}) %collective-permute-start.34) | collective-permute-done | bytes 8224 | tf_op jit(solution)/shard_map/ppermute | solution.py:160
  298.7 2.7 collective-permute-start.26
  303.6 2.7 collective-permute-start.19
  306.5 2.7 collective-permute-start.27
  309.4 8.1 %collective-permute-done.19 = bf16[2,32,4480]{2,1,0:T(8,128)(2,1)S(1)} collective-permute-done((bf16[2,32,4480]{2,1,0:T(8,128)(2,1)S(1)}, bf16[2,32,4480]{2,1,0:T(8,128)(2,1)S(1)}, u32[]{:S(2)}, u32[]{:S(2)}) %collective-permute-start.19) | collective-permute-done | bytes 573472 | tf_op jit(solution)/shard_map/ppermute | solution.py:160
  318.2 10.9 %collective-permute-done.16 = bf16[2,32,4480]{2,1,0:T(8,128)(2,1)S(1)} collective-permute-done((bf16[2,32,4480]{2,1,0:T(8,128)(2,1)S(1)}, bf16[2,32,4480]{2,1,0:T(8,128)(2,1)S(1)}, u32[]{:S(2)}, u32[]{:S(2)}) %collective-permute-start.16) | collective-permute-done | bytes 573472 | tf_op jit(solution)/shard_map/ppermute | solution.py:160
  331.2 6.5 %collective-permute-done.20 = bf16[2,32,4480]{2,1,0:T(8,128)(2,1)S(1)} collective-permute-done((bf16[2,32,4480]{2,1,0:T(8,128)(2,1)S(1)}, bf16[2,32,4480]{2,1,0:T(8,128)(2,1)S(1)}, u32[]{:S(2)}, u32[]{:S(2)}) %collective-permute-start.20) | collective-permute-done | bytes 573472 | tf_op jit(solution)/shard_map/ppermute | solution.py:160
  344.0 7.8 %collective-permute-done.36 = f32[16,128]{1,0:T(8,128)S(1)} collective-permute-done((f32[16,128]{1,0:T(8,128)S(1)}, f32[16,128]{1,0:T(8,128)S(1)}, u32[]{:S(2)}, u32[]{:S(2)}) %collective-permute-start.36) | collective-permute-done | bytes 8224 | tf_op jit(solution)/shard_map/ppermute | solution.py:175
  361.7 3.2 collective-permute-done.37
  365.0 2.7 collective-permute-start.40
  369.3 3.6 collective-permute-done.40
  372.9 5.7 %collective-permute-done.38 = f32[832,128]{1,0:T(8,128)S(1)} collective-permute-done((f32[832,128]{1,0:T(8,128)S(1)}, f32[832,128]{1,0:T(8,128)S(1)}, u32[]{:S(2)}, u32[]{:S(2)}) %collective-permute-start.38) | collective-permute-done | bytes 426016 | tf_op jit(solution)/shard_map/ppermute | solution.py:196
  379.8 2.7 collective-permute-start.41
  384.5 3.8 collective-permute-done.41
  388.5 2.7 collective-permute-start.42
  391.2 3.3 fusion.42
  397.1 2.9 collective-permute-start.45
  400.1 2.9 collective-permute-done.44
  408.1 14.2 %collective-permute-start.46 = (f32[64,4480]{1,0:T(8,128)}, f32[64,4480]{1,0:T(8,128)}, u32[]{:S(2)}, u32[]{:S(2)}) collective-permute-start(f32[64,4480]{1,0:T(8,128)} %reshape.789), channel_id=1, source_target_pairs={{0,8},{8,0},{1,9},{9,1},{2,10},{10,2},{3,11},{11,3},{4,12},{12,4},... | collective-permute-start | bytes 3440648 | tf_op jit(solution)/shard_map/ppermute | solution.py:259
  (394 shorter events, 155.6 us)
Async XLA Ops:
  7.2 146.0 %all-gather.3.cloned.1.call-start = ((), (), s32[]{:S(2)}) async-start(), calls=%async_computation | async-start | bytes 2359296 | tf_op jit(solution)/shard_map/all_gather | solution.py:271
  9.3 7.8 %collective-permute-start = (f32[8,1836]{1,0:T(8,128)S(1)}, f32[8,1836]{1,0:T(8,128)S(1)}, u32[]{:S(2)}, u32[]{:S(2)}) collective-permute-start(f32[8,1836]{1,0:T(8,128)S(1)} %broadcast_select_fusion.7), channel_id=1, source_target_pairs={{0,1},{1,0},{2,3},{3,2},{4,5},{5,4},{6,7},{7,6},{8,9},{9,8},{10,11... | collective-permute-start | bytes 176264 | tf_op jit(solution)/shard_map/ppermute | solution.py:338
  15.9 17.6 %collective-permute-start.3 = (bf16[64,4384]{1,0:T(8,128)(2,1)S(1)}, bf16[64,4384]{1,0:T(8,128)(2,1)}, u32[]{:S(2)}, u32[]{:S(2)}) collective-permute-start(bf16[64,4384]{1,0:T(8,128)(2,1)S(1)} %copy.120), channel_id=1, source_target_pairs={{0,1},{1,0},{2,3},{3,2},{4,5},{5,4},{6,7},{7,6},{8,9},{9,8},{10,11... | collective-permute-start | bytes 1683464 | tf_op jit(solution)/shard_map/ppermute | solution.py:241
  21.0 6.5 %collective-permute-start.2 = (f32[8,1836]{1,0:T(8,128)S(1)}, f32[8,1836]{1,0:T(8,128)S(1)}, u32[]{:S(2)}, u32[]{:S(2)}) collective-permute-start(f32[8,1836]{1,0:T(8,128)S(1)} %fusion.159), channel_id=1, source_target_pairs={{0,4},{2,6},{4,0},{6,2},{1,5},{3,7},{5,1},{7,3},{8,12},{10,14},{12... | collective-permute-start | bytes 176264 | tf_op jit(solution)/shard_map/ppermute | solution.py:338
  34.9 44.2 %collective-permute-start.5 = (bf16[2,64,4384]{2,1,0:T(8,128)(2,1)S(1)}, bf16[2,64,4384]{2,1,0:T(8,128)(2,1)S(1)}, u32[]{:S(2)}, u32[]{:S(2)}) collective-permute-start(bf16[2,64,4384]{2,1,0:T(8,128)(2,1)S(1)} %maximum_select_fusion.1), channel_id=1, source_target_pairs={{0,2},{2,4},{4,6},{6,0},{1,3},{3,5},{5,7},{7,1},{8,10},{10,12},{12... | collective-permute-start | bytes 3366920 | tf_op jit(solution)/shard_map/ppermute | solution.py:243
  37.1 42.2 %collective-permute-start.4 = (bf16[2,64,4384]{2,1,0:T(8,128)(2,1)S(1)}, bf16[2,64,4384]{2,1,0:T(8,128)(2,1)S(1)}, u32[]{:S(2)}, u32[]{:S(2)}) collective-permute-start(bf16[2,64,4384]{2,1,0:T(8,128)(2,1)S(1)} %maximum_select_fusion.1), channel_id=1, source_target_pairs={{0,6},{2,0},{4,2},{6,4},{1,7},{3,1},{5,3},{7,5},{8,14},{10,8},{12,... | collective-permute-start | bytes 3366920 | tf_op jit(solution)/shard_map/ppermute | solution.py:244
  40.0 7.6 %collective-permute-start.8 = (bf16[64,4384]{1,0:T(8,128)(2,1)}, bf16[64,4384]{1,0:T(8,128)(2,1)S(1)}, u32[]{:S(2)}, u32[]{:S(2)}) collective-permute-start(bf16[64,4384]{1,0:T(8,128)(2,1)} %collective-permute-done.3), channel_id=1, source_target_pairs={{0,8},{8,0},{1,9},{9,1},{2,10},{10,2},{3,11},{11,3},{4,12},{12,4},... | collective-permute-start | bytes 1683464 | tf_op jit(solution)/shard_map/ppermute | solution.py:259
  79.2 12.7 %collective-permute-start.6 = (bf16[2,32,4384]{2,1,0:T(8,128)(2,1)S(1)}, bf16[2,32,4384]{2,1,0:T(8,128)(2,1)S(1)}, u32[]{:S(2)}, u32[]{:S(2)}) collective-permute-start(bf16[2,32,4384]{2,1,0:T(8,128)(2,1)S(1)} %slice.418), channel_id=1, source_target_pairs={{0,2},{2,4},{4,6},{6,0},{1,3},{3,5},{5,7},{7,1},{8,10},{10,12},{12... | collective-permute-start | bytes 1683464 | tf_op jit(solution)/shard_map/ppermute | solution.py:246
  79.3 12.6 %collective-permute-start.7 = (bf16[2,32,4384]{2,1,0:T(8,128)(2,1)S(1)}, bf16[2,32,4384]{2,1,0:T(8,128)(2,1)S(1)}, u32[]{:S(2)}, u32[]{:S(2)}) collective-permute-start(bf16[2,32,4384]{2,1,0:T(8,128)(2,1)S(1)} %slice.419), channel_id=1, source_target_pairs={{0,6},{2,0},{4,2},{6,4},{1,7},{3,1},{5,3},{7,5},{8,14},{10,8},{12,... | collective-permute-start | bytes 1683464 | tf_op jit(solution)/shard_map/ppermute | solution.py:247
  82.0 27.3 %collective-permute-start.11 = (bf16[2,64,4384]{2,1,0:T(8,128)(2,1)S(1)}, bf16[2,64,4384]{2,1,0:T(8,128)(2,1)S(1)}, u32[]{:S(2)}, u32[]{:S(2)}) collective-permute-start(bf16[2,64,4384]{2,1,0:T(8,128)(2,1)S(1)} %collective-permute-done.5), channel_id=1, source_target_pairs={{0,8},{8,0},{1,9},{9,1},{2,10},{10,2},{3,11},{11,3},{4,12},{12,4},... | collective-permute-start | bytes 3366920 | tf_op jit(solution)/shard_map/ppermute | solution.py:259
  85.6 23.4 %collective-permute-start.9 = (bf16[2,64,4384]{2,1,0:T(8,128)(2,1)S(1)}, bf16[2,64,4384]{2,1,0:T(8,128)(2,1)S(1)}, u32[]{:S(2)}, u32[]{:S(2)}) collective-permute-start(bf16[2,64,4384]{2,1,0:T(8,128)(2,1)S(1)} %collective-permute-done.4), channel_id=1, source_target_pairs={{0,8},{8,0},{1,9},{9,1},{2,10},{10,2},{3,11},{11,3},{4,12},{12,4},... | collective-permute-start | bytes 3366920 | tf_op jit(solution)/shard_map/ppermute | solution.py:259
  92.0 17.2 %collective-permute-start.10 = (bf16[2,64,4384]{2,1,0:T(8,128)(2,1)S(1)}, bf16[2,64,4384]{2,1,0:T(8,128)(2,1)S(1)}, u32[]{:S(2)}, u32[]{:S(2)}) collective-permute-start(bf16[2,64,4384]{2,1,0:T(8,128)(2,1)S(1)} %constant_dynamic-update-slice_fusion), channel_id=1, source_target_pairs={{0,8},{8,0},{1,9},{9,1},{2,10},{10,2},{3,11},{11,3},{4,12},{12,4},... | collective-permute-start | bytes 3366920 | tf_op jit(solution)/shard_map/ppermute | solution.py:259
  153.2 13.4 %collective-permute-start.13 = (f32[8,128,1024]{2,1,0:T(8,128)}, f32[8,128,1024]{2,1,0:T(8,128)}, u32[]{:S(2)}, u32[]{:S(2)}) collective-permute-start(f32[8,128,1024]{2,1,0:T(8,128)} %dynamic-slice_bitcast_fusion.1), channel_id=1, source_target_pairs={{0,8},{8,0},{1,9},{9,1},{2,10},{10,2},{3,11},{11,3},{4,12},{12,4},... | collective-permute-start | bytes 12582920 | tf_op jit(solution)/shard_map/ppermute | solution.py:259
  153.2 10.5 %collective-permute-start.12 = (bf16[8,128,1024]{2,1,0:T(8,128)(2,1)}, bf16[8,128,1024]{2,1,0:T(8,128)(2,1)}, u32[]{:S(2)}, u32[]{:S(2)}) collective-permute-start(bf16[8,128,1024]{2,1,0:T(8,128)(2,1)} %bitcast.314), channel_id=1, source_target_pairs={{0,8},{8,0},{1,9},{9,1},{2,10},{10,2},{3,11},{11,3},{4,12},{12,4},... | collective-permute-start | bytes 6291464 | tf_op jit(solution)/shard_map/ppermute | solution.py:259
  227.7 25.8 %collective-permute-start.14 = (f32[8,64,4480]{2,1,0:T(8,128)}, f32[8,64,4480]{2,1,0:T(8,128)}, u32[]{:S(2)}, u32[]{:S(2)}) collective-permute-start(f32[8,64,4480]{2,1,0:T(8,128)} %dynamic-slice_bitcast_fusion), channel_id=1, source_target_pairs={{0,8},{8,0},{1,9},{9,1},{2,10},{10,2},{3,11},{11,3},{4,12},{12,4},... | collective-permute-start | bytes 27525128 | tf_op jit(solution)/shard_map/ppermute | solution.py:259
  241.5 9.1 %collective-permute-start.29 = (f32[8,16,128]{2,0,1:T(8,128)S(1)}, f32[8,16,128]{2,0,1:T(8,128)S(1)}, u32[]{:S(2)}, u32[]{:S(2)}) collective-permute-start(f32[8,16,128]{2,0,1:T(8,128)S(1)} %pad_bitcast_fusion), channel_id=1, source_target_pairs={{0,8},{8,0},{1,9},{9,1},{2,10},{10,2},{3,11},{11,3},{4,12},{12,4},... | collective-permute-start | bytes 196616 | tf_op jit(solution)/shard_map/ppermute | solution.py:259
  247.8 49.3 %collective-permute-start.25 = (bf16[2,64,1024]{2,1,0:T(8,128)(2,1)S(1)}, bf16[2,64,1024]{2,1,0:T(8,128)(2,1)}, u32[]{:S(2)}, u32[]{:S(2)}) collective-permute-start(bf16[2,64,1024]{2,1,0:T(8,128)(2,1)S(1)} %slice.603), channel_id=1, source_target_pairs={{0,6},{2,0},{4,2},{6,4},{1,7},{3,1},{5,3},{7,5},{8,14},{10,8},{12,... | collective-permute-start | bytes 786440 | tf_op jit(solution)/shard_map/ppermute | solution.py:160
  250.6 46.6 %collective-permute-start.22 = (bf16[2,64,1024]{2,1,0:T(8,128)(2,1)S(1)}, bf16[2,64,1024]{2,1,0:T(8,128)(2,1)}, u32[]{:S(2)}, u32[]{:S(2)}) collective-permute-start(bf16[2,64,1024]{2,1,0:T(8,128)(2,1)S(1)} %slice.604), channel_id=1, source_target_pairs={{0,2},{2,4},{4,6},{6,0},{1,3},{3,5},{5,7},{7,1},{8,10},{10,12},{12... | collective-permute-start | bytes 786440 | tf_op jit(solution)/shard_map/ppermute | solution.py:160
  250.7 32.1 %collective-permute-start.33 = (f32[2,8,128]{2,0,1:T(2,128)S(1)}, f32[2,8,128]{2,0,1:T(2,128)S(1)}, u32[]{:S(2)}, u32[]{:S(2)}) collective-permute-start(f32[2,8,128]{2,0,1:T(2,128)S(1)} %slice.470), channel_id=1, source_target_pairs={{0,6},{2,0},{4,2},{6,4},{1,7},{3,1},{5,3},{7,5},{8,14},{10,8},{12,... | collective-permute-start | bytes 24584 | tf_op jit(solution)/shard_map/ppermute | solution.py:160
  281.4 20.0 %collective-permute-start.18 = (bf16[2,32,4480]{2,1,0:T(8,128)(2,1)}, bf16[2,32,4480]{2,1,0:T(8,128)(2,1)S(1)}, u32[]{:S(2)}, u32[]{:S(2)}) collective-permute-start(bf16[2,32,4480]{2,1,0:T(8,128)(2,1)} %slice.601), channel_id=1, source_target_pairs={{0,6},{2,0},{4,2},{6,4},{1,7},{3,1},{5,3},{7,5},{8,14},{10,8},{12,... | collective-permute-start | bytes 1720328 | tf_op jit(solution)/shard_map/ppermute | solution.py:160
  281.5 20.0 %collective-permute-start.15 = (bf16[2,32,4480]{2,1,0:T(8,128)(2,1)}, bf16[2,32,4480]{2,1,0:T(8,128)(2,1)}, u32[]{:S(2)}, u32[]{:S(2)}) collective-permute-start(bf16[2,32,4480]{2,1,0:T(8,128)(2,1)} %slice.602), channel_id=1, source_target_pairs={{0,2},{2,4},{4,6},{6,0},{1,3},{3,5},{5,7},{7,1},{8,10},{10,12},{12... | collective-permute-start | bytes 1720328 | tf_op jit(solution)/shard_map/ppermute | solution.py:160
  282.9 12.6 %collective-permute-start.34 = (f32[2,8,128]{2,0,1:T(2,128)S(1)}, f32[2,8,128]{2,0,1:T(2,128)S(1)}, u32[]{:S(2)}, u32[]{:S(2)}) collective-permute-start(f32[2,8,128]{2,0,1:T(2,128)S(1)} %slice_add_fusion.15), channel_id=1, source_target_pairs={{0,6},{2,0},{4,2},{6,4},{1,7},{3,1},{5,3},{7,5},{8,14},{10,8},{12,... | collective-permute-start | bytes 24584 | tf_op jit(solution)/shard_map/ppermute | solution.py:160
  295.5 46.9 %collective-permute-start.35 = (f32[2,8,128]{2,0,1:T(2,128)S(1)}, f32[2,8,128]{2,0,1:T(2,128)S(1)}, u32[]{:S(2)}, u32[]{:S(2)}) collective-permute-start(f32[2,8,128]{2,0,1:T(2,128)S(1)} %get-tuple-element.133), channel_id=1, source_target_pairs={{0,6},{2,0},{4,2},{6,4},{1,7},{3,1},{5,3},{7,5},{8,14},{10,8},{12,... | collective-permute-start | bytes 24584 | tf_op jit(solution)/shard_map/ppermute | solution.py:160
  297.0 9.3 %collective-permute-start.30 = (f32[2,8,128]{2,0,1:T(2,128)S(1)}, f32[2,8,128]{2,0,1:T(2,128)S(1)}, u32[]{:S(2)}, u32[]{:S(2)}) collective-permute-start(f32[2,8,128]{2,0,1:T(2,128)S(1)} %get-tuple-element.134), channel_id=1, source_target_pairs={{0,2},{2,4},{4,6},{6,0},{1,3},{3,5},{5,7},{7,1},{8,10},{10,12},{12... | collective-permute-start | bytes 24584 | tf_op jit(solution)/shard_map/ppermute | solution.py:160
  298.7 7.7 %collective-permute-start.26 = (bf16[2,64,1024]{2,1,0:T(8,128)(2,1)S(1)}, bf16[2,64,1024]{2,1,0:T(8,128)(2,1)S(1)}, u32[]{:S(2)}, u32[]{:S(2)}) collective-permute-start(bf16[2,64,1024]{2,1,0:T(8,128)(2,1)S(1)} %get-tuple-element.112), channel_id=1, source_target_pairs={{0,6},{2,0},{4,2},{6,4},{1,7},{3,1},{5,3},{7,5},{8,14},{10,8},{12,... | collective-permute-start | bytes 786440 | tf_op jit(solution)/shard_map/ppermute | solution.py:160
  301.4 7.8 %collective-permute-start.23 = (bf16[2,64,1024]{2,1,0:T(8,128)(2,1)S(1)}, bf16[2,64,1024]{2,1,0:T(8,128)(2,1)S(1)}, u32[]{:S(2)}, u32[]{:S(2)}) collective-permute-start(bf16[2,64,1024]{2,1,0:T(8,128)(2,1)S(1)} %get-tuple-element.113), channel_id=1, source_target_pairs={{0,2},{2,4},{4,6},{6,0},{1,3},{3,5},{5,7},{7,1},{8,10},{10,12},{12... | collective-permute-start | bytes 786440 | tf_op jit(solution)/shard_map/ppermute | solution.py:160
  303.6 13.9 %collective-permute-start.19 = (bf16[2,32,4480]{2,1,0:T(8,128)(2,1)S(1)}, bf16[2,32,4480]{2,1,0:T(8,128)(2,1)S(1)}, u32[]{:S(2)}, u32[]{:S(2)}) collective-permute-start(bf16[2,32,4480]{2,1,0:T(8,128)(2,1)S(1)} %get-tuple-element.96), channel_id=1, source_target_pairs={{0,6},{2,0},{4,2},{6,4},{1,7},{3,1},{5,3},{7,5},{8,14},{10,8},{12,... | collective-permute-start | bytes 1720328 | tf_op jit(solution)/shard_map/ppermute | solution.py:160
  306.3 24.1 %collective-permute-start.31 = (f32[2,8,128]{2,0,1:T(2,128)S(1)}, f32[2,8,128]{2,0,1:T(2,128)S(1)}, u32[]{:S(2)}, u32[]{:S(2)}) collective-permute-start(f32[2,8,128]{2,0,1:T(2,128)S(1)} %slice_add_fusion.18), channel_id=1, source_target_pairs={{0,2},{2,4},{4,6},{6,0},{1,3},{3,5},{5,7},{7,1},{8,10},{10,12},{12... | collective-permute-start | bytes 24584 | tf_op jit(solution)/shard_map/ppermute | solution.py:160
  306.5 24.3 %collective-permute-start.27 = (bf16[2,64,1024]{2,1,0:T(8,128)(2,1)S(1)}, bf16[2,64,1024]{2,1,0:T(8,128)(2,1)S(1)}, u32[]{:S(2)}, u32[]{:S(2)}) collective-permute-start(bf16[2,64,1024]{2,1,0:T(8,128)(2,1)S(1)} %fusion.80), channel_id=1, source_target_pairs={{0,6},{2,0},{4,2},{6,4},{1,7},{3,1},{5,3},{7,5},{8,14},{10,8},{12,... | collective-permute-start | bytes 786440 | tf_op jit(solution)/shard_map/ppermute | solution.py:160
  309.3 21.6 %collective-permute-start.24 = (bf16[2,64,1024]{2,1,0:T(8,128)(2,1)S(1)}, bf16[2,64,1024]{2,1,0:T(8,128)(2,1)S(1)}, u32[]{:S(2)}, u32[]{:S(2)}) collective-permute-start(bf16[2,64,1024]{2,1,0:T(8,128)(2,1)S(1)} %fusion.82), channel_id=1, source_target_pairs={{0,2},{2,4},{4,6},{6,0},{1,3},{3,5},{5,7},{7,1},{8,10},{10,12},{12... | collective-permute-start | bytes 786440 | tf_op jit(solution)/shard_map/ppermute | solution.py:160
  317.5 11.6 %collective-permute-start.16 = (bf16[2,32,4480]{2,1,0:T(8,128)(2,1)S(1)}, bf16[2,32,4480]{2,1,0:T(8,128)(2,1)S(1)}, u32[]{:S(2)}, u32[]{:S(2)}) collective-permute-start(bf16[2,32,4480]{2,1,0:T(8,128)(2,1)S(1)} %get-tuple-element.97), channel_id=1, source_target_pairs={{0,2},{2,4},{4,6},{6,0},{1,3},{3,5},{5,7},{7,1},{8,10},{10,12},{12... | collective-permute-start | bytes 1720328 | tf_op jit(solution)/shard_map/ppermute | solution.py:160
  329.2 8.6 %collective-permute-start.20 = (bf16[2,32,4480]{2,1,0:T(8,128)(2,1)S(1)}, bf16[2,32,4480]{2,1,0:T(8,128)(2,1)S(1)}, u32[]{:S(2)}, u32[]{:S(2)}) collective-permute-start(bf16[2,32,4480]{2,1,0:T(8,128)(2,1)S(1)} %fusion.54), channel_id=1, source_target_pairs={{0,6},{2,0},{4,2},{6,4},{1,7},{3,1},{5,3},{7,5},{8,14},{10,8},{12,... | collective-permute-start | bytes 1720328 | tf_op jit(solution)/shard_map/ppermute | solution.py:160
  330.5 9.8 %collective-permute-start.17 = (bf16[2,32,4480]{2,1,0:T(8,128)(2,1)S(1)}, bf16[2,32,4480]{2,1,0:T(8,128)(2,1)S(1)}, u32[]{:S(2)}, u32[]{:S(2)}) collective-permute-start(bf16[2,32,4480]{2,1,0:T(8,128)(2,1)S(1)} %fusion.56), channel_id=1, source_target_pairs={{0,2},{2,4},{4,6},{6,0},{1,3},{3,5},{5,7},{7,1},{8,10},{10,12},{12... | collective-permute-start | bytes 1720328 | tf_op jit(solution)/shard_map/ppermute | solution.py:160
  330.8 11.6 %collective-permute-start.32 = (f32[2,8,128]{2,0,1:T(2,128)S(1)}, f32[2,8,128]{2,0,1:T(2,128)S(1)}, u32[]{:S(2)}, u32[]{:S(2)}) collective-permute-start(f32[2,8,128]{2,0,1:T(2,128)S(1)} %slice_add_fusion.17), channel_id=1, source_target_pairs={{0,2},{2,4},{4,6},{6,0},{1,3},{3,5},{5,7},{7,1},{8,10},{10,12},{12... | collective-permute-start | bytes 24584 | tf_op jit(solution)/shard_map/ppermute | solution.py:160
  331.1 20.6 %collective-permute-start.28 = (bf16[128,1024]{1,0:T(8,128)(2,1)S(1)}, bf16[128,1024]{1,0:T(8,128)(2,1)}, u32[]{:S(2)}, u32[]{:S(2)}) collective-permute-start(bf16[128,1024]{1,0:T(8,128)(2,1)S(1)} %fusion.91), channel_id=1, source_target_pairs={{0,1},{1,0},{2,3},{3,2},{4,5},{5,4},{6,7},{7,6},{8,9},{9,8},{10,11... | collective-permute-start | bytes 786440 | tf_op jit(solution)/shard_map/ppermute | solution.py:175
  342.4 12.3 %collective-permute-start.21 = (bf16[64,4480]{1,0:T(8,128)(2,1)}, bf16[64,4480]{1,0:T(8,128)(2,1)}, u32[]{:S(2)}, u32[]{:S(2)}) collective-permute-start(bf16[64,4480]{1,0:T(8,128)(2,1)} %fusion.74), channel_id=1, source_target_pairs={{0,1},{1,0},{2,3},{3,2},{4,5},{5,4},{6,7},{7,6},{8,9},{9,8},{10,11... | collective-permute-start | bytes 1720328 | tf_op jit(solution)/shard_map/ppermute | solution.py:175
  342.5 9.3 %collective-permute-start.36 = (f32[16,128]{1,0:T(8,128)S(1)}, f32[16,128]{1,0:T(8,128)S(1)}, u32[]{:S(2)}, u32[]{:S(2)}) collective-permute-start(f32[16,128]{1,0:T(8,128)S(1)} %bitcast.354), channel_id=1, source_target_pairs={{0,1},{1,0},{2,3},{3,2},{4,5},{5,4},{6,7},{7,6},{8,9},{9,8},{10,11... | collective-permute-start | bytes 24584 | tf_op jit(solution)/shard_map/ppermute | solution.py:175
  359.0 6.0 %collective-permute-start.37 = (f32[416,128]{1,0:T(8,128)S(1)}, f32[416,128]{1,0:T(8,128)S(1)}, u32[]{:S(2)}, u32[]{:S(2)}) collective-permute-start(f32[416,128]{1,0:T(8,128)S(1)} %get-tuple-element.102), channel_id=1, source_target_pairs={{0,16},{16,32},{32,48},{48,0},{64,80},{80,96},{96,112},{112,64},{1... | collective-permute-start | bytes 638984 | tf_op jit(solution)/shard_map/ppermute | solution.py:192
  360.2 4.7 %collective-permute-start.39 = (f32[416,128]{1,0:T(8,128)S(1)}, f32[416,128]{1,0:T(8,128)S(1)}, u32[]{:S(2)}, u32[]{:S(2)}) collective-permute-start(f32[416,128]{1,0:T(8,128)S(1)} %get-tuple-element.103), channel_id=1, source_target_pairs={{0,48},{16,0},{32,16},{48,32},{64,112},{80,64},{96,80},{112,96},{1... | collective-permute-start | bytes 638984 | tf_op jit(solution)/shard_map/ppermute | solution.py:193
  365.0 7.8 %collective-permute-start.40 = (f32[832,128]{1,0:T(8,128)S(1)}, f32[832,128]{1,0:T(8,128)}, u32[]{:S(2)}, u32[]{:S(2)}) collective-permute-start(f32[832,128]{1,0:T(8,128)S(1)} %pad_maximum_fusion.3), channel_id=1, source_target_pairs={{0,48},{16,0},{32,16},{48,32},{64,112},{80,64},{96,80},{112,96},{1... | collective-permute-start | bytes 1277960 | tf_op jit(solution)/shard_map/ppermute | solution.py:196
  367.8 10.8 %collective-permute-start.38 = (f32[832,128]{1,0:T(8,128)S(1)}, f32[832,128]{1,0:T(8,128)S(1)}, u32[]{:S(2)}, u32[]{:S(2)}) collective-permute-start(f32[832,128]{1,0:T(8,128)S(1)} %pad_maximum_fusion.2), channel_id=1, source_target_pairs={{0,16},{16,32},{32,48},{48,0},{64,80},{80,96},{96,112},{112,64},{1... | collective-permute-start | bytes 1277960 | tf_op jit(solution)/shard_map/ppermute | solution.py:196
  379.8 8.6 %collective-permute-start.41 = (f32[832,128]{1,0:T(8,128)S(1)}, f32[832,128]{1,0:T(8,128)S(1)}, u32[]{:S(2)}, u32[]{:S(2)}) collective-permute-start(f32[832,128]{1,0:T(8,128)S(1)} %fusion.88), channel_id=1, source_target_pairs={{0,64},{16,80},{32,96},{48,112},{64,0},{80,16},{96,32},{112,48},{1... | collective-permute-start | bytes 1277960 | tf_op jit(solution)/shard_map/ppermute | solution.py:199
  388.4 8.6 %collective-permute-start.43 = (f32[832,128]{1,0:T(8,128)S(1)}, f32[832,128]{1,0:T(8,128)S(1)}, u32[]{:S(2)}, u32[]{:S(2)}) collective-permute-start(f32[832,128]{1,0:T(8,128)S(1)} %get-tuple-element.62), channel_id=1, source_target_pairs={{0,16},{16,32},{32,48},{48,0},{64,80},{80,96},{96,112},{112,64},{1... | collective-permute-start | bytes 1277960 | tf_op jit(solution)/shard_map/ppermute | solution.py:201
  388.5 8.6 %collective-permute-start.42 = (f32[832,128]{1,0:T(8,128)S(1)}, f32[832,128]{1,0:T(8,128)S(1)}, u32[]{:S(2)}, u32[]{:S(2)}) collective-permute-start(f32[832,128]{1,0:T(8,128)S(1)} %get-tuple-element.62), channel_id=1, source_target_pairs={{0,48},{16,0},{32,16},{48,32},{64,112},{80,64},{96,80},{112,96},{1... | collective-permute-start | bytes 1277960 | tf_op jit(solution)/shard_map/ppermute | solution.py:202
  397.0 6.0 %collective-permute-start.44 = (f32[416,128]{1,0:T(8,128)S(1)}, f32[416,128]{1,0:T(8,128)S(1)}, u32[]{:S(2)}, u32[]{:S(2)}) collective-permute-start(f32[416,128]{1,0:T(8,128)S(1)} %slice.481), channel_id=1, source_target_pairs={{0,16},{16,32},{32,48},{48,0},{64,80},{80,96},{96,112},{112,64},{1... | collective-permute-start | bytes 638984 | tf_op jit(solution)/shard_map/ppermute | solution.py:203
  397.1 5.9 %collective-permute-start.45 = (f32[416,128]{1,0:T(8,128)S(1)}, f32[416,128]{1,0:T(8,128)S(1)}, u32[]{:S(2)}, u32[]{:S(2)}) collective-permute-start(f32[416,128]{1,0:T(8,128)S(1)} %slice.482), channel_id=1, source_target_pairs={{0,48},{16,0},{32,16},{48,32},{64,112},{80,64},{96,80},{112,96},{1... | collective-permute-start | bytes 638984 | tf_op jit(solution)/shard_map/ppermute | solution.py:204
  408.1 27.0 %collective-permute-start.46 = (f32[64,4480]{1,0:T(8,128)}, f32[64,4480]{1,0:T(8,128)}, u32[]{:S(2)}, u32[]{:S(2)}) collective-permute-start(f32[64,4480]{1,0:T(8,128)} %reshape.789), channel_id=1, source_target_pairs={{0,8},{8,0},{1,9},{9,1},{2,10},{10,2},{3,11},{11,3},{4,12},{12,4},... | collective-permute-start | bytes 3440648 | tf_op jit(solution)/shard_map/ppermute | solution.py:259
  428.5 5.5 %collective-permute-start.47 = (f32[128,1024]{1,0:T(8,128)S(1)}, f32[128,1024]{1,0:T(8,128)S(1)}, u32[]{:S(2)}, u32[]{:S(2)}) collective-permute-start(f32[128,1024]{1,0:T(8,128)S(1)} %reshape.791), channel_id=1, source_target_pairs={{0,8},{8,0},{1,9},{9,1},{2,10},{10,2},{3,11},{11,3},{4,12},{12,4},... | collective-permute-start | bytes 1572872 | tf_op jit(solution)/shard_map/ppermute | solution.py:259
  (61 other events, 337.0 us)
Sparse Core Ops, SparseCore 0:
  12.3 61.2 all-gather.2

commit v12 on v11

--- a/solution.py
+++ b/solution.py
@@ -398,7 +398,6 @@
     cot_low = cotangent.astype(jnp.bfloat16)
     out_halves = reduce_core(row_product(gated, cot_low))
     gated_grad = halves_back(cot_low, out_whole, groups)
-    out_halves, gated_grad = lax.optimization_barrier((out_halves, gated_grad))
     out_group = reduce_group(out_halves)
     proj_grad, g_convw, g_convb, g_stepb, g_decay, g_skip, g_gategain = mixer_back(gated_grad)
     proj_low = proj_grad.astype(jnp.bfloat16)

time: 454 us -> 441 us (0.971)
  matrix products: 60.8 us -> 49.6 us
  starting transfers between devices: 80.4 us -> 73.6 us
    dot_general x4, matrix products: 13.4 us -> 4.29 us  [back_product(): lax.dot_general(left, right, (((1,), (1,)), ((), ())), preferred_element_...]
    ppermute x1, waiting for transfers between devices: 31.3 us -> 37.1 us  [gather_group(): from_prev = lax.ppermute(pair, 'shard_0', up)]
    ppermute x10, waiting for transfers between devices: 6.95 us -> 2.28 us  [core_swap(): return lax.ppermute(values, 'core', [(0, 1), (1, 0)])]
    unnamed x144 -> x146, local copies, waits for them, and re-layouts: 35.1 us -> 32.1 us
where the time goes in v12:
time: 441 us; the launch traced here: 433 us
  waiting for transfers between devices  119 us (27%)
  local copies, waits for them, and re-layouts  89.5 us (20%)
  other arithmetic  85.9 us (19%)
  starting transfers between devices  73.6 us (17%)
  matrix products  49.6 us (11%)
  between operations  15.8 us (4%)
    ppermute x1, waiting for transfers between devices, gather_group(): from_prev = lax.ppermute(pair, 'shard_0', up)  37.1 us
    ppermute x18, waiting for transfers between devices, send(): lax.ppermute(p.astype(w), 'shard_0', pairs)  36.7 us
    unnamed x146, local copies, waits for them, and re-layouts  32.1 us
    dot_general x3, matrix products, mixer(): y_intra = jnp.einsum('chij,cjhp->cihp', mixing, scaled_in, precision=HIGH)  28.9 us
    ppermute x10, starting transfers between devices, core_swap(): return lax.ppermute(values, 'core', [(0, 1), (1, 0)])  26.2 us
    ppermute x18, starting transfers between devices, send(): lax.ppermute(p.astype(w), 'shard_0', pairs)  22.1 us
    add x2, other arithmetic, reduce_core(): return keep + core_swap(give)  15.2 us
    concatenate x3, other arithmetic, reduce_group(): doubled = jnp.concatenate([blocks, blocks], axis=0)  9.34 us
  transfers between devices with their start and end apart: 49, of which 17 were waited for; matrix products, arithmetic and copies ran while one was open for 32% of the time, Pallas kernels for 0%

profile of v12, /device:TPU:1, one launch (start us, length us, event | category | flops | bytes accessed | tf_op | source)
XLA Modules:
  0.0 433.2 jit_solution(18325746086411543034)
XLA Ops:
  11.3 3.4 constant_dynamic-slice_fusion.5
  21.7 3.5 collective-permute-start.2
  25.6 2.6 copy.93
  35.9 3.6 collective-permute-start.8
  39.5 2.5 fusion.98
  42.2 37.1 %collective-permute-done.5 = bf16[2,64,4384]{2,1,0:T(8,128)(2,1)S(1)} collective-permute-done((bf16[2,64,4384]{2,1,0:T(8,128)(2,1)S(1)}, bf16[2,64,4384]{2,1,0:T(8,128)(2,1)S(1)}, u32[]{:S(2)}, u32[]{:S(2)}) %collective-permute-start.5) | collective-permute-done | bytes 1122336 | tf_op jit(solution)/shard_map/ppermute | solution.py:243
  79.5 2.7 collective-permute-start.7
  82.2 2.9 collective-permute-start.9
  86.2 6.5 %collective-permute-done.6 = bf16[2,32,4384]{2,1,0:T(8,128)(2,1)S(1)} collective-permute-done((bf16[2,32,4384]{2,1,0:T(8,128)(2,1)S(1)}, bf16[2,32,4384]{2,1,0:T(8,128)(2,1)S(1)}, u32[]{:S(2)}, u32[]{:S(2)}) %collective-permute-start.6) | collective-permute-done | bytes 561184 | tf_op jit(solution)/shard_map/ppermute | solution.py:246
  92.8 3.8 collective-permute-start.10
  104.7 2.6 constant_dynamic-slice_fusion.7
  119.0 7.2 %fusion.21 = (f32[256,2304]{0,1:T(8,128)S(1)}, f32[256,2304]{0,1:T(8,128)}) fusion(f32[253,2304]{0,1:T(8,128)} %slice.426, f32[2304]{0:T(1024)S(1)} %get-tuple-element.54, pred[256]{0:T(512)(128)(4,1)S(1)} %get-tuple-element.135, f32[254,2304]{0,1:T(8,128)} %slice.424, f32[2304]{0:T(1024)S(1)} %get-tuple-element.55, ...), kind=kLoop, calls=%fused_computation.54 | loop fusion | flops 8847360 | bytes 14147328 | tf_op jit(solution)/shard_map/jvp(jit(silu))/mul | solution.py:110
  130.7 10.0 %fusion.33 = f32[256,32,64]{0,2,1:T(8,128)S(1)} fusion(f32[256,32,64]{0,2,1:T(8,128)S(1)} %bitcast.347, f32[256,32,64]{0,2,1:T(8,128)S(1)} %fusion.86, f32[32]{0:T(128)S(1)} %mul.429, f32[256,32]{0,1:T(8,128)S(1)} %bitcast_multiply_fusion.8, f32[256,256]{1,0:T(8,128)S(1)} %fusion.102, f32[32,256]{1,0:T(8,128)S(1)} %bitcast_add_fusion.4, ...), kind=kOutput, calls=%fused_computation.77 | convolution fusion | flops 1619525632 | bytes 6717568 | tf_op jit(solution)/shard_map/jvp(chij,cjhp->cihp)/dot_general | solution.py:132
  146.4 3.3 multiply_reduce_fusion.5
  150.6 11.4 %fusion.7 = (f32[32,256]{1,0:T(8,128)S(1)}, f32[32,256]{1,0:T(8,128)S(1)}, f32[256,256]{1,0:T(8,128)S(1)}) fusion(f32[256,256]{1,0:T(8,128)S(1)} %fusion.102, f32[32,256]{1,0:T(8,128)S(1)} %copy-done.44, pred[256,256]{1,0:T(8,128)(4,1)S(1)} %copy-done.41, f32[32,64,256]{2,1,0:T(8,128)S(1)} %bitcast.315, f32[256,32,64]{0,2,1:T(8,128)S(1)} %bitcast.348, ...), kind=kOutput, calls=%fused_computation.15 | convolution fusion | flops 1629929472 | bytes 4915200 | tf_op jit(solution)/shard_map/transpose(jvp(chij,cjhp->cihp))/dot_general | solution.py:132
  161.9 7.5 %fusion.34 = (f32[256,32]{0,1:T(8,128)}, f32[1,256,32,64]{1,3,2,0:T(8,128)S(1)}) fusion(f32[1,256,32,64]{1,3,2,0:T(8,128)S(1)} %bitcast.349, f32[256,32]{0,1:T(8,128)S(1)} %get-tuple-element.73, f32[32,64,256]{2,1,0:T(8,128)S(1)} %bitcast.316, f32[256,256]{1,0:T(8,128)S(1)} %fusion.102, f32[32,256]{1,0:T(8,128)S(1)} %copy-done.44, ...), kind=kOutput, calls=%fused_computation.81 | convolution fusion | flops 1618468864 | bytes 6717440 | tf_op jit(solution)/shard_map/transpose(jvp(chij,cjhp->cihp))/dot_general | solution.py:132
  189.7 4.8 %fusion.133 = (f32[2304]{0:T(1024)S(1)}, f32[2304]{0:T(1024)S(1)}, f32[256,2304]{0,1:T(8,128)S(1)}) fusion(f32[256,2304]{0,1:T(8,128)S(1)} %get-tuple-element.65, f32[256,4384]{0,1:T(8,128)} %copy-done.2, f32[2304]{0:T(1024)S(1)} %get-tuple-element.53, f32[255,2304]{0,1:T(8,128)} %slice_multiply_fusion, f32[254,2304]{0,1:T(8,128)} %slice_multiply_fusion.1, ...), kind=kLoop, calls=%fused_computation.323 | loop fusion | flops 4124160 | bytes 14128128 | tf_op jit(solution)/shard_map/transpose(jvp())/reduce_sum | solution.py:104
  194.7 2.7 fusion.22
  197.4 4.6 %dynamic-slice_bitcast_fusion = f32[8,64,4480]{2,1,0:T(8,128)} fusion(f32[8,2,64,4480]{3,2,1,0:T(8,128)S(1)} %bitcast.310, s32[]{:T(128)S(6)} %select_n.186), kind=kLoop, calls=%fused_computation.4 | loop fusion | bytes 18350084 | tf_op jit(solution)/shard_map/jit(dynamic_index_in_dim)/squeeze | solution.py:312
  202.0 4.4 %copy-done.3 = f32[1024,4480]{1,0:T(8,128)} copy-done((f32[1024,4480]{1,0:T(8,128)}, f32[1024,4480]{1,0:T(8,128)S(1)}, u32[]{:S(2)}) %copy-start.3) | copy-done | bytes 18350104
  207.1 2.9 fusion.122
  212.4 2.6 copy-done.4
  227.2 2.8 collective-permute-start.33
  230.0 4.4 %bitcast_add_fusion.1 = f32[8,128,1024]{2,1,0:T(8,128)S(1)} fusion(f32[8,128,1024]{2,1,0:T(8,128)} %collective-permute-done.21, f32[8,2,128,1024]{3,2,1,0:T(8,128)} %bitcast.313, s32[]{:T(128)S(6)} %select_n.178), kind=kLoop, calls=%fused_computation.22 | loop fusion | flops 1048576 | bytes 12582916 | tf_op jit(solution)/shard_map/add | solution.py:313
  238.9 10.8 %bitcast_add_fusion = f32[8,64,4480]{2,1,0:T(8,128)} fusion(f32[8,64,4480]{2,1,0:T(8,128)} %collective-permute-done.13, f32[8,2,64,4480]{3,2,1,0:T(8,128)} %bitcast.311, s32[]{:T(128)S(6)} %select_n.178), kind=kLoop, calls=%fused_computation.3 | loop fusion | flops 2293760 | bytes 27525124 | tf_op jit(solution)/shard_map/add | solution.py:313
  249.7 8.2 %fusion = f32[4,2,64,4480]{3,2,1,0:T(8,128)} fusion(s32[]{:T(128)S(6)} %select_n.202, f32[4,2,64,4480]{3,2,1,0:T(8,128)} %bitcast.314), kind=kLoop, calls=%fused_computation.2 | loop fusion | flops 2293760 | bytes 18350084 | tf_op jit(solution)/shard_map/concatenate | solution.py:155
  257.9 6.4 %slice_bitcast_fusion.3 = (f32[2,64,4480]{2,1,0:T(8,128)S(1)}, f32[2,64,4480]{2,1,0:T(8,128)S(1)}, f32[2,64,4480]{2,1,0:T(8,128)}, f32[2,64,4480]{2,1,0:T(8,128)}) fusion(f32[4,2,64,4480]{3,2,1,0:T(8,128)} %fusion), kind=kLoop, calls=%fused_computation.60 | loop fusion | bytes 18350080 | tf_op jit(solution)/shard_map/squeeze | solution.py:162
  269.8 2.7 collective-permute-start.34
  272.5 8.2 %collective-permute-done.34 = f32[2,8,128]{2,0,1:T(2,128)S(1)} collective-permute-done((f32[2,8,128]{2,0,1:T(2,128)S(1)}, f32[2,8,128]{2,0,1:T(2,128)S(1)}, u32[]{:S(2)}, u32[]{:S(2)}) %collective-permute-start.34) | collective-permute-done | bytes 8224 | tf_op jit(solution)/shard_map/ppermute | solution.py:160
  280.8 3.4 collective-permute-start.35
  285.6 2.7 collective-permute-start.26
  290.5 2.7 collective-permute-start.18
  293.4 2.7 collective-permute-start.27
  296.3 7.9 %collective-permute-done.18 = bf16[2,32,4480]{2,1,0:T(8,128)(2,1)S(1)} collective-permute-done((bf16[2,32,4480]{2,1,0:T(8,128)(2,1)S(1)}, bf16[2,32,4480]{2,1,0:T(8,128)(2,1)S(1)}, u32[]{:S(2)}, u32[]{:S(2)}) %collective-permute-start.18) | collective-permute-done | bytes 573472 | tf_op jit(solution)/shard_map/ppermute | solution.py:160
  304.3 11.0 %collective-permute-done.15 = bf16[2,32,4480]{2,1,0:T(8,128)(2,1)S(1)} collective-permute-done((bf16[2,32,4480]{2,1,0:T(8,128)(2,1)S(1)}, bf16[2,32,4480]{2,1,0:T(8,128)(2,1)S(1)}, u32[]{:S(2)}, u32[]{:S(2)}) %collective-permute-start.15) | collective-permute-done | bytes 573472 | tf_op jit(solution)/shard_map/ppermute | solution.py:160
  317.4 6.5 %collective-permute-done.19 = bf16[2,32,4480]{2,1,0:T(8,128)(2,1)S(1)} collective-permute-done((bf16[2,32,4480]{2,1,0:T(8,128)(2,1)S(1)}, bf16[2,32,4480]{2,1,0:T(8,128)(2,1)S(1)}, u32[]{:S(2)}, u32[]{:S(2)}) %collective-permute-start.19) | collective-permute-done | bytes 573472 | tf_op jit(solution)/shard_map/ppermute | solution.py:160
  323.8 3.1 collective-permute-done.16
  330.7 8.3 %collective-permute-done.36 = f32[16,128]{1,0:T(8,128)S(1)} collective-permute-done((f32[16,128]{1,0:T(8,128)S(1)}, f32[16,128]{1,0:T(8,128)S(1)}, u32[]{:S(2)}, u32[]{:S(2)}) %collective-permute-start.36) | collective-permute-done | bytes 8224 | tf_op jit(solution)/shard_map/ppermute | solution.py:175
  349.1 3.2 collective-permute-done.37
  352.4 2.7 collective-permute-start.40
  356.6 3.6 collective-permute-done.40
  360.2 5.7 %collective-permute-done.38 = f32[832,128]{1,0:T(8,128)S(1)} collective-permute-done((f32[832,128]{1,0:T(8,128)S(1)}, f32[832,128]{1,0:T(8,128)S(1)}, u32[]{:S(2)}, u32[]{:S(2)}) %collective-permute-start.38) | collective-permute-done | bytes 426016 | tf_op jit(solution)/shard_map/ppermute | solution.py:196
  367.2 2.6 collective-permute-start.41
  371.9 3.9 collective-permute-done.41
  379.1 4.1 collective-permute-done.42
  384.8 3.1 collective-permute-done.45
  393.1 2.6 reshape.789
  395.7 14.2 %collective-permute-start.46 = (f32[64,4480]{1,0:T(8,128)}, f32[64,4480]{1,0:T(8,128)}, u32[]{:S(2)}, u32[]{:S(2)}) collective-permute-start(f32[64,4480]{1,0:T(8,128)} %reshape.789), channel_id=1, source_target_pairs={{0,8},{8,0},{1,9},{9,1},{2,10},{10,2},{3,11},{11,3},{4,12},{12,4},... | collective-permute-start | bytes 3440648 | tf_op jit(solution)/shard_map/ppermute | solution.py:259
  (396 shorter events, 147.2 us)
Async XLA Ops:
  7.2 121.4 %all-gather.3.cloned.1.call-start = ((), (), s32[]{:S(2)}) async-start(), calls=%async_computation | async-start | bytes 2359296 | tf_op jit(solution)/shard_map/all_gather | solution.py:271
  9.2 8.5 %collective-permute-start = (f32[8,1836]{1,0:T(8,128)S(1)}, f32[8,1836]{1,0:T(8,128)S(1)}, u32[]{:S(2)}, u32[]{:S(2)}) collective-permute-start(f32[8,1836]{1,0:T(8,128)S(1)} %broadcast_select_fusion.7), channel_id=1, source_target_pairs={{0,1},{1,0},{2,3},{3,2},{4,5},{5,4},{6,7},{7,6},{8,9},{9,8},{10,11... | collective-permute-start | bytes 176264 | tf_op jit(solution)/shard_map/ppermute | solution.py:338
  15.8 16.8 %collective-permute-start.3 = (bf16[64,4384]{1,0:T(8,128)(2,1)S(1)}, bf16[64,4384]{1,0:T(8,128)(2,1)}, u32[]{:S(2)}, u32[]{:S(2)}) collective-permute-start(bf16[64,4384]{1,0:T(8,128)(2,1)S(1)} %copy.120), channel_id=1, source_target_pairs={{0,1},{1,0},{2,3},{3,2},{4,5},{5,4},{6,7},{7,6},{8,9},{9,8},{10,11... | collective-permute-start | bytes 1683464 | tf_op jit(solution)/shard_map/ppermute | solution.py:241
  17.8 3.8 collective-permute-start.1
  21.7 6.5 %collective-permute-start.2 = (f32[8,1836]{1,0:T(8,128)S(1)}, f32[8,1836]{1,0:T(8,128)S(1)}, u32[]{:S(2)}, u32[]{:S(2)}) collective-permute-start(f32[8,1836]{1,0:T(8,128)S(1)} %fusion.160), channel_id=1, source_target_pairs={{0,4},{2,6},{4,0},{6,2},{1,5},{3,7},{5,1},{7,3},{8,12},{10,14},{12... | collective-permute-start | bytes 176264 | tf_op jit(solution)/shard_map/ppermute | solution.py:338
  34.1 45.3 %collective-permute-start.4 = (bf16[2,64,4384]{2,1,0:T(8,128)(2,1)S(1)}, bf16[2,64,4384]{2,1,0:T(8,128)(2,1)S(1)}, u32[]{:S(2)}, u32[]{:S(2)}) collective-permute-start(bf16[2,64,4384]{2,1,0:T(8,128)(2,1)S(1)} %maximum_select_fusion.1), channel_id=1, source_target_pairs={{0,6},{2,0},{4,2},{6,4},{1,7},{3,1},{5,3},{7,5},{8,14},{10,8},{12,... | collective-permute-start | bytes 3366920 | tf_op jit(solution)/shard_map/ppermute | solution.py:244
  35.9 43.4 %collective-permute-start.5 = (bf16[2,64,4384]{2,1,0:T(8,128)(2,1)S(1)}, bf16[2,64,4384]{2,1,0:T(8,128)(2,1)S(1)}, u32[]{:S(2)}, u32[]{:S(2)}) collective-permute-start(bf16[2,64,4384]{2,1,0:T(8,128)(2,1)S(1)} %maximum_select_fusion.1), channel_id=1, source_target_pairs={{0,2},{2,4},{4,6},{6,0},{1,3},{3,5},{5,7},{7,1},{8,10},{10,12},{12... | collective-permute-start | bytes 3366920 | tf_op jit(solution)/shard_map/ppermute | solution.py:243
  35.9 6.1 %collective-permute-start.8 = (bf16[64,4384]{1,0:T(8,128)(2,1)}, bf16[64,4384]{1,0:T(8,128)(2,1)S(1)}, u32[]{:S(2)}, u32[]{:S(2)}) collective-permute-start(bf16[64,4384]{1,0:T(8,128)(2,1)} %collective-permute-done.3), channel_id=1, source_target_pairs={{0,8},{8,0},{1,9},{9,1},{2,10},{10,2},{3,11},{11,3},{4,12},{12,4},... | collective-permute-start | bytes 1683464 | tf_op jit(solution)/shard_map/ppermute | solution.py:259
  79.3 13.4 %collective-permute-start.6 = (bf16[2,32,4384]{2,1,0:T(8,128)(2,1)S(1)}, bf16[2,32,4384]{2,1,0:T(8,128)(2,1)S(1)}, u32[]{:S(2)}, u32[]{:S(2)}) collective-permute-start(bf16[2,32,4384]{2,1,0:T(8,128)(2,1)S(1)} %slice.418), channel_id=1, source_target_pairs={{0,2},{2,4},{4,6},{6,0},{1,3},{3,5},{5,7},{7,1},{8,10},{10,12},{12... | collective-permute-start | bytes 1683464 | tf_op jit(solution)/shard_map/ppermute | solution.py:246
  79.5 13.3 %collective-permute-start.7 = (bf16[2,32,4384]{2,1,0:T(8,128)(2,1)S(1)}, bf16[2,32,4384]{2,1,0:T(8,128)(2,1)S(1)}, u32[]{:S(2)}, u32[]{:S(2)}) collective-permute-start(bf16[2,32,4384]{2,1,0:T(8,128)(2,1)S(1)} %slice.419), channel_id=1, source_target_pairs={{0,6},{2,0},{4,2},{6,4},{1,7},{3,1},{5,3},{7,5},{8,14},{10,8},{12,... | collective-permute-start | bytes 1683464 | tf_op jit(solution)/shard_map/ppermute | solution.py:247
  82.2 27.2 %collective-permute-start.9 = (bf16[2,64,4384]{2,1,0:T(8,128)(2,1)S(1)}, bf16[2,64,4384]{2,1,0:T(8,128)(2,1)S(1)}, u32[]{:S(2)}, u32[]{:S(2)}) collective-permute-start(bf16[2,64,4384]{2,1,0:T(8,128)(2,1)S(1)} %collective-permute-done.4), channel_id=1, source_target_pairs={{0,8},{8,0},{1,9},{9,1},{2,10},{10,2},{3,11},{11,3},{4,12},{12,4},... | collective-permute-start | bytes 3366920 | tf_op jit(solution)/shard_map/ppermute | solution.py:259
  85.1 24.6 %collective-permute-start.11 = (bf16[2,64,4384]{2,1,0:T(8,128)(2,1)S(1)}, bf16[2,64,4384]{2,1,0:T(8,128)(2,1)S(1)}, u32[]{:S(2)}, u32[]{:S(2)}) collective-permute-start(bf16[2,64,4384]{2,1,0:T(8,128)(2,1)S(1)} %collective-permute-done.5), channel_id=1, source_target_pairs={{0,8},{8,0},{1,9},{9,1},{2,10},{10,2},{3,11},{11,3},{4,12},{12,4},... | collective-permute-start | bytes 3366920 | tf_op jit(solution)/shard_map/ppermute | solution.py:259
  92.8 16.7 %collective-permute-start.10 = (bf16[2,64,4384]{2,1,0:T(8,128)(2,1)S(1)}, bf16[2,64,4384]{2,1,0:T(8,128)(2,1)S(1)}, u32[]{:S(2)}, u32[]{:S(2)}) collective-permute-start(bf16[2,64,4384]{2,1,0:T(8,128)(2,1)S(1)} %constant_dynamic-update-slice_fusion), channel_id=1, source_target_pairs={{0,8},{8,0},{1,9},{9,1},{2,10},{10,2},{3,11},{11,3},{4,12},{12,4},... | collective-permute-start | bytes 3366920 | tf_op jit(solution)/shard_map/ppermute | solution.py:259
  128.6 14.9 %collective-permute-start.12 = (bf16[8,128,1024]{2,1,0:T(8,128)(2,1)}, bf16[8,128,1024]{2,1,0:T(8,128)(2,1)S(1)}, u32[]{:S(2)}, u32[]{:S(2)}) collective-permute-start(bf16[8,128,1024]{2,1,0:T(8,128)(2,1)} %bitcast.327), channel_id=1, source_target_pairs={{0,8},{8,0},{1,9},{9,1},{2,10},{10,2},{3,11},{11,3},{4,12},{12,4},... | collective-permute-start | bytes 6291464 | tf_op jit(solution)/shard_map/ppermute | solution.py:259
  206.4 32.5 %collective-permute-start.13 = (f32[8,64,4480]{2,1,0:T(8,128)}, f32[8,64,4480]{2,1,0:T(8,128)}, u32[]{:S(2)}, u32[]{:S(2)}) collective-permute-start(f32[8,64,4480]{2,1,0:T(8,128)} %dynamic-slice_bitcast_fusion), channel_id=1, source_target_pairs={{0,8},{8,0},{1,9},{9,1},{2,10},{10,2},{3,11},{11,3},{4,12},{12,4},... | collective-permute-start | bytes 27525128 | tf_op jit(solution)/shard_map/ppermute | solution.py:259
  215.1 15.0 %collective-permute-start.21 = (f32[8,128,1024]{2,1,0:T(8,128)}, f32[8,128,1024]{2,1,0:T(8,128)}, u32[]{:S(2)}, u32[]{:S(2)}) collective-permute-start(f32[8,128,1024]{2,1,0:T(8,128)} %dynamic-slice_bitcast_fusion.1), channel_id=1, source_target_pairs={{0,8},{8,0},{1,9},{9,1},{2,10},{10,2},{3,11},{11,3},{4,12},{12,4},... | collective-permute-start | bytes 12582920 | tf_op jit(solution)/shard_map/ppermute | solution.py:259
  227.2 42.6 %collective-permute-start.33 = (f32[2,8,128]{2,0,1:T(2,128)S(1)}, f32[2,8,128]{2,0,1:T(2,128)S(1)}, u32[]{:S(2)}, u32[]{:S(2)}) collective-permute-start(f32[2,8,128]{2,0,1:T(2,128)S(1)} %slice.470), channel_id=1, source_target_pairs={{0,6},{2,0},{4,2},{6,4},{1,7},{3,1},{5,3},{7,5},{8,14},{10,8},{12,... | collective-permute-start | bytes 24584 | tf_op jit(solution)/shard_map/ppermute | solution.py:160
  236.8 47.4 %collective-permute-start.25 = (bf16[2,64,1024]{2,1,0:T(8,128)(2,1)S(1)}, bf16[2,64,1024]{2,1,0:T(8,128)(2,1)S(1)}, u32[]{:S(2)}, u32[]{:S(2)}) collective-permute-start(bf16[2,64,1024]{2,1,0:T(8,128)(2,1)S(1)} %slice.603), channel_id=1, source_target_pairs={{0,6},{2,0},{4,2},{6,4},{1,7},{3,1},{5,3},{7,5},{8,14},{10,8},{12,... | collective-permute-start | bytes 786440 | tf_op jit(solution)/shard_map/ppermute | solution.py:160
  238.1 46.1 %collective-permute-start.22 = (bf16[2,64,1024]{2,1,0:T(8,128)(2,1)S(1)}, bf16[2,64,1024]{2,1,0:T(8,128)(2,1)}, u32[]{:S(2)}, u32[]{:S(2)}) collective-permute-start(bf16[2,64,1024]{2,1,0:T(8,128)(2,1)S(1)} %slice.604), channel_id=1, source_target_pairs={{0,2},{2,4},{4,6},{6,0},{1,3},{3,5},{5,7},{7,1},{8,10},{10,12},{12... | collective-permute-start | bytes 786440 | tf_op jit(solution)/shard_map/ppermute | solution.py:160
  266.6 21.8 %collective-permute-start.17 = (bf16[2,32,4480]{2,1,0:T(8,128)(2,1)}, bf16[2,32,4480]{2,1,0:T(8,128)(2,1)S(1)}, u32[]{:S(2)}, u32[]{:S(2)}) collective-permute-start(bf16[2,32,4480]{2,1,0:T(8,128)(2,1)} %slice.601), channel_id=1, source_target_pairs={{0,6},{2,0},{4,2},{6,4},{1,7},{3,1},{5,3},{7,5},{8,14},{10,8},{12,... | collective-permute-start | bytes 1720328 | tf_op jit(solution)/shard_map/ppermute | solution.py:160
  269.8 18.6 %collective-permute-start.14 = (bf16[2,32,4480]{2,1,0:T(8,128)(2,1)}, bf16[2,32,4480]{2,1,0:T(8,128)(2,1)}, u32[]{:S(2)}, u32[]{:S(2)}) collective-permute-start(bf16[2,32,4480]{2,1,0:T(8,128)(2,1)} %slice.602), channel_id=1, source_target_pairs={{0,2},{2,4},{4,6},{6,0},{1,3},{3,5},{5,7},{7,1},{8,10},{10,12},{12... | collective-permute-start | bytes 1720328 | tf_op jit(solution)/shard_map/ppermute | solution.py:160
  269.8 11.0 %collective-permute-start.34 = (f32[2,8,128]{2,0,1:T(2,128)S(1)}, f32[2,8,128]{2,0,1:T(2,128)S(1)}, u32[]{:S(2)}, u32[]{:S(2)}) collective-permute-start(f32[2,8,128]{2,0,1:T(2,128)S(1)} %slice_add_fusion.15), channel_id=1, source_target_pairs={{0,6},{2,0},{4,2},{6,4},{1,7},{3,1},{5,3},{7,5},{8,14},{10,8},{12,... | collective-permute-start | bytes 24584 | tf_op jit(solution)/shard_map/ppermute | solution.py:160
  280.8 48.3 %collective-permute-start.35 = (f32[2,8,128]{2,0,1:T(2,128)S(1)}, f32[2,8,128]{2,0,1:T(2,128)S(1)}, u32[]{:S(2)}, u32[]{:S(2)}) collective-permute-start(f32[2,8,128]{2,0,1:T(2,128)S(1)} %get-tuple-element.130), channel_id=1, source_target_pairs={{0,6},{2,0},{4,2},{6,4},{1,7},{3,1},{5,3},{7,5},{8,14},{10,8},{12,... | collective-permute-start | bytes 24584 | tf_op jit(solution)/shard_map/ppermute | solution.py:160
  284.2 9.0 %collective-permute-start.30 = (f32[2,8,128]{2,0,1:T(2,128)S(1)}, f32[2,8,128]{2,0,1:T(2,128)S(1)}, u32[]{:S(2)}, u32[]{:S(2)}) collective-permute-start(f32[2,8,128]{2,0,1:T(2,128)S(1)} %get-tuple-element.131), channel_id=1, source_target_pairs={{0,2},{2,4},{4,6},{6,0},{1,3},{3,5},{5,7},{7,1},{8,10},{10,12},{12... | collective-permute-start | bytes 24584 | tf_op jit(solution)/shard_map/ppermute | solution.py:160
  285.6 7.7 %collective-permute-start.26 = (bf16[2,64,1024]{2,1,0:T(8,128)(2,1)S(1)}, bf16[2,64,1024]{2,1,0:T(8,128)(2,1)S(1)}, u32[]{:S(2)}, u32[]{:S(2)}) collective-permute-start(bf16[2,64,1024]{2,1,0:T(8,128)(2,1)S(1)} %get-tuple-element.109), channel_id=1, source_target_pairs={{0,6},{2,0},{4,2},{6,4},{1,7},{3,1},{5,3},{7,5},{8,14},{10,8},{12,... | collective-permute-start | bytes 786440 | tf_op jit(solution)/shard_map/ppermute | solution.py:160
  288.4 7.8 %collective-permute-start.23 = (bf16[2,64,1024]{2,1,0:T(8,128)(2,1)S(1)}, bf16[2,64,1024]{2,1,0:T(8,128)(2,1)S(1)}, u32[]{:S(2)}, u32[]{:S(2)}) collective-permute-start(bf16[2,64,1024]{2,1,0:T(8,128)(2,1)S(1)} %get-tuple-element.110), channel_id=1, source_target_pairs={{0,2},{2,4},{4,6},{6,0},{1,3},{3,5},{5,7},{7,1},{8,10},{10,12},{12... | collective-permute-start | bytes 786440 | tf_op jit(solution)/shard_map/ppermute | solution.py:160
  290.5 13.7 %collective-permute-start.18 = (bf16[2,32,4480]{2,1,0:T(8,128)(2,1)S(1)}, bf16[2,32,4480]{2,1,0:T(8,128)(2,1)S(1)}, u32[]{:S(2)}, u32[]{:S(2)}) collective-permute-start(bf16[2,32,4480]{2,1,0:T(8,128)(2,1)S(1)} %get-tuple-element.92), channel_id=1, source_target_pairs={{0,6},{2,0},{4,2},{6,4},{1,7},{3,1},{5,3},{7,5},{8,14},{10,8},{12,... | collective-permute-start | bytes 1720328 | tf_op jit(solution)/shard_map/ppermute | solution.py:160
  293.2 23.3 %collective-permute-start.31 = (f32[2,8,128]{2,0,1:T(2,128)S(1)}, f32[2,8,128]{2,0,1:T(2,128)S(1)}, u32[]{:S(2)}, u32[]{:S(2)}) collective-permute-start(f32[2,8,128]{2,0,1:T(2,128)S(1)} %slice_add_fusion.18), channel_id=1, source_target_pairs={{0,2},{2,4},{4,6},{6,0},{1,3},{3,5},{5,7},{7,1},{8,10},{10,12},{12... | collective-permute-start | bytes 24584 | tf_op jit(solution)/shard_map/ppermute | solution.py:160
  293.4 23.5 %collective-permute-start.27 = (bf16[2,64,1024]{2,1,0:T(8,128)(2,1)S(1)}, bf16[2,64,1024]{2,1,0:T(8,128)(2,1)S(1)}, u32[]{:S(2)}, u32[]{:S(2)}) collective-permute-start(bf16[2,64,1024]{2,1,0:T(8,128)(2,1)S(1)} %fusion.81), channel_id=1, source_target_pairs={{0,6},{2,0},{4,2},{6,4},{1,7},{3,1},{5,3},{7,5},{8,14},{10,8},{12,... | collective-permute-start | bytes 786440 | tf_op jit(solution)/shard_map/ppermute | solution.py:160
  296.2 20.8 %collective-permute-start.24 = (bf16[2,64,1024]{2,1,0:T(8,128)(2,1)S(1)}, bf16[2,64,1024]{2,1,0:T(8,128)(2,1)S(1)}, u32[]{:S(2)}, u32[]{:S(2)}) collective-permute-start(bf16[2,64,1024]{2,1,0:T(8,128)(2,1)S(1)} %fusion.83), channel_id=1, source_target_pairs={{0,2},{2,4},{4,6},{6,0},{1,3},{3,5},{5,7},{7,1},{8,10},{10,12},{12... | collective-permute-start | bytes 786440 | tf_op jit(solution)/shard_map/ppermute | solution.py:160
  304.2 11.1 %collective-permute-start.15 = (bf16[2,32,4480]{2,1,0:T(8,128)(2,1)S(1)}, bf16[2,32,4480]{2,1,0:T(8,128)(2,1)S(1)}, u32[]{:S(2)}, u32[]{:S(2)}) collective-permute-start(bf16[2,32,4480]{2,1,0:T(8,128)(2,1)S(1)} %get-tuple-element.93), channel_id=1, source_target_pairs={{0,2},{2,4},{4,6},{6,0},{1,3},{3,5},{5,7},{7,1},{8,10},{10,12},{12... | collective-permute-start | bytes 1720328 | tf_op jit(solution)/shard_map/ppermute | solution.py:160
  315.3 8.6 %collective-permute-start.19 = (bf16[2,32,4480]{2,1,0:T(8,128)(2,1)S(1)}, bf16[2,32,4480]{2,1,0:T(8,128)(2,1)S(1)}, u32[]{:S(2)}, u32[]{:S(2)}) collective-permute-start(bf16[2,32,4480]{2,1,0:T(8,128)(2,1)S(1)} %fusion.55), channel_id=1, source_target_pairs={{0,6},{2,0},{4,2},{6,4},{1,7},{3,1},{5,3},{7,5},{8,14},{10,8},{12,... | collective-permute-start | bytes 1720328 | tf_op jit(solution)/shard_map/ppermute | solution.py:160
  316.6 10.4 %collective-permute-start.16 = (bf16[2,32,4480]{2,1,0:T(8,128)(2,1)S(1)}, bf16[2,32,4480]{2,1,0:T(8,128)(2,1)S(1)}, u32[]{:S(2)}, u32[]{:S(2)}) collective-permute-start(bf16[2,32,4480]{2,1,0:T(8,128)(2,1)S(1)} %fusion.57), channel_id=1, source_target_pairs={{0,2},{2,4},{4,6},{6,0},{1,3},{3,5},{5,7},{7,1},{8,10},{10,12},{12... | collective-permute-start | bytes 1720328 | tf_op jit(solution)/shard_map/ppermute | solution.py:160
  317.0 12.1 %collective-permute-start.32 = (f32[2,8,128]{2,0,1:T(2,128)S(1)}, f32[2,8,128]{2,0,1:T(2,128)S(1)}, u32[]{:S(2)}, u32[]{:S(2)}) collective-permute-start(f32[2,8,128]{2,0,1:T(2,128)S(1)} %slice_add_fusion.17), channel_id=1, source_target_pairs={{0,2},{2,4},{4,6},{6,0},{1,3},{3,5},{5,7},{7,1},{8,10},{10,12},{12... | collective-permute-start | bytes 24584 | tf_op jit(solution)/shard_map/ppermute | solution.py:160
  317.3 21.7 %collective-permute-start.28 = (bf16[128,1024]{1,0:T(8,128)(2,1)S(1)}, bf16[128,1024]{1,0:T(8,128)(2,1)}, u32[]{:S(2)}, u32[]{:S(2)}) collective-permute-start(bf16[128,1024]{1,0:T(8,128)(2,1)S(1)} %fusion.92), channel_id=1, source_target_pairs={{0,1},{1,0},{2,3},{3,2},{4,5},{5,4},{6,7},{7,6},{8,9},{9,8},{10,11... | collective-permute-start | bytes 786440 | tf_op jit(solution)/shard_map/ppermute | solution.py:175
  329.1 12.8 %collective-permute-start.20 = (bf16[64,4480]{1,0:T(8,128)(2,1)}, bf16[64,4480]{1,0:T(8,128)(2,1)}, u32[]{:S(2)}, u32[]{:S(2)}) collective-permute-start(bf16[64,4480]{1,0:T(8,128)(2,1)} %fusion.75), channel_id=1, source_target_pairs={{0,1},{1,0},{2,3},{3,2},{4,5},{5,4},{6,7},{7,6},{8,9},{9,8},{10,11... | collective-permute-start | bytes 1720328 | tf_op jit(solution)/shard_map/ppermute | solution.py:175
  329.1 9.8 %collective-permute-start.36 = (f32[16,128]{1,0:T(8,128)S(1)}, f32[16,128]{1,0:T(8,128)S(1)}, u32[]{:S(2)}, u32[]{:S(2)}) collective-permute-start(f32[16,128]{1,0:T(8,128)S(1)} %bitcast.368), channel_id=1, source_target_pairs={{0,1},{1,0},{2,3},{3,2},{4,5},{5,4},{6,7},{7,6},{8,9},{9,8},{10,11... | collective-permute-start | bytes 24584 | tf_op jit(solution)/shard_map/ppermute | solution.py:175
  346.2 6.1 %collective-permute-start.37 = (f32[416,128]{1,0:T(8,128)S(1)}, f32[416,128]{1,0:T(8,128)S(1)}, u32[]{:S(2)}, u32[]{:S(2)}) collective-permute-start(f32[416,128]{1,0:T(8,128)S(1)} %get-tuple-element.99), channel_id=1, source_target_pairs={{0,16},{16,32},{32,48},{48,0},{64,80},{80,96},{96,112},{112,64},{1... | collective-permute-start | bytes 638984 | tf_op jit(solution)/shard_map/ppermute | solution.py:192
  347.6 4.7 %collective-permute-start.39 = (f32[416,128]{1,0:T(8,128)S(1)}, f32[416,128]{1,0:T(8,128)S(1)}, u32[]{:S(2)}, u32[]{:S(2)}) collective-permute-start(f32[416,128]{1,0:T(8,128)S(1)} %get-tuple-element.100), channel_id=1, source_target_pairs={{0,48},{16,0},{32,16},{48,32},{64,112},{80,64},{96,80},{112,96},{1... | collective-permute-start | bytes 638984 | tf_op jit(solution)/shard_map/ppermute | solution.py:193
  352.4 7.8 %collective-permute-start.40 = (f32[832,128]{1,0:T(8,128)S(1)}, f32[832,128]{1,0:T(8,128)}, u32[]{:S(2)}, u32[]{:S(2)}) collective-permute-start(f32[832,128]{1,0:T(8,128)S(1)} %pad_maximum_fusion.3), channel_id=1, source_target_pairs={{0,48},{16,0},{32,16},{48,32},{64,112},{80,64},{96,80},{112,96},{1... | collective-permute-start | bytes 1277960 | tf_op jit(solution)/shard_map/ppermute | solution.py:196
  355.2 10.8 %collective-permute-start.38 = (f32[832,128]{1,0:T(8,128)S(1)}, f32[832,128]{1,0:T(8,128)S(1)}, u32[]{:S(2)}, u32[]{:S(2)}) collective-permute-start(f32[832,128]{1,0:T(8,128)S(1)} %pad_maximum_fusion.2), channel_id=1, source_target_pairs={{0,16},{16,32},{32,48},{48,0},{64,80},{80,96},{96,112},{112,64},{1... | collective-permute-start | bytes 1277960 | tf_op jit(solution)/shard_map/ppermute | solution.py:196
  367.2 8.6 %collective-permute-start.41 = (f32[832,128]{1,0:T(8,128)S(1)}, f32[832,128]{1,0:T(8,128)S(1)}, u32[]{:S(2)}, u32[]{:S(2)}) collective-permute-start(f32[832,128]{1,0:T(8,128)S(1)} %fusion.89), channel_id=1, source_target_pairs={{0,64},{16,80},{32,96},{48,112},{64,0},{80,16},{96,32},{112,48},{1... | collective-permute-start | bytes 1277960 | tf_op jit(solution)/shard_map/ppermute | solution.py:199
  375.8 7.3 %collective-permute-start.42 = (f32[832,128]{1,0:T(8,128)S(1)}, f32[832,128]{1,0:T(8,128)S(1)}, u32[]{:S(2)}, u32[]{:S(2)}) collective-permute-start(f32[832,128]{1,0:T(8,128)S(1)} %get-tuple-element.58), channel_id=1, source_target_pairs={{0,48},{16,0},{32,16},{48,32},{64,112},{80,64},{96,80},{112,96},{1... | collective-permute-start | bytes 1277960 | tf_op jit(solution)/shard_map/ppermute | solution.py:202
  375.9 8.6 %collective-permute-start.43 = (f32[832,128]{1,0:T(8,128)S(1)}, f32[832,128]{1,0:T(8,128)S(1)}, u32[]{:S(2)}, u32[]{:S(2)}) collective-permute-start(f32[832,128]{1,0:T(8,128)S(1)} %get-tuple-element.58), channel_id=1, source_target_pairs={{0,16},{16,32},{32,48},{48,0},{64,80},{80,96},{96,112},{112,64},{1... | collective-permute-start | bytes 1277960 | tf_op jit(solution)/shard_map/ppermute | solution.py:201
  383.2 4.8 %collective-permute-start.45 = (f32[416,128]{1,0:T(8,128)S(1)}, f32[416,128]{1,0:T(8,128)S(1)}, u32[]{:S(2)}, u32[]{:S(2)}) collective-permute-start(f32[416,128]{1,0:T(8,128)S(1)} %slice.482), channel_id=1, source_target_pairs={{0,48},{16,0},{32,16},{48,32},{64,112},{80,64},{96,80},{112,96},{1... | collective-permute-start | bytes 638984 | tf_op jit(solution)/shard_map/ppermute | solution.py:204
  384.5 6.0 %collective-permute-start.44 = (f32[416,128]{1,0:T(8,128)S(1)}, f32[416,128]{1,0:T(8,128)S(1)}, u32[]{:S(2)}, u32[]{:S(2)}) collective-permute-start(f32[416,128]{1,0:T(8,128)S(1)} %slice.481), channel_id=1, source_target_pairs={{0,16},{16,32},{32,48},{48,0},{64,80},{80,96},{96,112},{112,64},{1... | collective-permute-start | bytes 638984 | tf_op jit(solution)/shard_map/ppermute | solution.py:203
  395.7 27.0 %collective-permute-start.46 = (f32[64,4480]{1,0:T(8,128)}, f32[64,4480]{1,0:T(8,128)}, u32[]{:S(2)}, u32[]{:S(2)}) collective-permute-start(f32[64,4480]{1,0:T(8,128)} %reshape.789), channel_id=1, source_target_pairs={{0,8},{8,0},{1,9},{9,1},{2,10},{10,2},{3,11},{11,3},{4,12},{12,4},... | collective-permute-start | bytes 3440648 | tf_op jit(solution)/shard_map/ppermute | solution.py:259
  416.0 5.5 %collective-permute-start.47 = (f32[128,1024]{1,0:T(8,128)S(1)}, f32[128,1024]{1,0:T(8,128)S(1)}, u32[]{:S(2)}, u32[]{:S(2)}) collective-permute-start(f32[128,1024]{1,0:T(8,128)S(1)} %reshape.791), channel_id=1, source_target_pairs={{0,8},{8,0},{1,9},{9,1},{2,10},{10,2},{3,11},{11,3},{4,12},{12,4},... | collective-permute-start | bytes 1572872 | tf_op jit(solution)/shard_map/ppermute | solution.py:259
  (62 other events, 624.9 us)
Sparse Core Ops, SparseCore 0:
  16.8 56.7 all-gather.2

commit v13 on v12

--- a/solution.py
+++ b/solution.py
@@ -376,7 +376,8 @@
     normed_f, norm_back = jax.vjp(norm_input, layer_in, norm_full)
     normed = normed_f.astype(jnp.bfloat16)
     in_whole = gather_rows(in_weight, by_permutes=True)
-    out_whole = gather_rows(out_weight)
+    in_whole, out_weight = lax.optimization_barrier((in_whole, out_weight))
+    out_whole = gather_rows(out_weight, by_permutes=True)
     projected = halves_product(normed, in_whole, groups)
 
     def bound_mixer(proj_arg, cw_arg, cb_arg, sb_arg, dl_arg, sk_arg, gg_arg):

time: 441 us -> 447 us (1.014)
  starting transfers between devices: 73.6 us -> 91.3 us
  between operations: 15.8 us -> 2.9 us
  waiting for transfers between devices: 119 us -> 107 us
  matrix products: 49.6 us -> 59.3 us
  local copies, waits for them, and re-layouts: 89.5 us -> 94.4 us
    ppermute x1 -> x2, waiting for transfers between devices: 37.1 us -> 26.5 us  [gather_group(): from_prev = lax.ppermute(pair, 'shard_0', up)]
    ppermute x10 -> x13, starting transfers between devices: 26.2 us -> 33.9 us  [core_swap(): return lax.ppermute(values, 'core', [(0, 1), (1, 0)])]
    dot_general x4, matrix products: 4.29 us -> 8.87 us  [back_product(): lax.dot_general(left, right, (((1,), (1,)), ((), ())), preferred_element_...]
    unnamed x146 -> x221, local copies, waits for them, and re-layouts: 32.1 us -> 36.2 us
  transfers between devices with their start and end apart: 49 -> 56, of which waited for: 17 -> 19; matrix products, arithmetic and copies ran while one was open for 32% -> 29% of each run, Pallas kernels for 0% -> 0%
where the time goes in v13:
time: 447 us; the launch traced here: 439 us
  waiting for transfers between devices  107 us (24%)
  local copies, waits for them, and re-layouts  94.4 us (21%)
  starting transfers between devices  91.3 us (20%)
  other arithmetic  83.6 us (19%)
  matrix products  59.3 us (13%)
    ppermute x18, waiting for transfers between devices, send(): lax.ppermute(p.astype(w), 'shard_0', pairs)  39.1 us
    unnamed x221, local copies, waits for them, and re-layouts  36.2 us
    ppermute x13, starting transfers between devices, core_swap(): return lax.ppermute(values, 'core', [(0, 1), (1, 0)])  33.9 us
    dot_general x3, matrix products, mixer(): y_intra = jnp.einsum('chij,cjhp->cihp', mixing, scaled_in, precision=HIGH)  31.8 us
    ppermute x2, waiting for transfers between devices, gather_group(): from_prev = lax.ppermute(pair, 'shard_0', up)  26.5 us
    ppermute x18, starting transfers between devices, send(): lax.ppermute(p.astype(w), 'shard_0', pairs)  21.4 us
    add x2, other arithmetic, reduce_core(): return keep + core_swap(give)  15.1 us
    concatenate x3, other arithmetic, reduce_group(): doubled = jnp.concatenate([blocks, blocks], axis=0)  9.36 us
  transfers between devices with their start and end apart: 56, of which 19 were waited for; matrix products, arithmetic and copies ran while one was open for 29% of the time, Pallas kernels for 0%

profile of v13, /device:TPU:1, one launch (start us, length us, event | category | flops | bytes accessed | tf_op | source)
XLA Modules:
  0.0 438.8 jit_solution(1949024215292129670)
XLA Ops:
  4.7 3.4 constant_dynamic-slice_fusion.8
  14.7 3.5 collective-permute-start.2
  31.9 3.3 collective-permute-start.8
  37.0 17.5 %collective-permute-done.5 = bf16[2,64,4384]{2,1,0:T(8,128)(2,1)S(1)} collective-permute-done((bf16[2,64,4384]{2,1,0:T(8,128)(2,1)S(1)}, bf16[2,64,4384]{2,1,0:T(8,128)(2,1)S(1)}, u32[]{:S(2)}, u32[]{:S(2)}) %collective-permute-start.5) | collective-permute-done | bytes 1122336 | tf_op jit(solution)/shard_map/ppermute | solution.py:243
  54.7 2.7 collective-permute-start.7
  57.4 4.2 collective-permute-start.11
  62.7 4.0 collective-permute-done.6
  66.9 4.8 %collective-permute-start.10 = (bf16[2,64,4384]{2,1,0:T(8,128)(2,1)S(1)}, bf16[2,64,4384]{2,1,0:T(8,128)(2,1)S(1)}, u32[]{:S(2)}, u32[]{:S(2)}) collective-permute-start(bf16[2,64,4384]{2,1,0:T(8,128)(2,1)S(1)} %constant_dynamic-update-slice_fusion), channel_id=1, source_target_pairs={{0,8},{8,0},{1,9},{9,1},{2,10},{10,2},{3,11},{11,3},{4,12},{12,4},... | collective-permute-start | bytes 3366920 | tf_op jit(solution)/shard_map/ppermute | solution.py:259
  96.2 4.9 %fusion.21 = (f32[256,2304]{0,1:T(8,128)S(1)}, f32[256,2304]{0,1:T(8,128)}) fusion(f32[253,2304]{0,1:T(8,128)S(1)} %slice.434, f32[2304]{0:T(1024)S(1)} %get-tuple-element.60, pred[256]{0:T(512)(128)(4,1)S(1)} %copy-done.79, f32[254,2304]{0,1:T(8,128)S(1)} %slice.432, f32[2304]{0:T(1024)S(1)} %get-tuple-element.61, pred[256]{0:T(512)(128)(4,1)S(1)} %copy-done.77, ...), kind=kLoop, calls=%fused_computation.54 | loop fusion | flops 8847360 | bytes 14147328 | tf_op jit(solution)/shard_map/jvp(jit(silu))/mul | solution.py:110
  111.4 11.8 %fusion.29 = f32[256,32,64]{0,2,1:T(8,128)S(1)} fusion(f32[256,32,64]{0,2,1:T(8,128)} %bitcast.366, f32[256,32,64]{0,2,1:T(8,128)S(1)} %fusion.76, f32[32]{0:T(128)} %copy-done.86, f32[256,32]{0,1:T(8,128)S(1)} %bitcast_multiply_fusion.8, f32[256,256]{1,0:T(8,128)} %fusion.92, f32[32,256]{1,0:T(8,128)S(1)} %bitcast_add_fusion.4, ...), kind=kOutput, calls=%fused_computation.73 | convolution fusion | flops 1619525632 | bytes 6717568 | tf_op jit(solution)/shard_map/jvp(chij,cjhp->cihp)/dot_general | solution.py:132
  124.4 2.8 collective-permute-start.13
  129.9 9.0 %collective-permute-done.14 = bf16[2,128,1024]{2,1,0:T(8,128)(2,1)S(1)} collective-permute-done((bf16[2,128,1024]{2,1,0:T(8,128)(2,1)S(1)}, bf16[2,128,1024]{2,1,0:T(8,128)(2,1)S(1)}, u32[]{:S(2)}, u32[]{:S(2)}) %collective-permute-start.14) | collective-permute-done | bytes 524320 | tf_op jit(solution)/shard_map/ppermute | solution.py:243
  139.2 2.7 collective-permute-start.16
  143.5 3.4 collective-permute-done.15
  156.8 4.0 multiply_reduce_fusion.5
  162.7 11.4 %fusion.7 = (f32[32,256]{1,0:T(8,128)S(1)}, f32[32,256]{1,0:T(8,128)S(1)}, f32[256,256]{1,0:T(8,128)S(1)}) fusion(f32[256,256]{1,0:T(8,128)S(1)} %copy-done.54, f32[32,256]{1,0:T(8,128)S(1)} %bitcast_add_fusion.4, pred[256,256]{1,0:T(8,128)(4,1)S(1)} %copy-done.62, f32[32,64,256]{2,1,0:T(8,128)S(1)} %bitcast.332, f32[256,32,64]{0,2,1:T(8,128)S(1)} %bitcast.367, ...), kind=kOutput, calls=%fused_computation.15 | convolution fusion | flops 1629929472 | bytes 4915200 | tf_op jit(solution)/shard_map/transpose(jvp(chij,cjhp->cihp))/dot_general | solution.py:132
  174.1 8.7 %fusion.30 = (f32[256,32]{0,1:T(8,128)}, f32[1,256,32,64]{1,3,2,0:T(8,128)}) fusion(f32[1,256,32,64]{1,3,2,0:T(8,128)S(1)} %bitcast.368, f32[256,32]{0,1:T(8,128)S(1)} %copy-done.56, f32[32,64,256]{2,1,0:T(8,128)S(1)} %bitcast.333, f32[256,256]{1,0:T(8,128)S(1)} %copy-done.54, f32[32,256]{1,0:T(8,128)S(1)} %bitcast_add_fusion.4, ...), kind=kOutput, calls=%fused_computation.77 | convolution fusion | flops 1618468864 | bytes 6717440 | tf_op jit(solution)/shard_map/transpose(jvp(chij,cjhp->cihp))/dot_general | solution.py:132
  191.5 2.8 multiply_reduce_fusion.4
  194.2 2.9 multiply_reduce_fusion.3
  206.4 4.6 %dynamic-slice_bitcast_fusion = f32[8,64,4480]{2,1,0:T(8,128)} fusion(f32[8,2,64,4480]{3,2,1,0:T(8,128)S(1)} %bitcast.326, s32[]{:T(128)S(6)} %select_n.227), kind=kLoop, calls=%fused_computation.4 | loop fusion | bytes 18350084 | tf_op jit(solution)/shard_map/jit(dynamic_index_in_dim)/squeeze | solution.py:312
  211.1 4.4 %copy-done.2 = f32[1024,4480]{1,0:T(8,128)} copy-done((f32[1024,4480]{1,0:T(8,128)}, f32[1024,4480]{1,0:T(8,128)S(1)}, u32[]{:S(2)}) %copy-start.2) | copy-done | bytes 18350104
  215.5 2.8 fusion.112
  224.8 3.7 fusion.132
  228.4 3.7 fusion.133
  236.5 2.9 collective-permute-start.41
  239.5 4.4 %bitcast_add_fusion.1 = f32[8,128,1024]{2,1,0:T(8,128)S(1)} fusion(f32[8,128,1024]{2,1,0:T(8,128)} %collective-permute-done.29, f32[8,2,128,1024]{3,2,1,0:T(8,128)} %bitcast.329, s32[]{:T(128)S(6)} %select_n.217), kind=kLoop, calls=%fused_computation.22 | loop fusion | flops 1048576 | bytes 12582916 | tf_op jit(solution)/shard_map/add | solution.py:313
  250.5 10.7 %bitcast_add_fusion = f32[8,64,4480]{2,1,0:T(8,128)} fusion(f32[8,64,4480]{2,1,0:T(8,128)} %collective-permute-done.21, f32[8,2,64,4480]{3,2,1,0:T(8,128)} %bitcast.327, s32[]{:T(128)S(6)} %select_n.217), kind=kLoop, calls=%fused_computation.3 | loop fusion | flops 2293760 | bytes 27525124 | tf_op jit(solution)/shard_map/add | solution.py:313
  261.2 8.2 %fusion = f32[4,2,64,4480]{3,2,1,0:T(8,128)} fusion(s32[]{:T(128)S(6)} %select_n.247, f32[4,2,64,4480]{3,2,1,0:T(8,128)} %bitcast.330), kind=kLoop, calls=%fused_computation.2 | loop fusion | flops 2293760 | bytes 18350084 | tf_op jit(solution)/shard_map/concatenate | solution.py:155
  269.5 5.7 %slice_bitcast_fusion.3 = (f32[2,64,4480]{2,1,0:T(8,128)S(1)}, f32[2,64,4480]{2,1,0:T(8,128)S(1)}, f32[2,64,4480]{2,1,0:T(8,128)S(1)}, f32[2,64,4480]{2,1,0:T(8,128)}) fusion(f32[4,2,64,4480]{3,2,1,0:T(8,128)} %fusion), kind=kLoop, calls=%fused_computation.60 | loop fusion | bytes 18350080 | tf_op jit(solution)/shard_map/squeeze | solution.py:162
  281.7 9.8 %collective-permute-done.42 = f32[2,8,128]{2,0,1:T(2,128)S(1)} collective-permute-done((f32[2,8,128]{2,0,1:T(2,128)S(1)}, f32[2,8,128]{2,0,1:T(2,128)S(1)}, u32[]{:S(2)}, u32[]{:S(2)}) %collective-permute-start.42) | collective-permute-done | bytes 8224 | tf_op jit(solution)/shard_map/ppermute | solution.py:160
  291.5 3.0 collective-permute-start.43
  296.0 2.7 collective-permute-start.34
  300.4 2.7 collective-permute-start.26
  303.3 2.7 collective-permute-start.35
  306.2 9.0 %collective-permute-done.26 = bf16[2,32,4480]{2,1,0:T(8,128)(2,1)S(1)} collective-permute-done((bf16[2,32,4480]{2,1,0:T(8,128)(2,1)S(1)}, bf16[2,32,4480]{2,1,0:T(8,128)(2,1)S(1)}, u32[]{:S(2)}, u32[]{:S(2)}) %collective-permute-start.26) | collective-permute-done | bytes 573472 | tf_op jit(solution)/shard_map/ppermute | solution.py:160
  315.3 12.1 %collective-permute-done.23 = bf16[2,32,4480]{2,1,0:T(8,128)(2,1)S(1)} collective-permute-done((bf16[2,32,4480]{2,1,0:T(8,128)(2,1)S(1)}, bf16[2,32,4480]{2,1,0:T(8,128)(2,1)S(1)}, u32[]{:S(2)}, u32[]{:S(2)}) %collective-permute-start.23) | collective-permute-done | bytes 573472 | tf_op jit(solution)/shard_map/ppermute | solution.py:160
  330.3 6.4 %collective-permute-done.27 = bf16[2,32,4480]{2,1,0:T(8,128)(2,1)S(1)} collective-permute-done((bf16[2,32,4480]{2,1,0:T(8,128)(2,1)S(1)}, bf16[2,32,4480]{2,1,0:T(8,128)(2,1)S(1)}, u32[]{:S(2)}, u32[]{:S(2)}) %collective-permute-start.27) | collective-permute-done | bytes 573472 | tf_op jit(solution)/shard_map/ppermute | solution.py:160
  341.2 8.5 %collective-permute-done.44 = f32[16,128]{1,0:T(8,128)S(1)} collective-permute-done((f32[16,128]{1,0:T(8,128)S(1)}, f32[16,128]{1,0:T(8,128)S(1)}, u32[]{:S(2)}, u32[]{:S(2)}) %collective-permute-start.44) | collective-permute-done | bytes 8224 | tf_op jit(solution)/shard_map/ppermute | solution.py:175
  360.4 3.2 collective-permute-done.45
  364.5 2.7 collective-permute-start.48
  369.3 5.2 %collective-permute-done.48 = f32[832,128]{1,0:T(8,128)} collective-permute-done((f32[832,128]{1,0:T(8,128)}, f32[832,128]{1,0:T(8,128)}, u32[]{:S(2)}, u32[]{:S(2)}) %collective-permute-start.48) | collective-permute-done | bytes 426016 | tf_op jit(solution)/shard_map/ppermute | solution.py:196
  374.5 3.1 collective-permute-done.46
  378.9 2.7 collective-permute-start.49
  383.7 3.8 collective-permute-done.49
  392.0 3.8 collective-permute-done.51
  396.1 2.7 collective-permute-start.53
  398.9 3.1 collective-permute-done.52
  406.1 16.1 %collective-permute-start.54 = (f32[64,4480]{1,0:T(8,128)S(1)}, f32[64,4480]{1,0:T(8,128)}, u32[]{:S(2)}, u32[]{:S(2)}) collective-permute-start(f32[64,4480]{1,0:T(8,128)S(1)} %reshape.883), channel_id=1, source_target_pairs={{0,8},{8,0},{1,9},{9,1},{2,10},{10,2},{3,11},{11,3},{4,12},{12,4},... | collective-permute-start | bytes 3440648 | tf_op jit(solution)/shard_map/ppermute | solution.py:259
  (495 shorter events, 173.6 us)
Async XLA Ops:
  2.6 8.3 %collective-permute-start = (f32[8,1836]{1,0:T(8,128)S(1)}, f32[8,1836]{1,0:T(8,128)S(1)}, u32[]{:S(2)}, u32[]{:S(2)}) collective-permute-start(f32[8,1836]{1,0:T(8,128)S(1)} %broadcast_select_fusion.7), channel_id=1, source_target_pairs={{0,1},{1,0},{2,3},{3,2},{4,5},{5,4},{6,7},{7,6},{8,9},{9,8},{10,11... | collective-permute-start | bytes 176264 | tf_op jit(solution)/shard_map/ppermute | solution.py:338
  9.1 19.8 %collective-permute-start.3 = (bf16[64,4384]{1,0:T(8,128)(2,1)S(1)}, bf16[64,4384]{1,0:T(8,128)(2,1)S(1)}, u32[]{:S(2)}, u32[]{:S(2)}) collective-permute-start(bf16[64,4384]{1,0:T(8,128)(2,1)S(1)} %copy.125), channel_id=1, source_target_pairs={{0,1},{1,0},{2,3},{3,2},{4,5},{5,4},{6,7},{7,6},{8,9},{9,8},{10,11... | collective-permute-start | bytes 1683464 | tf_op jit(solution)/shard_map/ppermute | solution.py:241
  14.7 6.1 %collective-permute-start.2 = (f32[8,1836]{1,0:T(8,128)S(1)}, f32[8,1836]{1,0:T(8,128)S(1)}, u32[]{:S(2)}, u32[]{:S(2)}) collective-permute-start(f32[8,1836]{1,0:T(8,128)S(1)} %fusion.154), channel_id=1, source_target_pairs={{0,4},{2,6},{4,0},{6,2},{1,5},{3,7},{5,1},{7,3},{8,12},{10,14},{12... | collective-permute-start | bytes 176264 | tf_op jit(solution)/shard_map/ppermute | solution.py:338
  29.2 25.4 %collective-permute-start.5 = (bf16[2,64,4384]{2,1,0:T(8,128)(2,1)S(1)}, bf16[2,64,4384]{2,1,0:T(8,128)(2,1)S(1)}, u32[]{:S(2)}, u32[]{:S(2)}) collective-permute-start(bf16[2,64,4384]{2,1,0:T(8,128)(2,1)S(1)} %maximum_select_fusion.1), channel_id=1, source_target_pairs={{0,2},{2,4},{4,6},{6,0},{1,3},{3,5},{5,7},{7,1},{8,10},{10,12},{12... | collective-permute-start | bytes 3366920 | tf_op jit(solution)/shard_map/ppermute | solution.py:243
  30.0 24.7 %collective-permute-start.4 = (bf16[2,64,4384]{2,1,0:T(8,128)(2,1)S(1)}, bf16[2,64,4384]{2,1,0:T(8,128)(2,1)S(1)}, u32[]{:S(2)}, u32[]{:S(2)}) collective-permute-start(bf16[2,64,4384]{2,1,0:T(8,128)(2,1)S(1)} %maximum_select_fusion.1), channel_id=1, source_target_pairs={{0,6},{2,0},{4,2},{6,4},{1,7},{3,1},{5,3},{7,5},{8,14},{10,8},{12,... | collective-permute-start | bytes 3366920 | tf_op jit(solution)/shard_map/ppermute | solution.py:244
  54.6 12.2 %collective-permute-start.6 = (bf16[2,32,4384]{2,1,0:T(8,128)(2,1)S(1)}, bf16[2,32,4384]{2,1,0:T(8,128)(2,1)S(1)}, u32[]{:S(2)}, u32[]{:S(2)}) collective-permute-start(bf16[2,32,4384]{2,1,0:T(8,128)(2,1)S(1)} %slice.426), channel_id=1, source_target_pairs={{0,2},{2,4},{4,6},{6,0},{1,3},{3,5},{5,7},{7,1},{8,10},{10,12},{12... | collective-permute-start | bytes 1683464 | tf_op jit(solution)/shard_map/ppermute | solution.py:246
  54.7 12.1 %collective-permute-start.7 = (bf16[2,32,4384]{2,1,0:T(8,128)(2,1)S(1)}, bf16[2,32,4384]{2,1,0:T(8,128)(2,1)S(1)}, u32[]{:S(2)}, u32[]{:S(2)}) collective-permute-start(bf16[2,32,4384]{2,1,0:T(8,128)(2,1)S(1)} %slice.427), channel_id=1, source_target_pairs={{0,6},{2,0},{4,2},{6,4},{1,7},{3,1},{5,3},{7,5},{8,14},{10,8},{12,... | collective-permute-start | bytes 1683464 | tf_op jit(solution)/shard_map/ppermute | solution.py:247
  57.4 24.0 %collective-permute-start.11 = (bf16[2,64,4384]{2,1,0:T(8,128)(2,1)S(1)}, bf16[2,64,4384]{2,1,0:T(8,128)(2,1)S(1)}, u32[]{:S(2)}, u32[]{:S(2)}) collective-permute-start(bf16[2,64,4384]{2,1,0:T(8,128)(2,1)S(1)} %collective-permute-done.5), channel_id=1, source_target_pairs={{0,8},{8,0},{1,9},{9,1},{2,10},{10,2},{3,11},{11,3},{4,12},{12,4},... | collective-permute-start | bytes 3366920 | tf_op jit(solution)/shard_map/ppermute | solution.py:259
  61.6 19.5 %collective-permute-start.9 = (bf16[2,64,4384]{2,1,0:T(8,128)(2,1)S(1)}, bf16[2,64,4384]{2,1,0:T(8,128)(2,1)S(1)}, u32[]{:S(2)}, u32[]{:S(2)}) collective-permute-start(bf16[2,64,4384]{2,1,0:T(8,128)(2,1)S(1)} %collective-permute-done.4), channel_id=1, source_target_pairs={{0,8},{8,0},{1,9},{9,1},{2,10},{10,2},{3,11},{11,3},{4,12},{12,4},... | collective-permute-start | bytes 3366920 | tf_op jit(solution)/shard_map/ppermute | solution.py:259
  66.9 14.4 %collective-permute-start.10 = (bf16[2,64,4384]{2,1,0:T(8,128)(2,1)S(1)}, bf16[2,64,4384]{2,1,0:T(8,128)(2,1)S(1)}, u32[]{:S(2)}, u32[]{:S(2)}) collective-permute-start(bf16[2,64,4384]{2,1,0:T(8,128)(2,1)S(1)} %constant_dynamic-update-slice_fusion), channel_id=1, source_target_pairs={{0,8},{8,0},{1,9},{9,1},{2,10},{10,2},{3,11},{11,3},{4,12},{12,4},... | collective-permute-start | bytes 3366920 | tf_op jit(solution)/shard_map/ppermute | solution.py:259
  106.6 16.5 %collective-permute-start.12 = (bf16[128,1024]{1,0:T(8,128)(2,1)S(1)}, bf16[128,1024]{1,0:T(8,128)(2,1)}, u32[]{:S(2)}, u32[]{:S(2)}) collective-permute-start(bf16[128,1024]{1,0:T(8,128)(2,1)S(1)} %get-tuple-element.120), channel_id=1, source_target_pairs={{0,1},{1,0},{2,3},{3,2},{4,5},{5,4},{6,7},{7,6},{8,9},{9,8},{10,11... | collective-permute-start | bytes 786440 | tf_op jit(solution)/shard_map/ppermute | solution.py:241
  124.3 14.6 %collective-permute-start.14 = (bf16[2,128,1024]{2,1,0:T(8,128)(2,1)S(1)}, bf16[2,128,1024]{2,1,0:T(8,128)(2,1)S(1)}, u32[]{:S(2)}, u32[]{:S(2)}) collective-permute-start(bf16[2,128,1024]{2,1,0:T(8,128)(2,1)S(1)} %maximum_select_fusion.4), channel_id=1, source_target_pairs={{0,2},{2,4},{4,6},{6,0},{1,3},{3,5},{5,7},{7,1},{8,10},{10,12},{12... | collective-permute-start | bytes 1572872 | tf_op jit(solution)/shard_map/ppermute | solution.py:243
  124.4 14.8 %collective-permute-start.13 = (bf16[2,128,1024]{2,1,0:T(8,128)(2,1)S(1)}, bf16[2,128,1024]{2,1,0:T(8,128)(2,1)S(1)}, u32[]{:S(2)}, u32[]{:S(2)}) collective-permute-start(bf16[2,128,1024]{2,1,0:T(8,128)(2,1)S(1)} %maximum_select_fusion.4), channel_id=1, source_target_pairs={{0,6},{2,0},{4,2},{6,4},{1,7},{3,1},{5,3},{7,5},{8,14},{10,8},{12,... | collective-permute-start | bytes 1572872 | tf_op jit(solution)/shard_map/ppermute | solution.py:244
  127.9 11.1 %collective-permute-start.17 = (bf16[128,1024]{1,0:T(8,128)(2,1)}, bf16[128,1024]{1,0:T(8,128)(2,1)S(1)}, u32[]{:S(2)}, u32[]{:S(2)}) collective-permute-start(bf16[128,1024]{1,0:T(8,128)(2,1)} %collective-permute-done.12), channel_id=1, source_target_pairs={{0,8},{8,0},{1,9},{9,1},{2,10},{10,2},{3,11},{11,3},{4,12},{12,4},... | collective-permute-start | bytes 786440 | tf_op jit(solution)/shard_map/ppermute | solution.py:259
  138.9 8.0 %collective-permute-start.15 = (bf16[2,64,1024]{2,1,0:T(8,128)(2,1)S(1)}, bf16[2,64,1024]{2,1,0:T(8,128)(2,1)S(1)}, u32[]{:S(2)}, u32[]{:S(2)}) collective-permute-start(bf16[2,64,1024]{2,1,0:T(8,128)(2,1)S(1)} %slice.445), channel_id=1, source_target_pairs={{0,2},{2,4},{4,6},{6,0},{1,3},{3,5},{5,7},{7,1},{8,10},{10,12},{12... | collective-permute-start | bytes 786440 | tf_op jit(solution)/shard_map/ppermute | solution.py:246
  139.2 7.8 %collective-permute-start.16 = (bf16[2,64,1024]{2,1,0:T(8,128)(2,1)S(1)}, bf16[2,64,1024]{2,1,0:T(8,128)(2,1)S(1)}, u32[]{:S(2)}, u32[]{:S(2)}) collective-permute-start(bf16[2,64,1024]{2,1,0:T(8,128)(2,1)S(1)} %slice.446), channel_id=1, source_target_pairs={{0,6},{2,0},{4,2},{6,4},{1,7},{3,1},{5,3},{7,5},{8,14},{10,8},{12,... | collective-permute-start | bytes 786440 | tf_op jit(solution)/shard_map/ppermute | solution.py:247
  141.9 10.9 %collective-permute-start.20 = (bf16[2,128,1024]{2,1,0:T(8,128)(2,1)S(1)}, bf16[2,128,1024]{2,1,0:T(8,128)(2,1)S(1)}, u32[]{:S(2)}, u32[]{:S(2)}) collective-permute-start(bf16[2,128,1024]{2,1,0:T(8,128)(2,1)S(1)} %collective-permute-done.14), channel_id=1, source_target_pairs={{0,8},{8,0},{1,9},{9,1},{2,10},{10,2},{3,11},{11,3},{4,12},{12,4},... | collective-permute-start | bytes 1572872 | tf_op jit(solution)/shard_map/ppermute | solution.py:259
  143.5 9.2 %collective-permute-start.18 = (bf16[2,128,1024]{2,1,0:T(8,128)(2,1)S(1)}, bf16[2,128,1024]{2,1,0:T(8,128)(2,1)S(1)}, u32[]{:S(2)}, u32[]{:S(2)}) collective-permute-start(bf16[2,128,1024]{2,1,0:T(8,128)(2,1)S(1)} %collective-permute-done.13), channel_id=1, source_target_pairs={{0,8},{8,0},{1,9},{9,1},{2,10},{10,2},{3,11},{11,3},{4,12},{12,4},... | collective-permute-start | bytes 1572872 | tf_op jit(solution)/shard_map/ppermute | solution.py:259
  215.5 35.0 %collective-permute-start.21 = (f32[8,64,4480]{2,1,0:T(8,128)}, f32[8,64,4480]{2,1,0:T(8,128)}, u32[]{:S(2)}, u32[]{:S(2)}) collective-permute-start(f32[8,64,4480]{2,1,0:T(8,128)} %dynamic-slice_bitcast_fusion), channel_id=1, source_target_pairs={{0,8},{8,0},{1,9},{9,1},{2,10},{10,2},{3,11},{11,3},{4,12},{12,4},... | collective-permute-start | bytes 27525128 | tf_op jit(solution)/shard_map/ppermute | solution.py:259
  223.3 16.1 %collective-permute-start.29 = (f32[8,128,1024]{2,1,0:T(8,128)}, f32[8,128,1024]{2,1,0:T(8,128)}, u32[]{:S(2)}, u32[]{:S(2)}) collective-permute-start(f32[8,128,1024]{2,1,0:T(8,128)} %dynamic-slice_bitcast_fusion.1), channel_id=1, source_target_pairs={{0,8},{8,0},{1,9},{9,1},{2,10},{10,2},{3,11},{11,3},{4,12},{12,4},... | collective-permute-start | bytes 12582920 | tf_op jit(solution)/shard_map/ppermute | solution.py:259
  236.5 42.6 %collective-permute-start.41 = (f32[2,8,128]{2,0,1:T(2,128)S(1)}, f32[2,8,128]{2,0,1:T(2,128)S(1)}, u32[]{:S(2)}, u32[]{:S(2)}) collective-permute-start(f32[2,8,128]{2,0,1:T(2,128)S(1)} %slice.480), channel_id=1, source_target_pairs={{0,6},{2,0},{4,2},{6,4},{1,7},{3,1},{5,3},{7,5},{8,14},{10,8},{12,... | collective-permute-start | bytes 24584 | tf_op jit(solution)/shard_map/ppermute | solution.py:160
  249.0 45.5 %collective-permute-start.33 = (bf16[2,64,1024]{2,1,0:T(8,128)(2,1)}, bf16[2,64,1024]{2,1,0:T(8,128)(2,1)}, u32[]{:S(2)}, u32[]{:S(2)}) collective-permute-start(bf16[2,64,1024]{2,1,0:T(8,128)(2,1)} %slice.613), channel_id=1, source_target_pairs={{0,6},{2,0},{4,2},{6,4},{1,7},{3,1},{5,3},{7,5},{8,14},{10,8},{12,... | collective-permute-start | bytes 786440 | tf_op jit(solution)/shard_map/ppermute | solution.py:160
  249.1 45.5 %collective-permute-start.30 = (bf16[2,64,1024]{2,1,0:T(8,128)(2,1)}, bf16[2,64,1024]{2,1,0:T(8,128)(2,1)}, u32[]{:S(2)}, u32[]{:S(2)}) collective-permute-start(bf16[2,64,1024]{2,1,0:T(8,128)(2,1)} %slice.614), channel_id=1, source_target_pairs={{0,2},{2,4},{4,6},{6,0},{1,3},{3,5},{5,7},{7,1},{8,10},{10,12},{12... | collective-permute-start | bytes 786440 | tf_op jit(solution)/shard_map/ppermute | solution.py:160
  277.7 21.1 %collective-permute-start.25 = (bf16[2,32,4480]{2,1,0:T(8,128)(2,1)}, bf16[2,32,4480]{2,1,0:T(8,128)(2,1)}, u32[]{:S(2)}, u32[]{:S(2)}) collective-permute-start(bf16[2,32,4480]{2,1,0:T(8,128)(2,1)} %slice.611), channel_id=1, source_target_pairs={{0,6},{2,0},{4,2},{6,4},{1,7},{3,1},{5,3},{7,5},{8,14},{10,8},{12,... | collective-permute-start | bytes 1720328 | tf_op jit(solution)/shard_map/ppermute | solution.py:160
  278.9 19.8 %collective-permute-start.22 = (bf16[2,32,4480]{2,1,0:T(8,128)(2,1)}, bf16[2,32,4480]{2,1,0:T(8,128)(2,1)}, u32[]{:S(2)}, u32[]{:S(2)}) collective-permute-start(bf16[2,32,4480]{2,1,0:T(8,128)(2,1)} %slice.612), channel_id=1, source_target_pairs={{0,2},{2,4},{4,6},{6,0},{1,3},{3,5},{5,7},{7,1},{8,10},{10,12},{12... | collective-permute-start | bytes 1720328 | tf_op jit(solution)/shard_map/ppermute | solution.py:160
  279.1 12.3 %collective-permute-start.42 = (f32[2,8,128]{2,0,1:T(2,128)S(1)}, f32[2,8,128]{2,0,1:T(2,128)S(1)}, u32[]{:S(2)}, u32[]{:S(2)}) collective-permute-start(f32[2,8,128]{2,0,1:T(2,128)S(1)} %slice_add_fusion.15), channel_id=1, source_target_pairs={{0,6},{2,0},{4,2},{6,4},{1,7},{3,1},{5,3},{7,5},{8,14},{10,8},{12,... | collective-permute-start | bytes 24584 | tf_op jit(solution)/shard_map/ppermute | solution.py:160
  291.5 48.3 %collective-permute-start.43 = (f32[2,8,128]{2,0,1:T(2,128)S(1)}, f32[2,8,128]{2,0,1:T(2,128)S(1)}, u32[]{:S(2)}, u32[]{:S(2)}) collective-permute-start(f32[2,8,128]{2,0,1:T(2,128)S(1)} %get-tuple-element.138), channel_id=1, source_target_pairs={{0,6},{2,0},{4,2},{6,4},{1,7},{3,1},{5,3},{7,5},{8,14},{10,8},{12,... | collective-permute-start | bytes 24584 | tf_op jit(solution)/shard_map/ppermute | solution.py:160
  294.5 8.6 %collective-permute-start.38 = (f32[2,8,128]{2,0,1:T(2,128)S(1)}, f32[2,8,128]{2,0,1:T(2,128)S(1)}, u32[]{:S(2)}, u32[]{:S(2)}) collective-permute-start(f32[2,8,128]{2,0,1:T(2,128)S(1)} %get-tuple-element.139), channel_id=1, source_target_pairs={{0,2},{2,4},{4,6},{6,0},{1,3},{3,5},{5,7},{7,1},{8,10},{10,12},{12... | collective-permute-start | bytes 24584 | tf_op jit(solution)/shard_map/ppermute | solution.py:160
  296.0 7.2 %collective-permute-start.34 = (bf16[2,64,1024]{2,1,0:T(8,128)(2,1)S(1)}, bf16[2,64,1024]{2,1,0:T(8,128)(2,1)S(1)}, u32[]{:S(2)}, u32[]{:S(2)}) collective-permute-start(bf16[2,64,1024]{2,1,0:T(8,128)(2,1)S(1)} %get-tuple-element.115), channel_id=1, source_target_pairs={{0,6},{2,0},{4,2},{6,4},{1,7},{3,1},{5,3},{7,5},{8,14},{10,8},{12,... | collective-permute-start | bytes 786440 | tf_op jit(solution)/shard_map/ppermute | solution.py:160
  298.8 7.2 %collective-permute-start.31 = (bf16[2,64,1024]{2,1,0:T(8,128)(2,1)S(1)}, bf16[2,64,1024]{2,1,0:T(8,128)(2,1)S(1)}, u32[]{:S(2)}, u32[]{:S(2)}) collective-permute-start(bf16[2,64,1024]{2,1,0:T(8,128)(2,1)S(1)} %get-tuple-element.116), channel_id=1, source_target_pairs={{0,2},{2,4},{4,6},{6,0},{1,3},{3,5},{5,7},{7,1},{8,10},{10,12},{12... | collective-permute-start | bytes 786440 | tf_op jit(solution)/shard_map/ppermute | solution.py:160
  300.4 14.8 %collective-permute-start.26 = (bf16[2,32,4480]{2,1,0:T(8,128)(2,1)S(1)}, bf16[2,32,4480]{2,1,0:T(8,128)(2,1)S(1)}, u32[]{:S(2)}, u32[]{:S(2)}) collective-permute-start(bf16[2,32,4480]{2,1,0:T(8,128)(2,1)S(1)} %get-tuple-element.98), channel_id=1, source_target_pairs={{0,6},{2,0},{4,2},{6,4},{1,7},{3,1},{5,3},{7,5},{8,14},{10,8},{12,... | collective-permute-start | bytes 1720328 | tf_op jit(solution)/shard_map/ppermute | solution.py:160
  303.1 25.6 %collective-permute-start.39 = (f32[2,8,128]{2,0,1:T(2,128)S(1)}, f32[2,8,128]{2,0,1:T(2,128)S(1)}, u32[]{:S(2)}, u32[]{:S(2)}) collective-permute-start(f32[2,8,128]{2,0,1:T(2,128)S(1)} %slice_add_fusion.18), channel_id=1, source_target_pairs={{0,2},{2,4},{4,6},{6,0},{1,3},{3,5},{5,7},{7,1},{8,10},{10,12},{12... | collective-permute-start | bytes 24584 | tf_op jit(solution)/shard_map/ppermute | solution.py:160
  303.3 25.8 %collective-permute-start.35 = (bf16[2,64,1024]{2,1,0:T(8,128)(2,1)S(1)}, bf16[2,64,1024]{2,1,0:T(8,128)(2,1)S(1)}, u32[]{:S(2)}, u32[]{:S(2)}) collective-permute-start(bf16[2,64,1024]{2,1,0:T(8,128)(2,1)S(1)} %fusion.71), channel_id=1, source_target_pairs={{0,6},{2,0},{4,2},{6,4},{1,7},{3,1},{5,3},{7,5},{8,14},{10,8},{12,... | collective-permute-start | bytes 786440 | tf_op jit(solution)/shard_map/ppermute | solution.py:160
  306.1 23.1 %collective-permute-start.32 = (bf16[2,64,1024]{2,1,0:T(8,128)(2,1)S(1)}, bf16[2,64,1024]{2,1,0:T(8,128)(2,1)S(1)}, u32[]{:S(2)}, u32[]{:S(2)}) collective-permute-start(bf16[2,64,1024]{2,1,0:T(8,128)(2,1)S(1)} %fusion.73), channel_id=1, source_target_pairs={{0,2},{2,4},{4,6},{6,0},{1,3},{3,5},{5,7},{7,1},{8,10},{10,12},{12... | collective-permute-start | bytes 786440 | tf_op jit(solution)/shard_map/ppermute | solution.py:160
  315.1 12.2 %collective-permute-start.23 = (bf16[2,32,4480]{2,1,0:T(8,128)(2,1)S(1)}, bf16[2,32,4480]{2,1,0:T(8,128)(2,1)S(1)}, u32[]{:S(2)}, u32[]{:S(2)}) collective-permute-start(bf16[2,32,4480]{2,1,0:T(8,128)(2,1)S(1)} %get-tuple-element.99), channel_id=1, source_target_pairs={{0,2},{2,4},{4,6},{6,0},{1,3},{3,5},{5,7},{7,1},{8,10},{10,12},{12... | collective-permute-start | bytes 1720328 | tf_op jit(solution)/shard_map/ppermute | solution.py:160
  327.4 9.4 %collective-permute-start.27 = (bf16[2,32,4480]{2,1,0:T(8,128)(2,1)S(1)}, bf16[2,32,4480]{2,1,0:T(8,128)(2,1)S(1)}, u32[]{:S(2)}, u32[]{:S(2)}) collective-permute-start(bf16[2,32,4480]{2,1,0:T(8,128)(2,1)S(1)} %fusion.45), channel_id=1, source_target_pairs={{0,6},{2,0},{4,2},{6,4},{1,7},{3,1},{5,3},{7,5},{8,14},{10,8},{12,... | collective-permute-start | bytes 1720328 | tf_op jit(solution)/shard_map/ppermute | solution.py:160
  328.7 9.8 %collective-permute-start.24 = (bf16[2,32,4480]{2,1,0:T(8,128)(2,1)S(1)}, bf16[2,32,4480]{2,1,0:T(8,128)(2,1)S(1)}, u32[]{:S(2)}, u32[]{:S(2)}) collective-permute-start(bf16[2,32,4480]{2,1,0:T(8,128)(2,1)S(1)} %fusion.47), channel_id=1, source_target_pairs={{0,2},{2,4},{4,6},{6,0},{1,3},{3,5},{5,7},{7,1},{8,10},{10,12},{12... | collective-permute-start | bytes 1720328 | tf_op jit(solution)/shard_map/ppermute | solution.py:160
  329.1 10.7 %collective-permute-start.40 = (f32[2,8,128]{2,0,1:T(2,128)S(1)}, f32[2,8,128]{2,0,1:T(2,128)S(1)}, u32[]{:S(2)}, u32[]{:S(2)}) collective-permute-start(f32[2,8,128]{2,0,1:T(2,128)S(1)} %slice_add_fusion.17), channel_id=1, source_target_pairs={{0,2},{2,4},{4,6},{6,0},{1,3},{3,5},{5,7},{7,1},{8,10},{10,12},{12... | collective-permute-start | bytes 24584 | tf_op jit(solution)/shard_map/ppermute | solution.py:160
  330.1 19.6 %collective-permute-start.36 = (bf16[128,1024]{1,0:T(8,128)(2,1)}, bf16[128,1024]{1,0:T(8,128)(2,1)}, u32[]{:S(2)}, u32[]{:S(2)}) collective-permute-start(bf16[128,1024]{1,0:T(8,128)(2,1)} %fusion.82), channel_id=1, source_target_pairs={{0,1},{1,0},{2,3},{3,2},{4,5},{5,4},{6,7},{7,6},{8,9},{9,8},{10,11... | collective-permute-start | bytes 786440 | tf_op jit(solution)/shard_map/ppermute | solution.py:175
  339.6 14.0 %collective-permute-start.28 = (bf16[64,4480]{1,0:T(8,128)(2,1)}, bf16[64,4480]{1,0:T(8,128)(2,1)}, u32[]{:S(2)}, u32[]{:S(2)}) collective-permute-start(bf16[64,4480]{1,0:T(8,128)(2,1)} %fusion.65), channel_id=1, source_target_pairs={{0,1},{1,0},{2,3},{3,2},{4,5},{5,4},{6,7},{7,6},{8,9},{9,8},{10,11... | collective-permute-start | bytes 1720328 | tf_op jit(solution)/shard_map/ppermute | solution.py:175
  339.9 9.8 %collective-permute-start.44 = (f32[16,128]{1,0:T(8,128)S(1)}, f32[16,128]{1,0:T(8,128)S(1)}, u32[]{:S(2)}, u32[]{:S(2)}) collective-permute-start(f32[16,128]{1,0:T(8,128)S(1)} %bitcast.391), channel_id=1, source_target_pairs={{0,1},{1,0},{2,3},{3,2},{4,5},{5,4},{6,7},{7,6},{8,9},{9,8},{10,11... | collective-permute-start | bytes 24584 | tf_op jit(solution)/shard_map/ppermute | solution.py:175
  364.5 10.0 %collective-permute-start.48 = (f32[832,128]{1,0:T(8,128)}, f32[832,128]{1,0:T(8,128)}, u32[]{:S(2)}, u32[]{:S(2)}) collective-permute-start(f32[832,128]{1,0:T(8,128)} %pad_maximum_fusion.3), channel_id=1, source_target_pairs={{0,48},{16,0},{32,16},{48,32},{64,112},{80,64},{96,80},{112,96},{1... | collective-permute-start | bytes 1277960 | tf_op jit(solution)/shard_map/ppermute | solution.py:196
  368.0 9.6 %collective-permute-start.46 = (f32[832,128]{1,0:T(8,128)}, f32[832,128]{1,0:T(8,128)}, u32[]{:S(2)}, u32[]{:S(2)}) collective-permute-start(f32[832,128]{1,0:T(8,128)} %pad_maximum_fusion.2), channel_id=1, source_target_pairs={{0,16},{16,32},{32,48},{48,0},{64,80},{80,96},{96,112},{112,64},{1... | collective-permute-start | bytes 1277960 | tf_op jit(solution)/shard_map/ppermute | solution.py:196
  378.9 8.6 %collective-permute-start.49 = (f32[832,128]{1,0:T(8,128)S(1)}, f32[832,128]{1,0:T(8,128)S(1)}, u32[]{:S(2)}, u32[]{:S(2)}) collective-permute-start(f32[832,128]{1,0:T(8,128)S(1)} %fusion.79), channel_id=1, source_target_pairs={{0,64},{16,80},{32,96},{48,112},{64,0},{80,16},{96,32},{112,48},{1... | collective-permute-start | bytes 1277960 | tf_op jit(solution)/shard_map/ppermute | solution.py:199
  387.5 8.3 %collective-permute-start.51 = (f32[832,128]{1,0:T(8,128)S(1)}, f32[832,128]{1,0:T(8,128)S(1)}, u32[]{:S(2)}, u32[]{:S(2)}) collective-permute-start(f32[832,128]{1,0:T(8,128)S(1)} %get-tuple-element.64), channel_id=1, source_target_pairs={{0,16},{16,32},{32,48},{48,0},{64,80},{80,96},{96,112},{112,64},{1... | collective-permute-start | bytes 1277960 | tf_op jit(solution)/shard_map/ppermute | solution.py:201
  387.6 8.5 %collective-permute-start.50 = (f32[832,128]{1,0:T(8,128)S(1)}, f32[832,128]{1,0:T(8,128)S(1)}, u32[]{:S(2)}, u32[]{:S(2)}) collective-permute-start(f32[832,128]{1,0:T(8,128)S(1)} %get-tuple-element.64), channel_id=1, source_target_pairs={{0,48},{16,0},{32,16},{48,32},{64,112},{80,64},{96,80},{112,96},{1... | collective-permute-start | bytes 1277960 | tf_op jit(solution)/shard_map/ppermute | solution.py:202
  395.8 6.2 %collective-permute-start.52 = (f32[416,128]{1,0:T(8,128)S(1)}, f32[416,128]{1,0:T(8,128)S(1)}, u32[]{:S(2)}, u32[]{:S(2)}) collective-permute-start(f32[416,128]{1,0:T(8,128)S(1)} %slice.491), channel_id=1, source_target_pairs={{0,16},{16,32},{32,48},{48,0},{64,80},{80,96},{96,112},{112,64},{1... | collective-permute-start | bytes 638984 | tf_op jit(solution)/shard_map/ppermute | solution.py:203
  406.1 28.9 %collective-permute-start.54 = (f32[64,4480]{1,0:T(8,128)S(1)}, f32[64,4480]{1,0:T(8,128)}, u32[]{:S(2)}, u32[]{:S(2)}) collective-permute-start(f32[64,4480]{1,0:T(8,128)S(1)} %reshape.883), channel_id=1, source_target_pairs={{0,8},{8,0},{1,9},{9,1},{2,10},{10,2},{3,11},{11,3},{4,12},{12,4},... | collective-permute-start | bytes 3440648 | tf_op jit(solution)/shard_map/ppermute | solution.py:259
  (101 other events, 544.6 us)

commit v14 on v12

--- a/solution.py
+++ b/solution.py
@@ -414,9 +414,13 @@
     cols = proj_low.shape[1]
     wide = -(-cols // 128) * 128
     proj_wide = jnp.pad(proj_low, ((0, 0), (0, wide - cols)))
-    in_group, small_group = reduce_group(
-        reduce_core(row_product(normed, proj_wide)), small_blocks
-    )
+    in_partial = row_product(normed, proj_wide)
+    pieces = in_partial.reshape(groups, 2, 2, -1, in_partial.shape[1])
+    first, small_group = reduce_group(
+        reduce_core(pieces[:, :, 0].reshape(-1, in_partial.shape[1])), small_blocks
+    )
+    second = reduce_group(reduce_core(pieces[:, :, 1].reshape(-1, in_partial.shape[1])))
+    in_group = jnp.concatenate([first, second], axis=0)
     in_shape, out_shape = in_group.shape, out_group.shape
     big_rows = (in_group.size + out_group.size) // 128
     tail_rows = -(-(big_rows + small_group.shape[0]) // 64) * 64 - big_rows

time: 441 us -> 452 us (1.025)
  starting transfers between devices: 73.6 us -> 87.9 us
  waiting for transfers between devices: 119 us -> 113 us
    ppermute x18 -> x24, waiting for transfers between devices: 36.7 us -> 27.5 us  [send(): lax.ppermute(p.astype(w), 'shard_0', pairs)]
    unnamed x146 -> x152, local copies, waits for them, and re-layouts: 32.1 us -> 24 us
    ppermute x10 -> x11, starting transfers between devices: 26.2 us -> 33.2 us  [core_swap(): return lax.ppermute(values, 'core', [(0, 1), (1, 0)])]
    ppermute x18 -> x24, starting transfers between devices: 22.1 us -> 29.1 us  [send(): lax.ppermute(p.astype(w), 'shard_0', pairs)]
    slice x1 -> x2, local copies, waits for them, and re-layouts: 0.16 us -> 7.04 us  [the longest x1 6.88 us: on_device(): pieces[:, :, 0].reshape(-1, in_partial.shape[1])]
    squeeze x2 -> x3, local copies, waits for them, and re-layouts: 6.95 us -> 12 us  [reduce_core(): give = lax.dynamic_index_in_dim(blocks, 1 - core, axis=1, keepdims=False)]
    add x2 -> x3, other arithmetic: 15.2 us -> 17.1 us  [reduce_core(): return keep + core_swap(give)]
  transfers between devices with their start and end apart: 49 -> 57, of which waited for: 17 -> 31; matrix products, arithmetic and copies ran while one was open for 32% -> 35% of each run, Pallas kernels for 0% -> 0%
where the time goes in v14:
time: 452 us; the launch traced here: 444 us
  waiting for transfers between devices  113 us (25%)
  local copies, waits for them, and re-layouts  89.1 us (20%)
  starting transfers between devices  87.9 us (19%)
  other arithmetic  86.4 us (19%)
  matrix products  52 us (12%)
  between operations  16 us (4%)
    ppermute x1, waiting for transfers between devices, gather_group(): from_prev = lax.ppermute(pair, 'shard_0', up)  36.3 us
    ppermute x11, starting transfers between devices, core_swap(): return lax.ppermute(values, 'core', [(0, 1), (1, 0)])  33.2 us
    dot_general x3, matrix products, mixer(): y_intra = jnp.einsum('chij,cjhp->cihp', mixing, scaled_in, precision=HIGH)  30.6 us
    ppermute x24, starting transfers between devices, send(): lax.ppermute(p.astype(w), 'shard_0', pairs)  29.1 us
    ppermute x24, waiting for transfers between devices, send(): lax.ppermute(p.astype(w), 'shard_0', pairs)  27.5 us
    unnamed x152, local copies, waits for them, and re-layouts  24 us
    add x3, other arithmetic, reduce_core(): return keep + core_swap(give)  17.1 us
    squeeze x3, local copies, waits for them, and re-layouts, reduce_core(): give = lax.dynamic_index_in_dim(blocks, 1 - core, axis=1, keepdims=False)  12 us
  transfers between devices with their start and end apart: 57, of which 31 were waited for; matrix products, arithmetic and copies ran while one was open for 35% of the time, Pallas kernels for 0%

profile of v14, /device:TPU:1, one launch (start us, length us, event | category | flops | bytes accessed | tf_op | source)
XLA Modules:
  0.0 444.1 jit_solution(14351766943121199408)
XLA Ops:
  12.0 3.3 constant_dynamic-slice_fusion.5
  22.1 3.5 collective-permute-start.2
  26.0 2.6 copy.93
  37.4 3.6 collective-permute-start.8
  43.6 36.3 %collective-permute-done.5 = bf16[2,64,4384]{2,1,0:T(8,128)(2,1)S(1)} collective-permute-done((bf16[2,64,4384]{2,1,0:T(8,128)(2,1)S(1)}, bf16[2,64,4384]{2,1,0:T(8,128)(2,1)S(1)}, u32[]{:S(2)}, u32[]{:S(2)}) %collective-permute-start.5) | collective-permute-done | bytes 1122336 | tf_op jit(solution)/shard_map/ppermute | solution.py:243
  80.1 2.7 collective-permute-start.7
  82.8 3.0 collective-permute-start.9
  87.0 6.3 %collective-permute-done.6 = bf16[2,32,4384]{2,1,0:T(8,128)(2,1)S(1)} collective-permute-done((bf16[2,32,4384]{2,1,0:T(8,128)(2,1)S(1)}, bf16[2,32,4384]{2,1,0:T(8,128)(2,1)S(1)}, u32[]{:S(2)}, u32[]{:S(2)}) %collective-permute-start.6) | collective-permute-done | bytes 561184 | tf_op jit(solution)/shard_map/ppermute | solution.py:246
  93.4 3.9 collective-permute-start.10
  105.3 2.6 constant_dynamic-slice_fusion.7
  119.7 7.3 %fusion.22 = (f32[256,2304]{0,1:T(8,128)S(1)}, f32[256,2304]{0,1:T(8,128)}) fusion(f32[253,2304]{0,1:T(8,128)} %slice.488, f32[2304]{0:T(1024)S(1)} %get-tuple-element.54, pred[256]{0:T(512)(128)(4,1)S(1)} %copy-done.49, f32[254,2304]{0,1:T(8,128)} %slice.486, f32[2304]{0:T(1024)S(1)} %get-tuple-element.55, pred[256]{0:T(512)(128)(4,1)S(1)} %copy-done.47, ...), kind=kLoop, calls=%fused_computation.55 | loop fusion | flops 8847360 | bytes 14147328 | tf_op jit(solution)/shard_map/jvp(jit(silu))/mul | solution.py:110
  131.3 11.6 %fusion.34 = f32[256,32,64]{0,2,1:T(8,128)S(1)} fusion(f32[256,32,64]{0,2,1:T(8,128)} %bitcast.366, f32[256,32,64]{0,2,1:T(8,128)S(1)} %fusion.95, f32[32]{0:T(128)S(1)} %copy-done.56, f32[256,32]{0,1:T(8,128)S(1)} %bitcast_multiply_fusion.8, f32[256,256]{1,0:T(8,128)S(1)} %fusion.113, f32[32,256]{1,0:T(8,128)S(1)} %bitcast_add_fusion.5, ...), kind=kOutput, calls=%fused_computation.74 | convolution fusion | flops 1619525632 | bytes 6717568 | tf_op jit(solution)/shard_map/jvp(chij,cjhp->cihp)/dot_general | solution.py:132
  148.1 3.3 multiply_reduce_fusion.5
  153.0 11.6 %fusion.6 = (f32[32,256]{1,0:T(8,128)S(1)}, f32[32,256]{1,0:T(8,128)S(1)}, f32[256,256]{1,0:T(8,128)S(1)}) fusion(f32[256,256]{1,0:T(8,128)S(1)} %fusion.113, f32[32,256]{1,0:T(8,128)S(1)} %copy-done.39, pred[256,256]{1,0:T(8,128)(4,1)S(1)} %fusion.104, f32[32,64,256]{2,1,0:T(8,128)S(1)} %bitcast.332, f32[256,32,64]{0,2,1:T(8,128)S(1)} %bitcast.367, ...), kind=kOutput, calls=%fused_computation.14 | convolution fusion | flops 1629929472 | bytes 4915200 | tf_op jit(solution)/shard_map/transpose(jvp(chij,cjhp->cihp))/dot_general | solution.py:132
  164.5 7.5 %fusion.35 = (f32[256,32]{0,1:T(8,128)}, f32[1,256,32,64]{1,3,2,0:T(8,128)S(1)}) fusion(f32[1,256,32,64]{1,3,2,0:T(8,128)S(1)} %bitcast.368, f32[256,32]{0,1:T(8,128)S(1)} %get-tuple-element.73, f32[32,64,256]{2,1,0:T(8,128)S(1)} %bitcast.333, f32[256,256]{1,0:T(8,128)S(1)} %fusion.113, f32[32,256]{1,0:T(8,128)S(1)} %copy-done.39, ...), kind=kOutput, calls=%fused_computation.78 | convolution fusion | flops 1618468864 | bytes 6717440 | tf_op jit(solution)/shard_map/transpose(jvp(chij,cjhp->cihp))/dot_general | solution.py:132
  176.5 2.6 multiply_reduce_fusion.4
  191.6 4.7 %fusion.144 = (f32[2304]{0:T(1024)S(1)}, f32[2304]{0:T(1024)S(1)}, f32[256,2304]{0,1:T(8,128)S(1)}) fusion(f32[256,2304]{0,1:T(8,128)S(1)} %get-tuple-element.65, f32[256,4384]{0,1:T(8,128)} %copy-done.2, f32[2304]{0:T(1024)S(1)} %get-tuple-element.53, f32[255,2304]{0,1:T(8,128)} %slice_multiply_fusion, f32[254,2304]{0,1:T(8,128)} %slice_multiply_fusion.1, ...), kind=kLoop, calls=%fused_computation.355 | loop fusion | flops 4124160 | bytes 14128128 | tf_op jit(solution)/shard_map/transpose(jvp())/reduce_sum | solution.py:104
  204.5 2.7 fusion.23
  207.1 6.9 %fusion.149 = (f32[8,2,1,32,4480]{4,3,2,1,0:T(8,128)}, f32[8,2,1,32,4480]{4,3,2,1,0:T(8,128)}) fusion(f32[8,2,2,32,4480]{4,3,2,1,0:T(8,128)S(1)} %bitcast.329), kind=kLoop, calls=%fused_computation.357 | loop fusion | bytes 36700160 | tf_op jit(solution)/shard_map/slice | solution.py:420
  214.0 4.8 %dynamic-slice_bitcast_fusion = f32[8,32,4480]{2,1,0:T(8,128)} fusion(f32[8,2,1,32,4480]{4,3,2,1,0:T(8,128)} %get-tuple-element.77, s32[]{:T(128)S(6)} %select_n.191), kind=kLoop, calls=%fused_computation.19 | loop fusion | bytes 9175044 | tf_op jit(solution)/shard_map/jit(dynamic_index_in_dim)/squeeze | solution.py:312
  218.9 3.8 fusion.45
  228.5 4.8 %dynamic-slice_bitcast_fusion.1 = f32[8,32,4480]{2,1,0:T(8,128)} fusion(f32[8,2,1,32,4480]{4,3,2,1,0:T(8,128)} %get-tuple-element.76, s32[]{:T(128)S(6)} %select_n.191), kind=kLoop, calls=%fused_computation.20 | loop fusion | bytes 9175044 | tf_op jit(solution)/shard_map/jit(dynamic_index_in_dim)/squeeze | solution.py:312
  234.6 6.7 %collective-permute-done.37 = f32[8,16,128]{2,0,1:T(8,128)S(1)} collective-permute-done((f32[8,16,128]{2,0,1:T(8,128)S(1)}, f32[8,16,128]{2,0,1:T(8,128)S(1)}, u32[]{:S(2)}, u32[]{:S(2)}) %collective-permute-start.37) | collective-permute-done | bytes 65568 | tf_op jit(solution)/shard_map/ppermute | solution.py:259
  241.4 2.8 collective-permute-start.41
  245.0 2.9 collective-permute-start.42
  248.7 3.9 collective-permute-done.38
  252.7 2.7 collective-permute-start.43
  256.8 4.4 bitcast_add_fusion.2
  263.6 2.7 collective-permute-start.33
  269.7 3.2 collective-permute-done.30
  275.3 6.3 %bitcast_add_fusion = f32[8,32,4480]{2,1,0:T(8,128)} fusion(f32[8,32,4480]{2,1,0:T(8,128)} %collective-permute-done.21, f32[8,2,1,32,4480]{4,3,2,1,0:T(8,128)} %get-tuple-element.77, s32[]{:T(128)S(6)} %select_n.183), kind=kLoop, calls=%fused_computation.17 | loop fusion | flops 1146880 | bytes 13762564 | tf_op jit(solution)/shard_map/add | solution.py:313
  281.6 6.4 %bitcast_add_fusion.1 = f32[8,32,4480]{2,1,0:T(8,128)} fusion(f32[8,32,4480]{2,1,0:T(8,128)} %collective-permute-done.13, f32[8,2,1,32,4480]{4,3,2,1,0:T(8,128)} %get-tuple-element.76, s32[]{:T(128)S(6)} %select_n.183), kind=kLoop, calls=%fused_computation.18 | loop fusion | flops 1146880 | bytes 13762564 | tf_op jit(solution)/shard_map/add | solution.py:313
  287.9 8.7 %fusion.7 = (f32[4,2,32,4480]{3,2,1,0:T(8,128)}, f32[4,2,32,4480]{3,2,1,0:T(8,128)}) fusion(s32[]{:T(128)S(6)} %select_n.207, f32[4,2,32,4480]{3,2,1,0:T(8,128)} %bitcast.343, f32[4,2,32,4480]{3,2,1,0:T(8,128)} %bitcast.344), kind=kLoop, calls=%fused_computation.15 | loop fusion | flops 2293760 | bytes 18350084 | tf_op jit(solution)/shard_map/concatenate | solution.py:155
  296.6 3.8 slice_bitcast_fusion.3
  305.1 2.7 collective-permute-start.35
  314.8 3.8 collective-permute-done.26
  321.8 2.9 collective-permute-done.18
  334.5 2.6 collective-permute-done.19
  342.8 3.4 collective-permute-done.20
  351.9 3.2 collective-permute-done.45
  359.4 3.6 collective-permute-done.48
  363.0 3.2 collective-permute-done.46
  367.4 3.1 collective-permute-start.49
  372.6 3.5 collective-permute-done.49
  379.4 5.2 %collective-permute-done.50 = f32[832,128]{1,0:T(8,128)S(1)} collective-permute-done((f32[832,128]{1,0:T(8,128)S(1)}, f32[832,128]{1,0:T(8,128)S(1)}, u32[]{:S(2)}, u32[]{:S(2)}) %collective-permute-start.50) | collective-permute-done | bytes 426016 | tf_op jit(solution)/shard_map/ppermute | solution.py:202
  384.7 3.2 collective-permute-start.53
  390.6 3.8 collective-permute-done.52
  399.6 21.1 %collective-permute-start.54 = (f32[64,4480]{1,0:T(8,128)}, f32[64,4480]{1,0:T(8,128)}, u32[]{:S(2)}, u32[]{:S(2)}) collective-permute-start(f32[64,4480]{1,0:T(8,128)} %reshape.802), channel_id=1, source_target_pairs={{0,8},{8,0},{1,9},{9,1},{2,10},{10,2},{3,11},{11,3},{4,12},{12,4},... | collective-permute-start | bytes 3440648 | tf_op jit(solution)/shard_map/ppermute | solution.py:259
  (431 shorter events, 168.9 us)
Async XLA Ops:
  7.2 122.2 %all-gather.3.cloned.1.call-start = ((), (), s32[]{:S(2)}) async-start(), calls=%async_computation | async-start | bytes 2359296 | tf_op jit(solution)/shard_map/all_gather | solution.py:271
  9.8 8.3 %collective-permute-start = (f32[8,1836]{1,0:T(8,128)}, f32[8,1836]{1,0:T(8,128)S(1)}, u32[]{:S(2)}, u32[]{:S(2)}) collective-permute-start(f32[8,1836]{1,0:T(8,128)} %broadcast_select_fusion.7), channel_id=1, source_target_pairs={{0,1},{1,0},{2,3},{3,2},{4,5},{5,4},{6,7},{7,6},{8,9},{9,8},{10,11... | collective-permute-start | bytes 176264 | tf_op jit(solution)/shard_map/ppermute | solution.py:338
  16.3 17.8 %collective-permute-start.3 = (bf16[64,4384]{1,0:T(8,128)(2,1)S(1)}, bf16[64,4384]{1,0:T(8,128)(2,1)}, u32[]{:S(2)}, u32[]{:S(2)}) collective-permute-start(bf16[64,4384]{1,0:T(8,128)(2,1)S(1)} %copy.120), channel_id=1, source_target_pairs={{0,1},{1,0},{2,3},{3,2},{4,5},{5,4},{6,7},{7,6},{8,9},{9,8},{10,11... | collective-permute-start | bytes 1683464 | tf_op jit(solution)/shard_map/ppermute | solution.py:241
  22.1 6.5 %collective-permute-start.2 = (f32[8,1836]{1,0:T(8,128)S(1)}, f32[8,1836]{1,0:T(8,128)S(1)}, u32[]{:S(2)}, u32[]{:S(2)}) collective-permute-start(f32[8,1836]{1,0:T(8,128)S(1)} %fusion.172), channel_id=1, source_target_pairs={{0,4},{2,6},{4,0},{6,2},{1,5},{3,7},{5,1},{7,3},{8,12},{10,14},{12... | collective-permute-start | bytes 176264 | tf_op jit(solution)/shard_map/ppermute | solution.py:338
  35.6 44.5 %collective-permute-start.4 = (bf16[2,64,4384]{2,1,0:T(8,128)(2,1)S(1)}, bf16[2,64,4384]{2,1,0:T(8,128)(2,1)S(1)}, u32[]{:S(2)}, u32[]{:S(2)}) collective-permute-start(bf16[2,64,4384]{2,1,0:T(8,128)(2,1)S(1)} %maximum_select_fusion.1), channel_id=1, source_target_pairs={{0,6},{2,0},{4,2},{6,4},{1,7},{3,1},{5,3},{7,5},{8,14},{10,8},{12,... | collective-permute-start | bytes 3366920 | tf_op jit(solution)/shard_map/ppermute | solution.py:244
  37.4 42.6 %collective-permute-start.5 = (bf16[2,64,4384]{2,1,0:T(8,128)(2,1)S(1)}, bf16[2,64,4384]{2,1,0:T(8,128)(2,1)S(1)}, u32[]{:S(2)}, u32[]{:S(2)}) collective-permute-start(bf16[2,64,4384]{2,1,0:T(8,128)(2,1)S(1)} %maximum_select_fusion.1), channel_id=1, source_target_pairs={{0,2},{2,4},{4,6},{6,0},{1,3},{3,5},{5,7},{7,1},{8,10},{10,12},{12... | collective-permute-start | bytes 3366920 | tf_op jit(solution)/shard_map/ppermute | solution.py:243
  37.4 6.1 %collective-permute-start.8 = (bf16[64,4384]{1,0:T(8,128)(2,1)}, bf16[64,4384]{1,0:T(8,128)(2,1)S(1)}, u32[]{:S(2)}, u32[]{:S(2)}) collective-permute-start(bf16[64,4384]{1,0:T(8,128)(2,1)} %collective-permute-done.3), channel_id=1, source_target_pairs={{0,8},{8,0},{1,9},{9,1},{2,10},{10,2},{3,11},{11,3},{4,12},{12,4},... | collective-permute-start | bytes 1683464 | tf_op jit(solution)/shard_map/ppermute | solution.py:259
  80.0 13.3 %collective-permute-start.6 = (bf16[2,32,4384]{2,1,0:T(8,128)(2,1)S(1)}, bf16[2,32,4384]{2,1,0:T(8,128)(2,1)S(1)}, u32[]{:S(2)}, u32[]{:S(2)}) collective-permute-start(bf16[2,32,4384]{2,1,0:T(8,128)(2,1)S(1)} %slice.480), channel_id=1, source_target_pairs={{0,2},{2,4},{4,6},{6,0},{1,3},{3,5},{5,7},{7,1},{8,10},{10,12},{12... | collective-permute-start | bytes 1683464 | tf_op jit(solution)/shard_map/ppermute | solution.py:246
  80.1 13.2 %collective-permute-start.7 = (bf16[2,32,4384]{2,1,0:T(8,128)(2,1)S(1)}, bf16[2,32,4384]{2,1,0:T(8,128)(2,1)S(1)}, u32[]{:S(2)}, u32[]{:S(2)}) collective-permute-start(bf16[2,32,4384]{2,1,0:T(8,128)(2,1)S(1)} %slice.481), channel_id=1, source_target_pairs={{0,6},{2,0},{4,2},{6,4},{1,7},{3,1},{5,3},{7,5},{8,14},{10,8},{12,... | collective-permute-start | bytes 1683464 | tf_op jit(solution)/shard_map/ppermute | solution.py:247
  82.8 27.3 %collective-permute-start.9 = (bf16[2,64,4384]{2,1,0:T(8,128)(2,1)S(1)}, bf16[2,64,4384]{2,1,0:T(8,128)(2,1)S(1)}, u32[]{:S(2)}, u32[]{:S(2)}) collective-permute-start(bf16[2,64,4384]{2,1,0:T(8,128)(2,1)S(1)} %collective-permute-done.4), channel_id=1, source_target_pairs={{0,8},{8,0},{1,9},{9,1},{2,10},{10,2},{3,11},{11,3},{4,12},{12,4},... | collective-permute-start | bytes 3366920 | tf_op jit(solution)/shard_map/ppermute | solution.py:259
  85.9 24.6 %collective-permute-start.11 = (bf16[2,64,4384]{2,1,0:T(8,128)(2,1)S(1)}, bf16[2,64,4384]{2,1,0:T(8,128)(2,1)S(1)}, u32[]{:S(2)}, u32[]{:S(2)}) collective-permute-start(bf16[2,64,4384]{2,1,0:T(8,128)(2,1)S(1)} %collective-permute-done.5), channel_id=1, source_target_pairs={{0,8},{8,0},{1,9},{9,1},{2,10},{10,2},{3,11},{11,3},{4,12},{12,4},... | collective-permute-start | bytes 3366920 | tf_op jit(solution)/shard_map/ppermute | solution.py:259
  93.4 16.9 %collective-permute-start.10 = (bf16[2,64,4384]{2,1,0:T(8,128)(2,1)S(1)}, bf16[2,64,4384]{2,1,0:T(8,128)(2,1)S(1)}, u32[]{:S(2)}, u32[]{:S(2)}) collective-permute-start(bf16[2,64,4384]{2,1,0:T(8,128)(2,1)S(1)} %constant_dynamic-update-slice_fusion), channel_id=1, source_target_pairs={{0,8},{8,0},{1,9},{9,1},{2,10},{10,2},{3,11},{11,3},{4,12},{12,4},... | collective-permute-start | bytes 3366920 | tf_op jit(solution)/shard_map/ppermute | solution.py:259
  129.4 16.2 %collective-permute-start.12 = (bf16[8,128,1024]{2,1,0:T(8,128)(2,1)}, bf16[8,128,1024]{2,1,0:T(8,128)(2,1)S(1)}, u32[]{:S(2)}, u32[]{:S(2)}) collective-permute-start(bf16[8,128,1024]{2,1,0:T(8,128)(2,1)} %bitcast.346), channel_id=1, source_target_pairs={{0,8},{8,0},{1,9},{9,1},{2,10},{10,2},{3,11},{11,3},{4,12},{12,4},... | collective-permute-start | bytes 6291464 | tf_op jit(solution)/shard_map/ppermute | solution.py:259
  202.6 54.2 %collective-permute-start.29 = (f32[8,128,1024]{2,1,0:T(8,128)}, f32[8,128,1024]{2,1,0:T(8,128)}, u32[]{:S(2)}, u32[]{:S(2)}) collective-permute-start(f32[8,128,1024]{2,1,0:T(8,128)} %dynamic-slice_bitcast_fusion.2), channel_id=1, source_target_pairs={{0,8},{8,0},{1,9},{9,1},{2,10},{10,2},{3,11},{11,3},{4,12},{12,4},... | collective-permute-start | bytes 12582920 | tf_op jit(solution)/shard_map/ppermute | solution.py:259
  218.9 56.4 %collective-permute-start.21 = (f32[8,32,4480]{2,1,0:T(8,128)}, f32[8,32,4480]{2,1,0:T(8,128)}, u32[]{:S(2)}, u32[]{:S(2)}) collective-permute-start(f32[8,32,4480]{2,1,0:T(8,128)} %dynamic-slice_bitcast_fusion), channel_id=1, source_target_pairs={{0,8},{8,0},{1,9},{9,1},{2,10},{10,2},{3,11},{11,3},{4,12},{12,4},... | collective-permute-start | bytes 13762568 | tf_op jit(solution)/shard_map/ppermute | solution.py:259
  233.4 48.2 %collective-permute-start.13 = (f32[8,32,4480]{2,1,0:T(8,128)}, f32[8,32,4480]{2,1,0:T(8,128)}, u32[]{:S(2)}, u32[]{:S(2)}) collective-permute-start(f32[8,32,4480]{2,1,0:T(8,128)} %dynamic-slice_bitcast_fusion.1), channel_id=1, source_target_pairs={{0,8},{8,0},{1,9},{9,1},{2,10},{10,2},{3,11},{11,3},{4,12},{12,4},... | collective-permute-start | bytes 13762568 | tf_op jit(solution)/shard_map/ppermute | solution.py:259
  234.4 6.8 %collective-permute-start.37 = (f32[8,16,128]{2,0,1:T(8,128)S(1)}, f32[8,16,128]{2,0,1:T(8,128)S(1)}, u32[]{:S(2)}, u32[]{:S(2)}) collective-permute-start(f32[8,16,128]{2,0,1:T(8,128)S(1)} %pad_bitcast_fusion), channel_id=1, source_target_pairs={{0,8},{8,0},{1,9},{9,1},{2,10},{10,2},{3,11},{11,3},{4,12},{12,4},... | collective-permute-start | bytes 196616 | tf_op jit(solution)/shard_map/ppermute | solution.py:259
  252.7 13.7 %collective-permute-start.43 = (f32[2,8,128]{2,0,1:T(2,128)S(1)}, f32[2,8,128]{2,0,1:T(2,128)S(1)}, u32[]{:S(2)}, u32[]{:S(2)}) collective-permute-start(f32[2,8,128]{2,0,1:T(2,128)S(1)} %get-tuple-element.140), channel_id=1, source_target_pairs={{0,6},{2,0},{4,2},{6,4},{1,7},{3,1},{5,3},{7,5},{8,14},{10,8},{12,... | collective-permute-start | bytes 24584 | tf_op jit(solution)/shard_map/ppermute | solution.py:160
  256.4 10.1 %collective-permute-start.40 = (f32[2,8,128]{2,0,1:T(2,128)S(1)}, f32[2,8,128]{2,0,1:T(2,128)S(1)}, u32[]{:S(2)}, u32[]{:S(2)}) collective-permute-start(f32[2,8,128]{2,0,1:T(2,128)S(1)} %slice_add_fusion.23), channel_id=1, source_target_pairs={{0,2},{2,4},{4,6},{6,0},{1,3},{3,5},{5,7},{7,1},{8,10},{10,12},{12... | collective-permute-start | bytes 24584 | tf_op jit(solution)/shard_map/ppermute | solution.py:160
  263.6 6.0 %collective-permute-start.33 = (bf16[2,64,1024]{2,1,0:T(8,128)(2,1)S(1)}, bf16[2,64,1024]{2,1,0:T(8,128)(2,1)S(1)}, u32[]{:S(2)}, u32[]{:S(2)}) collective-permute-start(bf16[2,64,1024]{2,1,0:T(8,128)(2,1)S(1)} %slice.701), channel_id=1, source_target_pairs={{0,6},{2,0},{4,2},{6,4},{1,7},{3,1},{5,3},{7,5},{8,14},{10,8},{12,... | collective-permute-start | bytes 786440 | tf_op jit(solution)/shard_map/ppermute | solution.py:160
  266.4 6.5 %collective-permute-start.30 = (bf16[2,64,1024]{2,1,0:T(8,128)(2,1)S(1)}, bf16[2,64,1024]{2,1,0:T(8,128)(2,1)S(1)}, u32[]{:S(2)}, u32[]{:S(2)}) collective-permute-start(bf16[2,64,1024]{2,1,0:T(8,128)(2,1)S(1)} %slice.702), channel_id=1, source_target_pairs={{0,2},{2,4},{4,6},{6,0},{1,3},{3,5},{5,7},{7,1},{8,10},{10,12},{12... | collective-permute-start | bytes 786440 | tf_op jit(solution)/shard_map/ppermute | solution.py:160
  273.8 31.2 %collective-permute-start.34 = (bf16[2,64,1024]{2,1,0:T(8,128)(2,1)}, bf16[2,64,1024]{2,1,0:T(8,128)(2,1)S(1)}, u32[]{:S(2)}, u32[]{:S(2)}) collective-permute-start(bf16[2,64,1024]{2,1,0:T(8,128)(2,1)} %get-tuple-element.119), channel_id=1, source_target_pairs={{0,6},{2,0},{4,2},{6,4},{1,7},{3,1},{5,3},{7,5},{8,14},{10,8},{12,... | collective-permute-start | bytes 786440 | tf_op jit(solution)/shard_map/ppermute | solution.py:160
  273.8 31.3 %collective-permute-start.31 = (bf16[2,64,1024]{2,1,0:T(8,128)(2,1)S(1)}, bf16[2,64,1024]{2,1,0:T(8,128)(2,1)S(1)}, u32[]{:S(2)}, u32[]{:S(2)}) collective-permute-start(bf16[2,64,1024]{2,1,0:T(8,128)(2,1)S(1)} %get-tuple-element.120), channel_id=1, source_target_pairs={{0,2},{2,4},{4,6},{6,0},{1,3},{3,5},{5,7},{7,1},{8,10},{10,12},{12... | collective-permute-start | bytes 786440 | tf_op jit(solution)/shard_map/ppermute | solution.py:160
  300.4 7.5 %collective-permute-start.25 = (bf16[2,16,4480]{2,1,0:T(8,128)(2,1)S(1)}, bf16[2,16,4480]{2,1,0:T(8,128)(2,1)S(1)}, u32[]{:S(2)}, u32[]{:S(2)}) collective-permute-start(bf16[2,16,4480]{2,1,0:T(8,128)(2,1)S(1)} %slice.697), channel_id=1, source_target_pairs={{0,6},{2,0},{4,2},{6,4},{1,7},{3,1},{5,3},{7,5},{8,14},{10,8},{12,... | collective-permute-start | bytes 860168 | tf_op jit(solution)/shard_map/ppermute | solution.py:160
  301.7 6.8 %collective-permute-start.22 = (bf16[2,16,4480]{2,1,0:T(8,128)(2,1)S(1)}, bf16[2,16,4480]{2,1,0:T(8,128)(2,1)S(1)}, u32[]{:S(2)}, u32[]{:S(2)}) collective-permute-start(bf16[2,16,4480]{2,1,0:T(8,128)(2,1)S(1)} %slice.698), channel_id=1, source_target_pairs={{0,2},{2,4},{4,6},{6,0},{1,3},{3,5},{5,7},{7,1},{8,10},{10,12},{12... | collective-permute-start | bytes 860168 | tf_op jit(solution)/shard_map/ppermute | solution.py:160
  302.4 8.5 %collective-permute-start.17 = (bf16[2,16,4480]{2,1,0:T(8,128)(2,1)S(1)}, bf16[2,16,4480]{2,1,0:T(8,128)(2,1)S(1)}, u32[]{:S(2)}, u32[]{:S(2)}) collective-permute-start(bf16[2,16,4480]{2,1,0:T(8,128)(2,1)S(1)} %slice.699), channel_id=1, source_target_pairs={{0,6},{2,0},{4,2},{6,4},{1,7},{3,1},{5,3},{7,5},{8,14},{10,8},{12,... | collective-permute-start | bytes 860168 | tf_op jit(solution)/shard_map/ppermute | solution.py:160
  305.0 6.8 %collective-permute-start.14 = (bf16[2,16,4480]{2,1,0:T(8,128)(2,1)S(1)}, bf16[2,16,4480]{2,1,0:T(8,128)(2,1)S(1)}, u32[]{:S(2)}, u32[]{:S(2)}) collective-permute-start(bf16[2,16,4480]{2,1,0:T(8,128)(2,1)S(1)} %slice.700), channel_id=1, source_target_pairs={{0,2},{2,4},{4,6},{6,0},{1,3},{3,5},{5,7},{7,1},{8,10},{10,12},{12... | collective-permute-start | bytes 860168 | tf_op jit(solution)/shard_map/ppermute | solution.py:160
  305.1 8.6 %collective-permute-start.35 = (bf16[2,64,1024]{2,1,0:T(8,128)(2,1)S(1)}, bf16[2,64,1024]{2,1,0:T(8,128)(2,1)S(1)}, u32[]{:S(2)}, u32[]{:S(2)}) collective-permute-start(bf16[2,64,1024]{2,1,0:T(8,128)(2,1)S(1)} %fusion.90), channel_id=1, source_target_pairs={{0,6},{2,0},{4,2},{6,4},{1,7},{3,1},{5,3},{7,5},{8,14},{10,8},{12,... | collective-permute-start | bytes 786440 | tf_op jit(solution)/shard_map/ppermute | solution.py:160
  307.9 6.6 %collective-permute-start.32 = (bf16[2,64,1024]{2,1,0:T(8,128)(2,1)S(1)}, bf16[2,64,1024]{2,1,0:T(8,128)(2,1)S(1)}, u32[]{:S(2)}, u32[]{:S(2)}) collective-permute-start(bf16[2,64,1024]{2,1,0:T(8,128)(2,1)S(1)} %fusion.92), channel_id=1, source_target_pairs={{0,2},{2,4},{4,6},{6,0},{1,3},{3,5},{5,7},{7,1},{8,10},{10,12},{12... | collective-permute-start | bytes 786440 | tf_op jit(solution)/shard_map/ppermute | solution.py:160
  308.6 10.0 %collective-permute-start.26 = (bf16[2,16,4480]{2,1,0:T(8,128)(2,1)S(1)}, bf16[2,16,4480]{2,1,0:T(8,128)(2,1)S(1)}, u32[]{:S(2)}, u32[]{:S(2)}) collective-permute-start(bf16[2,16,4480]{2,1,0:T(8,128)(2,1)S(1)} %get-tuple-element.111), channel_id=1, source_target_pairs={{0,6},{2,0},{4,2},{6,4},{1,7},{3,1},{5,3},{7,5},{8,14},{10,8},{12,... | collective-permute-start | bytes 860168 | tf_op jit(solution)/shard_map/ppermute | solution.py:160
  310.9 10.2 %collective-permute-start.23 = (bf16[2,16,4480]{2,1,0:T(8,128)(2,1)S(1)}, bf16[2,16,4480]{2,1,0:T(8,128)(2,1)S(1)}, u32[]{:S(2)}, u32[]{:S(2)}) collective-permute-start(bf16[2,16,4480]{2,1,0:T(8,128)(2,1)S(1)} %get-tuple-element.112), channel_id=1, source_target_pairs={{0,2},{2,4},{4,6},{6,0},{1,3},{3,5},{5,7},{7,1},{8,10},{10,12},{12... | collective-permute-start | bytes 860168 | tf_op jit(solution)/shard_map/ppermute | solution.py:160
  311.8 12.9 %collective-permute-start.18 = (bf16[2,16,4480]{2,1,0:T(8,128)(2,1)S(1)}, bf16[2,16,4480]{2,1,0:T(8,128)(2,1)S(1)}, u32[]{:S(2)}, u32[]{:S(2)}) collective-permute-start(bf16[2,16,4480]{2,1,0:T(8,128)(2,1)S(1)} %get-tuple-element.107), channel_id=1, source_target_pairs={{0,6},{2,0},{4,2},{6,4},{1,7},{3,1},{5,3},{7,5},{8,14},{10,8},{12,... | collective-permute-start | bytes 860168 | tf_op jit(solution)/shard_map/ppermute | solution.py:160
  313.7 14.1 %collective-permute-start.15 = (bf16[2,16,4480]{2,1,0:T(8,128)(2,1)S(1)}, bf16[2,16,4480]{2,1,0:T(8,128)(2,1)S(1)}, u32[]{:S(2)}, u32[]{:S(2)}) collective-permute-start(bf16[2,16,4480]{2,1,0:T(8,128)(2,1)S(1)} %get-tuple-element.108), channel_id=1, source_target_pairs={{0,2},{2,4},{4,6},{6,0},{1,3},{3,5},{5,7},{7,1},{8,10},{10,12},{12... | collective-permute-start | bytes 860168 | tf_op jit(solution)/shard_map/ppermute | solution.py:160
  314.8 13.9 %collective-permute-start.36 = (bf16[128,1024]{1,0:T(8,128)(2,1)S(1)}, bf16[128,1024]{1,0:T(8,128)(2,1)S(1)}, u32[]{:S(2)}, u32[]{:S(2)}) collective-permute-start(bf16[128,1024]{1,0:T(8,128)(2,1)S(1)} %fusion.103), channel_id=1, source_target_pairs={{0,1},{1,0},{2,3},{3,2},{4,5},{5,4},{6,7},{7,6},{8,9},{9,8},{10,11... | collective-permute-start | bytes 786440 | tf_op jit(solution)/shard_map/ppermute | solution.py:175
  318.7 12.2 %collective-permute-start.27 = (bf16[2,16,4480]{2,1,0:T(8,128)(2,1)S(1)}, bf16[2,16,4480]{2,1,0:T(8,128)(2,1)}, u32[]{:S(2)}, u32[]{:S(2)}) collective-permute-start(bf16[2,16,4480]{2,1,0:T(8,128)(2,1)S(1)} %fusion.77), channel_id=1, source_target_pairs={{0,6},{2,0},{4,2},{6,4},{1,7},{3,1},{5,3},{7,5},{8,14},{10,8},{12,... | collective-permute-start | bytes 860168 | tf_op jit(solution)/shard_map/ppermute | solution.py:160
  321.8 11.0 %collective-permute-start.24 = (bf16[2,16,4480]{2,1,0:T(8,128)(2,1)}, bf16[2,16,4480]{2,1,0:T(8,128)(2,1)}, u32[]{:S(2)}, u32[]{:S(2)}) collective-permute-start(bf16[2,16,4480]{2,1,0:T(8,128)(2,1)} %fusion.79), channel_id=1, source_target_pairs={{0,2},{2,4},{4,6},{6,0},{1,3},{3,5},{5,7},{7,1},{8,10},{10,12},{12... | collective-permute-start | bytes 860168 | tf_op jit(solution)/shard_map/ppermute | solution.py:160
  325.5 11.5 %collective-permute-start.19 = (bf16[2,16,4480]{2,1,0:T(8,128)(2,1)}, bf16[2,16,4480]{2,1,0:T(8,128)(2,1)}, u32[]{:S(2)}, u32[]{:S(2)}) collective-permute-start(bf16[2,16,4480]{2,1,0:T(8,128)(2,1)} %fusion.81), channel_id=1, source_target_pairs={{0,6},{2,0},{4,2},{6,4},{1,7},{3,1},{5,3},{7,5},{8,14},{10,8},{12,... | collective-permute-start | bytes 860168 | tf_op jit(solution)/shard_map/ppermute | solution.py:160
  328.6 10.3 %collective-permute-start.16 = (bf16[2,16,4480]{2,1,0:T(8,128)(2,1)}, bf16[2,16,4480]{2,1,0:T(8,128)(2,1)}, u32[]{:S(2)}, u32[]{:S(2)}) collective-permute-start(bf16[2,16,4480]{2,1,0:T(8,128)(2,1)} %fusion.83), channel_id=1, source_target_pairs={{0,2},{2,4},{4,6},{6,0},{1,3},{3,5},{5,7},{7,1},{8,10},{10,12},{12... | collective-permute-start | bytes 860168 | tf_op jit(solution)/shard_map/ppermute | solution.py:160
  334.4 8.3 %collective-permute-start.28 = (bf16[32,4480]{1,0:T(8,128)(2,1)S(1)}, bf16[32,4480]{1,0:T(8,128)(2,1)S(1)}, u32[]{:S(2)}, u32[]{:S(2)}) collective-permute-start(bf16[32,4480]{1,0:T(8,128)(2,1)S(1)} %fusion.102), channel_id=1, source_target_pairs={{0,1},{1,0},{2,3},{3,2},{4,5},{5,4},{6,7},{7,6},{8,9},{9,8},{10,11... | collective-permute-start | bytes 860168 | tf_op jit(solution)/shard_map/ppermute | solution.py:175
  349.1 6.0 %collective-permute-start.45 = (f32[416,128]{1,0:T(8,128)S(1)}, f32[416,128]{1,0:T(8,128)S(1)}, u32[]{:S(2)}, u32[]{:S(2)}) collective-permute-start(f32[416,128]{1,0:T(8,128)S(1)} %get-tuple-element.101), channel_id=1, source_target_pairs={{0,16},{16,32},{32,48},{48,0},{64,80},{80,96},{96,112},{112,64},{1... | collective-permute-start | bytes 638984 | tf_op jit(solution)/shard_map/ppermute | solution.py:192
  355.5 7.5 %collective-permute-start.48 = (f32[832,128]{1,0:T(8,128)S(1)}, f32[832,128]{1,0:T(8,128)}, u32[]{:S(2)}, u32[]{:S(2)}) collective-permute-start(f32[832,128]{1,0:T(8,128)S(1)} %pad_maximum_fusion.4), channel_id=1, source_target_pairs={{0,48},{16,0},{32,16},{48,32},{64,112},{80,64},{96,80},{112,96},{1... | collective-permute-start | bytes 1277960 | tf_op jit(solution)/shard_map/ppermute | solution.py:196
  358.0 8.3 %collective-permute-start.46 = (f32[832,128]{1,0:T(8,128)S(1)}, f32[832,128]{1,0:T(8,128)S(1)}, u32[]{:S(2)}, u32[]{:S(2)}) collective-permute-start(f32[832,128]{1,0:T(8,128)S(1)} %pad_maximum_fusion.3), channel_id=1, source_target_pairs={{0,16},{16,32},{32,48},{48,0},{64,80},{80,96},{96,112},{112,64},{1... | collective-permute-start | bytes 1277960 | tf_op jit(solution)/shard_map/ppermute | solution.py:196
  367.4 8.6 %collective-permute-start.49 = (f32[832,128]{1,0:T(8,128)S(1)}, f32[832,128]{1,0:T(8,128)S(1)}, u32[]{:S(2)}, u32[]{:S(2)}) collective-permute-start(f32[832,128]{1,0:T(8,128)S(1)} %fusion.98), channel_id=1, source_target_pairs={{0,64},{16,80},{32,96},{48,112},{64,0},{80,16},{96,32},{112,48},{1... | collective-permute-start | bytes 1277960 | tf_op jit(solution)/shard_map/ppermute | solution.py:199
  376.1 8.5 %collective-permute-start.50 = (f32[832,128]{1,0:T(8,128)S(1)}, f32[832,128]{1,0:T(8,128)S(1)}, u32[]{:S(2)}, u32[]{:S(2)}) collective-permute-start(f32[832,128]{1,0:T(8,128)S(1)} %get-tuple-element.58), channel_id=1, source_target_pairs={{0,48},{16,0},{32,16},{48,32},{64,112},{80,64},{96,80},{112,96},{1... | collective-permute-start | bytes 1277960 | tf_op jit(solution)/shard_map/ppermute | solution.py:202
  376.2 11.9 %collective-permute-start.51 = (f32[832,128]{1,0:T(8,128)S(1)}, f32[832,128]{1,0:T(8,128)S(1)}, u32[]{:S(2)}, u32[]{:S(2)}) collective-permute-start(f32[832,128]{1,0:T(8,128)S(1)} %get-tuple-element.58), channel_id=1, source_target_pairs={{0,16},{16,32},{32,48},{48,0},{64,80},{80,96},{96,112},{112,64},{1... | collective-permute-start | bytes 1277960 | tf_op jit(solution)/shard_map/ppermute | solution.py:201
  384.7 6.0 %collective-permute-start.53 = (f32[416,128]{1,0:T(8,128)S(1)}, f32[416,128]{1,0:T(8,128)S(1)}, u32[]{:S(2)}, u32[]{:S(2)}) collective-permute-start(f32[416,128]{1,0:T(8,128)S(1)} %slice.558), channel_id=1, source_target_pairs={{0,48},{16,0},{32,16},{48,32},{64,112},{80,64},{96,80},{112,96},{1... | collective-permute-start | bytes 638984 | tf_op jit(solution)/shard_map/ppermute | solution.py:204
  388.2 6.3 %collective-permute-start.52 = (f32[416,128]{1,0:T(8,128)S(1)}, f32[416,128]{1,0:T(8,128)S(1)}, u32[]{:S(2)}, u32[]{:S(2)}) collective-permute-start(f32[416,128]{1,0:T(8,128)S(1)} %slice.557), channel_id=1, source_target_pairs={{0,16},{16,32},{32,48},{48,0},{64,80},{80,96},{96,112},{112,64},{1... | collective-permute-start | bytes 638984 | tf_op jit(solution)/shard_map/ppermute | solution.py:203
  399.6 34.0 %collective-permute-start.54 = (f32[64,4480]{1,0:T(8,128)}, f32[64,4480]{1,0:T(8,128)}, u32[]{:S(2)}, u32[]{:S(2)}) collective-permute-start(f32[64,4480]{1,0:T(8,128)} %reshape.802), channel_id=1, source_target_pairs={{0,8},{8,0},{1,9},{9,1},{2,10},{10,2},{3,11},{11,3},{4,12},{12,4},... | collective-permute-start | bytes 3440648 | tf_op jit(solution)/shard_map/ppermute | solution.py:259
  (73 other events, 361.0 us)
Sparse Core Ops, SparseCore 0:
  17.2 56.7 all-gather.2

commit v15 on v12

--- a/solution.py
+++ b/solution.py
@@ -376,6 +376,7 @@
     normed_f, norm_back = jax.vjp(norm_input, layer_in, norm_full)
     normed = normed_f.astype(jnp.bfloat16)
     in_whole = gather_rows(in_weight, by_permutes=True)
+    in_whole, out_weight = lax.optimization_barrier((in_whole, out_weight))
     out_whole = gather_rows(out_weight)
     projected = halves_product(normed, in_whole, groups)
 

time: 441 us -> 453 us (1.027)
  waiting for transfers between devices: 119 us -> 129 us
    all_gather x1, waiting for transfers between devices: 0.02 us -> 24.9 us  [gather_rows(): part = lax.all_gather(mine, SHARD, axis=0, tiled=False)]
    ppermute x1, waiting for transfers between devices: 37.1 us -> 21.6 us  [gather_group(): from_prev = lax.ppermute(pair, 'shard_0', up)]
    unnamed x146 -> x200, local copies, waits for them, and re-layouts: 32.1 us -> 29 us
  transfers between devices with their start and end apart: 49 -> 49, of which waited for: 17 -> 20; matrix products, arithmetic and copies ran while one was open for 32% -> 29% of each run, Pallas kernels for 0% -> 0%
where the time goes in v15:
time: 453 us; the launch traced here: 446 us
  waiting for transfers between devices  129 us (28%)
  local copies, waits for them, and re-layouts  88.3 us (19%)
  other arithmetic  87.8 us (19%)
  starting transfers between devices  74.1 us (16%)
  matrix products  51.1 us (11%)
  between operations  16 us (4%)
    ppermute x18, waiting for transfers between devices, send(): lax.ppermute(p.astype(w), 'shard_0', pairs)  36.8 us
    unnamed x200, local copies, waits for them, and re-layouts  29 us
    dot_general x3, matrix products, mixer(): y_intra = jnp.einsum('chij,cjhp->cihp', mixing, scaled_in, precision=HIGH)  28 us
    ppermute x10, starting transfers between devices, core_swap(): return lax.ppermute(values, 'core', [(0, 1), (1, 0)])  26.6 us
    all_gather x1, waiting for transfers between devices, gather_rows(): part = lax.all_gather(mine, SHARD, axis=0, tiled=False)  24.9 us
    ppermute x1, waiting for transfers between devices, gather_group(): from_prev = lax.ppermute(pair, 'shard_0', up)  21.6 us
    ppermute x18, starting transfers between devices, send(): lax.ppermute(p.astype(w), 'shard_0', pairs)  20 us
    add x2, other arithmetic, reduce_core(): return keep + core_swap(give)  15.1 us
  transfers between devices with their start and end apart: 49, of which 20 were waited for; matrix products, arithmetic and copies ran while one was open for 29% of the time, Pallas kernels for 0%

profile of v15, /device:TPU:1, one launch (start us, length us, event | category | flops | bytes accessed | tf_op | source)
XLA Modules:
  0.0 446.4 jit_solution(4465253420903284715)
XLA Ops:
  11.3 3.8 constant_dynamic-slice_fusion.6
  22.5 3.5 collective-permute-start.2
  32.0 3.8 collective-permute-start.4
  40.0 21.6 %collective-permute-done.5 = bf16[2,64,4384]{2,1,0:T(8,128)(2,1)S(1)} collective-permute-done((bf16[2,64,4384]{2,1,0:T(8,128)(2,1)S(1)}, bf16[2,64,4384]{2,1,0:T(8,128)(2,1)S(1)}, u32[]{:S(2)}, u32[]{:S(2)}) %collective-permute-start.5) | collective-permute-done | bytes 1122336 | tf_op jit(solution)/shard_map/ppermute | solution.py:243
  61.8 2.7 collective-permute-start.7
  64.6 3.6 collective-permute-start.9
  68.3 6.0 %collective-permute-done.6 = bf16[2,32,4384]{2,1,0:T(8,128)(2,1)S(1)} collective-permute-done((bf16[2,32,4384]{2,1,0:T(8,128)(2,1)S(1)}, bf16[2,32,4384]{2,1,0:T(8,128)(2,1)S(1)}, u32[]{:S(2)}, u32[]{:S(2)}) %collective-permute-start.6) | collective-permute-done | bytes 561184 | tf_op jit(solution)/shard_map/ppermute | solution.py:246
  74.5 4.2 collective-permute-start.10
  84.7 2.5 constant_dynamic-slice_fusion.5
  93.8 4.4 fusion.130
  106.3 7.3 %fusion.21 = (f32[256,2304]{0,1:T(8,128)S(1)}, f32[256,2304]{0,1:T(8,128)}) fusion(f32[253,2304]{0,1:T(8,128)} %slice.426, f32[2304]{0:T(1024)S(1)} %get-tuple-element.60, pred[256]{0:T(512)(128)(4,1)S(1)} %copy-done.69, f32[254,2304]{0,1:T(8,128)} %slice.424, f32[2304]{0:T(1024)S(1)} %get-tuple-element.61, pred[256]{0:T(512)(128)(4,1)S(1)} %copy-done.67, ...), kind=kLoop, calls=%fused_computation.54 | loop fusion | flops 8847360 | bytes 14147328 | tf_op jit(solution)/shard_map/jvp(jit(silu))/mul | solution.py:110
  115.9 24.9 %all-gather.3.cloned.1.call-done = bf16[1024,1024]{1,0:T(8,128)(2,1)} async-done(((bf16[128,1024]{1,0:T(8,128)(2,1)}), bf16[1024,1024]{1,0:T(8,128)(2,1)}) %all-gather.3.cloned.1.call-update) | async-done | bytes 2097168 | tf_op jit(solution)/shard_map/all_gather | solution.py:271
  144.0 9.2 %fusion.29 = f32[256,32,64]{0,2,1:T(8,128)S(1)} fusion(f32[256,32,64]{0,2,1:T(8,128)S(1)} %bitcast.338, f32[256,32,64]{0,2,1:T(8,128)S(1)} %fusion.76, f32[32]{0:T(128)S(1)} %copy-done.77, f32[256,32]{0,1:T(8,128)S(1)} %bitcast_multiply_fusion.8, f32[256,256]{1,0:T(8,128)S(1)} %fusion.92, f32[32,256]{1,0:T(8,128)S(1)} %bitcast_add_fusion.4, ...), kind=kOutput, calls=%fused_computation.73 | convolution fusion | flops 1619525632 | bytes 6717568 | tf_op jit(solution)/shard_map/jvp(chij,cjhp->cihp)/dot_general | solution.py:132
  159.4 3.8 multiply_reduce_fusion.5
  164.1 11.4 %fusion.7 = (f32[32,256]{1,0:T(8,128)S(1)}, f32[32,256]{1,0:T(8,128)S(1)}, f32[256,256]{1,0:T(8,128)S(1)}) fusion(f32[256,256]{1,0:T(8,128)S(1)} %fusion.92, f32[32,256]{1,0:T(8,128)S(1)} %copy-done.57, pred[256,256]{1,0:T(8,128)(4,1)S(1)} %copy-done.47, f32[32,64,256]{2,1,0:T(8,128)S(1)} %bitcast.304, f32[256,32,64]{0,2,1:T(8,128)S(1)} %bitcast.339, ...), kind=kOutput, calls=%fused_computation.15 | convolution fusion | flops 1629929472 | bytes 4915200 | tf_op jit(solution)/shard_map/transpose(jvp(chij,cjhp->cihp))/dot_general | solution.py:132
  175.5 7.5 %fusion.30 = (f32[256,32]{0,1:T(8,128)}, f32[1,256,32,64]{1,3,2,0:T(8,128)S(1)}) fusion(f32[1,256,32,64]{1,3,2,0:T(8,128)S(1)} %bitcast.340, f32[256,32]{0,1:T(8,128)S(1)} %copy-done.41, f32[32,64,256]{2,1,0:T(8,128)S(1)} %bitcast.305, f32[256,256]{1,0:T(8,128)S(1)} %fusion.92, f32[32,256]{1,0:T(8,128)S(1)} %copy-done.57, pred[256,256]{1,0:T(8,128)(4,1)S(1)} %copy-done.47), kind=kOutput, calls=%fused_computation.77 | convolution fusion | flops 1618468864 | bytes 6717440 | tf_op jit(solution)/shard_map/transpose(jvp(chij,cjhp->cihp))/dot_general | solution.py:132
  187.5 2.8 multiply_reduce_fusion.4
  190.3 2.9 multiply_reduce_fusion.3
  204.8 4.7 %fusion.123 = (f32[2304]{0:T(1024)S(1)}, f32[2304]{0:T(1024)S(1)}, f32[256,2304]{0,1:T(8,128)S(1)}) fusion(f32[256,2304]{0,1:T(8,128)S(1)} %get-tuple-element.71, f32[256,4384]{0,1:T(8,128)} %copy-done.2, f32[2304]{0:T(1024)S(1)} %get-tuple-element.59, f32[255,2304]{0,1:T(8,128)} %slice_multiply_fusion, f32[254,2304]{0,1:T(8,128)} %slice_multiply_fusion.1, ...), kind=kLoop, calls=%fused_computation.317 | loop fusion | flops 4124160 | bytes 14128128 | tf_op jit(solution)/shard_map/transpose(jvp())/reduce_sum | solution.py:104
  209.8 2.7 fusion.22
  212.5 4.6 %dynamic-slice_bitcast_fusion = f32[8,64,4480]{2,1,0:T(8,128)} fusion(f32[8,2,64,4480]{3,2,1,0:T(8,128)S(1)} %bitcast.299, s32[]{:T(128)S(6)} %select_n.188), kind=kLoop, calls=%fused_computation.4 | loop fusion | bytes 18350084 | tf_op jit(solution)/shard_map/jit(dynamic_index_in_dim)/squeeze | solution.py:312
  217.2 4.4 copy-done.3
  222.0 2.9 fusion.112
  227.3 3.9 copy-done.4
  243.3 4.4 bitcast_add_fusion.1
  252.2 10.7 %bitcast_add_fusion = f32[8,64,4480]{2,1,0:T(8,128)} fusion(f32[8,64,4480]{2,1,0:T(8,128)} %collective-permute-done.13, f32[8,2,64,4480]{3,2,1,0:T(8,128)} %bitcast.300, s32[]{:T(128)S(6)} %select_n.178), kind=kLoop, calls=%fused_computation.3 | loop fusion | flops 2293760 | bytes 27525124 | tf_op jit(solution)/shard_map/add | solution.py:313
  262.9 8.2 %fusion = f32[4,2,64,4480]{3,2,1,0:T(8,128)} fusion(s32[]{:T(128)S(6)} %select_n.202, f32[4,2,64,4480]{3,2,1,0:T(8,128)} %bitcast.303), kind=kLoop, calls=%fused_computation.2 | loop fusion | flops 2293760 | bytes 18350084 | tf_op jit(solution)/shard_map/concatenate | solution.py:155
  271.2 6.4 %slice_bitcast_fusion.3 = (f32[2,64,4480]{2,1,0:T(8,128)S(1)}, f32[2,64,4480]{2,1,0:T(8,128)S(1)}, f32[2,64,4480]{2,1,0:T(8,128)}, f32[2,64,4480]{2,1,0:T(8,128)}) fusion(f32[4,2,64,4480]{3,2,1,0:T(8,128)} %fusion), kind=kLoop, calls=%fused_computation.60 | loop fusion | bytes 18350080 | tf_op jit(solution)/shard_map/squeeze | solution.py:162
  282.8 2.7 collective-permute-start.34
  285.5 8.5 %collective-permute-done.34 = f32[2,8,128]{2,0,1:T(2,128)S(1)} collective-permute-done((f32[2,8,128]{2,0,1:T(2,128)S(1)}, f32[2,8,128]{2,0,1:T(2,128)S(1)}, u32[]{:S(2)}, u32[]{:S(2)}) %collective-permute-start.34) | collective-permute-done | bytes 8224 | tf_op jit(solution)/shard_map/ppermute | solution.py:160
  294.1 3.1 collective-permute-start.35
  298.6 2.7 collective-permute-start.26
  303.5 2.7 collective-permute-start.18
  306.4 2.7 collective-permute-start.27
  309.3 7.8 %collective-permute-done.18 = bf16[2,32,4480]{2,1,0:T(8,128)(2,1)S(1)} collective-permute-done((bf16[2,32,4480]{2,1,0:T(8,128)(2,1)S(1)}, bf16[2,32,4480]{2,1,0:T(8,128)(2,1)S(1)}, u32[]{:S(2)}, u32[]{:S(2)}) %collective-permute-start.18) | collective-permute-done | bytes 573472 | tf_op jit(solution)/shard_map/ppermute | solution.py:160
  317.2 10.9 %collective-permute-done.15 = bf16[2,32,4480]{2,1,0:T(8,128)(2,1)S(1)} collective-permute-done((bf16[2,32,4480]{2,1,0:T(8,128)(2,1)S(1)}, bf16[2,32,4480]{2,1,0:T(8,128)(2,1)S(1)}, u32[]{:S(2)}, u32[]{:S(2)}) %collective-permute-start.15) | collective-permute-done | bytes 573472 | tf_op jit(solution)/shard_map/ppermute | solution.py:160
  330.4 6.3 %collective-permute-done.19 = bf16[2,32,4480]{2,1,0:T(8,128)(2,1)S(1)} collective-permute-done((bf16[2,32,4480]{2,1,0:T(8,128)(2,1)S(1)}, bf16[2,32,4480]{2,1,0:T(8,128)(2,1)S(1)}, u32[]{:S(2)}, u32[]{:S(2)}) %collective-permute-start.19) | collective-permute-done | bytes 573472 | tf_op jit(solution)/shard_map/ppermute | solution.py:160
  336.7 3.2 collective-permute-done.16
  343.6 8.6 %collective-permute-done.36 = f32[16,128]{1,0:T(8,128)S(1)} collective-permute-done((f32[16,128]{1,0:T(8,128)S(1)}, f32[16,128]{1,0:T(8,128)S(1)}, u32[]{:S(2)}, u32[]{:S(2)}) %collective-permute-start.36) | collective-permute-done | bytes 8224 | tf_op jit(solution)/shard_map/ppermute | solution.py:175
  362.3 3.2 collective-permute-done.37
  365.6 2.7 collective-permute-start.40
  369.8 3.6 collective-permute-done.40
  373.4 5.7 %collective-permute-done.38 = f32[832,128]{1,0:T(8,128)S(1)} collective-permute-done((f32[832,128]{1,0:T(8,128)S(1)}, f32[832,128]{1,0:T(8,128)S(1)}, u32[]{:S(2)}, u32[]{:S(2)}) %collective-permute-start.38) | collective-permute-done | bytes 426016 | tf_op jit(solution)/shard_map/ppermute | solution.py:196
  385.0 4.0 collective-permute-done.41
  392.3 4.1 collective-permute-done.42
  398.0 3.1 collective-permute-done.45
  408.8 14.2 %collective-permute-start.46 = (f32[64,4480]{1,0:T(8,128)}, f32[64,4480]{1,0:T(8,128)}, u32[]{:S(2)}, u32[]{:S(2)}) collective-permute-start(f32[64,4480]{1,0:T(8,128)} %reshape.773), channel_id=1, source_target_pairs={{0,8},{8,0},{1,9},{9,1},{2,10},{10,2},{3,11},{11,3},{4,12},{12,4},... | collective-permute-start | bytes 3440648 | tf_op jit(solution)/shard_map/ppermute | solution.py:259
  425.4 2.5 copy.117
  (451 shorter events, 148.8 us)
Async XLA Ops:
  7.2 133.6 %all-gather.3.cloned.1.call-start = ((), (), s32[]{:S(2)}) async-start(), calls=%async_computation | async-start | bytes 2359296 | tf_op jit(solution)/shard_map/all_gather | solution.py:271
  9.2 9.3 %collective-permute-start = (f32[8,1836]{1,0:T(8,128)S(1)}, f32[8,1836]{1,0:T(8,128)S(1)}, u32[]{:S(2)}, u32[]{:S(2)}) collective-permute-start(f32[8,1836]{1,0:T(8,128)S(1)} %broadcast_select_fusion.7), channel_id=1, source_target_pairs={{0,1},{1,0},{2,3},{3,2},{4,5},{5,4},{6,7},{7,6},{8,9},{9,8},{10,11... | collective-permute-start | bytes 176264 | tf_op jit(solution)/shard_map/ppermute | solution.py:338
  16.8 13.7 %collective-permute-start.3 = (bf16[64,4384]{1,0:T(8,128)(2,1)S(1)}, bf16[64,4384]{1,0:T(8,128)(2,1)}, u32[]{:S(2)}, u32[]{:S(2)}) collective-permute-start(bf16[64,4384]{1,0:T(8,128)(2,1)S(1)} %copy.125), channel_id=1, source_target_pairs={{0,1},{1,0},{2,3},{3,2},{4,5},{5,4},{6,7},{7,6},{8,9},{9,8},{10,11... | collective-permute-start | bytes 1683464 | tf_op jit(solution)/shard_map/ppermute | solution.py:241
  18.6 3.8 collective-permute-start.1
  22.5 5.9 %collective-permute-start.2 = (f32[8,1836]{1,0:T(8,128)S(1)}, f32[8,1836]{1,0:T(8,128)S(1)}, u32[]{:S(2)}, u32[]{:S(2)}) collective-permute-start(f32[8,1836]{1,0:T(8,128)S(1)} %fusion.154), channel_id=1, source_target_pairs={{0,4},{2,6},{4,0},{6,2},{1,5},{3,7},{5,1},{7,3},{8,12},{10,14},{12... | collective-permute-start | bytes 176264 | tf_op jit(solution)/shard_map/ppermute | solution.py:338
  32.0 29.8 %collective-permute-start.4 = (bf16[2,64,4384]{2,1,0:T(8,128)(2,1)S(1)}, bf16[2,64,4384]{2,1,0:T(8,128)(2,1)S(1)}, u32[]{:S(2)}, u32[]{:S(2)}) collective-permute-start(bf16[2,64,4384]{2,1,0:T(8,128)(2,1)S(1)} %maximum_select_fusion.1), channel_id=1, source_target_pairs={{0,6},{2,0},{4,2},{6,4},{1,7},{3,1},{5,3},{7,5},{8,14},{10,8},{12,... | collective-permute-start | bytes 3366920 | tf_op jit(solution)/shard_map/ppermute | solution.py:244
  35.8 25.8 %collective-permute-start.5 = (bf16[2,64,4384]{2,1,0:T(8,128)(2,1)S(1)}, bf16[2,64,4384]{2,1,0:T(8,128)(2,1)S(1)}, u32[]{:S(2)}, u32[]{:S(2)}) collective-permute-start(bf16[2,64,4384]{2,1,0:T(8,128)(2,1)S(1)} %maximum_select_fusion.1), channel_id=1, source_target_pairs={{0,2},{2,4},{4,6},{6,0},{1,3},{3,5},{5,7},{7,1},{8,10},{10,12},{12... | collective-permute-start | bytes 3366920 | tf_op jit(solution)/shard_map/ppermute | solution.py:243
  35.8 4.0 collective-permute-start.8
  61.7 12.7 %collective-permute-start.6 = (bf16[2,32,4384]{2,1,0:T(8,128)(2,1)S(1)}, bf16[2,32,4384]{2,1,0:T(8,128)(2,1)S(1)}, u32[]{:S(2)}, u32[]{:S(2)}) collective-permute-start(bf16[2,32,4384]{2,1,0:T(8,128)(2,1)S(1)} %slice.418), channel_id=1, source_target_pairs={{0,2},{2,4},{4,6},{6,0},{1,3},{3,5},{5,7},{7,1},{8,10},{10,12},{12... | collective-permute-start | bytes 1683464 | tf_op jit(solution)/shard_map/ppermute | solution.py:246
  61.8 12.6 %collective-permute-start.7 = (bf16[2,32,4384]{2,1,0:T(8,128)(2,1)S(1)}, bf16[2,32,4384]{2,1,0:T(8,128)(2,1)S(1)}, u32[]{:S(2)}, u32[]{:S(2)}) collective-permute-start(bf16[2,32,4384]{2,1,0:T(8,128)(2,1)S(1)} %slice.419), channel_id=1, source_target_pairs={{0,6},{2,0},{4,2},{6,4},{1,7},{3,1},{5,3},{7,5},{8,14},{10,8},{12,... | collective-permute-start | bytes 1683464 | tf_op jit(solution)/shard_map/ppermute | solution.py:247
  64.6 19.0 %collective-permute-start.9 = (bf16[2,64,4384]{2,1,0:T(8,128)(2,1)S(1)}, bf16[2,64,4384]{2,1,0:T(8,128)(2,1)S(1)}, u32[]{:S(2)}, u32[]{:S(2)}) collective-permute-start(bf16[2,64,4384]{2,1,0:T(8,128)(2,1)S(1)} %collective-permute-done.4), channel_id=1, source_target_pairs={{0,8},{8,0},{1,9},{9,1},{2,10},{10,2},{3,11},{11,3},{4,12},{12,4},... | collective-permute-start | bytes 3366920 | tf_op jit(solution)/shard_map/ppermute | solution.py:259
  68.2 15.6 %collective-permute-start.11 = (bf16[2,64,4384]{2,1,0:T(8,128)(2,1)S(1)}, bf16[2,64,4384]{2,1,0:T(8,128)(2,1)S(1)}, u32[]{:S(2)}, u32[]{:S(2)}) collective-permute-start(bf16[2,64,4384]{2,1,0:T(8,128)(2,1)S(1)} %collective-permute-done.5), channel_id=1, source_target_pairs={{0,8},{8,0},{1,9},{9,1},{2,10},{10,2},{3,11},{11,3},{4,12},{12,4},... | collective-permute-start | bytes 3366920 | tf_op jit(solution)/shard_map/ppermute | solution.py:259
  74.5 9.2 %collective-permute-start.10 = (bf16[2,64,4384]{2,1,0:T(8,128)(2,1)S(1)}, bf16[2,64,4384]{2,1,0:T(8,128)(2,1)S(1)}, u32[]{:S(2)}, u32[]{:S(2)}) collective-permute-start(bf16[2,64,4384]{2,1,0:T(8,128)(2,1)S(1)} %constant_dynamic-update-slice_fusion), channel_id=1, source_target_pairs={{0,8},{8,0},{1,9},{9,1},{2,10},{10,2},{3,11},{11,3},{4,12},{12,4},... | collective-permute-start | bytes 3366920 | tf_op jit(solution)/shard_map/ppermute | solution.py:259
  140.8 15.1 %collective-permute-start.12 = (bf16[8,128,1024]{2,1,0:T(8,128)(2,1)}, bf16[8,128,1024]{2,1,0:T(8,128)(2,1)S(1)}, u32[]{:S(2)}, u32[]{:S(2)}) collective-permute-start(bf16[8,128,1024]{2,1,0:T(8,128)(2,1)} %bitcast.318), channel_id=1, source_target_pairs={{0,8},{8,0},{1,9},{9,1},{2,10},{10,2},{3,11},{11,3},{4,12},{12,4},... | collective-permute-start | bytes 6291464 | tf_op jit(solution)/shard_map/ppermute | solution.py:259
  221.6 30.6 %collective-permute-start.13 = (f32[8,64,4480]{2,1,0:T(8,128)}, f32[8,64,4480]{2,1,0:T(8,128)}, u32[]{:S(2)}, u32[]{:S(2)}) collective-permute-start(f32[8,64,4480]{2,1,0:T(8,128)} %dynamic-slice_bitcast_fusion), channel_id=1, source_target_pairs={{0,8},{8,0},{1,9},{9,1},{2,10},{10,2},{3,11},{11,3},{4,12},{12,4},... | collective-permute-start | bytes 27525128 | tf_op jit(solution)/shard_map/ppermute | solution.py:259
  231.2 12.1 %collective-permute-start.21 = (f32[8,128,1024]{2,1,0:T(8,128)}, f32[8,128,1024]{2,1,0:T(8,128)}, u32[]{:S(2)}, u32[]{:S(2)}) collective-permute-start(f32[8,128,1024]{2,1,0:T(8,128)} %dynamic-slice_bitcast_fusion.1), channel_id=1, source_target_pairs={{0,8},{8,0},{1,9},{9,1},{2,10},{10,2},{3,11},{11,3},{4,12},{12,4},... | collective-permute-start | bytes 12582920 | tf_op jit(solution)/shard_map/ppermute | solution.py:259
  242.5 40.3 %collective-permute-start.33 = (f32[2,8,128]{2,0,1:T(2,128)S(1)}, f32[2,8,128]{2,0,1:T(2,128)S(1)}, u32[]{:S(2)}, u32[]{:S(2)}) collective-permute-start(f32[2,8,128]{2,0,1:T(2,128)S(1)} %slice.470), channel_id=1, source_target_pairs={{0,6},{2,0},{4,2},{6,4},{1,7},{3,1},{5,3},{7,5},{8,14},{10,8},{12,... | collective-permute-start | bytes 24584 | tf_op jit(solution)/shard_map/ppermute | solution.py:160
  250.0 47.1 %collective-permute-start.25 = (bf16[2,64,1024]{2,1,0:T(8,128)(2,1)S(1)}, bf16[2,64,1024]{2,1,0:T(8,128)(2,1)S(1)}, u32[]{:S(2)}, u32[]{:S(2)}) collective-permute-start(bf16[2,64,1024]{2,1,0:T(8,128)(2,1)S(1)} %slice.603), channel_id=1, source_target_pairs={{0,6},{2,0},{4,2},{6,4},{1,7},{3,1},{5,3},{7,5},{8,14},{10,8},{12,... | collective-permute-start | bytes 786440 | tf_op jit(solution)/shard_map/ppermute | solution.py:160
  251.3 45.8 %collective-permute-start.22 = (bf16[2,64,1024]{2,1,0:T(8,128)(2,1)S(1)}, bf16[2,64,1024]{2,1,0:T(8,128)(2,1)}, u32[]{:S(2)}, u32[]{:S(2)}) collective-permute-start(bf16[2,64,1024]{2,1,0:T(8,128)(2,1)S(1)} %slice.604), channel_id=1, source_target_pairs={{0,2},{2,4},{4,6},{6,0},{1,3},{3,5},{5,7},{7,1},{8,10},{10,12},{12... | collective-permute-start | bytes 786440 | tf_op jit(solution)/shard_map/ppermute | solution.py:160
  279.9 21.4 %collective-permute-start.17 = (bf16[2,32,4480]{2,1,0:T(8,128)(2,1)}, bf16[2,32,4480]{2,1,0:T(8,128)(2,1)S(1)}, u32[]{:S(2)}, u32[]{:S(2)}) collective-permute-start(bf16[2,32,4480]{2,1,0:T(8,128)(2,1)} %slice.601), channel_id=1, source_target_pairs={{0,6},{2,0},{4,2},{6,4},{1,7},{3,1},{5,3},{7,5},{8,14},{10,8},{12,... | collective-permute-start | bytes 1720328 | tf_op jit(solution)/shard_map/ppermute | solution.py:160
  282.8 18.6 %collective-permute-start.14 = (bf16[2,32,4480]{2,1,0:T(8,128)(2,1)}, bf16[2,32,4480]{2,1,0:T(8,128)(2,1)}, u32[]{:S(2)}, u32[]{:S(2)}) collective-permute-start(bf16[2,32,4480]{2,1,0:T(8,128)(2,1)} %slice.602), channel_id=1, source_target_pairs={{0,2},{2,4},{4,6},{6,0},{1,3},{3,5},{5,7},{7,1},{8,10},{10,12},{12... | collective-permute-start | bytes 1720328 | tf_op jit(solution)/shard_map/ppermute | solution.py:160
  282.8 11.3 %collective-permute-start.34 = (f32[2,8,128]{2,0,1:T(2,128)S(1)}, f32[2,8,128]{2,0,1:T(2,128)S(1)}, u32[]{:S(2)}, u32[]{:S(2)}) collective-permute-start(f32[2,8,128]{2,0,1:T(2,128)S(1)} %slice_add_fusion.15), channel_id=1, source_target_pairs={{0,6},{2,0},{4,2},{6,4},{1,7},{3,1},{5,3},{7,5},{8,14},{10,8},{12,... | collective-permute-start | bytes 24584 | tf_op jit(solution)/shard_map/ppermute | solution.py:160
  294.1 48.2 %collective-permute-start.35 = (f32[2,8,128]{2,0,1:T(2,128)S(1)}, f32[2,8,128]{2,0,1:T(2,128)S(1)}, u32[]{:S(2)}, u32[]{:S(2)}) collective-permute-start(f32[2,8,128]{2,0,1:T(2,128)S(1)} %get-tuple-element.136), channel_id=1, source_target_pairs={{0,6},{2,0},{4,2},{6,4},{1,7},{3,1},{5,3},{7,5},{8,14},{10,8},{12,... | collective-permute-start | bytes 24584 | tf_op jit(solution)/shard_map/ppermute | solution.py:160
  297.1 9.0 %collective-permute-start.30 = (f32[2,8,128]{2,0,1:T(2,128)S(1)}, f32[2,8,128]{2,0,1:T(2,128)S(1)}, u32[]{:S(2)}, u32[]{:S(2)}) collective-permute-start(f32[2,8,128]{2,0,1:T(2,128)S(1)} %get-tuple-element.137), channel_id=1, source_target_pairs={{0,2},{2,4},{4,6},{6,0},{1,3},{3,5},{5,7},{7,1},{8,10},{10,12},{12... | collective-permute-start | bytes 24584 | tf_op jit(solution)/shard_map/ppermute | solution.py:160
  298.6 7.7 %collective-permute-start.26 = (bf16[2,64,1024]{2,1,0:T(8,128)(2,1)S(1)}, bf16[2,64,1024]{2,1,0:T(8,128)(2,1)S(1)}, u32[]{:S(2)}, u32[]{:S(2)}) collective-permute-start(bf16[2,64,1024]{2,1,0:T(8,128)(2,1)S(1)} %get-tuple-element.115), channel_id=1, source_target_pairs={{0,6},{2,0},{4,2},{6,4},{1,7},{3,1},{5,3},{7,5},{8,14},{10,8},{12,... | collective-permute-start | bytes 786440 | tf_op jit(solution)/shard_map/ppermute | solution.py:160
  301.3 7.8 %collective-permute-start.23 = (bf16[2,64,1024]{2,1,0:T(8,128)(2,1)S(1)}, bf16[2,64,1024]{2,1,0:T(8,128)(2,1)S(1)}, u32[]{:S(2)}, u32[]{:S(2)}) collective-permute-start(bf16[2,64,1024]{2,1,0:T(8,128)(2,1)S(1)} %get-tuple-element.116), channel_id=1, source_target_pairs={{0,2},{2,4},{4,6},{6,0},{1,3},{3,5},{5,7},{7,1},{8,10},{10,12},{12... | collective-permute-start | bytes 786440 | tf_op jit(solution)/shard_map/ppermute | solution.py:160
  303.5 13.6 %collective-permute-start.18 = (bf16[2,32,4480]{2,1,0:T(8,128)(2,1)S(1)}, bf16[2,32,4480]{2,1,0:T(8,128)(2,1)S(1)}, u32[]{:S(2)}, u32[]{:S(2)}) collective-permute-start(bf16[2,32,4480]{2,1,0:T(8,128)(2,1)S(1)} %get-tuple-element.98), channel_id=1, source_target_pairs={{0,6},{2,0},{4,2},{6,4},{1,7},{3,1},{5,3},{7,5},{8,14},{10,8},{12,... | collective-permute-start | bytes 1720328 | tf_op jit(solution)/shard_map/ppermute | solution.py:160
  306.2 23.0 %collective-permute-start.31 = (f32[2,8,128]{2,0,1:T(2,128)S(1)}, f32[2,8,128]{2,0,1:T(2,128)S(1)}, u32[]{:S(2)}, u32[]{:S(2)}) collective-permute-start(f32[2,8,128]{2,0,1:T(2,128)S(1)} %slice_add_fusion.18), channel_id=1, source_target_pairs={{0,2},{2,4},{4,6},{6,0},{1,3},{3,5},{5,7},{7,1},{8,10},{10,12},{12... | collective-permute-start | bytes 24584 | tf_op jit(solution)/shard_map/ppermute | solution.py:160
  306.4 23.4 %collective-permute-start.27 = (bf16[2,64,1024]{2,1,0:T(8,128)(2,1)S(1)}, bf16[2,64,1024]{2,1,0:T(8,128)(2,1)S(1)}, u32[]{:S(2)}, u32[]{:S(2)}) collective-permute-start(bf16[2,64,1024]{2,1,0:T(8,128)(2,1)S(1)} %fusion.71), channel_id=1, source_target_pairs={{0,6},{2,0},{4,2},{6,4},{1,7},{3,1},{5,3},{7,5},{8,14},{10,8},{12,... | collective-permute-start | bytes 786440 | tf_op jit(solution)/shard_map/ppermute | solution.py:160
  309.2 20.7 %collective-permute-start.24 = (bf16[2,64,1024]{2,1,0:T(8,128)(2,1)S(1)}, bf16[2,64,1024]{2,1,0:T(8,128)(2,1)S(1)}, u32[]{:S(2)}, u32[]{:S(2)}) collective-permute-start(bf16[2,64,1024]{2,1,0:T(8,128)(2,1)S(1)} %fusion.73), channel_id=1, source_target_pairs={{0,2},{2,4},{4,6},{6,0},{1,3},{3,5},{5,7},{7,1},{8,10},{10,12},{12... | collective-permute-start | bytes 786440 | tf_op jit(solution)/shard_map/ppermute | solution.py:160
  317.1 11.0 %collective-permute-start.15 = (bf16[2,32,4480]{2,1,0:T(8,128)(2,1)S(1)}, bf16[2,32,4480]{2,1,0:T(8,128)(2,1)S(1)}, u32[]{:S(2)}, u32[]{:S(2)}) collective-permute-start(bf16[2,32,4480]{2,1,0:T(8,128)(2,1)S(1)} %get-tuple-element.99), channel_id=1, source_target_pairs={{0,2},{2,4},{4,6},{6,0},{1,3},{3,5},{5,7},{7,1},{8,10},{10,12},{12... | collective-permute-start | bytes 1720328 | tf_op jit(solution)/shard_map/ppermute | solution.py:160
  328.1 8.6 %collective-permute-start.19 = (bf16[2,32,4480]{2,1,0:T(8,128)(2,1)S(1)}, bf16[2,32,4480]{2,1,0:T(8,128)(2,1)S(1)}, u32[]{:S(2)}, u32[]{:S(2)}) collective-permute-start(bf16[2,32,4480]{2,1,0:T(8,128)(2,1)S(1)} %fusion.45), channel_id=1, source_target_pairs={{0,6},{2,0},{4,2},{6,4},{1,7},{3,1},{5,3},{7,5},{8,14},{10,8},{12,... | collective-permute-start | bytes 1720328 | tf_op jit(solution)/shard_map/ppermute | solution.py:160
  329.2 10.7 %collective-permute-start.16 = (bf16[2,32,4480]{2,1,0:T(8,128)(2,1)S(1)}, bf16[2,32,4480]{2,1,0:T(8,128)(2,1)S(1)}, u32[]{:S(2)}, u32[]{:S(2)}) collective-permute-start(bf16[2,32,4480]{2,1,0:T(8,128)(2,1)S(1)} %fusion.47), channel_id=1, source_target_pairs={{0,2},{2,4},{4,6},{6,0},{1,3},{3,5},{5,7},{7,1},{8,10},{10,12},{12... | collective-permute-start | bytes 1720328 | tf_op jit(solution)/shard_map/ppermute | solution.py:160
  329.8 12.5 %collective-permute-start.32 = (f32[2,8,128]{2,0,1:T(2,128)S(1)}, f32[2,8,128]{2,0,1:T(2,128)S(1)}, u32[]{:S(2)}, u32[]{:S(2)}) collective-permute-start(f32[2,8,128]{2,0,1:T(2,128)S(1)} %slice_add_fusion.17), channel_id=1, source_target_pairs={{0,2},{2,4},{4,6},{6,0},{1,3},{3,5},{5,7},{7,1},{8,10},{10,12},{12... | collective-permute-start | bytes 24584 | tf_op jit(solution)/shard_map/ppermute | solution.py:160
  330.1 22.1 %collective-permute-start.28 = (bf16[128,1024]{1,0:T(8,128)(2,1)S(1)}, bf16[128,1024]{1,0:T(8,128)(2,1)}, u32[]{:S(2)}, u32[]{:S(2)}) collective-permute-start(bf16[128,1024]{1,0:T(8,128)(2,1)S(1)} %fusion.82), channel_id=1, source_target_pairs={{0,1},{1,0},{2,3},{3,2},{4,5},{5,4},{6,7},{7,6},{8,9},{9,8},{10,11... | collective-permute-start | bytes 786440 | tf_op jit(solution)/shard_map/ppermute | solution.py:175
  342.0 13.2 %collective-permute-start.20 = (bf16[64,4480]{1,0:T(8,128)(2,1)}, bf16[64,4480]{1,0:T(8,128)(2,1)}, u32[]{:S(2)}, u32[]{:S(2)}) collective-permute-start(bf16[64,4480]{1,0:T(8,128)(2,1)} %fusion.65), channel_id=1, source_target_pairs={{0,1},{1,0},{2,3},{3,2},{4,5},{5,4},{6,7},{7,6},{8,9},{9,8},{10,11... | collective-permute-start | bytes 1720328 | tf_op jit(solution)/shard_map/ppermute | solution.py:175
  342.3 9.9 %collective-permute-start.36 = (f32[16,128]{1,0:T(8,128)S(1)}, f32[16,128]{1,0:T(8,128)S(1)}, u32[]{:S(2)}, u32[]{:S(2)}) collective-permute-start(f32[16,128]{1,0:T(8,128)S(1)} %bitcast.361), channel_id=1, source_target_pairs={{0,1},{1,0},{2,3},{3,2},{4,5},{5,4},{6,7},{7,6},{8,9},{9,8},{10,11... | collective-permute-start | bytes 24584 | tf_op jit(solution)/shard_map/ppermute | solution.py:175
  359.3 6.2 %collective-permute-start.37 = (f32[416,128]{1,0:T(8,128)S(1)}, f32[416,128]{1,0:T(8,128)S(1)}, u32[]{:S(2)}, u32[]{:S(2)}) collective-permute-start(f32[416,128]{1,0:T(8,128)S(1)} %get-tuple-element.105), channel_id=1, source_target_pairs={{0,16},{16,32},{32,48},{48,0},{64,80},{80,96},{96,112},{112,64},{1... | collective-permute-start | bytes 638984 | tf_op jit(solution)/shard_map/ppermute | solution.py:192
  360.8 4.7 %collective-permute-start.39 = (f32[416,128]{1,0:T(8,128)S(1)}, f32[416,128]{1,0:T(8,128)S(1)}, u32[]{:S(2)}, u32[]{:S(2)}) collective-permute-start(f32[416,128]{1,0:T(8,128)S(1)} %get-tuple-element.106), channel_id=1, source_target_pairs={{0,48},{16,0},{32,16},{48,32},{64,112},{80,64},{96,80},{112,96},{1... | collective-permute-start | bytes 638984 | tf_op jit(solution)/shard_map/ppermute | solution.py:193
  365.6 7.8 %collective-permute-start.40 = (f32[832,128]{1,0:T(8,128)S(1)}, f32[832,128]{1,0:T(8,128)}, u32[]{:S(2)}, u32[]{:S(2)}) collective-permute-start(f32[832,128]{1,0:T(8,128)S(1)} %pad_maximum_fusion.3), channel_id=1, source_target_pairs={{0,48},{16,0},{32,16},{48,32},{64,112},{80,64},{96,80},{112,96},{1... | collective-permute-start | bytes 1277960 | tf_op jit(solution)/shard_map/ppermute | solution.py:196
  368.4 10.8 %collective-permute-start.38 = (f32[832,128]{1,0:T(8,128)S(1)}, f32[832,128]{1,0:T(8,128)S(1)}, u32[]{:S(2)}, u32[]{:S(2)}) collective-permute-start(f32[832,128]{1,0:T(8,128)S(1)} %pad_maximum_fusion.2), channel_id=1, source_target_pairs={{0,16},{16,32},{32,48},{48,0},{64,80},{80,96},{96,112},{112,64},{1... | collective-permute-start | bytes 1277960 | tf_op jit(solution)/shard_map/ppermute | solution.py:196
  380.4 8.6 %collective-permute-start.41 = (f32[832,128]{1,0:T(8,128)S(1)}, f32[832,128]{1,0:T(8,128)S(1)}, u32[]{:S(2)}, u32[]{:S(2)}) collective-permute-start(f32[832,128]{1,0:T(8,128)S(1)} %fusion.79), channel_id=1, source_target_pairs={{0,64},{16,80},{32,96},{48,112},{64,0},{80,16},{96,32},{112,48},{1... | collective-permute-start | bytes 1277960 | tf_op jit(solution)/shard_map/ppermute | solution.py:199
  389.0 7.3 %collective-permute-start.42 = (f32[832,128]{1,0:T(8,128)S(1)}, f32[832,128]{1,0:T(8,128)S(1)}, u32[]{:S(2)}, u32[]{:S(2)}) collective-permute-start(f32[832,128]{1,0:T(8,128)S(1)} %get-tuple-element.64), channel_id=1, source_target_pairs={{0,48},{16,0},{32,16},{48,32},{64,112},{80,64},{96,80},{112,96},{1... | collective-permute-start | bytes 1277960 | tf_op jit(solution)/shard_map/ppermute | solution.py:202
  389.1 8.6 %collective-permute-start.43 = (f32[832,128]{1,0:T(8,128)S(1)}, f32[832,128]{1,0:T(8,128)S(1)}, u32[]{:S(2)}, u32[]{:S(2)}) collective-permute-start(f32[832,128]{1,0:T(8,128)S(1)} %get-tuple-element.64), channel_id=1, source_target_pairs={{0,16},{16,32},{32,48},{48,0},{64,80},{80,96},{96,112},{112,64},{1... | collective-permute-start | bytes 1277960 | tf_op jit(solution)/shard_map/ppermute | solution.py:201
  396.4 4.8 %collective-permute-start.45 = (f32[416,128]{1,0:T(8,128)S(1)}, f32[416,128]{1,0:T(8,128)S(1)}, u32[]{:S(2)}, u32[]{:S(2)}) collective-permute-start(f32[416,128]{1,0:T(8,128)S(1)} %slice.482), channel_id=1, source_target_pairs={{0,48},{16,0},{32,16},{48,32},{64,112},{80,64},{96,80},{112,96},{1... | collective-permute-start | bytes 638984 | tf_op jit(solution)/shard_map/ppermute | solution.py:204
  397.7 6.0 %collective-permute-start.44 = (f32[416,128]{1,0:T(8,128)S(1)}, f32[416,128]{1,0:T(8,128)S(1)}, u32[]{:S(2)}, u32[]{:S(2)}) collective-permute-start(f32[416,128]{1,0:T(8,128)S(1)} %slice.481), channel_id=1, source_target_pairs={{0,16},{16,32},{32,48},{48,0},{64,80},{80,96},{96,112},{112,64},{1... | collective-permute-start | bytes 638984 | tf_op jit(solution)/shard_map/ppermute | solution.py:203
  408.8 27.0 %collective-permute-start.46 = (f32[64,4480]{1,0:T(8,128)}, f32[64,4480]{1,0:T(8,128)}, u32[]{:S(2)}, u32[]{:S(2)}) collective-permute-start(f32[64,4480]{1,0:T(8,128)} %reshape.773), channel_id=1, source_target_pairs={{0,8},{8,0},{1,9},{9,1},{2,10},{10,2},{3,11},{11,3},{4,12},{12,4},... | collective-permute-start | bytes 3440648 | tf_op jit(solution)/shard_map/ppermute | solution.py:259
  429.1 5.5 %collective-permute-start.47 = (f32[128,1024]{1,0:T(8,128)S(1)}, f32[128,1024]{1,0:T(8,128)S(1)}, u32[]{:S(2)}, u32[]{:S(2)}) collective-permute-start(f32[128,1024]{1,0:T(8,128)S(1)} %reshape.775), channel_id=1, source_target_pairs={{0,8},{8,0},{1,9},{9,1},{2,10},{10,2},{3,11},{11,3},{4,12},{12,4},... | collective-permute-start | bytes 1572872 | tf_op jit(solution)/shard_map/ppermute | solution.py:259
  (89 other events, 758.1 us)
Sparse Core Ops, SparseCore 0:
  88.1 52.6 all-gather.2

commit v16 on v12

--- a/solution.py
+++ b/solution.py
@@ -310,7 +310,7 @@
     blocks = partial.reshape(groups, 2, -1, cols)
     keep = lax.dynamic_index_in_dim(blocks, core, axis=1, keepdims=False)
     give = lax.dynamic_index_in_dim(blocks, 1 - core, axis=1, keepdims=False)
-    return keep + core_swap(give)
+    return keep + core_swap(give.astype(jnp.bfloat16)).astype(jnp.float32)
 
 
 def reduce_rest(halves, wait_for=None):

time: 441 us -> 435 us (0.986)
  local copies, waits for them, and re-layouts: 89.5 us -> 80.4 us
  matrix products: 49.6 us -> 55.5 us
    squeeze x2 -> x0, local copies, waits for them, and re-layouts: 6.95 us -> none  [reduce_core(): give = lax.dynamic_index_in_dim(blocks, 1 - core, axis=1, keepdims=False)]
    unnamed x146 -> x132, local copies, waits for them, and re-layouts: 32.1 us -> 25.5 us
    convert_element_type x0 -> x2, local copies, waits for them, and re-layouts: none -> 4.69 us  [reduce_core(): return keep + core_swap(give.astype(jnp.bfloat16)).astype(jnp.float32)]
    dot_general x4, matrix products: 4.29 us -> 8.79 us  [back_product(): lax.dot_general(left, right, (((1,), (1,)), ((), ())), preferred_element_...]
  transfers between devices with their start and end apart: 49 -> 49, of which waited for: 17 -> 18; matrix products, arithmetic and copies ran while one was open for 32% -> 33% of each run, Pallas kernels for 0% -> 0%
where the time goes in v16:
time: 435 us; the launch traced here: 427 us
  waiting for transfers between devices  117 us (27%)
  other arithmetic  83.8 us (19%)
  local copies, waits for them, and re-layouts  80.4 us (18%)
  starting transfers between devices  74.1 us (17%)
  matrix products  55.5 us (13%)
  between operations  15.8 us (4%)
    ppermute x1, waiting for transfers between devices, gather_group(): from_prev = lax.ppermute(pair, 'shard_0', up)  37.1 us
    ppermute x18, waiting for transfers between devices, send(): lax.ppermute(p.astype(w), 'shard_0', pairs)  36 us
    dot_general x3, matrix products, mixer(): y_intra = jnp.einsum('chij,cjhp->cihp', mixing, scaled_in, precision=HIGH)  28.9 us
    ppermute x10, starting transfers between devices, core_swap(): return lax.ppermute(values, 'core', [(0, 1), (1, 0)])  26.8 us
    unnamed x132, local copies, waits for them, and re-layouts  25.5 us
    ppermute x18, starting transfers between devices, send(): lax.ppermute(p.astype(w), 'shard_0', pairs)  22 us
    add x2, other arithmetic, reduce_core(): return keep + core_swap(give.astype(jnp.bfloat16)).astype(jnp.float32)  13 us
    concatenate x3, other arithmetic, reduce_group(): doubled = jnp.concatenate([blocks, blocks], axis=0)  9.42 us
  transfers between devices with their start and end apart: 49, of which 18 were waited for; matrix products, arithmetic and copies ran while one was open for 33% of the time, Pallas kernels for 0%

profile of v16, /device:TPU:1, one launch (start us, length us, event | category | flops | bytes accessed | tf_op | source)
XLA Modules:
  0.0 426.8 jit_solution(17035400258168094886)
XLA Ops:
  11.3 3.3 constant_dynamic-slice_fusion.5
  21.5 3.5 collective-permute-start.2
  25.4 2.6 copy.93
  35.7 3.6 collective-permute-start.8
  42.0 37.1 %collective-permute-done.5 = bf16[2,64,4384]{2,1,0:T(8,128)(2,1)S(1)} collective-permute-done((bf16[2,64,4384]{2,1,0:T(8,128)(2,1)S(1)}, bf16[2,64,4384]{2,1,0:T(8,128)(2,1)S(1)}, u32[]{:S(2)}, u32[]{:S(2)}) %collective-permute-start.5) | collective-permute-done | bytes 1122336 | tf_op jit(solution)/shard_map/ppermute | solution.py:243
  79.3 2.7 collective-permute-start.7
  82.0 2.9 collective-permute-start.9
  86.0 6.5 %collective-permute-done.6 = bf16[2,32,4384]{2,1,0:T(8,128)(2,1)S(1)} collective-permute-done((bf16[2,32,4384]{2,1,0:T(8,128)(2,1)S(1)}, bf16[2,32,4384]{2,1,0:T(8,128)(2,1)S(1)}, u32[]{:S(2)}, u32[]{:S(2)}) %collective-permute-start.6) | collective-permute-done | bytes 561184 | tf_op jit(solution)/shard_map/ppermute | solution.py:246
  92.6 3.9 collective-permute-start.10
  104.5 2.6 constant_dynamic-slice_fusion.7
  118.9 7.2 %fusion.22 = (f32[256,2304]{0,1:T(8,128)S(1)}, f32[256,2304]{0,1:T(8,128)}) fusion(f32[253,2304]{0,1:T(8,128)} %slice.426, f32[2304]{0:T(1024)S(1)} %get-tuple-element.54, pred[256]{0:T(512)(128)(4,1)S(1)} %get-tuple-element.135, f32[254,2304]{0,1:T(8,128)} %slice.424, f32[2304]{0:T(1024)S(1)} %get-tuple-element.55, ...), kind=kLoop, calls=%fused_computation.55 | loop fusion | flops 8847360 | bytes 14147328 | tf_op jit(solution)/shard_map/jvp(jit(silu))/mul | solution.py:110
  130.7 10.0 %fusion.35 = f32[256,32,64]{0,2,1:T(8,128)S(1)} fusion(f32[256,32,64]{0,2,1:T(8,128)S(1)} %bitcast.345, f32[256,32,64]{0,2,1:T(8,128)S(1)} %fusion.88, f32[32]{0:T(128)S(1)} %mul.429, f32[256,32]{0,1:T(8,128)S(1)} %bitcast_multiply_fusion.8, f32[256,256]{1,0:T(8,128)S(1)} %fusion.104, f32[32,256]{1,0:T(8,128)S(1)} %bitcast_add_fusion.4, ...), kind=kOutput, calls=%fused_computation.79 | convolution fusion | flops 1619525632 | bytes 6717568 | tf_op jit(solution)/shard_map/jvp(chij,cjhp->cihp)/dot_general | solution.py:132
  146.3 3.3 multiply_reduce_fusion.5
  150.5 11.4 %fusion.7 = (f32[32,256]{1,0:T(8,128)S(1)}, f32[32,256]{1,0:T(8,128)S(1)}, f32[256,256]{1,0:T(8,128)S(1)}) fusion(f32[256,256]{1,0:T(8,128)S(1)} %fusion.104, f32[32,256]{1,0:T(8,128)S(1)} %copy-done.44, pred[256,256]{1,0:T(8,128)(4,1)S(1)} %copy-done.41, f32[32,64,256]{2,1,0:T(8,128)S(1)} %bitcast.315, f32[256,32,64]{0,2,1:T(8,128)S(1)} %bitcast.346, ...), kind=kOutput, calls=%fused_computation.15 | convolution fusion | flops 1629929472 | bytes 4915200 | tf_op jit(solution)/shard_map/transpose(jvp(chij,cjhp->cihp))/dot_general | solution.py:132
  161.8 7.5 %fusion.36 = (f32[256,32]{0,1:T(8,128)}, f32[1,256,32,64]{1,3,2,0:T(8,128)S(1)}) fusion(f32[1,256,32,64]{1,3,2,0:T(8,128)S(1)} %bitcast.347, f32[256,32]{0,1:T(8,128)S(1)} %get-tuple-element.73, f32[32,64,256]{2,1,0:T(8,128)S(1)} %bitcast.316, f32[256,256]{1,0:T(8,128)S(1)} %fusion.104, f32[32,256]{1,0:T(8,128)S(1)} %copy-done.44, ...), kind=kOutput, calls=%fused_computation.83 | convolution fusion | flops 1618468864 | bytes 6717440 | tf_op jit(solution)/shard_map/transpose(jvp(chij,cjhp->cihp))/dot_general | solution.py:132
  189.7 4.8 %fusion.135 = (f32[2304]{0:T(1024)S(1)}, f32[2304]{0:T(1024)S(1)}, f32[256,2304]{0,1:T(8,128)S(1)}) fusion(f32[256,2304]{0,1:T(8,128)S(1)} %get-tuple-element.65, f32[256,4384]{0,1:T(8,128)} %copy-done.2, f32[2304]{0:T(1024)S(1)} %get-tuple-element.53, f32[255,2304]{0,1:T(8,128)} %slice_multiply_fusion, f32[254,2304]{0,1:T(8,128)} %slice_multiply_fusion.1, ...), kind=kLoop, calls=%fused_computation.325 | loop fusion | flops 4124160 | bytes 14128128 | tf_op jit(solution)/shard_map/transpose(jvp())/reduce_sum | solution.py:104
  194.7 2.7 fusion.23
  197.3 3.0 fusion.8
  201.1 4.4 %fusion.124 = f32[2048,1024]{1,0:T(8,128)S(1)} fusion(bf16[256,2048]{0,1:T(8,128)(2,1)} %get-tuple-element.94, f32[256,1024]{1,0:T(8,128)} %param.13), kind=kOutput, calls=%fused_computation.314 | convolution fusion | flops 1074003968 | bytes 10485760 | tf_op jit(solution)/shard_map/dot_general | solution.py:76
  208.8 5.9 %fusion.46 = f32[256,8,1,64]{0,3,1,2:T(8,128)S(1)} fusion(bf16[8,64,4384]{2,1,0:T(8,128)(2,1)} %bitcast.319, bf16[256,4384]{0,1:T(8,128)(2,1)S(1)} %copy-done.26), kind=kOutput, calls=%fused_computation.111 | convolution fusion | flops 1149239296 | bytes 7258112 | tf_op jit(solution)/shard_map/dot_general | solution.py:82
  222.8 2.8 collective-permute-start.33
  225.6 3.5 bitcast_add_fusion.1
  233.6 9.4 %bitcast_add_fusion = f32[8,64,4480]{2,1,0:T(8,128)} fusion(bf16[8,64,4480]{2,1,0:T(8,128)(2,1)} %collective-permute-done.13, f32[8,2,64,4480]{3,2,1,0:T(8,128)} %bitcast.311, s32[]{:T(128)S(6)} %select_n.178), kind=kLoop, calls=%fused_computation.3 | loop fusion | flops 4587520 | bytes 22937604 | tf_op jit(solution)/shard_map/add | solution.py:313
  243.0 8.3 %fusion = f32[4,2,64,4480]{3,2,1,0:T(8,128)} fusion(s32[]{:T(128)S(6)} %select_n.202, f32[4,2,64,4480]{3,2,1,0:T(8,128)} %bitcast.314), kind=kLoop, calls=%fused_computation.2 | loop fusion | flops 2293760 | bytes 18350084 | tf_op jit(solution)/shard_map/concatenate | solution.py:155
  251.3 6.4 %slice_bitcast_fusion.3 = (f32[2,64,4480]{2,1,0:T(8,128)S(1)}, f32[2,64,4480]{2,1,0:T(8,128)S(1)}, f32[2,64,4480]{2,1,0:T(8,128)}, f32[2,64,4480]{2,1,0:T(8,128)}) fusion(f32[4,2,64,4480]{3,2,1,0:T(8,128)} %fusion), kind=kLoop, calls=%fused_computation.61 | loop fusion | bytes 18350080 | tf_op jit(solution)/shard_map/squeeze | solution.py:162
  263.8 2.7 collective-permute-start.34
  266.5 7.6 %collective-permute-done.34 = f32[2,8,128]{2,0,1:T(2,128)S(1)} collective-permute-done((f32[2,8,128]{2,0,1:T(2,128)}, f32[2,8,128]{2,0,1:T(2,128)S(1)}, u32[]{:S(2)}, u32[]{:S(2)}) %collective-permute-start.34) | collective-permute-done | bytes 8224 | tf_op jit(solution)/shard_map/ppermute | solution.py:160
  274.1 3.4 collective-permute-start.35
  278.9 2.7 collective-permute-start.26
  283.8 2.7 collective-permute-start.18
  286.7 2.7 collective-permute-start.27
  289.6 7.8 %collective-permute-done.18 = bf16[2,32,4480]{2,1,0:T(8,128)(2,1)S(1)} collective-permute-done((bf16[2,32,4480]{2,1,0:T(8,128)(2,1)S(1)}, bf16[2,32,4480]{2,1,0:T(8,128)(2,1)S(1)}, u32[]{:S(2)}, u32[]{:S(2)}) %collective-permute-start.18) | collective-permute-done | bytes 573472 | tf_op jit(solution)/shard_map/ppermute | solution.py:160
  297.5 10.8 %collective-permute-done.15 = bf16[2,32,4480]{2,1,0:T(8,128)(2,1)S(1)} collective-permute-done((bf16[2,32,4480]{2,1,0:T(8,128)(2,1)S(1)}, bf16[2,32,4480]{2,1,0:T(8,128)(2,1)S(1)}, u32[]{:S(2)}, u32[]{:S(2)}) %collective-permute-start.15) | collective-permute-done | bytes 573472 | tf_op jit(solution)/shard_map/ppermute | solution.py:160
  310.4 6.5 %collective-permute-done.19 = bf16[2,32,4480]{2,1,0:T(8,128)(2,1)S(1)} collective-permute-done((bf16[2,32,4480]{2,1,0:T(8,128)(2,1)S(1)}, bf16[2,32,4480]{2,1,0:T(8,128)(2,1)S(1)}, u32[]{:S(2)}, u32[]{:S(2)}) %collective-permute-start.19) | collective-permute-done | bytes 573472 | tf_op jit(solution)/shard_map/ppermute | solution.py:160
  316.9 3.3 collective-permute-done.16
  323.9 8.8 %collective-permute-done.36 = f32[16,128]{1,0:T(8,128)S(1)} collective-permute-done((f32[16,128]{1,0:T(8,128)S(1)}, f32[16,128]{1,0:T(8,128)S(1)}, u32[]{:S(2)}, u32[]{:S(2)}) %collective-permute-start.36) | collective-permute-done | bytes 8224 | tf_op jit(solution)/shard_map/ppermute | solution.py:175
  342.7 3.1 collective-permute-done.37
  346.0 2.8 collective-permute-start.40
  350.3 3.6 collective-permute-done.40
  353.9 5.7 %collective-permute-done.38 = f32[832,128]{1,0:T(8,128)S(1)} collective-permute-done((f32[832,128]{1,0:T(8,128)S(1)}, f32[832,128]{1,0:T(8,128)S(1)}, u32[]{:S(2)}, u32[]{:S(2)}) %collective-permute-start.38) | collective-permute-done | bytes 426016 | tf_op jit(solution)/shard_map/ppermute | solution.py:196
  360.8 2.6 collective-permute-start.41
  365.5 3.9 collective-permute-done.41
  372.7 4.1 collective-permute-done.42
  378.4 3.1 collective-permute-done.45
  381.5 2.5 collective-permute-done.44
  386.7 2.5 reshape.791
  389.2 14.2 %collective-permute-start.46 = (f32[64,4480]{1,0:T(8,128)}, f32[64,4480]{1,0:T(8,128)}, u32[]{:S(2)}, u32[]{:S(2)}) collective-permute-start(f32[64,4480]{1,0:T(8,128)} %reshape.791), channel_id=1, source_target_pairs={{0,8},{8,0},{1,9},{9,1},{2,10},{10,2},{3,11},{11,3},{4,12},{12,4},... | collective-permute-start | bytes 3440648 | tf_op jit(solution)/shard_map/ppermute | solution.py:259
  405.9 2.5 copy.114
  (381 shorter events, 142.3 us)
Async XLA Ops:
  7.2 121.4 %all-gather.3.cloned.1.call-start = ((), (), s32[]{:S(2)}) async-start(), calls=%async_computation | async-start | bytes 2359296 | tf_op jit(solution)/shard_map/all_gather | solution.py:271
  9.2 8.3 %collective-permute-start = (f32[8,1836]{1,0:T(8,128)S(1)}, f32[8,1836]{1,0:T(8,128)S(1)}, u32[]{:S(2)}, u32[]{:S(2)}) collective-permute-start(f32[8,1836]{1,0:T(8,128)S(1)} %broadcast_select_fusion.7), channel_id=1, source_target_pairs={{0,1},{1,0},{2,3},{3,2},{4,5},{5,4},{6,7},{7,6},{8,9},{9,8},{10,11... | collective-permute-start | bytes 176264 | tf_op jit(solution)/shard_map/ppermute | solution.py:338
  15.6 16.8 %collective-permute-start.3 = (bf16[64,4384]{1,0:T(8,128)(2,1)S(1)}, bf16[64,4384]{1,0:T(8,128)(2,1)}, u32[]{:S(2)}, u32[]{:S(2)}) collective-permute-start(bf16[64,4384]{1,0:T(8,128)(2,1)S(1)} %copy.120), channel_id=1, source_target_pairs={{0,1},{1,0},{2,3},{3,2},{4,5},{5,4},{6,7},{7,6},{8,9},{9,8},{10,11... | collective-permute-start | bytes 1683464 | tf_op jit(solution)/shard_map/ppermute | solution.py:241
  17.6 3.8 collective-permute-start.1
  21.5 6.5 %collective-permute-start.2 = (f32[8,1836]{1,0:T(8,128)S(1)}, f32[8,1836]{1,0:T(8,128)S(1)}, u32[]{:S(2)}, u32[]{:S(2)}) collective-permute-start(f32[8,1836]{1,0:T(8,128)S(1)} %fusion.162), channel_id=1, source_target_pairs={{0,4},{2,6},{4,0},{6,2},{1,5},{3,7},{5,1},{7,3},{8,12},{10,14},{12... | collective-permute-start | bytes 176264 | tf_op jit(solution)/shard_map/ppermute | solution.py:338
  33.9 45.3 %collective-permute-start.4 = (bf16[2,64,4384]{2,1,0:T(8,128)(2,1)S(1)}, bf16[2,64,4384]{2,1,0:T(8,128)(2,1)S(1)}, u32[]{:S(2)}, u32[]{:S(2)}) collective-permute-start(bf16[2,64,4384]{2,1,0:T(8,128)(2,1)S(1)} %maximum_select_fusion.1), channel_id=1, source_target_pairs={{0,6},{2,0},{4,2},{6,4},{1,7},{3,1},{5,3},{7,5},{8,14},{10,8},{12,... | collective-permute-start | bytes 3366920 | tf_op jit(solution)/shard_map/ppermute | solution.py:244
  35.7 43.4 %collective-permute-start.5 = (bf16[2,64,4384]{2,1,0:T(8,128)(2,1)S(1)}, bf16[2,64,4384]{2,1,0:T(8,128)(2,1)S(1)}, u32[]{:S(2)}, u32[]{:S(2)}) collective-permute-start(bf16[2,64,4384]{2,1,0:T(8,128)(2,1)S(1)} %maximum_select_fusion.1), channel_id=1, source_target_pairs={{0,2},{2,4},{4,6},{6,0},{1,3},{3,5},{5,7},{7,1},{8,10},{10,12},{12... | collective-permute-start | bytes 3366920 | tf_op jit(solution)/shard_map/ppermute | solution.py:243
  35.7 6.1 %collective-permute-start.8 = (bf16[64,4384]{1,0:T(8,128)(2,1)}, bf16[64,4384]{1,0:T(8,128)(2,1)S(1)}, u32[]{:S(2)}, u32[]{:S(2)}) collective-permute-start(bf16[64,4384]{1,0:T(8,128)(2,1)} %collective-permute-done.3), channel_id=1, source_target_pairs={{0,8},{8,0},{1,9},{9,1},{2,10},{10,2},{3,11},{11,3},{4,12},{12,4},... | collective-permute-start | bytes 1683464 | tf_op jit(solution)/shard_map/ppermute | solution.py:259
  79.1 13.4 %collective-permute-start.6 = (bf16[2,32,4384]{2,1,0:T(8,128)(2,1)S(1)}, bf16[2,32,4384]{2,1,0:T(8,128)(2,1)S(1)}, u32[]{:S(2)}, u32[]{:S(2)}) collective-permute-start(bf16[2,32,4384]{2,1,0:T(8,128)(2,1)S(1)} %slice.418), channel_id=1, source_target_pairs={{0,2},{2,4},{4,6},{6,0},{1,3},{3,5},{5,7},{7,1},{8,10},{10,12},{12... | collective-permute-start | bytes 1683464 | tf_op jit(solution)/shard_map/ppermute | solution.py:246
  79.3 13.3 %collective-permute-start.7 = (bf16[2,32,4384]{2,1,0:T(8,128)(2,1)S(1)}, bf16[2,32,4384]{2,1,0:T(8,128)(2,1)S(1)}, u32[]{:S(2)}, u32[]{:S(2)}) collective-permute-start(bf16[2,32,4384]{2,1,0:T(8,128)(2,1)S(1)} %slice.419), channel_id=1, source_target_pairs={{0,6},{2,0},{4,2},{6,4},{1,7},{3,1},{5,3},{7,5},{8,14},{10,8},{12,... | collective-permute-start | bytes 1683464 | tf_op jit(solution)/shard_map/ppermute | solution.py:247
  82.0 27.4 %collective-permute-start.9 = (bf16[2,64,4384]{2,1,0:T(8,128)(2,1)S(1)}, bf16[2,64,4384]{2,1,0:T(8,128)(2,1)S(1)}, u32[]{:S(2)}, u32[]{:S(2)}) collective-permute-start(bf16[2,64,4384]{2,1,0:T(8,128)(2,1)S(1)} %collective-permute-done.4), channel_id=1, source_target_pairs={{0,8},{8,0},{1,9},{9,1},{2,10},{10,2},{3,11},{11,3},{4,12},{12,4},... | collective-permute-start | bytes 3366920 | tf_op jit(solution)/shard_map/ppermute | solution.py:259
  84.9 24.7 %collective-permute-start.11 = (bf16[2,64,4384]{2,1,0:T(8,128)(2,1)S(1)}, bf16[2,64,4384]{2,1,0:T(8,128)(2,1)S(1)}, u32[]{:S(2)}, u32[]{:S(2)}) collective-permute-start(bf16[2,64,4384]{2,1,0:T(8,128)(2,1)S(1)} %collective-permute-done.5), channel_id=1, source_target_pairs={{0,8},{8,0},{1,9},{9,1},{2,10},{10,2},{3,11},{11,3},{4,12},{12,4},... | collective-permute-start | bytes 3366920 | tf_op jit(solution)/shard_map/ppermute | solution.py:259
  92.6 16.9 %collective-permute-start.10 = (bf16[2,64,4384]{2,1,0:T(8,128)(2,1)S(1)}, bf16[2,64,4384]{2,1,0:T(8,128)(2,1)S(1)}, u32[]{:S(2)}, u32[]{:S(2)}) collective-permute-start(bf16[2,64,4384]{2,1,0:T(8,128)(2,1)S(1)} %constant_dynamic-update-slice_fusion), channel_id=1, source_target_pairs={{0,8},{8,0},{1,9},{9,1},{2,10},{10,2},{3,11},{11,3},{4,12},{12,4},... | collective-permute-start | bytes 3366920 | tf_op jit(solution)/shard_map/ppermute | solution.py:259
  128.6 14.9 %collective-permute-start.12 = (bf16[8,128,1024]{2,1,0:T(8,128)(2,1)}, bf16[8,128,1024]{2,1,0:T(8,128)(2,1)S(1)}, u32[]{:S(2)}, u32[]{:S(2)}) collective-permute-start(bf16[8,128,1024]{2,1,0:T(8,128)(2,1)} %bitcast.325), channel_id=1, source_target_pairs={{0,8},{8,0},{1,9},{9,1},{2,10},{10,2},{3,11},{11,3},{4,12},{12,4},... | collective-permute-start | bytes 6291464 | tf_op jit(solution)/shard_map/ppermute | solution.py:259
  200.4 33.2 %collective-permute-start.13 = (bf16[8,64,4480]{2,1,0:T(8,128)(2,1)}, bf16[8,64,4480]{2,1,0:T(8,128)(2,1)}, u32[]{:S(2)}, u32[]{:S(2)}) collective-permute-start(bf16[8,64,4480]{2,1,0:T(8,128)(2,1)} %fusion.8), channel_id=1, source_target_pairs={{0,8},{8,0},{1,9},{9,1},{2,10},{10,2},{3,11},{11,3},{4,12},{12,4},... | collective-permute-start | bytes 13762568 | tf_op jit(solution)/shard_map/ppermute | solution.py:259
  207.2 18.4 %collective-permute-start.21 = (bf16[8,128,1024]{2,1,0:T(8,128)(2,1)}, bf16[8,128,1024]{2,1,0:T(8,128)(2,1)}, u32[]{:S(2)}, u32[]{:S(2)}) collective-permute-start(bf16[8,128,1024]{2,1,0:T(8,128)(2,1)} %fusion.31), channel_id=1, source_target_pairs={{0,8},{8,0},{1,9},{9,1},{2,10},{10,2},{3,11},{11,3},{4,12},{12,4},... | collective-permute-start | bytes 6291464 | tf_op jit(solution)/shard_map/ppermute | solution.py:259
  222.8 40.4 %collective-permute-start.33 = (f32[2,8,128]{2,0,1:T(2,128)S(1)}, f32[2,8,128]{2,0,1:T(2,128)S(1)}, u32[]{:S(2)}, u32[]{:S(2)}) collective-permute-start(f32[2,8,128]{2,0,1:T(2,128)S(1)} %slice.470), channel_id=1, source_target_pairs={{0,6},{2,0},{4,2},{6,4},{1,7},{3,1},{5,3},{7,5},{8,14},{10,8},{12,... | collective-permute-start | bytes 24584 | tf_op jit(solution)/shard_map/ppermute | solution.py:160
  231.5 45.9 %collective-permute-start.25 = (bf16[2,64,1024]{2,1,0:T(8,128)(2,1)S(1)}, bf16[2,64,1024]{2,1,0:T(8,128)(2,1)S(1)}, u32[]{:S(2)}, u32[]{:S(2)}) collective-permute-start(bf16[2,64,1024]{2,1,0:T(8,128)(2,1)S(1)} %slice.603), channel_id=1, source_target_pairs={{0,6},{2,0},{4,2},{6,4},{1,7},{3,1},{5,3},{7,5},{8,14},{10,8},{12,... | collective-permute-start | bytes 786440 | tf_op jit(solution)/shard_map/ppermute | solution.py:160
  232.8 44.7 %collective-permute-start.22 = (bf16[2,64,1024]{2,1,0:T(8,128)(2,1)S(1)}, bf16[2,64,1024]{2,1,0:T(8,128)(2,1)}, u32[]{:S(2)}, u32[]{:S(2)}) collective-permute-start(bf16[2,64,1024]{2,1,0:T(8,128)(2,1)S(1)} %slice.604), channel_id=1, source_target_pairs={{0,2},{2,4},{4,6},{6,0},{1,3},{3,5},{5,7},{7,1},{8,10},{10,12},{12... | collective-permute-start | bytes 786440 | tf_op jit(solution)/shard_map/ppermute | solution.py:160
  260.0 21.6 %collective-permute-start.17 = (bf16[2,32,4480]{2,1,0:T(8,128)(2,1)}, bf16[2,32,4480]{2,1,0:T(8,128)(2,1)S(1)}, u32[]{:S(2)}, u32[]{:S(2)}) collective-permute-start(bf16[2,32,4480]{2,1,0:T(8,128)(2,1)} %slice.601), channel_id=1, source_target_pairs={{0,6},{2,0},{4,2},{6,4},{1,7},{3,1},{5,3},{7,5},{8,14},{10,8},{12,... | collective-permute-start | bytes 1720328 | tf_op jit(solution)/shard_map/ppermute | solution.py:160
  263.2 18.5 %collective-permute-start.14 = (bf16[2,32,4480]{2,1,0:T(8,128)(2,1)}, bf16[2,32,4480]{2,1,0:T(8,128)(2,1)}, u32[]{:S(2)}, u32[]{:S(2)}) collective-permute-start(bf16[2,32,4480]{2,1,0:T(8,128)(2,1)} %slice.602), channel_id=1, source_target_pairs={{0,2},{2,4},{4,6},{6,0},{1,3},{3,5},{5,7},{7,1},{8,10},{10,12},{12... | collective-permute-start | bytes 1720328 | tf_op jit(solution)/shard_map/ppermute | solution.py:160
  263.8 10.3 %collective-permute-start.34 = (f32[2,8,128]{2,0,1:T(2,128)}, f32[2,8,128]{2,0,1:T(2,128)S(1)}, u32[]{:S(2)}, u32[]{:S(2)}) collective-permute-start(f32[2,8,128]{2,0,1:T(2,128)} %slice_add_fusion.15), channel_id=1, source_target_pairs={{0,6},{2,0},{4,2},{6,4},{1,7},{3,1},{5,3},{7,5},{8,14},{10,8},{12,... | collective-permute-start | bytes 24584 | tf_op jit(solution)/shard_map/ppermute | solution.py:160
  274.1 48.2 %collective-permute-start.35 = (f32[2,8,128]{2,0,1:T(2,128)S(1)}, f32[2,8,128]{2,0,1:T(2,128)S(1)}, u32[]{:S(2)}, u32[]{:S(2)}) collective-permute-start(f32[2,8,128]{2,0,1:T(2,128)S(1)} %get-tuple-element.130), channel_id=1, source_target_pairs={{0,6},{2,0},{4,2},{6,4},{1,7},{3,1},{5,3},{7,5},{8,14},{10,8},{12,... | collective-permute-start | bytes 24584 | tf_op jit(solution)/shard_map/ppermute | solution.py:160
  277.5 9.0 %collective-permute-start.30 = (f32[2,8,128]{2,0,1:T(2,128)S(1)}, f32[2,8,128]{2,0,1:T(2,128)S(1)}, u32[]{:S(2)}, u32[]{:S(2)}) collective-permute-start(f32[2,8,128]{2,0,1:T(2,128)S(1)} %get-tuple-element.131), channel_id=1, source_target_pairs={{0,2},{2,4},{4,6},{6,0},{1,3},{3,5},{5,7},{7,1},{8,10},{10,12},{12... | collective-permute-start | bytes 24584 | tf_op jit(solution)/shard_map/ppermute | solution.py:160
  278.9 7.7 %collective-permute-start.26 = (bf16[2,64,1024]{2,1,0:T(8,128)(2,1)S(1)}, bf16[2,64,1024]{2,1,0:T(8,128)(2,1)S(1)}, u32[]{:S(2)}, u32[]{:S(2)}) collective-permute-start(bf16[2,64,1024]{2,1,0:T(8,128)(2,1)S(1)} %get-tuple-element.109), channel_id=1, source_target_pairs={{0,6},{2,0},{4,2},{6,4},{1,7},{3,1},{5,3},{7,5},{8,14},{10,8},{12,... | collective-permute-start | bytes 786440 | tf_op jit(solution)/shard_map/ppermute | solution.py:160
  281.6 7.8 %collective-permute-start.23 = (bf16[2,64,1024]{2,1,0:T(8,128)(2,1)S(1)}, bf16[2,64,1024]{2,1,0:T(8,128)(2,1)S(1)}, u32[]{:S(2)}, u32[]{:S(2)}) collective-permute-start(bf16[2,64,1024]{2,1,0:T(8,128)(2,1)S(1)} %get-tuple-element.110), channel_id=1, source_target_pairs={{0,2},{2,4},{4,6},{6,0},{1,3},{3,5},{5,7},{7,1},{8,10},{10,12},{12... | collective-permute-start | bytes 786440 | tf_op jit(solution)/shard_map/ppermute | solution.py:160
  283.8 13.6 %collective-permute-start.18 = (bf16[2,32,4480]{2,1,0:T(8,128)(2,1)S(1)}, bf16[2,32,4480]{2,1,0:T(8,128)(2,1)S(1)}, u32[]{:S(2)}, u32[]{:S(2)}) collective-permute-start(bf16[2,32,4480]{2,1,0:T(8,128)(2,1)S(1)} %get-tuple-element.92), channel_id=1, source_target_pairs={{0,6},{2,0},{4,2},{6,4},{1,7},{3,1},{5,3},{7,5},{8,14},{10,8},{12,... | collective-permute-start | bytes 1720328 | tf_op jit(solution)/shard_map/ppermute | solution.py:160
  286.5 23.0 %collective-permute-start.31 = (f32[2,8,128]{2,0,1:T(2,128)S(1)}, f32[2,8,128]{2,0,1:T(2,128)S(1)}, u32[]{:S(2)}, u32[]{:S(2)}) collective-permute-start(f32[2,8,128]{2,0,1:T(2,128)S(1)} %slice_add_fusion.18), channel_id=1, source_target_pairs={{0,2},{2,4},{4,6},{6,0},{1,3},{3,5},{5,7},{7,1},{8,10},{10,12},{12... | collective-permute-start | bytes 24584 | tf_op jit(solution)/shard_map/ppermute | solution.py:160
  286.7 23.3 %collective-permute-start.27 = (bf16[2,64,1024]{2,1,0:T(8,128)(2,1)S(1)}, bf16[2,64,1024]{2,1,0:T(8,128)(2,1)S(1)}, u32[]{:S(2)}, u32[]{:S(2)}) collective-permute-start(bf16[2,64,1024]{2,1,0:T(8,128)(2,1)S(1)} %fusion.83), channel_id=1, source_target_pairs={{0,6},{2,0},{4,2},{6,4},{1,7},{3,1},{5,3},{7,5},{8,14},{10,8},{12,... | collective-permute-start | bytes 786440 | tf_op jit(solution)/shard_map/ppermute | solution.py:160
  289.5 20.6 %collective-permute-start.24 = (bf16[2,64,1024]{2,1,0:T(8,128)(2,1)S(1)}, bf16[2,64,1024]{2,1,0:T(8,128)(2,1)S(1)}, u32[]{:S(2)}, u32[]{:S(2)}) collective-permute-start(bf16[2,64,1024]{2,1,0:T(8,128)(2,1)S(1)} %fusion.85), channel_id=1, source_target_pairs={{0,2},{2,4},{4,6},{6,0},{1,3},{3,5},{5,7},{7,1},{8,10},{10,12},{12... | collective-permute-start | bytes 786440 | tf_op jit(solution)/shard_map/ppermute | solution.py:160
  297.4 10.9 %collective-permute-start.15 = (bf16[2,32,4480]{2,1,0:T(8,128)(2,1)S(1)}, bf16[2,32,4480]{2,1,0:T(8,128)(2,1)S(1)}, u32[]{:S(2)}, u32[]{:S(2)}) collective-permute-start(bf16[2,32,4480]{2,1,0:T(8,128)(2,1)S(1)} %get-tuple-element.93), channel_id=1, source_target_pairs={{0,2},{2,4},{4,6},{6,0},{1,3},{3,5},{5,7},{7,1},{8,10},{10,12},{12... | collective-permute-start | bytes 1720328 | tf_op jit(solution)/shard_map/ppermute | solution.py:160
  308.3 8.6 %collective-permute-start.19 = (bf16[2,32,4480]{2,1,0:T(8,128)(2,1)S(1)}, bf16[2,32,4480]{2,1,0:T(8,128)(2,1)S(1)}, u32[]{:S(2)}, u32[]{:S(2)}) collective-permute-start(bf16[2,32,4480]{2,1,0:T(8,128)(2,1)S(1)} %fusion.57), channel_id=1, source_target_pairs={{0,6},{2,0},{4,2},{6,4},{1,7},{3,1},{5,3},{7,5},{8,14},{10,8},{12,... | collective-permute-start | bytes 1720328 | tf_op jit(solution)/shard_map/ppermute | solution.py:160
  309.5 10.7 %collective-permute-start.16 = (bf16[2,32,4480]{2,1,0:T(8,128)(2,1)S(1)}, bf16[2,32,4480]{2,1,0:T(8,128)(2,1)S(1)}, u32[]{:S(2)}, u32[]{:S(2)}) collective-permute-start(bf16[2,32,4480]{2,1,0:T(8,128)(2,1)S(1)} %fusion.59), channel_id=1, source_target_pairs={{0,2},{2,4},{4,6},{6,0},{1,3},{3,5},{5,7},{7,1},{8,10},{10,12},{12... | collective-permute-start | bytes 1720328 | tf_op jit(solution)/shard_map/ppermute | solution.py:160
  310.0 12.3 %collective-permute-start.32 = (f32[2,8,128]{2,0,1:T(2,128)S(1)}, f32[2,8,128]{2,0,1:T(2,128)S(1)}, u32[]{:S(2)}, u32[]{:S(2)}) collective-permute-start(f32[2,8,128]{2,0,1:T(2,128)S(1)} %slice_add_fusion.17), channel_id=1, source_target_pairs={{0,2},{2,4},{4,6},{6,0},{1,3},{3,5},{5,7},{7,1},{8,10},{10,12},{12... | collective-permute-start | bytes 24584 | tf_op jit(solution)/shard_map/ppermute | solution.py:160
  310.3 22.4 %collective-permute-start.28 = (bf16[128,1024]{1,0:T(8,128)(2,1)S(1)}, bf16[128,1024]{1,0:T(8,128)(2,1)}, u32[]{:S(2)}, u32[]{:S(2)}) collective-permute-start(bf16[128,1024]{1,0:T(8,128)(2,1)S(1)} %fusion.94), channel_id=1, source_target_pairs={{0,1},{1,0},{2,3},{3,2},{4,5},{5,4},{6,7},{7,6},{8,9},{9,8},{10,11... | collective-permute-start | bytes 786440 | tf_op jit(solution)/shard_map/ppermute | solution.py:175
  322.3 13.3 %collective-permute-start.20 = (bf16[64,4480]{1,0:T(8,128)(2,1)}, bf16[64,4480]{1,0:T(8,128)(2,1)}, u32[]{:S(2)}, u32[]{:S(2)}) collective-permute-start(bf16[64,4480]{1,0:T(8,128)(2,1)} %fusion.77), channel_id=1, source_target_pairs={{0,1},{1,0},{2,3},{3,2},{4,5},{5,4},{6,7},{7,6},{8,9},{9,8},{10,11... | collective-permute-start | bytes 1720328 | tf_op jit(solution)/shard_map/ppermute | solution.py:175
  322.4 10.3 %collective-permute-start.36 = (f32[16,128]{1,0:T(8,128)S(1)}, f32[16,128]{1,0:T(8,128)S(1)}, u32[]{:S(2)}, u32[]{:S(2)}) collective-permute-start(f32[16,128]{1,0:T(8,128)S(1)} %bitcast.366), channel_id=1, source_target_pairs={{0,1},{1,0},{2,3},{3,2},{4,5},{5,4},{6,7},{7,6},{8,9},{9,8},{10,11... | collective-permute-start | bytes 24584 | tf_op jit(solution)/shard_map/ppermute | solution.py:175
  339.8 6.0 %collective-permute-start.37 = (f32[416,128]{1,0:T(8,128)S(1)}, f32[416,128]{1,0:T(8,128)S(1)}, u32[]{:S(2)}, u32[]{:S(2)}) collective-permute-start(f32[416,128]{1,0:T(8,128)S(1)} %get-tuple-element.99), channel_id=1, source_target_pairs={{0,16},{16,32},{32,48},{48,0},{64,80},{80,96},{96,112},{112,64},{1... | collective-permute-start | bytes 638984 | tf_op jit(solution)/shard_map/ppermute | solution.py:192
  341.1 4.9 %collective-permute-start.39 = (f32[416,128]{1,0:T(8,128)S(1)}, f32[416,128]{1,0:T(8,128)S(1)}, u32[]{:S(2)}, u32[]{:S(2)}) collective-permute-start(f32[416,128]{1,0:T(8,128)S(1)} %get-tuple-element.100), channel_id=1, source_target_pairs={{0,48},{16,0},{32,16},{48,32},{64,112},{80,64},{96,80},{112,96},{1... | collective-permute-start | bytes 638984 | tf_op jit(solution)/shard_map/ppermute | solution.py:193
  346.0 7.9 %collective-permute-start.40 = (f32[832,128]{1,0:T(8,128)S(1)}, f32[832,128]{1,0:T(8,128)}, u32[]{:S(2)}, u32[]{:S(2)}) collective-permute-start(f32[832,128]{1,0:T(8,128)S(1)} %pad_maximum_fusion.3), channel_id=1, source_target_pairs={{0,48},{16,0},{32,16},{48,32},{64,112},{80,64},{96,80},{112,96},{1... | collective-permute-start | bytes 1277960 | tf_op jit(solution)/shard_map/ppermute | solution.py:196
  348.9 10.7 %collective-permute-start.38 = (f32[832,128]{1,0:T(8,128)S(1)}, f32[832,128]{1,0:T(8,128)S(1)}, u32[]{:S(2)}, u32[]{:S(2)}) collective-permute-start(f32[832,128]{1,0:T(8,128)S(1)} %pad_maximum_fusion.2), channel_id=1, source_target_pairs={{0,16},{16,32},{32,48},{48,0},{64,80},{80,96},{96,112},{112,64},{1... | collective-permute-start | bytes 1277960 | tf_op jit(solution)/shard_map/ppermute | solution.py:196
  360.8 8.6 %collective-permute-start.41 = (f32[832,128]{1,0:T(8,128)S(1)}, f32[832,128]{1,0:T(8,128)S(1)}, u32[]{:S(2)}, u32[]{:S(2)}) collective-permute-start(f32[832,128]{1,0:T(8,128)S(1)} %fusion.91), channel_id=1, source_target_pairs={{0,64},{16,80},{32,96},{48,112},{64,0},{80,16},{96,32},{112,48},{1... | collective-permute-start | bytes 1277960 | tf_op jit(solution)/shard_map/ppermute | solution.py:199
  369.4 7.3 %collective-permute-start.42 = (f32[832,128]{1,0:T(8,128)S(1)}, f32[832,128]{1,0:T(8,128)S(1)}, u32[]{:S(2)}, u32[]{:S(2)}) collective-permute-start(f32[832,128]{1,0:T(8,128)S(1)} %get-tuple-element.58), channel_id=1, source_target_pairs={{0,48},{16,0},{32,16},{48,32},{64,112},{80,64},{96,80},{112,96},{1... | collective-permute-start | bytes 1277960 | tf_op jit(solution)/shard_map/ppermute | solution.py:202
  369.5 8.6 %collective-permute-start.43 = (f32[832,128]{1,0:T(8,128)S(1)}, f32[832,128]{1,0:T(8,128)S(1)}, u32[]{:S(2)}, u32[]{:S(2)}) collective-permute-start(f32[832,128]{1,0:T(8,128)S(1)} %get-tuple-element.58), channel_id=1, source_target_pairs={{0,16},{16,32},{32,48},{48,0},{64,80},{80,96},{96,112},{112,64},{1... | collective-permute-start | bytes 1277960 | tf_op jit(solution)/shard_map/ppermute | solution.py:201
  376.8 4.8 %collective-permute-start.45 = (f32[416,128]{1,0:T(8,128)S(1)}, f32[416,128]{1,0:T(8,128)S(1)}, u32[]{:S(2)}, u32[]{:S(2)}) collective-permute-start(f32[416,128]{1,0:T(8,128)S(1)} %slice.482), channel_id=1, source_target_pairs={{0,48},{16,0},{32,16},{48,32},{64,112},{80,64},{96,80},{112,96},{1... | collective-permute-start | bytes 638984 | tf_op jit(solution)/shard_map/ppermute | solution.py:204
  378.1 6.0 %collective-permute-start.44 = (f32[416,128]{1,0:T(8,128)S(1)}, f32[416,128]{1,0:T(8,128)S(1)}, u32[]{:S(2)}, u32[]{:S(2)}) collective-permute-start(f32[416,128]{1,0:T(8,128)S(1)} %slice.481), channel_id=1, source_target_pairs={{0,16},{16,32},{32,48},{48,0},{64,80},{80,96},{96,112},{112,64},{1... | collective-permute-start | bytes 638984 | tf_op jit(solution)/shard_map/ppermute | solution.py:203
  389.2 27.0 %collective-permute-start.46 = (f32[64,4480]{1,0:T(8,128)}, f32[64,4480]{1,0:T(8,128)}, u32[]{:S(2)}, u32[]{:S(2)}) collective-permute-start(f32[64,4480]{1,0:T(8,128)} %reshape.791), channel_id=1, source_target_pairs={{0,8},{8,0},{1,9},{9,1},{2,10},{10,2},{3,11},{11,3},{4,12},{12,4},... | collective-permute-start | bytes 3440648 | tf_op jit(solution)/shard_map/ppermute | solution.py:259
  409.6 5.5 %collective-permute-start.47 = (f32[128,1024]{1,0:T(8,128)S(1)}, f32[128,1024]{1,0:T(8,128)S(1)}, u32[]{:S(2)}, u32[]{:S(2)}) collective-permute-start(f32[128,1024]{1,0:T(8,128)S(1)} %reshape.793), channel_id=1, source_target_pairs={{0,8},{8,0},{1,9},{9,1},{2,10},{10,2},{3,11},{11,3},{4,12},{12,4},... | collective-permute-start | bytes 1572872 | tf_op jit(solution)/shard_map/ppermute | solution.py:259
  (55 other events, 483.8 us)
Sparse Core Ops, SparseCore 0:
  16.6 56.7 all-gather.2

commit v17 on v16

--- a/solution.py
+++ b/solution.py
@@ -212,9 +212,9 @@
 def core_join(owned):
     core = lax.axis_index("core")
     other = core_swap(owned)
-    first = jnp.where(core == 0, owned, other)
-    second = jnp.where(core == 0, other, owned)
-    return jnp.concatenate([first, second], axis=0)
+    rows = owned.shape[0]
+    trio = jnp.concatenate([owned, other, owned], axis=0)
+    return lax.dynamic_slice_in_dim(trio, core * rows, 2 * rows, axis=0)
 
 
 def core_swap(values):
@@ -230,7 +230,8 @@
     half = block.shape[0] // 2
 
     def place(own, got):
-        return jnp.where(y == 0, jnp.stack([own, got]), jnp.stack([got, own]))
+        pair = jnp.stack([own, got, own])
+        return lax.dynamic_slice_in_dim(pair, y, 2, axis=0)
 
     def arrange(pair, from_next, opposite, from_prev):
         ordered = jnp.stack([pair, from_next, opposite, from_prev])

time: 435 us -> 432 us (level)
  waiting for transfers between devices: 117 us -> 112 us
    unnamed x132 -> x134, local copies, waits for them, and re-layouts: 25.5 us -> 26.8 us
where the time goes in v17:
time: 432 us; the launch traced here: 424 us
  waiting for transfers between devices  112 us (26%)
  local copies, waits for them, and re-layouts  82 us (19%)
  other arithmetic  80.8 us (19%)
  starting transfers between devices  76.9 us (18%)
  matrix products  57.1 us (13%)
  between operations  15.7 us (4%)
    ppermute x18, waiting for transfers between devices, send(): lax.ppermute(p.astype(w), 'shard_0', pairs)  36 us
    ppermute x1, waiting for transfers between devices, gather_group(): from_prev = lax.ppermute(pair, 'shard_0', up)  35.3 us
    ppermute x10, starting transfers between devices, core_swap(): return lax.ppermute(values, 'core', [(0, 1), (1, 0)])  28.9 us
    dot_general x3, matrix products, mixer(): y_intra = jnp.einsum('chij,cjhp->cihp', mixing, scaled_in, precision=HIGH)  28 us
    unnamed x134, local copies, waits for them, and re-layouts  26.8 us
    ppermute x18, starting transfers between devices, send(): lax.ppermute(p.astype(w), 'shard_0', pairs)  21.9 us
    add x2, other arithmetic, reduce_core(): return keep + core_swap(give.astype(jnp.bfloat16)).astype(jnp.float32)  13 us
    concatenate x3, other arithmetic, reduce_group(): doubled = jnp.concatenate([blocks, blocks], axis=0)  9.42 us
  transfers between devices with their start and end apart: 49, of which 18 were waited for; matrix products, arithmetic and copies ran while one was open for 33% of the time, Pallas kernels for 0%

profile of v17, /device:TPU:1, one launch (start us, length us, event | category | flops | bytes accessed | tf_op | source)
XLA Modules:
  0.0 424.1 jit_solution(888238076760395638)
XLA Ops:
  12.0 3.3 constant_dynamic-slice_fusion.5
  21.5 3.5 collective-permute-start.2
  25.4 2.6 copy.93
  30.9 2.5 bitcast_dynamic-update-slice_fusion.12
  33.4 2.8 collective-permute-start.4
  36.2 4.6 %collective-permute-start.8 = (bf16[64,4384]{1,0:T(8,128)(2,1)}, bf16[64,4384]{1,0:T(8,128)(2,1)S(1)}, u32[]{:S(2)}, u32[]{:S(2)}) collective-permute-start(bf16[64,4384]{1,0:T(8,128)(2,1)} %collective-permute-done.3), channel_id=1, source_target_pairs={{0,8},{8,0},{1,9},{9,1},{2,10},{10,2},{3,11},{11,3},{4,12},{12,4},... | collective-permute-start | bytes 1683464 | tf_op jit(solution)/shard_map/ppermute | solution.py:260
  43.9 35.3 %collective-permute-done.5 = bf16[2,64,4384]{2,1,0:T(8,128)(2,1)S(1)} collective-permute-done((bf16[2,64,4384]{2,1,0:T(8,128)(2,1)S(1)}, bf16[2,64,4384]{2,1,0:T(8,128)(2,1)S(1)}, u32[]{:S(2)}, u32[]{:S(2)}) %collective-permute-start.5) | collective-permute-done | bytes 1122336 | tf_op jit(solution)/shard_map/ppermute | solution.py:244
  79.3 2.7 collective-permute-start.7
  82.0 3.4 collective-permute-start.9
  86.5 5.5 %collective-permute-done.6 = bf16[2,32,4384]{2,1,0:T(8,128)(2,1)S(1)} collective-permute-done((bf16[2,32,4384]{2,1,0:T(8,128)(2,1)S(1)}, bf16[2,32,4384]{2,1,0:T(8,128)(2,1)S(1)}, u32[]{:S(2)}, u32[]{:S(2)}) %collective-permute-start.6) | collective-permute-done | bytes 561184 | tf_op jit(solution)/shard_map/ppermute | solution.py:247
  92.2 4.3 %collective-permute-start.10 = (bf16[2,64,4384]{2,1,0:T(8,128)(2,1)S(1)}, bf16[2,64,4384]{2,1,0:T(8,128)(2,1)S(1)}, u32[]{:S(2)}, u32[]{:S(2)}) collective-permute-start(bf16[2,64,4384]{2,1,0:T(8,128)(2,1)S(1)} %constant_dynamic-update-slice_fusion), channel_id=1, source_target_pairs={{0,8},{8,0},{1,9},{9,1},{2,10},{10,2},{3,11},{11,3},{4,12},{12,4},... | collective-permute-start | bytes 3366920 | tf_op jit(solution)/shard_map/ppermute | solution.py:260
  103.2 2.6 constant_dynamic-slice_fusion.7
  117.5 7.2 %fusion.22 = (f32[256,2304]{0,1:T(8,128)S(1)}, f32[256,2304]{0,1:T(8,128)}) fusion(f32[253,2304]{0,1:T(8,128)} %slice.426, f32[2304]{0:T(1024)S(1)} %get-tuple-element.54, pred[256]{0:T(512)(128)(4,1)S(1)} %get-tuple-element.135, f32[254,2304]{0,1:T(8,128)} %slice.424, f32[2304]{0:T(1024)S(1)} %get-tuple-element.55, ...), kind=kLoop, calls=%fused_computation.58 | loop fusion | flops 8847360 | bytes 14147328 | tf_op jit(solution)/shard_map/jvp(jit(silu))/mul | solution.py:110
  129.2 9.2 %fusion.37 = f32[256,32,64]{0,2,1:T(8,128)S(1)} fusion(f32[256,32,64]{0,2,1:T(8,128)S(1)} %bitcast.344, f32[256,32,64]{0,2,1:T(8,128)S(1)} %fusion.97, f32[32]{0:T(128)S(1)} %copy-done.48, f32[256,32]{0,1:T(8,128)S(1)} %bitcast_multiply_fusion.8, f32[256,256]{1,0:T(8,128)S(1)} %fusion.109, f32[32,256]{1,0:T(8,128)S(1)} %bitcast_add_fusion.4, ...), kind=kOutput, calls=%fused_computation.83 | convolution fusion | flops 1619525632 | bytes 6717568 | tf_op jit(solution)/shard_map/jvp(chij,cjhp->cihp)/dot_general | solution.py:132
  144.0 3.3 multiply_reduce_fusion.5
  148.1 11.4 %fusion.7 = (f32[32,256]{1,0:T(8,128)S(1)}, f32[32,256]{1,0:T(8,128)S(1)}, f32[256,256]{1,0:T(8,128)S(1)}) fusion(f32[256,256]{1,0:T(8,128)S(1)} %fusion.109, f32[32,256]{1,0:T(8,128)S(1)} %copy-done.42, pred[256,256]{1,0:T(8,128)(4,1)S(1)} %fusion.104, f32[32,64,256]{2,1,0:T(8,128)S(1)} %bitcast.319, f32[256,32,64]{0,2,1:T(8,128)S(1)} %bitcast.345, ...), kind=kOutput, calls=%fused_computation.15 | convolution fusion | flops 1629929472 | bytes 4915200 | tf_op jit(solution)/shard_map/transpose(jvp(chij,cjhp->cihp))/dot_general | solution.py:132
  159.4 7.5 %fusion.38 = (f32[256,32]{0,1:T(8,128)}, f32[1,256,32,64]{1,3,2,0:T(8,128)S(1)}) fusion(f32[1,256,32,64]{1,3,2,0:T(8,128)S(1)} %bitcast.346, f32[256,32]{0,1:T(8,128)S(1)} %get-tuple-element.73, f32[32,64,256]{2,1,0:T(8,128)S(1)} %bitcast.320, f32[256,256]{1,0:T(8,128)S(1)} %fusion.109, f32[32,256]{1,0:T(8,128)S(1)} %copy-done.42, ...), kind=kOutput, calls=%fused_computation.87 | convolution fusion | flops 1618468864 | bytes 6717440 | tf_op jit(solution)/shard_map/transpose(jvp(chij,cjhp->cihp))/dot_general | solution.py:132
  187.3 4.8 %fusion.140 = (f32[2304]{0:T(1024)S(1)}, f32[2304]{0:T(1024)S(1)}, f32[256,2304]{0,1:T(8,128)S(1)}) fusion(f32[256,2304]{0,1:T(8,128)S(1)} %get-tuple-element.65, f32[256,4384]{0,1:T(8,128)} %copy-done.2, f32[2304]{0:T(1024)S(1)} %get-tuple-element.53, f32[255,2304]{0,1:T(8,128)} %slice_multiply_fusion, f32[254,2304]{0,1:T(8,128)} %slice_multiply_fusion.1, ...), kind=kLoop, calls=%fused_computation.337 | loop fusion | flops 4124160 | bytes 14128128 | tf_op jit(solution)/shard_map/transpose(jvp())/reduce_sum | solution.py:104
  192.3 2.7 fusion.25
  194.9 3.0 fusion.8
  198.7 4.4 %fusion.129 = f32[2048,1024]{1,0:T(8,128)S(1)} fusion(bf16[256,2048]{0,1:T(8,128)(2,1)} %get-tuple-element.96, f32[256,1024]{1,0:T(8,128)} %param.13), kind=kOutput, calls=%fused_computation.326 | convolution fusion | flops 1074003968 | bytes 10485760 | tf_op jit(solution)/shard_map/dot_general | solution.py:76
  206.4 5.9 %fusion.48 = f32[256,8,1,64]{0,3,1,2:T(8,128)S(1)} fusion(bf16[8,64,4384]{2,1,0:T(8,128)(2,1)} %bitcast.323, bf16[256,4384]{0,1:T(8,128)(2,1)S(1)} %copy-done.25), kind=kOutput, calls=%fused_computation.124 | convolution fusion | flops 1149239296 | bytes 7258112 | tf_op jit(solution)/shard_map/dot_general | solution.py:82
  221.0 2.7 collective-permute-start.33
  223.7 3.5 bitcast_add_fusion.1
  231.7 9.4 %bitcast_add_fusion = f32[8,64,4480]{2,1,0:T(8,128)} fusion(bf16[8,64,4480]{2,1,0:T(8,128)(2,1)} %collective-permute-done.13, f32[8,2,64,4480]{3,2,1,0:T(8,128)} %bitcast.315, s32[]{:T(128)S(6)} %select_n.134), kind=kLoop, calls=%fused_computation.3 | loop fusion | flops 4587520 | bytes 22937604 | tf_op jit(solution)/shard_map/add | solution.py:314
  241.2 8.3 %fusion = f32[4,2,64,4480]{3,2,1,0:T(8,128)} fusion(s32[]{:T(128)S(6)} %select_n.154, f32[4,2,64,4480]{3,2,1,0:T(8,128)} %bitcast.318), kind=kLoop, calls=%fused_computation.2 | loop fusion | flops 2293760 | bytes 18350084 | tf_op jit(solution)/shard_map/concatenate | solution.py:155
  249.5 6.4 %slice_bitcast_fusion.3 = (f32[2,64,4480]{2,1,0:T(8,128)S(1)}, f32[2,64,4480]{2,1,0:T(8,128)S(1)}, f32[2,64,4480]{2,1,0:T(8,128)}, f32[2,64,4480]{2,1,0:T(8,128)}) fusion(f32[4,2,64,4480]{3,2,1,0:T(8,128)} %fusion), kind=kLoop, calls=%fused_computation.65 | loop fusion | bytes 18350080 | tf_op jit(solution)/shard_map/squeeze | solution.py:162
  261.9 2.7 collective-permute-start.34
  264.6 7.6 %collective-permute-done.34 = f32[2,8,128]{2,0,1:T(2,128)S(1)} collective-permute-done((f32[2,8,128]{2,0,1:T(2,128)}, f32[2,8,128]{2,0,1:T(2,128)S(1)}, u32[]{:S(2)}, u32[]{:S(2)}) %collective-permute-start.34) | collective-permute-done | bytes 8224 | tf_op jit(solution)/shard_map/ppermute | solution.py:160
  272.2 3.4 collective-permute-start.35
  277.0 2.7 collective-permute-start.26
  281.9 2.7 collective-permute-start.18
  284.8 2.7 collective-permute-start.27
  287.7 7.8 %collective-permute-done.18 = bf16[2,32,4480]{2,1,0:T(8,128)(2,1)S(1)} collective-permute-done((bf16[2,32,4480]{2,1,0:T(8,128)(2,1)S(1)}, bf16[2,32,4480]{2,1,0:T(8,128)(2,1)S(1)}, u32[]{:S(2)}, u32[]{:S(2)}) %collective-permute-start.18) | collective-permute-done | bytes 573472 | tf_op jit(solution)/shard_map/ppermute | solution.py:160
  295.7 10.8 %collective-permute-done.15 = bf16[2,32,4480]{2,1,0:T(8,128)(2,1)S(1)} collective-permute-done((bf16[2,32,4480]{2,1,0:T(8,128)(2,1)S(1)}, bf16[2,32,4480]{2,1,0:T(8,128)(2,1)S(1)}, u32[]{:S(2)}, u32[]{:S(2)}) %collective-permute-start.15) | collective-permute-done | bytes 573472 | tf_op jit(solution)/shard_map/ppermute | solution.py:160
  308.5 6.5 %collective-permute-done.19 = bf16[2,32,4480]{2,1,0:T(8,128)(2,1)S(1)} collective-permute-done((bf16[2,32,4480]{2,1,0:T(8,128)(2,1)S(1)}, bf16[2,32,4480]{2,1,0:T(8,128)(2,1)S(1)}, u32[]{:S(2)}, u32[]{:S(2)}) %collective-permute-start.19) | collective-permute-done | bytes 573472 | tf_op jit(solution)/shard_map/ppermute | solution.py:160
  315.0 3.3 collective-permute-done.16
  322.0 8.8 %collective-permute-done.36 = f32[16,128]{1,0:T(8,128)S(1)} collective-permute-done((f32[16,128]{1,0:T(8,128)S(1)}, f32[16,128]{1,0:T(8,128)S(1)}, u32[]{:S(2)}, u32[]{:S(2)}) %collective-permute-start.36) | collective-permute-done | bytes 8224 | tf_op jit(solution)/shard_map/ppermute | solution.py:175
  340.9 3.1 collective-permute-done.37
  344.2 2.7 collective-permute-start.40
  348.4 3.6 collective-permute-done.40
  352.0 5.7 %collective-permute-done.38 = f32[832,128]{1,0:T(8,128)} collective-permute-done((f32[832,128]{1,0:T(8,128)S(1)}, f32[832,128]{1,0:T(8,128)}, u32[]{:S(2)}, u32[]{:S(2)}) %collective-permute-start.38) | collective-permute-done | bytes 426016 | tf_op jit(solution)/shard_map/ppermute | solution.py:196
  364.0 2.6 copy.114
  371.0 4.0 collective-permute-done.42
  376.7 3.1 collective-permute-done.45
  379.8 2.5 collective-permute-done.44
  387.5 14.3 %collective-permute-start.46 = (f32[64,4480]{1,0:T(8,128)}, f32[64,4480]{1,0:T(8,128)}, u32[]{:S(2)}, u32[]{:S(2)}) collective-permute-start(f32[64,4480]{1,0:T(8,128)} %reshape.673), channel_id=1, source_target_pairs={{0,8},{8,0},{1,9},{9,1},{2,10},{10,2},{3,11},{11,3},{4,12},{12,4},... | collective-permute-start | bytes 3440648 | tf_op jit(solution)/shard_map/ppermute | solution.py:260
  401.8 3.2 fusion.47
  (378 shorter events, 141.7 us)
Async XLA Ops:
  7.2 119.9 %all-gather.3.cloned.1.call-start = ((), (), s32[]{:S(2)}) async-start(), calls=%async_computation | async-start | bytes 2359296 | tf_op jit(solution)/shard_map/all_gather | solution.py:272
  9.8 7.7 %collective-permute-start = (f32[8,1836]{1,0:T(8,128)}, f32[8,1836]{1,0:T(8,128)S(1)}, u32[]{:S(2)}, u32[]{:S(2)}) collective-permute-start(f32[8,1836]{1,0:T(8,128)} %broadcast_select_fusion.3), channel_id=1, source_target_pairs={{0,1},{1,0},{2,3},{3,2},{4,5},{5,4},{6,7},{7,6},{8,9},{9,8},{10,11... | collective-permute-start | bytes 176264 | tf_op jit(solution)/shard_map/ppermute | solution.py:339
  16.2 14.7 %collective-permute-start.3 = (bf16[64,4384]{1,0:T(8,128)(2,1)S(1)}, bf16[64,4384]{1,0:T(8,128)(2,1)}, u32[]{:S(2)}, u32[]{:S(2)}) collective-permute-start(bf16[64,4384]{1,0:T(8,128)(2,1)S(1)} %copy.120), channel_id=1, source_target_pairs={{0,1},{1,0},{2,3},{3,2},{4,5},{5,4},{6,7},{7,6},{8,9},{9,8},{10,11... | collective-permute-start | bytes 1683464 | tf_op jit(solution)/shard_map/ppermute | solution.py:242
  17.6 3.8 collective-permute-start.1
  21.5 6.5 %collective-permute-start.2 = (f32[8,1836]{1,0:T(8,128)S(1)}, f32[8,1836]{1,0:T(8,128)S(1)}, u32[]{:S(2)}, u32[]{:S(2)}) collective-permute-start(f32[8,1836]{1,0:T(8,128)S(1)} %fusion.169), channel_id=1, source_target_pairs={{0,4},{2,6},{4,0},{6,2},{1,5},{3,7},{5,1},{7,3},{8,12},{10,14},{12... | collective-permute-start | bytes 176264 | tf_op jit(solution)/shard_map/ppermute | solution.py:339
  33.4 45.8 %collective-permute-start.4 = (bf16[2,64,4384]{2,1,0:T(8,128)(2,1)S(1)}, bf16[2,64,4384]{2,1,0:T(8,128)(2,1)S(1)}, u32[]{:S(2)}, u32[]{:S(2)}) collective-permute-start(bf16[2,64,4384]{2,1,0:T(8,128)(2,1)S(1)} %get-tuple-element.79), channel_id=1, source_target_pairs={{0,6},{2,0},{4,2},{6,4},{1,7},{3,1},{5,3},{7,5},{8,14},{10,8},{12,... | collective-permute-start | bytes 3366920 | tf_op jit(solution)/shard_map/ppermute | solution.py:245
  36.2 42.9 %collective-permute-start.5 = (bf16[2,64,4384]{2,1,0:T(8,128)(2,1)S(1)}, bf16[2,64,4384]{2,1,0:T(8,128)(2,1)S(1)}, u32[]{:S(2)}, u32[]{:S(2)}) collective-permute-start(bf16[2,64,4384]{2,1,0:T(8,128)(2,1)S(1)} %get-tuple-element.79), channel_id=1, source_target_pairs={{0,2},{2,4},{4,6},{6,0},{1,3},{3,5},{5,7},{7,1},{8,10},{10,12},{12... | collective-permute-start | bytes 3366920 | tf_op jit(solution)/shard_map/ppermute | solution.py:244
  36.2 7.1 %collective-permute-start.8 = (bf16[64,4384]{1,0:T(8,128)(2,1)}, bf16[64,4384]{1,0:T(8,128)(2,1)S(1)}, u32[]{:S(2)}, u32[]{:S(2)}) collective-permute-start(bf16[64,4384]{1,0:T(8,128)(2,1)} %collective-permute-done.3), channel_id=1, source_target_pairs={{0,8},{8,0},{1,9},{9,1},{2,10},{10,2},{3,11},{11,3},{4,12},{12,4},... | collective-permute-start | bytes 1683464 | tf_op jit(solution)/shard_map/ppermute | solution.py:260
  79.2 12.9 %collective-permute-start.6 = (bf16[2,32,4384]{2,1,0:T(8,128)(2,1)S(1)}, bf16[2,32,4384]{2,1,0:T(8,128)(2,1)S(1)}, u32[]{:S(2)}, u32[]{:S(2)}) collective-permute-start(bf16[2,32,4384]{2,1,0:T(8,128)(2,1)S(1)} %slice.418), channel_id=1, source_target_pairs={{0,2},{2,4},{4,6},{6,0},{1,3},{3,5},{5,7},{7,1},{8,10},{10,12},{12... | collective-permute-start | bytes 1683464 | tf_op jit(solution)/shard_map/ppermute | solution.py:247
  79.3 12.8 %collective-permute-start.7 = (bf16[2,32,4384]{2,1,0:T(8,128)(2,1)S(1)}, bf16[2,32,4384]{2,1,0:T(8,128)(2,1)S(1)}, u32[]{:S(2)}, u32[]{:S(2)}) collective-permute-start(bf16[2,32,4384]{2,1,0:T(8,128)(2,1)S(1)} %slice.419), channel_id=1, source_target_pairs={{0,6},{2,0},{4,2},{6,4},{1,7},{3,1},{5,3},{7,5},{8,14},{10,8},{12,... | collective-permute-start | bytes 1683464 | tf_op jit(solution)/shard_map/ppermute | solution.py:248
  82.0 26.0 %collective-permute-start.9 = (bf16[2,64,4384]{2,1,0:T(8,128)(2,1)S(1)}, bf16[2,64,4384]{2,1,0:T(8,128)(2,1)S(1)}, u32[]{:S(2)}, u32[]{:S(2)}) collective-permute-start(bf16[2,64,4384]{2,1,0:T(8,128)(2,1)S(1)} %collective-permute-done.4), channel_id=1, source_target_pairs={{0,8},{8,0},{1,9},{9,1},{2,10},{10,2},{3,11},{11,3},{4,12},{12,4},... | collective-permute-start | bytes 3366920 | tf_op jit(solution)/shard_map/ppermute | solution.py:260
  85.4 22.9 %collective-permute-start.11 = (bf16[2,64,4384]{2,1,0:T(8,128)(2,1)S(1)}, bf16[2,64,4384]{2,1,0:T(8,128)(2,1)S(1)}, u32[]{:S(2)}, u32[]{:S(2)}) collective-permute-start(bf16[2,64,4384]{2,1,0:T(8,128)(2,1)S(1)} %collective-permute-done.5), channel_id=1, source_target_pairs={{0,8},{8,0},{1,9},{9,1},{2,10},{10,2},{3,11},{11,3},{4,12},{12,4},... | collective-permute-start | bytes 3366920 | tf_op jit(solution)/shard_map/ppermute | solution.py:260
  92.2 16.0 %collective-permute-start.10 = (bf16[2,64,4384]{2,1,0:T(8,128)(2,1)S(1)}, bf16[2,64,4384]{2,1,0:T(8,128)(2,1)S(1)}, u32[]{:S(2)}, u32[]{:S(2)}) collective-permute-start(bf16[2,64,4384]{2,1,0:T(8,128)(2,1)S(1)} %constant_dynamic-update-slice_fusion), channel_id=1, source_target_pairs={{0,8},{8,0},{1,9},{9,1},{2,10},{10,2},{3,11},{11,3},{4,12},{12,4},... | collective-permute-start | bytes 3366920 | tf_op jit(solution)/shard_map/ppermute | solution.py:260
  127.1 14.0 %collective-permute-start.12 = (bf16[8,128,1024]{2,1,0:T(8,128)(2,1)}, bf16[8,128,1024]{2,1,0:T(8,128)(2,1)S(1)}, u32[]{:S(2)}, u32[]{:S(2)}) collective-permute-start(bf16[8,128,1024]{2,1,0:T(8,128)(2,1)} %bitcast.329), channel_id=1, source_target_pairs={{0,8},{8,0},{1,9},{9,1},{2,10},{10,2},{3,11},{11,3},{4,12},{12,4},... | collective-permute-start | bytes 6291464 | tf_op jit(solution)/shard_map/ppermute | solution.py:260
  198.0 33.7 %collective-permute-start.13 = (bf16[8,64,4480]{2,1,0:T(8,128)(2,1)}, bf16[8,64,4480]{2,1,0:T(8,128)(2,1)}, u32[]{:S(2)}, u32[]{:S(2)}) collective-permute-start(bf16[8,64,4480]{2,1,0:T(8,128)(2,1)} %fusion.8), channel_id=1, source_target_pairs={{0,8},{8,0},{1,9},{9,1},{2,10},{10,2},{3,11},{11,3},{4,12},{12,4},... | collective-permute-start | bytes 13762568 | tf_op jit(solution)/shard_map/ppermute | solution.py:260
  204.8 18.9 %collective-permute-start.21 = (bf16[8,128,1024]{2,1,0:T(8,128)(2,1)}, bf16[8,128,1024]{2,1,0:T(8,128)(2,1)}, u32[]{:S(2)}, u32[]{:S(2)}) collective-permute-start(bf16[8,128,1024]{2,1,0:T(8,128)(2,1)} %fusion.33), channel_id=1, source_target_pairs={{0,8},{8,0},{1,9},{9,1},{2,10},{10,2},{3,11},{11,3},{4,12},{12,4},... | collective-permute-start | bytes 6291464 | tf_op jit(solution)/shard_map/ppermute | solution.py:260
  221.0 40.3 %collective-permute-start.33 = (f32[2,8,128]{2,0,1:T(2,128)}, f32[2,8,128]{2,0,1:T(2,128)S(1)}, u32[]{:S(2)}, u32[]{:S(2)}) collective-permute-start(f32[2,8,128]{2,0,1:T(2,128)} %slice.470), channel_id=1, source_target_pairs={{0,6},{2,0},{4,2},{6,4},{1,7},{3,1},{5,3},{7,5},{8,14},{10,8},{12,... | collective-permute-start | bytes 24584 | tf_op jit(solution)/shard_map/ppermute | solution.py:160
  229.7 45.9 %collective-permute-start.25 = (bf16[2,64,1024]{2,1,0:T(8,128)(2,1)S(1)}, bf16[2,64,1024]{2,1,0:T(8,128)(2,1)S(1)}, u32[]{:S(2)}, u32[]{:S(2)}) collective-permute-start(bf16[2,64,1024]{2,1,0:T(8,128)(2,1)S(1)} %slice.603), channel_id=1, source_target_pairs={{0,6},{2,0},{4,2},{6,4},{1,7},{3,1},{5,3},{7,5},{8,14},{10,8},{12,... | collective-permute-start | bytes 786440 | tf_op jit(solution)/shard_map/ppermute | solution.py:160
  230.9 44.7 %collective-permute-start.22 = (bf16[2,64,1024]{2,1,0:T(8,128)(2,1)S(1)}, bf16[2,64,1024]{2,1,0:T(8,128)(2,1)}, u32[]{:S(2)}, u32[]{:S(2)}) collective-permute-start(bf16[2,64,1024]{2,1,0:T(8,128)(2,1)S(1)} %slice.604), channel_id=1, source_target_pairs={{0,2},{2,4},{4,6},{6,0},{1,3},{3,5},{5,7},{7,1},{8,10},{10,12},{12... | collective-permute-start | bytes 786440 | tf_op jit(solution)/shard_map/ppermute | solution.py:160
  258.1 21.6 %collective-permute-start.17 = (bf16[2,32,4480]{2,1,0:T(8,128)(2,1)}, bf16[2,32,4480]{2,1,0:T(8,128)(2,1)S(1)}, u32[]{:S(2)}, u32[]{:S(2)}) collective-permute-start(bf16[2,32,4480]{2,1,0:T(8,128)(2,1)} %slice.601), channel_id=1, source_target_pairs={{0,6},{2,0},{4,2},{6,4},{1,7},{3,1},{5,3},{7,5},{8,14},{10,8},{12,... | collective-permute-start | bytes 1720328 | tf_op jit(solution)/shard_map/ppermute | solution.py:160
  261.3 18.5 %collective-permute-start.14 = (bf16[2,32,4480]{2,1,0:T(8,128)(2,1)}, bf16[2,32,4480]{2,1,0:T(8,128)(2,1)}, u32[]{:S(2)}, u32[]{:S(2)}) collective-permute-start(bf16[2,32,4480]{2,1,0:T(8,128)(2,1)} %slice.602), channel_id=1, source_target_pairs={{0,2},{2,4},{4,6},{6,0},{1,3},{3,5},{5,7},{7,1},{8,10},{10,12},{12... | collective-permute-start | bytes 1720328 | tf_op jit(solution)/shard_map/ppermute | solution.py:160
  261.9 10.3 %collective-permute-start.34 = (f32[2,8,128]{2,0,1:T(2,128)}, f32[2,8,128]{2,0,1:T(2,128)S(1)}, u32[]{:S(2)}, u32[]{:S(2)}) collective-permute-start(f32[2,8,128]{2,0,1:T(2,128)} %slice_add_fusion.15), channel_id=1, source_target_pairs={{0,6},{2,0},{4,2},{6,4},{1,7},{3,1},{5,3},{7,5},{8,14},{10,8},{12,... | collective-permute-start | bytes 24584 | tf_op jit(solution)/shard_map/ppermute | solution.py:160
  272.2 48.2 %collective-permute-start.35 = (f32[2,8,128]{2,0,1:T(2,128)S(1)}, f32[2,8,128]{2,0,1:T(2,128)S(1)}, u32[]{:S(2)}, u32[]{:S(2)}) collective-permute-start(f32[2,8,128]{2,0,1:T(2,128)S(1)} %get-tuple-element.130), channel_id=1, source_target_pairs={{0,6},{2,0},{4,2},{6,4},{1,7},{3,1},{5,3},{7,5},{8,14},{10,8},{12,... | collective-permute-start | bytes 24584 | tf_op jit(solution)/shard_map/ppermute | solution.py:160
  275.6 9.0 %collective-permute-start.30 = (f32[2,8,128]{2,0,1:T(2,128)S(1)}, f32[2,8,128]{2,0,1:T(2,128)S(1)}, u32[]{:S(2)}, u32[]{:S(2)}) collective-permute-start(f32[2,8,128]{2,0,1:T(2,128)S(1)} %get-tuple-element.131), channel_id=1, source_target_pairs={{0,2},{2,4},{4,6},{6,0},{1,3},{3,5},{5,7},{7,1},{8,10},{10,12},{12... | collective-permute-start | bytes 24584 | tf_op jit(solution)/shard_map/ppermute | solution.py:160
  277.0 7.7 %collective-permute-start.26 = (bf16[2,64,1024]{2,1,0:T(8,128)(2,1)S(1)}, bf16[2,64,1024]{2,1,0:T(8,128)(2,1)S(1)}, u32[]{:S(2)}, u32[]{:S(2)}) collective-permute-start(bf16[2,64,1024]{2,1,0:T(8,128)(2,1)S(1)} %get-tuple-element.109), channel_id=1, source_target_pairs={{0,6},{2,0},{4,2},{6,4},{1,7},{3,1},{5,3},{7,5},{8,14},{10,8},{12,... | collective-permute-start | bytes 786440 | tf_op jit(solution)/shard_map/ppermute | solution.py:160
  279.8 7.8 %collective-permute-start.23 = (bf16[2,64,1024]{2,1,0:T(8,128)(2,1)S(1)}, bf16[2,64,1024]{2,1,0:T(8,128)(2,1)S(1)}, u32[]{:S(2)}, u32[]{:S(2)}) collective-permute-start(bf16[2,64,1024]{2,1,0:T(8,128)(2,1)S(1)} %get-tuple-element.110), channel_id=1, source_target_pairs={{0,2},{2,4},{4,6},{6,0},{1,3},{3,5},{5,7},{7,1},{8,10},{10,12},{12... | collective-permute-start | bytes 786440 | tf_op jit(solution)/shard_map/ppermute | solution.py:160
  281.9 13.6 %collective-permute-start.18 = (bf16[2,32,4480]{2,1,0:T(8,128)(2,1)S(1)}, bf16[2,32,4480]{2,1,0:T(8,128)(2,1)S(1)}, u32[]{:S(2)}, u32[]{:S(2)}) collective-permute-start(bf16[2,32,4480]{2,1,0:T(8,128)(2,1)S(1)} %get-tuple-element.94), channel_id=1, source_target_pairs={{0,6},{2,0},{4,2},{6,4},{1,7},{3,1},{5,3},{7,5},{8,14},{10,8},{12,... | collective-permute-start | bytes 1720328 | tf_op jit(solution)/shard_map/ppermute | solution.py:160
  284.6 23.0 %collective-permute-start.31 = (f32[2,8,128]{2,0,1:T(2,128)S(1)}, f32[2,8,128]{2,0,1:T(2,128)S(1)}, u32[]{:S(2)}, u32[]{:S(2)}) collective-permute-start(f32[2,8,128]{2,0,1:T(2,128)S(1)} %slice_add_fusion.18), channel_id=1, source_target_pairs={{0,2},{2,4},{4,6},{6,0},{1,3},{3,5},{5,7},{7,1},{8,10},{10,12},{12... | collective-permute-start | bytes 24584 | tf_op jit(solution)/shard_map/ppermute | solution.py:160
  284.8 23.3 %collective-permute-start.27 = (bf16[2,64,1024]{2,1,0:T(8,128)(2,1)S(1)}, bf16[2,64,1024]{2,1,0:T(8,128)(2,1)S(1)}, u32[]{:S(2)}, u32[]{:S(2)}) collective-permute-start(bf16[2,64,1024]{2,1,0:T(8,128)(2,1)S(1)} %fusion.92), channel_id=1, source_target_pairs={{0,6},{2,0},{4,2},{6,4},{1,7},{3,1},{5,3},{7,5},{8,14},{10,8},{12,... | collective-permute-start | bytes 786440 | tf_op jit(solution)/shard_map/ppermute | solution.py:160
  287.6 20.6 %collective-permute-start.24 = (bf16[2,64,1024]{2,1,0:T(8,128)(2,1)S(1)}, bf16[2,64,1024]{2,1,0:T(8,128)(2,1)S(1)}, u32[]{:S(2)}, u32[]{:S(2)}) collective-permute-start(bf16[2,64,1024]{2,1,0:T(8,128)(2,1)S(1)} %fusion.94), channel_id=1, source_target_pairs={{0,2},{2,4},{4,6},{6,0},{1,3},{3,5},{5,7},{7,1},{8,10},{10,12},{12... | collective-permute-start | bytes 786440 | tf_op jit(solution)/shard_map/ppermute | solution.py:160
  295.5 10.9 %collective-permute-start.15 = (bf16[2,32,4480]{2,1,0:T(8,128)(2,1)S(1)}, bf16[2,32,4480]{2,1,0:T(8,128)(2,1)S(1)}, u32[]{:S(2)}, u32[]{:S(2)}) collective-permute-start(bf16[2,32,4480]{2,1,0:T(8,128)(2,1)S(1)} %get-tuple-element.95), channel_id=1, source_target_pairs={{0,2},{2,4},{4,6},{6,0},{1,3},{3,5},{5,7},{7,1},{8,10},{10,12},{12... | collective-permute-start | bytes 1720328 | tf_op jit(solution)/shard_map/ppermute | solution.py:160
  306.5 8.6 %collective-permute-start.19 = (bf16[2,32,4480]{2,1,0:T(8,128)(2,1)S(1)}, bf16[2,32,4480]{2,1,0:T(8,128)(2,1)S(1)}, u32[]{:S(2)}, u32[]{:S(2)}) collective-permute-start(bf16[2,32,4480]{2,1,0:T(8,128)(2,1)S(1)} %fusion.64), channel_id=1, source_target_pairs={{0,6},{2,0},{4,2},{6,4},{1,7},{3,1},{5,3},{7,5},{8,14},{10,8},{12,... | collective-permute-start | bytes 1720328 | tf_op jit(solution)/shard_map/ppermute | solution.py:160
  307.6 10.7 %collective-permute-start.16 = (bf16[2,32,4480]{2,1,0:T(8,128)(2,1)S(1)}, bf16[2,32,4480]{2,1,0:T(8,128)(2,1)S(1)}, u32[]{:S(2)}, u32[]{:S(2)}) collective-permute-start(bf16[2,32,4480]{2,1,0:T(8,128)(2,1)S(1)} %fusion.66), channel_id=1, source_target_pairs={{0,2},{2,4},{4,6},{6,0},{1,3},{3,5},{5,7},{7,1},{8,10},{10,12},{12... | collective-permute-start | bytes 1720328 | tf_op jit(solution)/shard_map/ppermute | solution.py:160
  308.1 12.3 %collective-permute-start.32 = (f32[2,8,128]{2,0,1:T(2,128)S(1)}, f32[2,8,128]{2,0,1:T(2,128)S(1)}, u32[]{:S(2)}, u32[]{:S(2)}) collective-permute-start(f32[2,8,128]{2,0,1:T(2,128)S(1)} %slice_add_fusion.17), channel_id=1, source_target_pairs={{0,2},{2,4},{4,6},{6,0},{1,3},{3,5},{5,7},{7,1},{8,10},{10,12},{12... | collective-permute-start | bytes 24584 | tf_op jit(solution)/shard_map/ppermute | solution.py:160
  308.4 22.4 %collective-permute-start.28 = (bf16[128,1024]{1,0:T(8,128)(2,1)S(1)}, bf16[128,1024]{1,0:T(8,128)(2,1)}, u32[]{:S(2)}, u32[]{:S(2)}) collective-permute-start(bf16[128,1024]{1,0:T(8,128)(2,1)S(1)} %fusion.103), channel_id=1, source_target_pairs={{0,1},{1,0},{2,3},{3,2},{4,5},{5,4},{6,7},{7,6},{8,9},{9,8},{10,11... | collective-permute-start | bytes 786440 | tf_op jit(solution)/shard_map/ppermute | solution.py:175
  320.4 13.3 %collective-permute-start.20 = (bf16[64,4480]{1,0:T(8,128)(2,1)}, bf16[64,4480]{1,0:T(8,128)(2,1)}, u32[]{:S(2)}, u32[]{:S(2)}) collective-permute-start(bf16[64,4480]{1,0:T(8,128)(2,1)} %fusion.86), channel_id=1, source_target_pairs={{0,1},{1,0},{2,3},{3,2},{4,5},{5,4},{6,7},{7,6},{8,9},{9,8},{10,11... | collective-permute-start | bytes 1720328 | tf_op jit(solution)/shard_map/ppermute | solution.py:175
  320.5 10.3 %collective-permute-start.36 = (f32[16,128]{1,0:T(8,128)S(1)}, f32[16,128]{1,0:T(8,128)S(1)}, u32[]{:S(2)}, u32[]{:S(2)}) collective-permute-start(f32[16,128]{1,0:T(8,128)S(1)} %bitcast.366), channel_id=1, source_target_pairs={{0,1},{1,0},{2,3},{3,2},{4,5},{5,4},{6,7},{7,6},{8,9},{9,8},{10,11... | collective-permute-start | bytes 24584 | tf_op jit(solution)/shard_map/ppermute | solution.py:175
  338.0 6.0 %collective-permute-start.37 = (f32[416,128]{1,0:T(8,128)S(1)}, f32[416,128]{1,0:T(8,128)S(1)}, u32[]{:S(2)}, u32[]{:S(2)}) collective-permute-start(f32[416,128]{1,0:T(8,128)S(1)} %get-tuple-element.101), channel_id=1, source_target_pairs={{0,16},{16,32},{32,48},{48,0},{64,80},{80,96},{96,112},{112,64},{1... | collective-permute-start | bytes 638984 | tf_op jit(solution)/shard_map/ppermute | solution.py:192
  339.3 4.9 %collective-permute-start.39 = (f32[416,128]{1,0:T(8,128)S(1)}, f32[416,128]{1,0:T(8,128)S(1)}, u32[]{:S(2)}, u32[]{:S(2)}) collective-permute-start(f32[416,128]{1,0:T(8,128)S(1)} %get-tuple-element.102), channel_id=1, source_target_pairs={{0,48},{16,0},{32,16},{48,32},{64,112},{80,64},{96,80},{112,96},{1... | collective-permute-start | bytes 638984 | tf_op jit(solution)/shard_map/ppermute | solution.py:193
  344.2 7.8 %collective-permute-start.40 = (f32[832,128]{1,0:T(8,128)S(1)}, f32[832,128]{1,0:T(8,128)}, u32[]{:S(2)}, u32[]{:S(2)}) collective-permute-start(f32[832,128]{1,0:T(8,128)S(1)} %pad_maximum_fusion.1), channel_id=1, source_target_pairs={{0,48},{16,0},{32,16},{48,32},{64,112},{80,64},{96,80},{112,96},{1... | collective-permute-start | bytes 1277960 | tf_op jit(solution)/shard_map/ppermute | solution.py:196
  347.0 10.7 %collective-permute-start.38 = (f32[832,128]{1,0:T(8,128)S(1)}, f32[832,128]{1,0:T(8,128)}, u32[]{:S(2)}, u32[]{:S(2)}) collective-permute-start(f32[832,128]{1,0:T(8,128)S(1)} %pad_maximum_fusion), channel_id=1, source_target_pairs={{0,16},{16,32},{32,48},{48,0},{64,80},{80,96},{96,112},{112,64},{1... | collective-permute-start | bytes 1277960 | tf_op jit(solution)/shard_map/ppermute | solution.py:196
  359.0 8.6 %collective-permute-start.41 = (f32[832,128]{1,0:T(8,128)S(1)}, f32[832,128]{1,0:T(8,128)S(1)}, u32[]{:S(2)}, u32[]{:S(2)}) collective-permute-start(f32[832,128]{1,0:T(8,128)S(1)} %fusion.100), channel_id=1, source_target_pairs={{0,64},{16,80},{32,96},{48,112},{64,0},{80,16},{96,32},{112,48},{1... | collective-permute-start | bytes 1277960 | tf_op jit(solution)/shard_map/ppermute | solution.py:199
  367.7 7.3 %collective-permute-start.42 = (f32[832,128]{1,0:T(8,128)S(1)}, f32[832,128]{1,0:T(8,128)S(1)}, u32[]{:S(2)}, u32[]{:S(2)}) collective-permute-start(f32[832,128]{1,0:T(8,128)S(1)} %get-tuple-element.58), channel_id=1, source_target_pairs={{0,48},{16,0},{32,16},{48,32},{64,112},{80,64},{96,80},{112,96},{1... | collective-permute-start | bytes 1277960 | tf_op jit(solution)/shard_map/ppermute | solution.py:202
  367.8 8.6 %collective-permute-start.43 = (f32[832,128]{1,0:T(8,128)S(1)}, f32[832,128]{1,0:T(8,128)S(1)}, u32[]{:S(2)}, u32[]{:S(2)}) collective-permute-start(f32[832,128]{1,0:T(8,128)S(1)} %get-tuple-element.58), channel_id=1, source_target_pairs={{0,16},{16,32},{32,48},{48,0},{64,80},{80,96},{96,112},{112,64},{1... | collective-permute-start | bytes 1277960 | tf_op jit(solution)/shard_map/ppermute | solution.py:201
  375.0 4.8 %collective-permute-start.45 = (f32[416,128]{1,0:T(8,128)S(1)}, f32[416,128]{1,0:T(8,128)S(1)}, u32[]{:S(2)}, u32[]{:S(2)}) collective-permute-start(f32[416,128]{1,0:T(8,128)S(1)} %slice.482), channel_id=1, source_target_pairs={{0,48},{16,0},{32,16},{48,32},{64,112},{80,64},{96,80},{112,96},{1... | collective-permute-start | bytes 638984 | tf_op jit(solution)/shard_map/ppermute | solution.py:204
  376.3 6.0 %collective-permute-start.44 = (f32[416,128]{1,0:T(8,128)S(1)}, f32[416,128]{1,0:T(8,128)S(1)}, u32[]{:S(2)}, u32[]{:S(2)}) collective-permute-start(f32[416,128]{1,0:T(8,128)S(1)} %slice.481), channel_id=1, source_target_pairs={{0,16},{16,32},{32,48},{48,0},{64,80},{80,96},{96,112},{112,64},{1... | collective-permute-start | bytes 638984 | tf_op jit(solution)/shard_map/ppermute | solution.py:203
  387.5 25.5 %collective-permute-start.46 = (f32[64,4480]{1,0:T(8,128)}, f32[64,4480]{1,0:T(8,128)}, u32[]{:S(2)}, u32[]{:S(2)}) collective-permute-start(f32[64,4480]{1,0:T(8,128)} %reshape.673), channel_id=1, source_target_pairs={{0,8},{8,0},{1,9},{9,1},{2,10},{10,2},{3,11},{11,3},{4,12},{12,4},... | collective-permute-start | bytes 3440648 | tf_op jit(solution)/shard_map/ppermute | solution.py:260
  406.2 5.4 %collective-permute-start.47 = (f32[128,1024]{1,0:T(8,128)S(1)}, f32[128,1024]{1,0:T(8,128)S(1)}, u32[]{:S(2)}, u32[]{:S(2)}) collective-permute-start(f32[128,1024]{1,0:T(8,128)S(1)} %reshape.675), channel_id=1, source_target_pairs={{0,8},{8,0},{1,9},{9,1},{2,10},{10,2},{3,11},{11,3},{4,12},{12,4},... | collective-permute-start | bytes 1572872 | tf_op jit(solution)/shard_map/ppermute | solution.py:260
  (55 other events, 304.0 us)
Sparse Core Ops, SparseCore 0:
  17.2 56.7 all-gather.2
